TPU v7x, 256 devices: a whole 4x4x8 slice. The times are simulated.
256 devices in a mesh: kv: 4 (over y), blk: 64 (over z, x, core).
Axes of the slice: x: 4, y: 4, z: 8, core: 2. Of those that a mesh axis runs over, the one named last changes fastest.
Arguments:
- embeds: bfloat16 [3, 512, 4096], P(None, None, 'blk'), may hold values from -6 to 6
- attn_gain: float32 [4096], P('blk'), may hold values from 0.25 to 1.75
- w_query: bfloat16 [4096, 4096], P('blk', 'kv'), may hold values from -0.1875 to 0.1875
- w_key: bfloat16 [4096, 512], P('blk', 'kv'), may hold values from -0.09375 to 0.09375
- w_value: bfloat16 [4096, 512], P('blk', 'kv'), may hold values from -0.09375 to 0.09375
- w_out: bfloat16 [4096, 4096], P('kv', 'blk'), may hold values from -0.375 to 0.375
- cache_kv: bfloat16 [2048, 4, 2, 128, 128], P('blk', 'kv'), may hold values from -102 to 102, as said below
- lengths: int32 [512], replicated, may hold values from 1 to 8192, as said below
- block_table: int32 [512, 64], replicated, may hold values from 0 to 2048, as said below
- parents: int32 [3, 512], replicated, may hold values from 0 to 511, as said below
Outputs:
- out_rows: bfloat16 [3, 512, 4096], P(None, None, 'blk')
- appended: bfloat16 [3, 512, 4, 2, 128], P(None, 'blk', 'kv')
Inputs may be any that keep to these rules, and one draw needn't show every extreme that they name: `lengths`: one beam holds exactly 8192 tokens. `block_table`: row b names the slots of beam b's blocks of 128 tokens in order; entries at and past ceil(lengths[b] / 128) equal 2048; no slot is named twice. parents[s, b] lies in the aligned group of 8 beams that holds b. `cache_kv`: slots that no row of block_table names are never read.
All inputs are finite; a program needn't handle non-finite values.
Results may differ from a plain program's by a relative error of at most 0.0044.
The roundings to bfloat16 on the way count: a program that leaves them out, or rounds other values in their place, can miss the bound.
Values may be sent and summed in bfloat16 or wider, within the bound.
No kernel may reach another device: no remote copies, remote signals or barrier semaphores. Data moves between devices by JAX's collectives and lax.ppermute only.
A program may use at most 64 MiB of HBM per device.

v0:
```python
import math

import jax
import jax.numpy as jnp
from jax import lax
from jax.sharding import PartitionSpec as P

GROUP = 8


NEGATIVE = -1e30
EPSILON = 1e-05
ROPE_BASE = 5000000.0


def rotate(vector, position):
    half_dim = vector.shape[-1] // 2
    exponent = jnp.arange(half_dim, dtype=jnp.float32) * (2.0 / vector.shape[-1])
    frequency = ROPE_BASE ** (-exponent)
    angles = position.astype(jnp.float32)[:, None] * frequency[None, :]
    target_shape = (position.shape[0],) + (1,) * (vector.ndim - 2) + (half_dim,)
    cosines = jnp.cos(angles).reshape(target_shape)
    sine_part = jnp.sin(angles).reshape(target_shape)
    first_half = vector[..., :half_dim]
    second_half = vector[..., half_dim:]
    return jnp.concatenate(
        [
            first_half * cosines - second_half * sine_part,
            second_half * cosines + first_half * sine_part,
        ],
        axis=-1,
    )


def body(
    embeds, attn_gain, w_query, w_key, w_value, w_out, cache_kv, lengths, block_table, parents
):
    axis_count = lax.axis_size("blk")
    shard_index = lax.axis_index("blk")
    step_total, beam_count, width_part = embeds.shape
    beams_here = beam_count // axis_count
    slot_count = cache_kv.shape[0]
    total_slots = slot_count * axis_count
    block_len = cache_kv.shape[3]
    head_dim = cache_kv.shape[4]
    heads_per_group = w_query.shape[1] // head_dim
    group_count = beam_count // GROUP
    model_width = width_part * axis_count
    scaling = 1.0 / math.sqrt(head_dim)
    row_offset = shard_index * beams_here
    joined_weights = jnp.concatenate([w_query, w_key, w_value], axis=1)
    cached_keys = cache_kv[:, 0, 0]
    cached_values = cache_kv[:, 0, 1]
    max_blocks = block_table.shape[1]
    beam_ids = jnp.broadcast_to(jnp.arange(beam_count, dtype=jnp.int32)[:, None], block_table.shape)
    block_ids = jnp.broadcast_to(
        jnp.arange(max_blocks, dtype=jnp.int32)[None, :], block_table.shape
    )
    flat_table = block_table.reshape(-1)
    owner_all = jnp.full((total_slots + 1,), -1, jnp.int32).at[flat_table].set(beam_ids.reshape(-1))
    logical_all = jnp.zeros((total_slots + 1,), jnp.int32).at[flat_table].set(block_ids.reshape(-1))
    owner_beam = lax.dynamic_slice_in_dim(owner_all, shard_index * slot_count, slot_count)
    logical_block = lax.dynamic_slice_in_dim(logical_all, shard_index * slot_count, slot_count)
    filled = owner_beam >= 0
    safe_owner = jnp.maximum(owner_beam, 0)
    group_of = safe_owner // GROUP
    group_onehot = (
        (group_of[:, None] == jnp.arange(group_count, dtype=jnp.int32)[None, :]) & filled[:, None]
    ).astype(jnp.float32)
    token_index = jnp.arange(block_len, dtype=jnp.int32)
    in_length = (
        logical_block[:, None] * block_len + token_index[None, :] < lengths[safe_owner][:, None]
    )
    members = group_of[:, None] * GROUP + jnp.arange(GROUP, dtype=jnp.int32)[None, :]
    root_beams = jnp.arange(beam_count, dtype=jnp.int32)
    new_keys = jnp.zeros((step_total, beams_here, head_dim), jnp.bfloat16)
    new_values = jnp.zeros((step_total, beams_here, head_dim), jnp.bfloat16)
    outputs = []
    for step_index in range(step_total):
        root_beams = root_beams[parents[step_index]]
        local_parent = (
            lax.dynamic_slice_in_dim(parents[step_index], row_offset, beams_here) - row_offset
        )
        new_keys = new_keys[:, local_parent]
        new_values = new_values[:, local_parent]
        stream = embeds[step_index].astype(jnp.float32)
        squares = lax.psum(jnp.sum(stream * stream, axis=1), "blk")
        inverse_rms = lax.rsqrt(squares / model_width + EPSILON)
        normed = (stream * inverse_rms[:, None] * attn_gain[None, :]).astype(jnp.bfloat16)
        projected = lax.psum_scatter(
            jnp.dot(normed, joined_weights, preferred_element_type=jnp.float32),
            "blk",
            scatter_dimension=0,
            tiled=True,
        )
        position = (
            lax.dynamic_slice_in_dim(lengths[root_beams], row_offset, beams_here) + step_index
        )
        rotated_query = rotate(
            projected[:, : heads_per_group * head_dim].reshape(
                beams_here, heads_per_group, head_dim
            ),
            position,
        ).astype(jnp.bfloat16)
        key_new = rotate(
            projected[:, heads_per_group * head_dim : (heads_per_group + 1) * head_dim], position
        ).astype(jnp.bfloat16)
        value_new = projected[:, (heads_per_group + 1) * head_dim :].astype(jnp.bfloat16)
        new_keys = new_keys.at[step_index].set(key_new)
        new_values = new_values.at[step_index].set(value_new)
        queries = lax.all_gather(
            rotated_query.reshape(beams_here, heads_per_group * head_dim), "blk", axis=0, tiled=True
        )
        slot_query = queries.reshape(group_count, GROUP * heads_per_group, head_dim)[group_of]
        scores = (
            jnp.einsum("sqd,skd->sqk", slot_query, cached_keys, preferred_element_type=jnp.float32)
            * scaling
        )
        scores = scores.reshape(slot_count, GROUP, heads_per_group, block_len)
        active = ((root_beams[members] == owner_beam[:, None])[:, :, None] & in_length[:, None, :])[
            :, :, None, :
        ]
        slot_top = jnp.max(jnp.where(active, scores, NEGATIVE), axis=-1)
        group_top = jnp.max(
            jnp.where(group_onehot[:, :, None, None] > 0, slot_top[:, None], NEGATIVE), axis=0
        ).reshape(beam_count, heads_per_group)
        latest_key_rows = new_keys[: step_index + 1]
        new_scores = (
            jnp.einsum(
                "pam,fpm->paf", rotated_query, latest_key_rows, preferred_element_type=jnp.float32
            )
            * scaling
        )
        own_top = jnp.maximum(
            lax.dynamic_slice_in_dim(group_top, row_offset, beams_here),
            jnp.max(new_scores, axis=-1),
        )
        local_top = lax.dynamic_update_slice_in_dim(group_top, own_top, row_offset, 0)
        ceiling = lax.pmax(local_top, "blk")
        slot_ceiling = ceiling.reshape(group_count, GROUP, heads_per_group)[group_of]
        prob_weights = jnp.exp(jnp.where(active, scores - slot_ceiling[..., None], NEGATIVE))
        slot_denominator = jnp.sum(prob_weights, axis=-1)
        slot_numer = jnp.einsum(
            "sgqk,skd->sgqd",
            prob_weights.astype(jnp.bfloat16),
            cached_values,
            preferred_element_type=jnp.float32,
        )
        numerator = jnp.einsum(
            "sg,sx->gx",
            group_onehot,
            slot_numer.reshape(slot_count, -1),
            precision=lax.Precision.HIGHEST,
        ).reshape(beam_count, heads_per_group, head_dim)
        denominator = jnp.einsum(
            "sg,sx->gx",
            group_onehot,
            slot_denominator.reshape(slot_count, -1),
            precision=lax.Precision.HIGHEST,
        ).reshape(beam_count, heads_per_group)
        own_ceiling = lax.dynamic_slice_in_dim(ceiling, row_offset, beams_here)
        new_weights = jnp.exp(new_scores - own_ceiling[..., None])
        updated_denominator = jnp.sum(new_weights, axis=-1)
        new_numer = jnp.einsum(
            "pjz,zpc->pjc",
            new_weights.astype(jnp.bfloat16),
            new_values[: step_index + 1],
            preferred_element_type=jnp.float32,
        )
        numerator, denominator = (
            lax.psum_scatter(numerator, "blk", scatter_dimension=0, tiled=True),
            lax.psum_scatter(denominator, "blk", scatter_dimension=0, tiled=True),
        )
        own_rows = (
            ((numerator + new_numer) / (denominator + updated_denominator)[..., None])
            .astype(jnp.bfloat16)
            .reshape(beams_here, heads_per_group * head_dim)
        )
        attended = lax.all_gather(own_rows, "blk", axis=0, tiled=True)
        partial_value = jnp.dot(attended, w_out, preferred_element_type=jnp.float32)
        head_total = lax.psum(partial_value, "kv")
        outputs.append((stream + head_total).astype(jnp.bfloat16))
    appended = jnp.stack([new_keys, new_values], axis=2)[:, :, None]
    return (jnp.stack(outputs), appended)


def solution(mesh):
    return jax.shard_map(
        body,
        mesh=mesh,
        in_specs=(
            P(None, None, "blk"),
            P("blk"),
            P("blk", "kv"),
            P("blk", "kv"),
            P("blk", "kv"),
            P("kv", "blk"),
            P("blk", "kv", None, None, None),
            P(),
            P(),
            P(),
        ),
        out_specs=(P(None, None, "blk"), P(None, "blk", "kv", None, None)),
        check_vma=False,
    )
```

profile of v0, /device:TPU:1, one launch (start us, length us, event | category | flops | bytes accessed | tf_op | source)
XLA Modules:
  0.0 1691.2 jit_solution(13006681837210420839)
XLA Ops:
  9.2 130.0 %all-reduce.7 = (f32[512]{0:T(512)S(1)}, f32[512]{0:T(512)S(1)}, f32[512]{0:T(512)S(1)}) all-reduce(f32[512]{0:T(512)S(1)} %get-tuple-element.102, f32[512]{0:T(512)S(1)} %get-tuple-element.101, f32[512]{0:T(512)S(1)} %get-tuple-element.100), channel_id=1, replica_groups=mesh['kv'=4,'blk'=64] {'blk'}, use_global_device_ids=true, to_apply=%region_25.26 | all-reduce | flops 1536 | bytes 12288 | tf_op jit(solution)/shard_map/psum | solution.py:87
  140.7 3.0 fusion.73
  143.7 2.1 fusion.76
  145.8 2.2 fusion.79
  148.7 3.5 gather_fusion
  152.3 3.5 gather_fusion.6
  155.9 3.5 gather_fusion.3
  159.4 3.5 gather_fusion.14
  162.9 3.5 gather_fusion.16
  166.5 3.5 gather_fusion.8
  171.8 178.1 %all-reduce.14.cloned.1.call-done = (f32[512,1280]{1,0:T(8,128)}, f32[512,1280]{1,0:T(8,128)}, f32[512,1280]{1,0:T(8,128)}) async-done(((f32[512,1280]{1,0:T(8,128)}, f32[512,1280]{1,0:T(8,128)}, f32[512,1280]{1,0:T(8,128)}), (f32[512,1280]{1,0:T(8,128)}, f32[512,1280]{1,0:T(8,128)}, f32[512,1280]{1,0:T(8,128)})) %all-reduce.14.cloned.1.call-update) | async-done | bytes 7864336
  352.7 120.1 %scatter_custom_fusion = s32[2049]{0:T(1024)S(1)} fusion(s32[32768]{0:T(1024)S(1)} %bitcast.296, s32[32768]{0:T(1024)S(1)} %reshape.1134, s32[]{:T(128)} %constant.196.clone.1), kind=kCustom, calls=%fused_computation.206 | custom fusion | bytes 8200 | tf_op jit(solution)/shard_map/scatter | solution.py:60
  474.8 1.9 gather_fusion.15
  476.7 1.9 gather_fusion.7
  478.7 1.9 gather_fusion.1
  481.7 120.1 %scatter_custom_fusion.1 = s32[2049]{0:T(1024)S(1)} fusion(s32[32768]{0:T(1024)S(1)} %bitcast.297, s32[32768]{0:T(1024)S(1)} %reshape.1142, s32[]{:T(128)} %constant.197.clone.1), kind=kCustom, calls=%fused_computation.204 | custom fusion | bytes 8200 | tf_op jit(solution)/shard_map/scatter | solution.py:61
  614.9 1.9 fusion.9
  619.1 2.3 reshape.931
  621.4 2.8 gather_fusion.4
  624.1 2.8 fusion.6
  629.1 52.4 %all-gather.15.cloned.1.call-done = bf16[512,1024]{1,0:T(8,128)(2,1)} async-done(((bf16[8,1024]{1,0:T(8,128)(2,1)}), bf16[512,1024]{1,0:T(8,128)(2,1)}) %all-gather.15.cloned.1.call-update) | async-done | bytes 1048592 | tf_op jit(solution)/shard_map/all_gather | solution.py:111
  681.5 2.3 reshape.950
  683.8 2.8 gather_fusion.17
  686.6 2.9 fusion.12
  691.6 2.5 select_reduce_fusion.2
  694.2 1.6 copy.294
  708.0 1.6 copy.319
  709.6 1.7 reshape.952
  718.1 243.1 %all-reduce.9 = (f32[512,8]{0,1:T(8,128)}, f32[512,8]{0,1:T(8,128)}, f32[512,8]{0,1:T(8,128)}) all-reduce(f32[512,8]{0,1:T(8,128)} %dynamic_update_slice.11, f32[512,8]{0,1:T(8,128)S(1)} %dynamic_update_slice.10, f32[512,8]{0,1:T(8,128)} %copy-done.7), channel_id=1, replica_groups=mesh['kv'=4,'blk'=64] {'blk'}, use_global_device_ids=true, to_apply=%region_30.31 | all-reduce | flops 12288 | bytes 98304 | tf_op jit(solution)/shard_map/pmax | solution.py:139
  962.8 2.3 gather_fusion.5
  965.1 1.8 fusion.28
  966.8 3.1 fusion.21
  969.9 2.7 reshape.936
  974.3 2.3 gather_fusion.12
  978.1 3.1 fusion.18
  981.2 2.7 reshape.945
  985.5 2.3 gather_fusion.19
  987.8 1.7 fusion.24
  989.5 1.7 fusion.15
  1007.2 253.0 %all-reduce.6 = (f32[512,8]{1,0:T(8,128)S(1)}, f32[512,8]{1,0:T(8,128)S(1)}, f32[512,8]{1,0:T(8,128)S(1)}) all-reduce(f32[512,8]{1,0:T(8,128)S(1)} %reshape.957, f32[512,8]{1,0:T(8,128)S(1)} %reshape.947, f32[512,8]{1,0:T(8,128)S(1)} %reshape.937), channel_id=10, replica_groups=mesh['kv'=4,'blk'=64] {'blk'}, use_global_device_ids=true, to_apply=%region_33.34.clone | all-reduce | flops 12288 | bytes 98304
  1269.1 129.5 %reduce-scatter.8.cloned.1.call-done = f32[8,8,128]{2,1,0:T(8,128)} async-done(((f32[512,8,128]{2,1,0:T(8,128)}), f32[8,8,128]{2,1,0:T(8,128)}) %reduce-scatter.8.cloned.1.call-update) | async-done | bytes 32784 | tf_op jit(solution)/shard_map/reduce_scatter | solution.py:171
  1400.3 81.7 %all-gather.9.cloned.1.call-done = bf16[512,1024]{1,0:T(8,128)(2,1)} async-done(((bf16[8,1024]{1,0:T(8,128)(2,1)}), bf16[512,1024]{1,0:T(8,128)(2,1)}) %all-gather.9.cloned.1.call-update) | async-done | bytes 1048592 | tf_op jit(solution)/shard_map/all_gather | solution.py:179
  1482.0 2.3 fusion.158
  1484.3 74.9 %all-gather.13.cloned.1.call-done = bf16[512,1024]{1,0:T(8,128)(2,1)} async-done(((bf16[8,1024]{1,0:T(8,128)(2,1)}), bf16[512,1024]{1,0:T(8,128)(2,1)}) %all-gather.13.cloned.1.call-update) | async-done | bytes 1048592 | tf_op jit(solution)/shard_map/all_gather | solution.py:179
  1559.2 2.3 fusion.159
  1561.5 75.3 %all-gather.17.cloned.1.call-done = bf16[512,1024]{1,0:T(8,128)(2,1)} async-done(((bf16[8,1024]{1,0:T(8,128)(2,1)}), bf16[512,1024]{1,0:T(8,128)(2,1)}) %all-gather.17.cloned.1.call-update) | async-done | bytes 1048592 | tf_op jit(solution)/shard_map/all_gather | solution.py:179
  1636.9 2.3 fusion.160
  1639.9 43.1 %all-reduce.16.cloned.1.call-done = (f32[512,64]{0,1:T(8,128)}, f32[512,64]{0,1:T(8,128)}, f32[512,64]{0,1:T(8,128)}) async-done(((f32[512,64]{0,1:T(8,128)}, f32[512,64]{0,1:T(8,128)}, f32[512,64]{0,1:T(8,128)}), (f32[512,64]{0,1:T(8,128)}, f32[512,64]{0,1:T(8,128)}, f32[512,64]{0,1:T(8,128)})) %all-reduce.16.cloned.1.call-update) | async-done | bytes 393232 | tf_op jit(solution)/shard_map/psum | solution.py:181
  (255 shorter events, 84.6 us)
Async XLA Ops:
  7.2 1474.8 %copy-start = (bf16[1024,64]{0,1:T(8,128)(2,1)S(1)}, bf16[1024,64]{0,1:T(8,128)(2,1)}, u32[]{:S(2)}) copy-start(bf16[1024,64]{0,1:T(8,128)(2,1)} %param.27) | copy-start | bytes 393220
  7.2 136.5 %copy-start.5 = (bf16[3,512,64]{1,2,0:T(8,128)(2,1)S(1)}, bf16[3,512,64]{1,2,0:T(8,128)(2,1)}, u32[]{:S(2)}) copy-start(bf16[3,512,64]{1,2,0:T(8,128)(2,1)} %param.22) | copy-start | bytes 589828
  7.2 136.5 %copy-start.32 = (f32[64]{0:T(128)S(1)}, f32[64]{0:T(128)}, u32[]{:S(2)}) copy-start(f32[64]{0:T(128)} %param.23) | copy-start | bytes 772
  7.2 342.7 %all-reduce.14.cloned.1.call-start = ((), (), s32[]{:S(2)}) async-start(), calls=%async_computation.12 | async-start | bytes 15728640
  148.0 0.7 copy-start.15
  148.0 463.9 %all-gather.11.cloned.1.call-start = ((), (), s32[]{:S(2)}) async-start(), calls=%async_computation.6 | async-start | bytes 1064960 | tf_op jit(solution)/shard_map/all_gather | solution.py:111
  148.7 7.1 copy-start.1
  155.9 452.6 %copy-start.30 = (s32[1024]{0:T(1024)}, s32[1024]{0:T(1024)S(1)}, u32[]{:S(2)}) copy-start(s32[1024]{0:T(1024)S(1)} %get-tuple-element.185) | copy-start | bytes 12292
  162.9 7.0 copy-start.6
  162.9 7.4 copy-start.33
  352.4 266.6 %all-gather.7.cloned.1.call-start = ((), (), s32[]{:S(2)}) async-start(), calls=%async_computation.3 | async-start | bytes 1064960 | tf_op jit(solution)/shard_map/all_gather | solution.py:111
  472.9 129.1 %copy-start.17 = (pred[32]{0:T(512)(128)(4,1)}, pred[32]{0:T(512)(128)(4,1)S(1)}, u32[]{:S(2)}) copy-start(pred[32]{0:T(512)(128)(4,1)S(1)} %get-tuple-element.121) | copy-start | bytes 100
  473.0 129.1 %copy-start.22 = (s32[32]{0:T(128)}, s32[32]{0:T(128)S(1)}, u32[]{:S(2)}) copy-start(s32[32]{0:T(128)S(1)} %get-tuple-element.124) | copy-start | bytes 388
  474.5 207.0 %all-gather.15.cloned.1.call-start = ((), (), s32[]{:S(2)}) async-start(), calls=%async_computation.9 | async-start | bytes 1064960 | tf_op jit(solution)/shard_map/all_gather | solution.py:111
  481.7 133.2 %copy-start.2 = (bf16[32,1,2,128,128]{4,3,2,1,0:T(8,128)(2,1)S(1)}, bf16[32,1,2,128,128]{4,3,2,1,0:T(8,128)(2,1)}, u32[]{:S(2)}) copy-start(bf16[32,1,2,128,128]{4,3,2,1,0:T(8,128)(2,1)} %param.28) | copy-start | bytes 6291460
  602.0 9.9 copy-start.31
  604.5 656.6 %reduce-scatter.4.cloned.1.call-start = ((), (), s32[]{:S(2)}) async-start(), calls=%async_computation.4 | async-start | bytes 2129920 | tf_op jit(solution)/shard_map/reduce_scatter | solution.py:171
  604.5 10.4 copy-start.27
  609.2 2.8 copy-start.9
  699.1 0.6 copy-start.7
  961.2 5.7 copy-start.18
  961.2 5.7 copy-start.23
  972.7 0.7 copy-start.13
  972.7 292.4 %reduce-scatter.6.cloned.1.call-start = ((), (), s32[]{:S(2)}) async-start(), calls=%async_computation.7 | async-start | bytes 2129920 | tf_op jit(solution)/shard_map/reduce_scatter | solution.py:171
  974.3 3.8 copy-start.19
  974.3 3.8 copy-start.24
  983.9 0.7 copy-start.12
  983.9 414.7 %reduce-scatter.8.cloned.1.call-start = ((), (), s32[]{:S(2)}) async-start(), calls=%async_computation.10 | async-start | bytes 2129920 | tf_op jit(solution)/shard_map/reduce_scatter | solution.py:171
  985.5 4.0 copy-start.20
  985.5 4.0 copy-start.25
  992.7 7.2 copy-start.4
  992.8 13.3 copy-start.3
  992.8 489.2 %all-gather.9.cloned.1.call-start = ((), (), s32[]{:S(2)}) async-start(), calls=%async_computation.5 | async-start | bytes 1064960 | tf_op jit(solution)/shard_map/all_gather | solution.py:179
  1001.4 5.3 copy-start.21
  1001.4 5.3 copy-start.26
  1002.4 257.8 %copy-start.11 = (f32[8,1,8]{0,2,1:T(8,128)S(1)}, f32[8,1,8]{0,2,1:T(8,128)}, u32[]{:S(2)}) copy-start(f32[8,1,8]{0,2,1:T(8,128)} %copy.332) | copy-start | bytes 772
  1002.4 258.7 %copy-start.16 = (f32[8,128]{1,0:T(8,128)S(1)}, f32[8,128]{1,0:T(8,128)}, u32[]{:S(2)}) copy-start(f32[8,128]{1,0:T(8,128)} %get-tuple-element.131) | copy-start | bytes 12292
  1002.6 260.1 %copy-start.29 = (bf16[1,8,128]{2,1,0:T(8,128)(2,1)S(1)}, bf16[1,8,128]{2,1,0:T(8,128)(2,1)}, u32[]{:S(2)}) copy-start(bf16[1,8,128]{2,1,0:T(8,128)(2,1)} %get-tuple-element.132) | copy-start | bytes 6148
  1002.6 260.1 %copy-start.14 = (bf16[3,8,128]{2,0,1:T(4,128)(2,1)S(1)}, bf16[3,8,128]{2,0,1:T(4,128)(2,1)}, u32[]{:S(2)}) copy-start(bf16[3,8,128]{2,0,1:T(4,128)(2,1)} %copy.390) | copy-start | bytes 18436
  1002.6 262.5 %copy-start.28 = (f32[8,8,2]{1,2,0:T(2,128)S(1)}, f32[8,8,2]{1,2,0:T(2,128)}, u32[]{:S(2)}) copy-start(f32[8,8,2]{1,2,0:T(2,128)} %get-tuple-element.180) | copy-start | bytes 1540
  1003.4 265.6 %copy-start.8 = (f32[8,8,3]{1,2,0:T(4,128)S(1)}, f32[8,8,3]{1,2,0:T(4,128)}, u32[]{:S(2)}) copy-start(f32[8,8,3]{1,2,0:T(4,128)} %get-tuple-element.178) | copy-start | bytes 2308
  1262.6 296.6 %all-gather.13.cloned.1.call-start = ((), (), s32[]{:S(2)}) async-start(), calls=%async_computation.8 | async-start | bytes 1064960 | tf_op jit(solution)/shard_map/all_gather | solution.py:179
  1266.7 370.2 %all-gather.17.cloned.1.call-start = ((), (), s32[]{:S(2)}) async-start(), calls=%async_computation.11 | async-start | bytes 1064960 | tf_op jit(solution)/shard_map/all_gather | solution.py:179
  1400.2 239.0 %copy-start.10 = (bf16[3,8,128]{2,0,1:T(4,128)(2,1)S(1)}, bf16[3,8,128]{2,0,1:T(4,128)(2,1)}, u32[]{:S(2)}) copy-start(bf16[3,8,128]{2,0,1:T(4,128)(2,1)} %copy-done.9) | copy-start | bytes 18436
  1400.2 282.7 %all-reduce.16.cloned.1.call-start = ((), (), s32[]{:S(2)}) async-start(), calls=%async_computation.13 | async-start | bytes 786432 | tf_op jit(solution)/shard_map/psum | solution.py:181
Sparse Core Ops, SparseCore 0:
  148.1 201.7 all-reduce.13
  353.3 76.8 all-gather.10
  474.6 76.8 all-gather.6
  604.6 76.8 all-gather.14
  972.8 139.7 reduce-scatter.3
  1117.1 138.5 reduce-scatter.5
  1259.7 138.8 reduce-scatter.7
  1401.8 80.1 all-gather.8
  1485.1 74.0 all-gather.12
  1562.8 74.0 all-gather.16
  1640.1 42.7 all-reduce.15
where the time goes:
time: 1700 us; the launch traced here: 1690 us
  waiting for transfers between devices  635 us (37%)
  blocking collectives  626 us (37%)
  local copies, waits for them, and re-layouts  352 us (21%)
  matrix products  41.8 us (2%)
  other arithmetic  20 us (1%)
    unnamed x1, blocking collectives  253 us
    pmax x1, blocking collectives, body(): ceiling = lax.pmax(local_top, 'blk')  243 us
    all_gather x3, waiting for transfers between devices, body(): attended = lax.all_gather(own_rows, 'blk', axis=0, tiled=True)  232 us
    unnamed x12, waiting for transfers between devices  178 us
    psum x1, blocking collectives, body(): squares = lax.psum(jnp.sum(stream * stream, axis=1), 'blk')  130 us
    reduce_scatter x3, waiting for transfers between devices, body(): lax.psum_scatter(numerator, 'blk', scatter_dimension=0, tiled=True)  130 us
    scatter x1, local copies, waits for them, and re-layouts, body(): jnp.full((total_slots + 1,), -1, jnp.int32).at[flat_table]  120 us
    scatter x1, local copies, waits for them, and re-layouts, body(): jnp.zeros((total_slots + 1,), jnp.int32).at[flat_table]  120 us
  transfers between devices with their start and end apart: 11, of which 7 were waited for; matrix products, arithmetic and copies ran while one was open for 21% of the time, Pallas kernels for 0%

commit v1 on v0

v1 whole, which is shorter than its diff:
```python
import functools
import math

import jax
import jax.numpy as jnp
from jax import lax
from jax.experimental import pallas as pl
from jax.experimental.pallas import tpu as pltpu
from jax.sharding import Mesh
from jax.sharding import PartitionSpec as P

GROUP = 8
NEGATIVE = -1e30
EPSILON = 1e-05
ROPE_BASE = 5000000.0
STEPS = 3
HEADS = 8
HD = 128
SB = STEPS * GROUP
ROWS = HEADS * SB
BLOCK = ROWS + 8
ZN, XN, CN = 8, 4, 2
JN = XN * CN
PAIRS = [(s, u) for s in range(STEPS) for u in range(s + 1)]
SCALE = 1.0 / math.sqrt(HD)
XC = ("x", "core")
BLK = ("z", "x", "core")


def exchange(value, axis):
    return lax.all_to_all(value, axis, 0, 0, tiled=True)


def spread(value, axis, count):
    return exchange(jnp.broadcast_to(value[None], (count,) + value.shape), axis)


def after_projection(parent_ref, parts_ref, cos_ref, sin_ref, q_ref, k_ref, v_ref, hold):
    total = parts_ref[0]
    for source in range(1, ZN):
        total = total + parts_ref[source]
    cosines = cos_ref[...]
    sines = sin_ref[...]

    def turn(part):
        return part * cosines + pltpu.roll(part, HD // 2, 1) * sines

    for head in range(HEADS):
        hold[head * SB : (head + 1) * SB] = turn(total[:, head * HD : (head + 1) * HD])
    q_ref[...] = hold[...].astype(jnp.bfloat16)
    start = HEADS * HD
    fresh_key = turn(total[:, start : start + HD]).astype(jnp.bfloat16).astype(jnp.float32)
    fresh_value = total[:, start + HD :].astype(jnp.bfloat16).astype(jnp.float32)
    for index, (step, token) in enumerate(PAIRS):
        for ref, fresh in ((k_ref, fresh_key), (v_ref, fresh_value)):
            if token == step:
                ref[index] = fresh[step * GROUP : (step + 1) * GROUP]
            else:
                before = PAIRS.index((step - 1, token))
                for beam in range(GROUP):
                    parent = parent_ref[step * GROUP + beam]
                    ref[index, pl.ds(beam, 1), :] = ref[before, pl.ds(parent, 1), :]


def attention(
    owner_ref, group_ref, count_ref, q_ref, root_ref, own_ref, other_ref, out_ref, top_ref, sum_ref
):
    groups = ZN * XN
    top_ref[...] = jnp.full_like(top_ref, NEGATIVE)
    sum_ref[...] = jnp.zeros_like(sum_ref)
    out_ref[...] = jnp.zeros_like(out_ref)
    tokens = lax.broadcasted_iota(jnp.int32, (SB, HD), 1)
    slots = own_ref.shape[0]

    def visit(cache_ref, offset):
        def step(slot, carry):
            count = count_ref[offset + slot]

            @pl.when(count > 0)
            def _():
                group = group_ref[offset + slot]
                owner = owner_ref[offset + slot]
                keys = cache_ref[slot, 0]
                values = cache_ref[slot, 1]
                live = (root_ref[group] == owner) & (tokens < count)
                live = jnp.concatenate([live] * HEADS, axis=0)
                scores = (
                    lax.dot_general(
                        q_ref[group],
                        keys,
                        (((1,), (1,)), ((), ())),
                        preferred_element_type=jnp.float32,
                    )
                    * SCALE
                )
                scores = jnp.where(live, scores, NEGATIVE)
                old = top_ref[group]
                new = jnp.maximum(old, jnp.max(scores, axis=1, keepdims=True))
                weights = jnp.where(live, jnp.exp(scores - new), 0.0)
                fade = jnp.exp(old - new)
                top_ref[group] = new
                sum_ref[group] = sum_ref[group] * fade + jnp.sum(weights, axis=1, keepdims=True)
                out_ref[group, 0:ROWS, :] = out_ref[group, 0:ROWS, :] * fade + jnp.dot(
                    weights.astype(jnp.bfloat16), values, preferred_element_type=jnp.float32
                )

            return carry

        lax.fori_loop(0, slots, step, 0)

    visit(own_ref, 0)
    visit(other_ref, slots)
    lanes = lax.broadcasted_iota(jnp.int32, (GROUP, HD), 1)

    def pack(group, carry):
        tile = jnp.zeros((GROUP, HD), jnp.float32)
        for part in range(HEADS * STEPS):
            rows = slice(part * GROUP, (part + 1) * GROUP)
            tile = jnp.where(lanes == part, top_ref[group, rows, :], tile)
            tile = jnp.where(lanes == part + HD // 2, sum_ref[group, rows, :], tile)
        out_ref[group, ROWS:BLOCK, :] = tile
        return carry

    lax.fori_loop(0, groups, pack, 0)


def merge(parts_ref, out_ref):
    count = parts_ref.shape[0]
    stats = [parts_ref[source, 0, ROWS:BLOCK, :] for source in range(count)]
    top = functools.reduce(jnp.maximum, stats)
    fades = [jnp.exp(stat - top) for stat in stats]
    total = sum(fade * pltpu.roll(stat, HD // 2, 1) for fade, stat in zip(fades, stats))
    lanes = lax.broadcasted_iota(jnp.int32, (GROUP, HD), 1)
    out_ref[0, ROWS:BLOCK, :] = jnp.where(lanes < HD // 2, top, pltpu.roll(total, HD // 2, 1))
    for part in range(HEADS * STEPS):
        rows = slice(part * GROUP, (part + 1) * GROUP)
        out_ref[0, rows, :] = sum(
            fades[source][:, part : part + 1] * parts_ref[source, 0, rows, :]
            for source in range(count)
        )


def finish(parts_ref, q_ref, k_ref, v_ref, out_ref, hold):
    count = parts_ref.shape[0]
    stats = [parts_ref[source, ROWS:BLOCK, :] for source in range(count)]
    cached_top = functools.reduce(jnp.maximum, stats)
    queries = q_ref[...].astype(jnp.float32)
    lanes = lax.broadcasted_iota(jnp.int32, (GROUP, HD), 1)
    fresh = {}
    tops = cached_top
    for head in range(HEADS):
        for step in range(STEPS):
            part = head * STEPS + step
            row = head * SB + step * GROUP
            tile = queries[row : row + GROUP]
            for token in range(step + 1):
                key = k_ref[PAIRS.index((step, token))]
                score = jnp.sum(tile * key, axis=1, keepdims=True) * SCALE
                fresh[part, token] = score
                tops = jnp.where(lanes == part, jnp.maximum(tops, score), tops)
    fades = [jnp.exp(stat - tops) for stat in stats]
    total = sum(fade * pltpu.roll(stat, HD // 2, 1) for fade, stat in zip(fades, stats))
    for head in range(HEADS):
        for step in range(STEPS):
            part = head * STEPS + step
            rows = slice(part * GROUP, (part + 1) * GROUP)
            ceiling = tops[:, part : part + 1]
            below = total[:, part : part + 1]
            above = sum(
                fades[source][:, part : part + 1] * parts_ref[source, rows, :]
                for source in range(count)
            )
            for token in range(step + 1):
                weight = jnp.exp(fresh[part, token] - ceiling)
                below = below + weight
                above = above + weight.astype(jnp.bfloat16).astype(jnp.float32) * v_ref[
                    PAIRS.index((step, token))
                ]
            hold[step * GROUP : (step + 1) * GROUP, head * HD : (head + 1) * HD] = above / below
    out_ref[...] = hold[...].astype(jnp.bfloat16)


def compose(parents_near):
    digits = jnp.arange(GROUP, dtype=jnp.int32)
    roots = [parents_near[0]]
    for step in range(1, STEPS):
        pick = parents_near[step][:, :, None] == digits
        roots.append(jnp.sum(jnp.where(pick, roots[-1][:, None, :], 0), axis=-1))
    return jnp.stack(roots)


def body(
    embeds, attn_gain, w_query, w_key, w_value, w_out, cache_kv, lengths, block_table, parents
):
    z = lax.axis_index("z")
    x = lax.axis_index("x")
    core = lax.axis_index("core")
    here = (z * XN + x) * CN + core
    width_part = embeds.shape[2]
    groups = ZN * JN
    beams = groups * GROUP
    slots = cache_kv.shape[0]
    width = width_part * groups
    gathered = width_part * JN

    cache = cache_kv[:, 0]
    other_cache = lax.ppermute(cache, "core", [(0, 1), (1, 0)])

    base = jnp.arange(groups, dtype=jnp.int32)[None, :, None] * GROUP
    parents_near = parents.reshape(STEPS, groups, GROUP) - base
    roots_near = compose(parents_near)
    roots = roots_near + base
    length_of = lengths.reshape(groups, GROUP)
    own_roots = lax.dynamic_slice_in_dim(roots_near, here, 1, 1)[:, 0]
    own_parents = lax.dynamic_slice_in_dim(parents_near, here, 1, 1)[:, 0]
    own_lengths = lax.dynamic_slice_in_dim(length_of, here, 1, 0)[0]
    digits = jnp.arange(GROUP, dtype=jnp.int32)
    position = jnp.sum(
        jnp.where(own_roots[:, :, None] == digits, own_lengths[None, None, :], 0), axis=-1
    ) + jnp.arange(STEPS, dtype=jnp.int32)[:, None]
    exponent = jnp.arange(HD // 2, dtype=jnp.float32) * (2.0 / HD)
    frequency = ROPE_BASE ** (-exponent)
    angles = position.reshape(SB).astype(jnp.float32)[:, None] * frequency[None, :]
    cosines = jnp.cos(angles)
    sines = jnp.sin(angles)
    cosines = jnp.concatenate([cosines, cosines], axis=1)
    sines = jnp.concatenate([-sines, sines], axis=1)
    own_ids = here * slots + jnp.arange(slots, dtype=jnp.int32)
    other_ids = (here + 1 - 2 * core) * slots + jnp.arange(slots, dtype=jnp.int32)
    ids = jnp.concatenate([own_ids, other_ids])
    table = block_table.reshape(-1, 128)
    codes = jnp.arange(table.size, dtype=jnp.int32).reshape(table.shape)
    code = jnp.max(jnp.where(table[None] == ids[:, None, None], codes[None], -1), axis=(1, 2))
    spans = jnp.broadcast_to(lengths[:, None], block_table.shape).reshape(table.shape)
    span = jnp.max(jnp.where(table[None] == ids[:, None, None], spans[None], 0), axis=(1, 2))
    owner = code // block_table.shape[1]
    count = span - (code % block_table.shape[1]) * HD
    group = owner // GROUP
    mine = (code >= 0) & (group % CN == core)
    count = jnp.where(mine, count, 0)
    group = jnp.where(mine, (group // CN % XN) * ZN + group // JN, 0)
    root_tiles = lax.dynamic_slice_in_dim(roots.reshape(STEPS, ZN, XN, CN, GROUP), core, 1, 3)
    root_tiles = root_tiles[:, :, :, 0].transpose(2, 1, 0, 3).reshape(ZN * XN, SB)
    root_tiles = jnp.broadcast_to(root_tiles[:, :, None], (ZN * XN, SB, HD))

    rows = ZN * SB
    half = rows // 2
    by_row = embeds.reshape(STEPS, ZN, JN, GROUP, width_part).transpose(2, 1, 0, 3, 4)
    by_row = by_row.reshape(JN, rows, width_part)
    high = lax.reduce_precision(attn_gain, 8, 7)
    middle = lax.reduce_precision(attn_gain - high, 8, 7)
    low = attn_gain - high - middle
    gain_rows = jnp.stack(
        [jnp.concatenate([high, middle]), jnp.concatenate([low, jnp.zeros_like(low)])]
    ).astype(jnp.bfloat16)
    gain_rows = jnp.concatenate([gain_rows, jnp.zeros((6, HD), jnp.bfloat16)])
    packed = jnp.concatenate(
        [
            jnp.concatenate([by_row[:, :half], by_row[:, half:]], axis=2),
            jnp.broadcast_to(gain_rows[None], (JN, 8, HD)),
        ],
        axis=1,
    )
    packed = exchange(packed, XC)
    stream = jnp.concatenate(
        [packed[:, :half, :width_part], packed[:, :half, width_part:]], axis=1
    )
    stream = stream.transpose(1, 0, 2).reshape(rows, gathered).astype(jnp.float32)
    tails = packed[:, half : half + 2].astype(jnp.float32)
    gain = tails[:, 0, :width_part] + tails[:, 0, width_part:] + tails[:, 1, :width_part]
    gain = gain.reshape(gathered)
    squares = jnp.sum(stream * stream, axis=1)
    squares = jnp.pad(squares, (0, 256 - rows)).reshape(2, 128)
    squares = jnp.sum(spread(squares, "z", ZN), axis=0).reshape(256)[:rows]
    inverse = lax.rsqrt(squares / width + EPSILON)
    normed = (stream * inverse[:, None] * gain[None, :]).astype(jnp.bfloat16)

    weights = jnp.concatenate([w_query, w_key, w_value], axis=1)
    weights = spread(weights, "x", XN)
    weights = spread(weights, "core", CN)
    weights = weights.reshape(CN, XN, width_part, -1).transpose(1, 0, 2, 3)
    weights = weights.reshape(gathered, -1)
    projected = jnp.dot(normed, weights, preferred_element_type=jnp.float32)
    projected = exchange(projected.reshape(ZN, SB, -1), "z")

    small = jax.ShapeDtypeStruct((len(PAIRS), GROUP, HD), jnp.float32)
    vmem = pl.BlockSpec(memory_space=pltpu.VMEM)
    smem = pl.BlockSpec(memory_space=pltpu.SMEM)
    queries, key_chain, value_chain = pl.pallas_call(
        after_projection,
        out_shape=(jax.ShapeDtypeStruct((ROWS, HD), jnp.bfloat16), small, small),
        in_specs=[smem, vmem, vmem, vmem],
        out_specs=(vmem, vmem, vmem),
        scratch_shapes=[pltpu.VMEM((ROWS, HD), jnp.float32)],
    )(own_parents.reshape(SB), projected, cosines, sines)
    last = PAIRS.index((STEPS - 1, 0))
    appended = jnp.stack([key_chain[last:], value_chain[last:]], axis=2)
    appended = appended[:, :, None].astype(jnp.bfloat16)

    everyone = spread(queries, "z", ZN)
    everyone = spread(everyone.reshape(ZN * ROWS, HD), "x", XN).reshape(XN * ZN, ROWS, HD)
    partial = pl.pallas_call(
        attention,
        out_shape=jax.ShapeDtypeStruct((XN * ZN, BLOCK, HD), jnp.float32),
        in_specs=[smem, smem, smem, vmem, vmem, vmem, vmem],
        out_specs=vmem,
        scratch_shapes=[
            pltpu.VMEM((XN * ZN, ROWS, HD), jnp.float32),
            pltpu.VMEM((XN * ZN, ROWS, HD), jnp.float32),
        ],
        compiler_params=pltpu.CompilerParams(vmem_limit_bytes=40 << 20),
    )(owner, group, count, everyone, root_tiles, cache, other_cache)

    partial = exchange(partial.reshape(XN, ZN * BLOCK, HD), "x").reshape(XN, ZN, BLOCK, HD)
    partial = pl.pallas_call(
        merge,
        grid=(ZN,),
        out_shape=jax.ShapeDtypeStruct((ZN, BLOCK, HD), jnp.float32),
        in_specs=[pl.BlockSpec((XN, 1, BLOCK, HD), lambda i: (0, i, 0, 0))],
        out_specs=pl.BlockSpec((1, BLOCK, HD), lambda i: (i, 0, 0)),
    )(partial)
    partial = exchange(partial, "z")
    attended = pl.pallas_call(
        finish,
        out_shape=jax.ShapeDtypeStruct((SB, HEADS * HD), jnp.bfloat16),
        in_specs=[vmem] * 4,
        out_specs=vmem,
        scratch_shapes=[pltpu.VMEM((SB, HEADS * HD), jnp.float32)],
    )(partial, queries, key_chain, value_chain)

    attended = spread(attended, "z", ZN).reshape(rows, HEADS * HD)
    turned = spread(w_out.T, "x", XN)
    turned = spread(turned, "core", CN)
    turned = turned.reshape(CN, XN, width_part, -1).transpose(1, 0, 2, 3).reshape(gathered, -1)
    result = lax.dot_general(
        attended, turned, (((1,), (1,)), ((), ())), preferred_element_type=jnp.float32
    )
    result = lax.psum(result, "kv")
    result = (stream + result).astype(jnp.bfloat16)
    result = result.reshape(rows, JN, width_part).transpose(1, 0, 2)
    result = jnp.concatenate([result[:, :half], result[:, half:]], axis=2)
    result = exchange(result, XC)
    result = jnp.concatenate([result[:, :, :width_part], result[:, :, width_part:]], axis=1)
    result = result.reshape(JN, ZN, STEPS, GROUP, width_part).transpose(2, 1, 0, 3, 4)
    return (result.reshape(STEPS, beams, width_part), appended)


def solution(mesh):
    fine = Mesh(mesh.devices.reshape(-1, ZN, XN, CN), ("kv",) + BLK)
    return jax.shard_map(
        body,
        mesh=fine,
        in_specs=(
            P(None, None, BLK),
            P(BLK),
            P(BLK, "kv"),
            P(BLK, "kv"),
            P(BLK, "kv"),
            P("kv", BLK),
            P(BLK, "kv", None, None, None),
            P(),
            P(),
            P(),
        ),
        out_specs=(P(None, None, BLK), P(None, BLK, "kv", None, None)),
        check_vma=False,
    )
```

time: 1700 us -> 318 us (0.19)
  blocking collectives: 626 us -> 72.2 us
  waiting for transfers between devices: 635 us -> 126 us
  local copies, waits for them, and re-layouts: 352 us -> 18.1 us
  starting transfers between devices: 0.68 us -> 51.9 us
  matrix products: 41.8 us -> 2.65 us
  Pallas kernels: 0 us -> 23.2 us
    all_gather x6 -> x0, waiting for transfers between devices: 284 us -> none  [the longest x3 232 us: body(): attended = lax.all_gather(own_rows, 'blk', axis=0, tiled=True)]
    unnamed x1 -> x0, blocking collectives: 253 us -> none
    pmax x1 -> x0, blocking collectives: 243 us -> none  [body(): ceiling = lax.pmax(local_top, 'blk')]
    scatter x7 -> x0, local copies, waits for them, and re-layouts: 241 us -> none  [the longest x1 120 us: body(): jnp.full((total_slots + 1,), -1, jnp.int32).at[flat_table]]
    unnamed x12 -> x1, waiting for transfers between devices: 178 us -> 0.02 us
    psum x1 -> x0, blocking collectives: 130 us -> none  [body(): squares = lax.psum(jnp.sum(stream * stream, axis=1), 'blk')]
    reduce_scatter x3 -> x0, waiting for transfers between devices: 130 us -> none  [body(): lax.psum_scatter(numerator, 'blk', scatter_dimension=0, tiled=True)]
    all_to_all x0 -> x10, waiting for transfers between devices: none -> 86 us  [exchange(): return lax.all_to_all(value, axis, 0, 0, tiled=True)]
  transfers between devices with their start and end apart: 11 -> 12, of which waited for: 7 -> 10; matrix products, arithmetic and copies ran while one was open for 21% -> 4% of each run, Pallas kernels for 0% -> 3%
where the time goes in v1:
time: 318 us; the launch traced here: 317 us
  waiting for transfers between devices  126 us (40%)
  blocking collectives  72.2 us (23%)
  starting transfers between devices  51.9 us (16%)
  Pallas kernels  23.2 us (7%)
  local copies, waits for them, and re-layouts  18.1 us (6%)
  between operations  14.5 us (5%)
  other arithmetic  8.6 us (3%)
    all_to_all x10, waiting for transfers between devices, exchange(): return lax.all_to_all(value, axis, 0, 0, tiled=True)  86 us
    all_to_all x3, blocking collectives, exchange(): return lax.all_to_all(value, axis, 0, 0, tiled=True)  72.2 us
    all_to_all x10, starting transfers between devices, exchange(): return lax.all_to_all(value, axis, 0, 0, tiled=True)  51.4 us
    psum x1, waiting for transfers between devices, body(): result = lax.psum(result, 'kv')  39.7 us
    pallas_call x1, Pallas kernels, body(): pl.pallas_call(attention, out_shape=jax.ShapeDtypeStruct((XN * ZN, BLOCK,...  12.4 us
    broadcast_in_dim x9, local copies, waits for them, and re-layouts, spread(): return exchange(jnp.broadcast_to(value[None], (count,) + value.shape), axis)  8.12 us
    pallas_call x1, Pallas kernels, body(): pl.pallas_call(merge, grid=(ZN,), out_shape=jax.ShapeDtypeStruct((ZN, BLO...  6.37 us
  transfers between devices with their start and end apart: 12, of which 10 were waited for; matrix products, arithmetic and copies ran while one was open for 4% of the time, Pallas kernels for 3%

profile of v1, /device:TPU:1, one launch (start us, length us, event | category | flops | bytes accessed | tf_op | source)
XLA Modules:
  0.0 316.7 jit_solution(2007279171829304083)
XLA Ops:
  7.2 0.7 reduce-precision_convert_fusion.1
  7.9 1.1 copy.114
  9.3 0.8 pad_maximum_fusion.3
  10.1 6.5 %all-to-all-start = ((bf16[8,104,128]{2,1,0:T(8,128)(2,1)}), bf16[8,104,128]{2,1,0:T(8,128)(2,1)S(1)}, u32[]{:S(2)}, u32[]{:S(2)}) async-start(bf16[8,104,128]{2,1,0:T(8,128)(2,1)} %pad_maximum_fusion.3), calls=%async_computation | async-start | bytes 425984 | tf_op jit(solution)/shard_map/all_to_all | solution.py:31
  16.7 6.0 %all-to-all-done = bf16[8,104,128]{2,1,0:T(8,128)(2,1)S(1)} async-done(((bf16[8,104,128]{2,1,0:T(8,128)(2,1)}), bf16[8,104,128]{2,1,0:T(8,128)(2,1)S(1)}, u32[]{:S(2)}, u32[]{:S(2)}) %all-to-all-start) | async-done | bytes 213024 | tf_op jit(solution)/shard_map/all_to_all | solution.py:31
  23.0 0.6 broadcast_in_dim.153
  23.6 7.4 %all-to-all-start.1 = ((f32[8,2,128]{2,1,0:T(2,128)}), f32[8,2,128]{2,1,0:T(2,128)S(1)}, u32[]{:S(2)}, u32[]{:S(2)}) async-start(f32[8,2,128]{2,1,0:T(2,128)} %broadcast_in_dim.153), calls=%async_computation.1 | async-start | bytes 16384 | tf_op jit(solution)/shard_map/all_to_all | solution.py:31
  31.1 6.6 %all-to-all-done.1 = f32[8,2,128]{2,1,0:T(2,128)S(1)} async-done(((f32[8,2,128]{2,1,0:T(2,128)}), f32[8,2,128]{2,1,0:T(2,128)S(1)}, u32[]{:S(2)}, u32[]{:S(2)}) %all-to-all-start.1) | async-done | bytes 8224 | tf_op jit(solution)/shard_map/all_to_all | solution.py:31
  37.6 0.9 broadcast_in_dim.154
  38.5 3.5 %all-to-all-start.2 = ((bf16[4,64,1280]{2,1,0:T(8,128)(2,1)}), bf16[4,64,1280]{2,1,0:T(8,128)(2,1)S(1)}, u32[]{:S(2)}, u32[]{:S(2)}) async-start(bf16[4,64,1280]{2,1,0:T(8,128)(2,1)} %broadcast_in_dim.154), calls=%async_computation.2 | async-start | bytes 1310720 | tf_op jit(solution)/shard_map/all_to_all | solution.py:31
  42.8 7.4 %all-to-all-done.2 = bf16[4,64,1280]{2,1,0:T(8,128)(2,1)S(1)} async-done(((bf16[4,64,1280]{2,1,0:T(8,128)(2,1)}), bf16[4,64,1280]{2,1,0:T(8,128)(2,1)S(1)}, u32[]{:S(2)}, u32[]{:S(2)}) %all-to-all-start.2) | async-done | bytes 655392 | tf_op jit(solution)/shard_map/all_to_all | solution.py:31
  50.3 8.0 %all_to_all.65 = bf16[2,4,64,1280]{3,2,1,0:T(8,128)(2,1)S(1)} all-to-all(bf16[2,4,64,1280]{3,2,1,0:T(8,128)(2,1)S(1)} %broadcast_in_dim.155), channel_id=1, replica_groups=mesh['kv'=4,'z'=8,'x'=4,'core'=2] {'core'}, dimensions={0} | all-to-all | bytes 2621440 | tf_op jit(solution)/shard_map/all_to_all | solution.py:31
  58.5 1.4 fusion.31
  59.8 3.6 %all-to-all-start.4 = ((f32[8,24,1280]{2,1,0:T(8,128)}), f32[8,24,1280]{2,1,0:T(8,128)S(1)}, u32[]{:S(2)}, u32[]{:S(2)}) async-start(f32[8,24,1280]{2,1,0:T(8,128)} %fusion.31), calls=%async_computation.4 | async-start | bytes 1966080 | tf_op jit(solution)/shard_map/all_to_all | solution.py:31
  65.2 0.6 reshape_squeeze.3.parent_ref
  65.9 0.7 pad_maximum_fusion.5
  66.5 22.3 %all-to-all-done.4.parts_ref = f32[8,24,1280]{2,1,0:T(8,128)S(1)} async-done(((f32[8,24,1280]{2,1,0:T(8,128)}), f32[8,24,1280]{2,1,0:T(8,128)S(1)}, u32[]{:S(2)}, u32[]{:S(2)}) %all-to-all-start.4) | async-done | bytes 983072 | tf_op jit(solution)/shard_map/all_to_all | solution.py:31
  88.8 0.9 copy-done
  89.8 2.0 shard_map.113
  91.8 1.6 broadcast_in_dim.163
  93.4 3.6 %all-to-all-start.5 = ((bf16[8,192,128]{2,1,0:T(8,128)(2,1)}), bf16[8,192,128]{2,1,0:T(8,128)(2,1)S(1)}, u32[]{:S(2)}, u32[]{:S(2)}) async-start(bf16[8,192,128]{2,1,0:T(8,128)(2,1)} %broadcast_in_dim.163), calls=%async_computation.5 | async-start | bytes 786432 | tf_op jit(solution)/shard_map/all_to_all | solution.py:31
  97.3 11.5 %all-to-all-done.5 = bf16[8,192,128]{2,1,0:T(8,128)(2,1)S(1)} async-done(((bf16[8,192,128]{2,1,0:T(8,128)(2,1)}), bf16[8,192,128]{2,1,0:T(8,128)(2,1)S(1)}, u32[]{:S(2)}, u32[]{:S(2)}) %all-to-all-start.5) | async-done | bytes 393248 | tf_op jit(solution)/shard_map/all_to_all | solution.py:31
  108.8 1.4 broadcast_in_dim.165
  110.2 3.7 %all-to-all-start.6 = ((bf16[4,1536,128]{2,1,0:T(8,128)(2,1)}), bf16[4,1536,128]{2,1,0:T(8,128)(2,1)S(1)}, u32[]{:S(2)}, u32[]{:S(2)}) async-start(bf16[4,1536,128]{2,1,0:T(8,128)(2,1)} %broadcast_in_dim.165), calls=%async_computation.6 | async-start | bytes 3145728 | tf_op jit(solution)/shard_map/all_to_all | solution.py:31
  114.8 3.6 %fusion.1 = (s32[64]{0:T(128)S(1)}, s32[64]{0:T(128)S(1)}) fusion(s32[256,128]{1,0:T(8,128)S(1)} %copy.119, s32[256,128]{1,0:T(8,128)S(1)} %eq.77, s32[64]{0:T(128)S(1)} %pad_add_fusion, s32[256,128]{1,0:T(8,128)S(1)} %multiply_add_fusion), kind=kLoop, calls=%fused_computation.3 | loop fusion | flops 10485632 | bytes 393984 | tf_op jit(solution)/shard_map/reduce_max | solution.py:235
  118.4 12.1 %all-to-all-done.6 = bf16[4,1536,128]{2,1,0:T(8,128)(2,1)S(1)} async-done(((bf16[4,1536,128]{2,1,0:T(8,128)(2,1)}), bf16[4,1536,128]{2,1,0:T(8,128)(2,1)S(1)}, u32[]{:S(2)}, u32[]{:S(2)}) %all-to-all-start.6) | async-done | bytes 1572896 | tf_op jit(solution)/shard_map/all_to_all | solution.py:31
  130.7 12.4 %shard_map.114 = f32[32,200,128]{2,1,0:T(8,128)S(1)} custom-call(s32[64]{0:T(128)S(1)} %get-tuple-element.27.owner_ref, s32[64]{0:T(128)S(1)} %fusion.20.group_ref, s32[64]{0:T(128)S(1)} %get-tuple-element.24.count_ref, bf16[32,192,128]{2,1,0:T(8,128)(2,1)S(1)} %bitcast.66, s32[32,24,128]{2,1,0:T(8,128)S(1)} %broadcast_in_dim.167.root_ref, ...), custom_call_target="tpu_custom_call" | custom-call | tf_op jit(solution)/shard_map/pallas_call | solution.py:302
  143.2 40.2 %all_to_all.66 = f32[4,1600,128]{2,1,0:T(8,128)} all-to-all(f32[4,1600,128]{2,1,0:T(8,128)S(1)} %bitcast.65), channel_id=1, replica_groups=mesh['kv'=4,'z'=8,'x'=4,'core'=2] {'x'}, dimensions={0} | all-to-all | bytes 6553600 | tf_op jit(solution)/shard_map/all_to_all | solution.py:31
  183.4 0.9 broadcast_in_dim.169
  184.2 3.5 %all-to-all-start.10 = ((bf16[4,64,1024]{2,1,0:T(8,128)(2,1)}), bf16[4,64,1024]{2,1,0:T(8,128)(2,1)S(1)}, u32[]{:S(2)}, u32[]{:S(2)}) async-start(bf16[4,64,1024]{2,1,0:T(8,128)(2,1)} %broadcast_in_dim.169), calls=%async_computation.10 | async-start | bytes 1048576 | tf_op jit(solution)/shard_map/all_to_all | solution.py:31
  187.7 6.4 %shard_map.115 = f32[8,200,128]{2,1,0:T(8,128)} custom-call(f32[4,8,200,128]{3,2,1,0:T(8,128)} %bitcast.67), custom_call_target="tpu_custom_call" | custom-call | tf_op jit(solution)/shard_map/pallas_call | solution.py:315
  194.6 24.0 %all_to_all.67.parts_ref = f32[8,200,128]{2,1,0:T(8,128)} all-to-all(f32[8,200,128]{2,1,0:T(8,128)} %shard_map.115), channel_id=1, replica_groups=mesh['kv'=4,'z'=8,'x'=4,'core'=2] {'z'}, dimensions={0} | all-to-all | bytes 1638400 | tf_op jit(solution)/shard_map/all_to_all | solution.py:31
  218.6 1.1 broadcast_in_dim.170
  219.7 9.2 %all-to-all-start.11 = ((bf16[2,4,64,1024]{3,2,1,0:T(8,128)(2,1)}), bf16[2,4,64,1024]{3,2,1,0:T(8,128)(2,1)S(1)}, u32[]{:S(2)}, u32[]{:S(2)}) async-start(bf16[2,4,64,1024]{3,2,1,0:T(8,128)(2,1)} %broadcast_in_dim.170), calls=%async_computation.11 | async-start | bytes 2097152 | tf_op jit(solution)/shard_map/all_to_all | solution.py:31
  228.9 2.3 shard_map.116
  231.2 1.6 broadcast_in_dim.168
  232.8 3.5 %all-to-all-start.9 = ((bf16[8,24,1024]{2,1,0:T(8,128)(2,1)}), bf16[8,24,1024]{2,1,0:T(8,128)(2,1)S(1)}, u32[]{:S(2)}, u32[]{:S(2)}) async-start(bf16[8,24,1024]{2,1,0:T(8,128)(2,1)} %broadcast_in_dim.168), calls=%async_computation.9 | async-start | bytes 786432 | tf_op jit(solution)/shard_map/all_to_all | solution.py:31
  236.4 15.0 %all-to-all-done.9 = bf16[8,24,1024]{2,1,0:T(8,128)(2,1)S(1)} async-done(((bf16[8,24,1024]{2,1,0:T(8,128)(2,1)}), bf16[8,24,1024]{2,1,0:T(8,128)(2,1)S(1)}, u32[]{:S(2)}, u32[]{:S(2)}) %all-to-all-start.9) | async-done | bytes 393248 | tf_op jit(solution)/shard_map/all_to_all | solution.py:31
  251.4 1.3 fusion.32
  253.3 0.7 fusion.10
  254.0 39.7 %all-reduce.5.cloned.1.call-done = f32[192,512]{1,0:T(8,128)} async-done(((f32[192,512]{1,0:T(8,128)}), f32[192,512]{1,0:T(8,128)}) %all-reduce.5.cloned.1.call-update) | async-done | bytes 393232 | tf_op jit(solution)/shard_map/psum | solution.py:338
  293.7 1.0 add_convert_fusion
  295.1 0.8 copy.135
  295.9 6.9 %all-to-all-start.12 = ((bf16[8,96,128]{2,1,0:T(8,128)(2,1)}), bf16[8,96,128]{2,1,0:T(8,128)(2,1)S(1)}, u32[]{:S(2)}, u32[]{:S(2)}) async-start(bf16[8,96,128]{2,1,0:T(8,128)(2,1)} %copy.135), calls=%async_computation.12 | async-start | bytes 393216 | tf_op jit(solution)/shard_map/all_to_all | solution.py:31
  302.8 0.7 fusion.11
  303.5 0.6 copy.138
  304.1 4.6 %all-to-all-done.12 = bf16[8,96,128]{2,1,0:T(8,128)(2,1)S(1)} async-done(((bf16[8,96,128]{2,1,0:T(8,128)(2,1)}), bf16[8,96,128]{2,1,0:T(8,128)(2,1)S(1)}, u32[]{:S(2)}, u32[]{:S(2)}) %all-to-all-start.12) | async-done | bytes 196640 | tf_op jit(solution)/shard_map/all_to_all | solution.py:31
  309.0 0.8 copy.137
  (89 shorter events, 6.5 us)
Async XLA Ops:
  7.2 9.5 %copy-start.3 = (bf16[64,1024]{1,0:T(8,128)(2,1)S(1)}, bf16[64,1024]{1,0:T(8,128)(2,1)}, u32[]{:S(2)}) copy-start(bf16[64,1024]{1,0:T(8,128)(2,1)} %param.12) | copy-start | bytes 393220
  7.2 9.5 %copy-start.5 = (bf16[64,128]{1,0:T(8,128)(2,1)S(1)}, bf16[64,128]{1,0:T(8,128)(2,1)}, u32[]{:S(2)}) copy-start(bf16[64,128]{1,0:T(8,128)(2,1)} %param.13) | copy-start | bytes 49156
  7.2 9.5 %copy-start.4 = (bf16[64,128]{1,0:T(8,128)(2,1)S(1)}, bf16[64,128]{1,0:T(8,128)(2,1)}, u32[]{:S(2)}) copy-start(bf16[64,128]{1,0:T(8,128)(2,1)} %param.14) | copy-start | bytes 49156
  10.1 12.6 %all-to-all-start = ((bf16[8,104,128]{2,1,0:T(8,128)(2,1)}), bf16[8,104,128]{2,1,0:T(8,128)(2,1)S(1)}, u32[]{:S(2)}, u32[]{:S(2)}) async-start(bf16[8,104,128]{2,1,0:T(8,128)(2,1)} %pad_maximum_fusion.3), calls=%async_computation | async-start | bytes 425984 | tf_op jit(solution)/shard_map/all_to_all | solution.py:31
  23.6 14.0 %all-to-all-start.1 = ((f32[8,2,128]{2,1,0:T(2,128)}), f32[8,2,128]{2,1,0:T(2,128)S(1)}, u32[]{:S(2)}, u32[]{:S(2)}) async-start(f32[8,2,128]{2,1,0:T(2,128)} %broadcast_in_dim.153), calls=%async_computation.1 | async-start | bytes 16384 | tf_op jit(solution)/shard_map/all_to_all | solution.py:31
  38.5 11.7 %all-to-all-start.2 = ((bf16[4,64,1280]{2,1,0:T(8,128)(2,1)}), bf16[4,64,1280]{2,1,0:T(8,128)(2,1)S(1)}, u32[]{:S(2)}, u32[]{:S(2)}) async-start(bf16[4,64,1280]{2,1,0:T(8,128)(2,1)} %broadcast_in_dim.154), calls=%async_computation.2 | async-start | bytes 1310720 | tf_op jit(solution)/shard_map/all_to_all | solution.py:31
  58.4 5.4 %copy-start.7 = (s32[3,512]{1,0:T(4,128)S(1)}, s32[3,512]{1,0:T(4,128)}, u32[]{:S(2)}) copy-start(s32[3,512]{1,0:T(4,128)} %param.19) | copy-start | bytes 18436
  58.4 5.9 %copy-start.6 = (s32[512]{0:T(512)S(1)}, s32[512]{0:T(512)}, u32[]{:S(2)}) copy-start(s32[512]{0:T(512)} %param.17) | copy-start | bytes 6148
  59.8 29.0 %all-to-all-start.4 = ((f32[8,24,1280]{2,1,0:T(8,128)}), f32[8,24,1280]{2,1,0:T(8,128)S(1)}, u32[]{:S(2)}, u32[]{:S(2)}) async-start(f32[8,24,1280]{2,1,0:T(8,128)} %fusion.31), calls=%async_computation.4 | async-start | bytes 1966080 | tf_op jit(solution)/shard_map/all_to_all | solution.py:31
  63.4 55.0 %collective-permute-start = (bf16[32,2,128,128]{3,2,1,0:T(8,128)(2,1)}, bf16[32,2,128,128]{3,2,1,0:T(8,128)(2,1)}, u32[]{:S(2)}, u32[]{:S(2)}) collective-permute-start(bf16[32,2,128,128]{3,2,1,0:T(8,128)(2,1)} %bitcast.28.own_ref), channel_id=1, source_target_pairs={{0,1},{1,0},{2,3},{3,2},{4,5},{5,4},{6,7},{7,6},{8,9},{9,8},{10,11... | collective-permute-start | bytes 6291464 | tf_op jit(solution)/shard_map/ppermute | solution.py:207
  88.8 1.0 copy-start
  93.4 15.5 %all-to-all-start.5 = ((bf16[8,192,128]{2,1,0:T(8,128)(2,1)}), bf16[8,192,128]{2,1,0:T(8,128)(2,1)S(1)}, u32[]{:S(2)}, u32[]{:S(2)}) async-start(bf16[8,192,128]{2,1,0:T(8,128)(2,1)} %broadcast_in_dim.163), calls=%async_computation.5 | async-start | bytes 786432 | tf_op jit(solution)/shard_map/all_to_all | solution.py:31
  110.2 4.1 %copy-start.1 = (s32[512,64]{0,1:T(8,128)S(1)}, s32[512,64]{0,1:T(8,128)}, u32[]{:S(2)}) copy-start(s32[512,64]{0,1:T(8,128)} %param.18) | copy-start | bytes 393220
  110.2 20.3 %all-to-all-start.6 = ((bf16[4,1536,128]{2,1,0:T(8,128)(2,1)}), bf16[4,1536,128]{2,1,0:T(8,128)(2,1)S(1)}, u32[]{:S(2)}, u32[]{:S(2)}) async-start(bf16[4,1536,128]{2,1,0:T(8,128)(2,1)} %broadcast_in_dim.165), calls=%async_computation.6 | async-start | bytes 3145728 | tf_op jit(solution)/shard_map/all_to_all | solution.py:31
  143.2 40.2 %copy-start.2 = (bf16[1024,64]{0,1:T(8,128)(2,1)S(1)}, bf16[1024,64]{0,1:T(8,128)(2,1)}, u32[]{:S(2)}) copy-start(bf16[1024,64]{0,1:T(8,128)(2,1)} %param.15) | copy-start | bytes 393220
  184.2 10.4 %all-to-all-start.10 = ((bf16[4,64,1024]{2,1,0:T(8,128)(2,1)}), bf16[4,64,1024]{2,1,0:T(8,128)(2,1)S(1)}, u32[]{:S(2)}, u32[]{:S(2)}) async-start(bf16[4,64,1024]{2,1,0:T(8,128)(2,1)} %broadcast_in_dim.169), calls=%async_computation.10 | async-start | bytes 1048576 | tf_op jit(solution)/shard_map/all_to_all | solution.py:31
  219.7 11.6 %all-to-all-start.11 = ((bf16[2,4,64,1024]{3,2,1,0:T(8,128)(2,1)}), bf16[2,4,64,1024]{3,2,1,0:T(8,128)(2,1)S(1)}, u32[]{:S(2)}, u32[]{:S(2)}) async-start(bf16[2,4,64,1024]{3,2,1,0:T(8,128)(2,1)} %broadcast_in_dim.170), calls=%async_computation.11 | async-start | bytes 2097152 | tf_op jit(solution)/shard_map/all_to_all | solution.py:31
  232.8 18.6 %all-to-all-start.9 = ((bf16[8,24,1024]{2,1,0:T(8,128)(2,1)}), bf16[8,24,1024]{2,1,0:T(8,128)(2,1)S(1)}, u32[]{:S(2)}, u32[]{:S(2)}) async-start(bf16[8,24,1024]{2,1,0:T(8,128)(2,1)} %broadcast_in_dim.168), calls=%async_computation.9 | async-start | bytes 786432 | tf_op jit(solution)/shard_map/all_to_all | solution.py:31
  236.3 57.4 %all-reduce.5.cloned.1.call-start = ((), (), s32[]{:S(2)}) async-start(), calls=%async_computation.13 | async-start | bytes 786432 | tf_op jit(solution)/shard_map/psum | solution.py:338
  295.9 12.8 %all-to-all-start.12 = ((bf16[8,96,128]{2,1,0:T(8,128)(2,1)}), bf16[8,96,128]{2,1,0:T(8,128)(2,1)S(1)}, u32[]{:S(2)}, u32[]{:S(2)}) async-start(bf16[8,96,128]{2,1,0:T(8,128)(2,1)} %copy.135), calls=%async_computation.12 | async-start | bytes 393216 | tf_op jit(solution)/shard_map/all_to_all | solution.py:31
Sparse Core Ops, SparseCore 0:
  252.8 40.8 all-reduce.4

commit v2 on v1

--- a/solution.py
+++ b/solution.py
@@ -18,9 +18,12 @@
 HD = 128
 SB = STEPS * GROUP
 ROWS = HEADS * SB
-BLOCK = ROWS + 8
+BLOCK = ROWS + 3 * GROUP
 ZN, XN, CN = 8, 4, 2
 JN = XN * CN
+KN = 4
+PART = 64
+QUARTER = ZN * SB // KN
 PAIRS = [(s, u) for s in range(STEPS) for u in range(s + 1)]
 SCALE = 1.0 / math.sqrt(HD)
 XC = ("x", "core")
@@ -35,7 +38,69 @@
     return exchange(jnp.broadcast_to(value[None], (count,) + value.shape), axis)
 
 
-def after_projection(parent_ref, parts_ref, cos_ref, sin_ref, q_ref, k_ref, v_ref, hold):
+def ring(value):
+    own = [value]
+    for hop in range(1, XN):
+        own.append(lax.ppermute(value, "x", [(i, (i + hop) % XN) for i in range(XN)]))
+    return own + [lax.ppermute(part, "core", [(0, 1), (1, 0)]) for part in own]
+
+
+def join(place_ref, chunks, wide):
+    core = place_ref[1]
+    for hop in range(XN):
+        wide[hop, pl.ds(pl.multiple_of(core * PART, PART), PART), :] = chunks[hop][...]
+        wide[hop, pl.ds(pl.multiple_of((1 - core) * PART, PART), PART), :] = chunks[XN + hop][...]
+
+
+def project(place_ref, rows_ref, *rest):
+    chunks, out_ref, wide = rest[: 2 * XN], rest[2 * XN], rest[2 * XN + 1]
+    join(place_ref, chunks, wide)
+    x = place_ref[0]
+    for start in range(0, out_ref.shape[1], 256):
+        out_ref[:, start : start + 256] = sum(
+            jnp.dot(
+                rows_ref[(x + XN - hop) % XN],
+                wide[hop, :, start : start + 256],
+                preferred_element_type=jnp.float32,
+            )
+            for hop in range(XN)
+        )
+
+
+def deliver(place_ref, rows_ref, *rest):
+    chunks, out_ref, wide = rest[: 2 * XN], rest[2 * XN], rest[2 * XN + 1]
+    join(place_ref, chunks, wide)
+    x = place_ref[0]
+    for hop in range(XN):
+        result = lax.dot_general(
+            rows_ref[...],
+            wide[hop],
+            (((1,), (1,)), ((), ())),
+            preferred_element_type=jnp.float32,
+        )
+        for kv in range(KN):
+            out_ref[kv, (x + XN - hop) % XN] = result[kv * QUARTER : (kv + 1) * QUARTER]
+
+
+def settle(place_ref, parts_ref, stream_ref, out_ref):
+    kv = place_ref[2]
+    lanes = lax.broadcasted_iota(jnp.int32, (SB, 2 * PART), 1)
+    for x in range(XN):
+        total = parts_ref[0, x]
+        for source in range(1, KN):
+            total = total + parts_ref[source, x]
+        total = stream_ref[x, pl.ds(pl.multiple_of(kv * QUARTER, 8), QUARTER), :] + total
+        upper, lower = total[:SB], total[SB:]
+        first = jnp.where(lanes < PART, upper, pltpu.roll(lower, PART, 1)).astype(jnp.bfloat16)
+        second = jnp.where(lanes < PART, pltpu.roll(upper, PART, 1), lower).astype(jnp.bfloat16)
+        for target in range(KN):
+            out_ref[target, x, 0] = first
+            out_ref[target, x, 1] = second
+
+
+def after_projection(
+    parent_ref, parts_ref, cos_ref, sin_ref, q_ref, all_ref, k_ref, v_ref, hold
+):
     total = parts_ref[0]
     for source in range(1, ZN):
         total = total + parts_ref[source]
@@ -47,7 +112,10 @@
 
     for head in range(HEADS):
         hold[head * SB : (head + 1) * SB] = turn(total[:, head * HD : (head + 1) * HD])
-    q_ref[...] = hold[...].astype(jnp.bfloat16)
+    queries = hold[...].astype(jnp.bfloat16)
+    q_ref[...] = queries
+    for target in range(ZN):
+        all_ref[target] = queries
     start = HEADS * HD
     fresh_key = turn(total[:, start : start + HD]).astype(jnp.bfloat16).astype(jnp.float32)
     fresh_value = total[:, start + HD :].astype(jnp.bfloat16).astype(jnp.float32)
@@ -63,12 +131,22 @@
 
 
 def attention(
-    owner_ref, group_ref, count_ref, q_ref, root_ref, own_ref, other_ref, out_ref, top_ref, sum_ref
+    owner_ref,
+    group_ref,
+    count_ref,
+    q_ref,
+    root_ref,
+    own_ref,
+    other_ref,
+    out_ref,
+    top_ref,
+    sum_ref,
+    hold,
 ):
     groups = ZN * XN
     top_ref[...] = jnp.full_like(top_ref, NEGATIVE)
     sum_ref[...] = jnp.zeros_like(sum_ref)
-    out_ref[...] = jnp.zeros_like(out_ref)
+    hold[...] = jnp.zeros_like(hold)
     tokens = lax.broadcasted_iota(jnp.int32, (SB, HD), 1)
     slots = own_ref.shape[0]
 
@@ -100,7 +178,7 @@
                 fade = jnp.exp(old - new)
                 top_ref[group] = new
                 sum_ref[group] = sum_ref[group] * fade + jnp.sum(weights, axis=1, keepdims=True)
-                out_ref[group, 0:ROWS, :] = out_ref[group, 0:ROWS, :] * fade + jnp.dot(
+                hold[group] = hold[group] * fade + jnp.dot(
                     weights.astype(jnp.bfloat16), values, preferred_element_type=jnp.float32
                 )
 
@@ -118,31 +196,45 @@
             rows = slice(part * GROUP, (part + 1) * GROUP)
             tile = jnp.where(lanes == part, top_ref[group, rows, :], tile)
             tile = jnp.where(lanes == part + HD // 2, sum_ref[group, rows, :], tile)
-        out_ref[group, ROWS:BLOCK, :] = tile
+        out_ref[group] = seal([hold[group]], tile)
         return carry
 
     lax.fori_loop(0, groups, pack, 0)
+
+
+def seal(sums, stat):
+    high = stat.astype(jnp.bfloat16).astype(jnp.float32)
+    middle = (stat - high).astype(jnp.bfloat16).astype(jnp.float32)
+    low = stat - high - middle
+    return jnp.concatenate(sums + [high, middle, low], axis=0).astype(jnp.bfloat16)
+
+
+def unseal(block):
+    block = block.astype(jnp.float32)
+    stat = block[ROWS : ROWS + GROUP] + block[ROWS + GROUP : ROWS + 2 * GROUP]
+    return block[:ROWS], stat + block[ROWS + 2 * GROUP :]
 
 
 def merge(parts_ref, out_ref):
     count = parts_ref.shape[0]
-    stats = [parts_ref[source, 0, ROWS:BLOCK, :] for source in range(count)]
+    sums, stats = zip(*[unseal(parts_ref[source, 0]) for source in range(count)])
     top = functools.reduce(jnp.maximum, stats)
     fades = [jnp.exp(stat - top) for stat in stats]
     total = sum(fade * pltpu.roll(stat, HD // 2, 1) for fade, stat in zip(fades, stats))
     lanes = lax.broadcasted_iota(jnp.int32, (GROUP, HD), 1)
-    out_ref[0, ROWS:BLOCK, :] = jnp.where(lanes < HD // 2, top, pltpu.roll(total, HD // 2, 1))
+    stat = jnp.where(lanes < HD // 2, top, pltpu.roll(total, HD // 2, 1))
+    merged = []
     for part in range(HEADS * STEPS):
         rows = slice(part * GROUP, (part + 1) * GROUP)
-        out_ref[0, rows, :] = sum(
-            fades[source][:, part : part + 1] * parts_ref[source, 0, rows, :]
-            for source in range(count)
+        merged.append(
+            sum(fades[source][:, part : part + 1] * sums[source][rows] for source in range(count))
         )
+    out_ref[0] = seal(merged, stat)
 
 
 def finish(parts_ref, q_ref, k_ref, v_ref, out_ref, hold):
     count = parts_ref.shape[0]
-    stats = [parts_ref[source, ROWS:BLOCK, :] for source in range(count)]
+    sums, stats = zip(*[unseal(parts_ref[source]) for source in range(count)])
     cached_top = functools.reduce(jnp.maximum, stats)
     queries = q_ref[...].astype(jnp.float32)
     lanes = lax.broadcasted_iota(jnp.int32, (GROUP, HD), 1)
@@ -167,8 +259,7 @@
             ceiling = tops[:, part : part + 1]
             below = total[:, part : part + 1]
             above = sum(
-                fades[source][:, part : part + 1] * parts_ref[source, rows, :]
-                for source in range(count)
+                fades[source][:, part : part + 1] * sums[source][rows] for source in range(count)
             )
             for token in range(step + 1):
                 weight = jnp.exp(fresh[part, token] - ceiling)
@@ -177,7 +268,9 @@
                     PAIRS.index((step, token))
                 ]
             hold[step * GROUP : (step + 1) * GROUP, head * HD : (head + 1) * HD] = above / below
-    out_ref[...] = hold[...].astype(jnp.bfloat16)
+    attended = hold[...].astype(jnp.bfloat16)
+    for target in range(ZN):
+        out_ref[target] = attended
 
 
 def compose(parents_near):
@@ -196,13 +289,16 @@
     x = lax.axis_index("x")
     core = lax.axis_index("core")
     here = (z * XN + x) * CN + core
-    width_part = embeds.shape[2]
     groups = ZN * JN
     beams = groups * GROUP
     slots = cache_kv.shape[0]
-    width = width_part * groups
-    gathered = width_part * JN
-
+    width = PART * groups
+
+    weights = ring(jnp.concatenate([w_query, w_key, w_value], axis=1))
+    turned = ring(w_out.T)
+    place = jnp.stack([x, core, lax.axis_index("kv")]).astype(jnp.int32)
+    vmem = pl.BlockSpec(memory_space=pltpu.VMEM)
+    smem = pl.BlockSpec(memory_space=pltpu.SMEM)
     cache = cache_kv[:, 0]
     other_cache = lax.ppermute(cache, "core", [(0, 1), (1, 0)])
 
@@ -245,8 +341,8 @@
 
     rows = ZN * SB
     half = rows // 2
-    by_row = embeds.reshape(STEPS, ZN, JN, GROUP, width_part).transpose(2, 1, 0, 3, 4)
-    by_row = by_row.reshape(JN, rows, width_part)
+    by_row = embeds.reshape(STEPS, ZN // 2, 2, JN, GROUP, PART).transpose(3, 1, 0, 4, 2, 5)
+    by_row = by_row.reshape(JN, half, 2 * PART)
     high = lax.reduce_precision(attn_gain, 8, 7)
     middle = lax.reduce_precision(attn_gain - high, 8, 7)
     low = attn_gain - high - middle
@@ -254,59 +350,56 @@
         [jnp.concatenate([high, middle]), jnp.concatenate([low, jnp.zeros_like(low)])]
     ).astype(jnp.bfloat16)
     gain_rows = jnp.concatenate([gain_rows, jnp.zeros((6, HD), jnp.bfloat16)])
-    packed = jnp.concatenate(
-        [
-            jnp.concatenate([by_row[:, :half], by_row[:, half:]], axis=2),
-            jnp.broadcast_to(gain_rows[None], (JN, 8, HD)),
-        ],
-        axis=1,
-    )
+    packed = jnp.concatenate([by_row, jnp.broadcast_to(gain_rows[None], (JN, 8, HD))], axis=1)
     packed = exchange(packed, XC)
-    stream = jnp.concatenate(
-        [packed[:, :half, :width_part], packed[:, :half, width_part:]], axis=1
-    )
-    stream = stream.transpose(1, 0, 2).reshape(rows, gathered).astype(jnp.float32)
+    stream = packed[:, :half].reshape(XN, CN, ZN // 2, SB, 2, PART).transpose(0, 2, 4, 3, 1, 5)
+    stream = stream.reshape(XN, rows, 2 * PART).astype(jnp.float32)
     tails = packed[:, half : half + 2].astype(jnp.float32)
-    gain = tails[:, 0, :width_part] + tails[:, 0, width_part:] + tails[:, 1, :width_part]
-    gain = gain.reshape(gathered)
-    squares = jnp.sum(stream * stream, axis=1)
+    gain = tails[:, 0, :PART] + tails[:, 0, PART:] + tails[:, 1, :PART]
+    gain = gain.reshape(XN, 1, 2 * PART)
+    squares = jnp.sum(stream * stream, axis=(0, 2))
     squares = jnp.pad(squares, (0, 256 - rows)).reshape(2, 128)
     squares = jnp.sum(spread(squares, "z", ZN), axis=0).reshape(256)[:rows]
     inverse = lax.rsqrt(squares / width + EPSILON)
-    normed = (stream * inverse[:, None] * gain[None, :]).astype(jnp.bfloat16)
-
-    weights = jnp.concatenate([w_query, w_key, w_value], axis=1)
-    weights = spread(weights, "x", XN)
-    weights = spread(weights, "core", CN)
-    weights = weights.reshape(CN, XN, width_part, -1).transpose(1, 0, 2, 3)
-    weights = weights.reshape(gathered, -1)
-    projected = jnp.dot(normed, weights, preferred_element_type=jnp.float32)
-    projected = exchange(projected.reshape(ZN, SB, -1), "z")
+    normed = (stream * inverse[None, :, None] * gain).astype(jnp.bfloat16)
+    columns = weights[0].shape[1]
+    projected = pl.pallas_call(
+        project,
+        out_shape=jax.ShapeDtypeStruct((rows, columns), jnp.float32),
+        in_specs=[smem] + [vmem] * (1 + 2 * XN),
+        out_specs=vmem,
+        scratch_shapes=[pltpu.VMEM((XN, 2 * PART, columns), jnp.bfloat16)],
+    )(place, normed, *weights)
+    projected = exchange(projected.reshape(ZN, SB, columns), "z")
 
     small = jax.ShapeDtypeStruct((len(PAIRS), GROUP, HD), jnp.float32)
-    vmem = pl.BlockSpec(memory_space=pltpu.VMEM)
-    smem = pl.BlockSpec(memory_space=pltpu.SMEM)
-    queries, key_chain, value_chain = pl.pallas_call(
+    queries, everyone, key_chain, value_chain = pl.pallas_call(
         after_projection,
-        out_shape=(jax.ShapeDtypeStruct((ROWS, HD), jnp.bfloat16), small, small),
+        out_shape=(
+            jax.ShapeDtypeStruct((ROWS, HD), jnp.bfloat16),
+            jax.ShapeDtypeStruct((ZN, ROWS, HD), jnp.bfloat16),
+            small,
+            small,
+        ),
         in_specs=[smem, vmem, vmem, vmem],
-        out_specs=(vmem, vmem, vmem),
+        out_specs=(vmem,) * 4,
         scratch_shapes=[pltpu.VMEM((ROWS, HD), jnp.float32)],
     )(own_parents.reshape(SB), projected, cosines, sines)
     last = PAIRS.index((STEPS - 1, 0))
     appended = jnp.stack([key_chain[last:], value_chain[last:]], axis=2)
     appended = appended[:, :, None].astype(jnp.bfloat16)
 
-    everyone = spread(queries, "z", ZN)
+    everyone = exchange(everyone, "z")
     everyone = spread(everyone.reshape(ZN * ROWS, HD), "x", XN).reshape(XN * ZN, ROWS, HD)
     partial = pl.pallas_call(
         attention,
-        out_shape=jax.ShapeDtypeStruct((XN * ZN, BLOCK, HD), jnp.float32),
+        out_shape=jax.ShapeDtypeStruct((XN * ZN, BLOCK, HD), jnp.bfloat16),
         in_specs=[smem, smem, smem, vmem, vmem, vmem, vmem],
         out_specs=vmem,
         scratch_shapes=[
             pltpu.VMEM((XN * ZN, ROWS, HD), jnp.float32),
             pltpu.VMEM((XN * ZN, ROWS, HD), jnp.float32),
+            pltpu.VMEM((XN * ZN, ROWS, HD), jnp.float32),
         ],
         compiler_params=pltpu.CompilerParams(vmem_limit_bytes=40 << 20),
     )(owner, group, count, everyone, root_tiles, cache, other_cache)
@@ -315,34 +408,37 @@
     partial = pl.pallas_call(
         merge,
         grid=(ZN,),
-        out_shape=jax.ShapeDtypeStruct((ZN, BLOCK, HD), jnp.float32),
+        out_shape=jax.ShapeDtypeStruct((ZN, BLOCK, HD), jnp.bfloat16),
         in_specs=[pl.BlockSpec((XN, 1, BLOCK, HD), lambda i: (0, i, 0, 0))],
         out_specs=pl.BlockSpec((1, BLOCK, HD), lambda i: (i, 0, 0)),
     )(partial)
     partial = exchange(partial, "z")
     attended = pl.pallas_call(
         finish,
-        out_shape=jax.ShapeDtypeStruct((SB, HEADS * HD), jnp.bfloat16),
+        out_shape=jax.ShapeDtypeStruct((ZN, SB, HEADS * HD), jnp.bfloat16),
         in_specs=[vmem] * 4,
         out_specs=vmem,
         scratch_shapes=[pltpu.VMEM((SB, HEADS * HD), jnp.float32)],
     )(partial, queries, key_chain, value_chain)
 
-    attended = spread(attended, "z", ZN).reshape(rows, HEADS * HD)
-    turned = spread(w_out.T, "x", XN)
-    turned = spread(turned, "core", CN)
-    turned = turned.reshape(CN, XN, width_part, -1).transpose(1, 0, 2, 3).reshape(gathered, -1)
-    result = lax.dot_general(
-        attended, turned, (((1,), (1,)), ((), ())), preferred_element_type=jnp.float32
-    )
-    result = lax.psum(result, "kv")
-    result = (stream + result).astype(jnp.bfloat16)
-    result = result.reshape(rows, JN, width_part).transpose(1, 0, 2)
-    result = jnp.concatenate([result[:, :half], result[:, half:]], axis=2)
-    result = exchange(result, XC)
-    result = jnp.concatenate([result[:, :, :width_part], result[:, :, width_part:]], axis=1)
-    result = result.reshape(JN, ZN, STEPS, GROUP, width_part).transpose(2, 1, 0, 3, 4)
-    return (result.reshape(STEPS, beams, width_part), appended)
+    attended = exchange(attended, "z").reshape(rows, HEADS * HD)
+    result = pl.pallas_call(
+        deliver,
+        out_shape=jax.ShapeDtypeStruct((KN, XN, QUARTER, 2 * PART), jnp.float32),
+        in_specs=[smem] + [vmem] * (1 + 2 * XN),
+        out_specs=vmem,
+        scratch_shapes=[pltpu.VMEM((XN, 2 * PART, HEADS * HD), jnp.bfloat16)],
+    )(place, attended, *turned)
+    result = exchange(result, "kv")
+    result = pl.pallas_call(
+        settle,
+        out_shape=jax.ShapeDtypeStruct((KN, XN, CN, SB, 2 * PART), jnp.bfloat16),
+        in_specs=[smem, vmem, vmem],
+        out_specs=vmem,
+    )(place, result, stream)
+    result = exchange(result.reshape(KN * JN, SB, 2 * PART), ("kv",) + XC)
+    result = result.reshape(KN, JN, STEPS, GROUP, 2, PART).transpose(2, 0, 4, 1, 3, 5)
+    return (result.reshape(STEPS, beams, PART), appended)
 
 
 def solution(mesh):

time: 318 us -> 236 us (0.74)
  waiting for transfers between devices: 126 us -> 76.9 us
  blocking collectives: 72.2 us -> 38.1 us
  between operations: 14.5 us -> 1.19 us
  starting transfers between devices: 51.9 us -> 63.9 us
  Pallas kernels: 23.2 us -> 29.3 us
    psum x1 -> x0, waiting for transfers between devices: 39.7 us -> none  [body(): result = lax.psum(result, 'kv')]
    all_to_all x3 -> x2, blocking collectives: 72.2 us -> 38.1 us  [exchange(): return lax.all_to_all(value, axis, 0, 0, tiled=True)]
    ppermute x0 -> x14, starting transfers between devices: none -> 22 us  [the longest x8 14.1 us: ring(): return own + [lax.ppermute(part, 'core', [(0, 1), (1, 0)]) for part in own]]
    all_to_all x10 -> x8, waiting for transfers between devices: 86 us -> 70.6 us  [exchange(): return lax.all_to_all(value, axis, 0, 0, tiled=True)]
    all_to_all x10 -> x8, starting transfers between devices: 51.4 us -> 40 us  [exchange(): return lax.all_to_all(value, axis, 0, 0, tiled=True)]
    pallas_call x1 -> x4, Pallas kernels: 2.34 us -> 10.2 us  [the longest x1 3.17 us: body(): pl.pallas_call(project, out_shape=jax.ShapeDtypeStruct((rows, columns), j...]
    ppermute x0 -> x14, waiting for transfers between devices: none -> 6.29 us  [the longest x6 5.3 us: ring(): lax.ppermute(value, 'x', [(i, (i + hop) % XN) for i in range(XN)])]
    broadcast_in_dim x9 -> x3, local copies, waits for them, and re-layouts: 8.12 us -> 1.96 us  [spread(): return exchange(jnp.broadcast_to(value[None], (count,) + value.shape), axis)]
  transfers between devices with their start and end apart: 12 -> 23, of which waited for: 10 -> 11; matrix products, arithmetic and copies ran while one was open for 4% -> 6% of each run, Pallas kernels for 3% -> 1%
where the time goes in v2:
time: 236 us; the launch traced here: 233 us
  waiting for transfers between devices  76.9 us (33%)
  starting transfers between devices  63.9 us (27%)
  blocking collectives  38.1 us (16%)
  Pallas kernels  29.3 us (12%)
  local copies, waits for them, and re-layouts  15.1 us (6%)
  other arithmetic  8.58 us (4%)
    all_to_all x8, waiting for transfers between devices, exchange(): return lax.all_to_all(value, axis, 0, 0, tiled=True)  70.6 us
    all_to_all x8, starting transfers between devices, exchange(): return lax.all_to_all(value, axis, 0, 0, tiled=True)  40 us
    all_to_all x2, blocking collectives, exchange(): return lax.all_to_all(value, axis, 0, 0, tiled=True)  38.1 us
    ppermute x8, starting transfers between devices, ring(): return own + [lax.ppermute(part, 'core', [(0, 1), (1, 0)]) for part in own]  14.1 us
    pallas_call x1, Pallas kernels, body(): pl.pallas_call(attention, out_shape=jax.ShapeDtypeStruct((XN * ZN, BLOCK,...  10.9 us
    ppermute x6, starting transfers between devices, ring(): lax.ppermute(value, 'x', [(i, (i + hop) % XN) for i in range(XN)])  7.91 us
    unnamed x59, local copies, waits for them, and re-layouts  6.77 us
    pallas_call x1, Pallas kernels, body(): pl.pallas_call(merge, grid=(ZN,), out_shape=jax.ShapeDtypeStruct((ZN, BLO...  6.07 us
  transfers between devices with their start and end apart: 23, of which 11 were waited for; matrix products, arithmetic and copies ran while one was open for 6% of the time, Pallas kernels for 1%

profile of v2, /device:TPU:1, one launch (start us, length us, event | category | flops | bytes accessed | tf_op | source)
XLA Modules:
  0.0 233.1 jit_solution(18292543205084394945)
XLA Ops:
  0.7 0.7 reduce-precision_convert_fusion.1
  1.4 1.1 copy.111
  3.4 0.7 pad_maximum_fusion
  4.1 6.5 %all-to-all-start = ((bf16[8,104,128]{2,1,0:T(8,128)(2,1)}), bf16[8,104,128]{2,1,0:T(8,128)(2,1)S(1)}, u32[]{:S(2)}, u32[]{:S(2)}) async-start(bf16[8,104,128]{2,1,0:T(8,128)(2,1)} %pad_maximum_fusion), calls=%async_computation | async-start | bytes 425984 | tf_op jit(solution)/shard_map/all_to_all | solution.py:34
  10.7 1.5 collective-permute-start
  12.2 2.4 %collective-permute-start.1 = (bf16[64,1280]{1,0:T(8,128)(2,1)S(1)}, bf16[64,1280]{1,0:T(8,128)(2,1)S(1)}, u32[]{:S(2)}, u32[]{:S(2)}) collective-permute-start(bf16[64,1280]{1,0:T(8,128)(2,1)S(1)} %constant_dynamic-update-slice_fusion.rest_0_), channel_id=1, source_target_pairs={{0,4},{2,6},{4,0},{6,2},{1,5},{3,7},{5,1},{7,3},{8,12},{10,14},{12... | collective-permute-start | bytes 491528 | tf_op jit(solution)/shard_map/ppermute | solution.py:44
  14.6 1.2 collective-permute-start.2
  15.8 1.2 collective-permute-start.3
  17.6 2.6 %collective-permute-done.rest_1_ = bf16[64,1280]{1,0:T(8,128)(2,1)S(1)} collective-permute-done((bf16[64,1280]{1,0:T(8,128)(2,1)S(1)}, bf16[64,1280]{1,0:T(8,128)(2,1)S(1)}, u32[]{:S(2)}, u32[]{:S(2)}) %collective-permute-start) | collective-permute-done | bytes 163872 | tf_op jit(solution)/shard_map/ppermute | solution.py:44
  20.2 0.9 collective-permute-start.4
  21.1 2.7 %collective-permute-done.1.rest_2_ = bf16[64,1280]{1,0:T(8,128)(2,1)S(1)} collective-permute-done((bf16[64,1280]{1,0:T(8,128)(2,1)S(1)}, bf16[64,1280]{1,0:T(8,128)(2,1)S(1)}, u32[]{:S(2)}, u32[]{:S(2)}) %collective-permute-start.1) | collective-permute-done | bytes 163872 | tf_op jit(solution)/shard_map/ppermute | solution.py:44
  23.8 0.9 collective-permute-start.5
  25.9 7.4 %all-to-all-start.1 = ((f32[8,2,128]{2,1,0:T(2,128)}), f32[8,2,128]{2,1,0:T(2,128)S(1)}, u32[]{:S(2)}, u32[]{:S(2)}) async-start(f32[8,2,128]{2,1,0:T(2,128)} %broadcast_in_dim.117), calls=%async_computation.1 | async-start | bytes 16384 | tf_op jit(solution)/shard_map/all_to_all | solution.py:34
  35.2 4.8 %all-to-all-done.1 = f32[8,2,128]{2,1,0:T(2,128)S(1)} async-done(((f32[8,2,128]{2,1,0:T(2,128)}), f32[8,2,128]{2,1,0:T(2,128)S(1)}, u32[]{:S(2)}, u32[]{:S(2)}) %all-to-all-start.1) | async-done | bytes 8224 | tf_op jit(solution)/shard_map/all_to_all | solution.py:34
  40.0 0.8 multiply_convert_fusion.rows_ref
  42.2 3.2 %shard_map.113 = f32[192,1280]{1,0:T(8,128)} custom-call(s32[3]{0:T(128)} %pad_add_fusion.place_ref, bf16[4,192,128]{2,1,0:T(8,128)(2,1)} %multiply_convert_fusion.rows_ref, bf16[64,1280]{1,0:T(8,128)(2,1)} %copy-done.4, bf16[64,1280]{1,0:T(8,128)(2,1)} %copy-done.5, bf16[64,1280]{1,0:T(8,128)(2,1)} %copy-done.6, bf16[64,1280]{1,0:T(8,128)(2,1)} %copy-done.7, ...), custom_call_target="tpu_custom_call" | custom-call | tf_op jit(solution)/shard_map/pallas_call | solution.py:366
  45.4 3.6 %all-to-all-start.2 = ((f32[8,24,1280]{2,1,0:T(8,128)}), f32[8,24,1280]{2,1,0:T(8,128)S(1)}, u32[]{:S(2)}, u32[]{:S(2)}) async-start(f32[8,24,1280]{2,1,0:T(8,128)} %bitcast.52), calls=%async_computation.2 | async-start | bytes 1966080 | tf_op jit(solution)/shard_map/all_to_all | solution.py:34
  49.0 1.9 collective-permute-start.7
  53.6 23.1 %all-to-all-done.2.parts_ref = f32[8,24,1280]{2,1,0:T(8,128)S(1)} async-done(((f32[8,24,1280]{2,1,0:T(8,128)}), f32[8,24,1280]{2,1,0:T(8,128)S(1)}, u32[]{:S(2)}, u32[]{:S(2)}) %all-to-all-start.2) | async-done | bytes 983072 | tf_op jit(solution)/shard_map/all_to_all | solution.py:34
  76.7 1.0 copy-done
  77.6 2.1 shard_map.114
  79.7 3.5 %all-to-all-start.3 = ((bf16[8,192,128]{2,1,0:T(8,128)(2,1)}), bf16[8,192,128]{2,1,0:T(8,128)(2,1)S(1)}, u32[]{:S(2)}, u32[]{:S(2)}) async-start(bf16[8,192,128]{2,1,0:T(8,128)(2,1)} %get-tuple-element.6), calls=%async_computation.3 | async-start | bytes 786432 | tf_op jit(solution)/shard_map/all_to_all | solution.py:34
  83.6 14.7 %all-to-all-done.3 = bf16[8,192,128]{2,1,0:T(8,128)(2,1)S(1)} async-done(((bf16[8,192,128]{2,1,0:T(8,128)(2,1)}), bf16[8,192,128]{2,1,0:T(8,128)(2,1)S(1)}, u32[]{:S(2)}, u32[]{:S(2)}) %all-to-all-start.3) | async-done | bytes 393248 | tf_op jit(solution)/shard_map/all_to_all | solution.py:34
  98.3 1.3 broadcast_in_dim.126
  99.6 3.9 %all-to-all-start.4 = ((bf16[4,1536,128]{2,1,0:T(8,128)(2,1)}), bf16[4,1536,128]{2,1,0:T(8,128)(2,1)S(1)}, u32[]{:S(2)}, u32[]{:S(2)}) async-start(bf16[4,1536,128]{2,1,0:T(8,128)(2,1)} %broadcast_in_dim.126), calls=%async_computation.4 | async-start | bytes 3145728 | tf_op jit(solution)/shard_map/all_to_all | solution.py:34
  104.3 3.6 %fusion.1 = (s32[64]{0:T(128)S(1)}, s32[64]{0:T(128)S(1)}) fusion(s32[256,128]{1,0:T(8,128)S(1)} %copy.110, s32[256,128]{1,0:T(8,128)S(1)} %eq.77, s32[64]{0:T(128)S(1)} %pad_add_fusion.1, s32[256,128]{1,0:T(8,128)S(1)} %multiply_add_fusion), kind=kLoop, calls=%fused_computation.3 | loop fusion | flops 10485632 | bytes 393984 | tf_op jit(solution)/shard_map/reduce_max | solution.py:331
  108.0 15.6 %all-to-all-done.4 = bf16[4,1536,128]{2,1,0:T(8,128)(2,1)S(1)} async-done(((bf16[4,1536,128]{2,1,0:T(8,128)(2,1)}), bf16[4,1536,128]{2,1,0:T(8,128)(2,1)S(1)}, u32[]{:S(2)}, u32[]{:S(2)}) %all-to-all-start.4) | async-done | bytes 1572896 | tf_op jit(solution)/shard_map/all_to_all | solution.py:34
  123.8 10.9 %shard_map.115 = bf16[32,216,128]{2,1,0:T(8,128)(2,1)S(1)} custom-call(s32[64]{0:T(128)S(1)} %get-tuple-element.31.owner_ref, s32[64]{0:T(128)S(1)} %fusion.17.group_ref, s32[64]{0:T(128)S(1)} %get-tuple-element.28.count_ref, bf16[32,192,128]{2,1,0:T(8,128)(2,1)S(1)} %bitcast.50, s32[32,24,128]{2,1,0:T(8,128)S(1)} %broadcast_in_dim.128.root_ref, ...), custom_call_target="tpu_custom_call" | custom-call | tf_op jit(solution)/shard_map/pallas_call | solution.py:394
  134.7 22.6 %all_to_all.50 = bf16[4,1728,128]{2,1,0:T(8,128)(2,1)} all-to-all(bf16[4,1728,128]{2,1,0:T(8,128)(2,1)S(1)} %bitcast.49), channel_id=1, replica_groups=mesh['kv'=4,'z'=8,'x'=4,'core'=2] {'x'}, dimensions={0} | all-to-all | bytes 3538944 | tf_op jit(solution)/shard_map/all_to_all | solution.py:34
  157.3 6.1 %shard_map.116 = bf16[8,216,128]{2,1,0:T(8,128)(2,1)} custom-call(bf16[4,8,216,128]{3,2,1,0:T(8,128)(2,1)} %bitcast.51), custom_call_target="tpu_custom_call" | custom-call | tf_op jit(solution)/shard_map/pallas_call | solution.py:408
  163.4 15.5 %all_to_all.51.parts_ref = bf16[8,216,128]{2,1,0:T(8,128)(2,1)} all-to-all(bf16[8,216,128]{2,1,0:T(8,128)(2,1)} %shard_map.116), channel_id=1, replica_groups=mesh['kv'=4,'z'=8,'x'=4,'core'=2] {'z'}, dimensions={0} | all-to-all | bytes 884736 | tf_op jit(solution)/shard_map/all_to_all | solution.py:34
  178.9 2.3 %shard_map.117 = bf16[8,24,1024]{2,1,0:T(8,128)(2,1)} custom-call(bf16[8,216,128]{2,1,0:T(8,128)(2,1)} %all_to_all.51.parts_ref, bf16[192,128]{1,0:T(8,128)(2,1)} %get-tuple-element.7.q_ref, f32[6,8,128]{2,1,0:T(8,128)} %get-tuple-element.8.k_ref, f32[6,8,128]{2,1,0:T(8,128)} %get-tuple-element.9.v_ref), custom_call_target="tpu_custom_call" | custom-call | tf_op jit(solution)/shard_map/pallas_call | solution.py:416
  181.2 3.5 %all-to-all-start.7 = ((bf16[8,24,1024]{2,1,0:T(8,128)(2,1)}), bf16[8,24,1024]{2,1,0:T(8,128)(2,1)S(1)}, u32[]{:S(2)}, u32[]{:S(2)}) async-start(bf16[8,24,1024]{2,1,0:T(8,128)(2,1)} %shard_map.117), calls=%async_computation.7 | async-start | bytes 786432 | tf_op jit(solution)/shard_map/all_to_all | solution.py:34
  185.1 1.8 collective-permute-start.9
  186.8 0.7 collective-permute-start.10
  187.5 6.2 %collective-permute-start.11 = (bf16[64,1024]{1,0:T(8,128)(2,1)S(1)}, bf16[64,1024]{1,0:T(8,128)(2,1)S(1)}, u32[]{:S(2)}, u32[]{:S(2)}) collective-permute-start(bf16[64,1024]{1,0:T(8,128)(2,1)S(1)} %bitcast.69), channel_id=1, source_target_pairs={{0,1},{1,0},{2,3},{3,2},{4,5},{5,4},{6,7},{7,6},{8,9},{9,8},{10,11... | collective-permute-start | bytes 393224 | tf_op jit(solution)/shard_map/ppermute | solution.py:45
  193.8 3.9 %collective-permute-start.12 = (bf16[64,1024]{1,0:T(8,128)(2,1)S(1)}, bf16[64,1024]{1,0:T(8,128)(2,1)S(1)}, u32[]{:S(2)}, u32[]{:S(2)}) collective-permute-start(bf16[64,1024]{1,0:T(8,128)(2,1)S(1)} %collective-permute-done.8.rest_1_), channel_id=1, source_target_pairs={{0,1},{1,0},{2,3},{3,2},{4,5},{5,4},{6,7},{7,6},{8,9},{9,8},{10,11... | collective-permute-start | bytes 393224 | tf_op jit(solution)/shard_map/ppermute | solution.py:45
  197.8 0.7 collective-permute-start.14
  200.4 2.8 %shard_map.118 = f32[4,4,48,128]{3,2,1,0:T(8,128)} custom-call(s32[3]{0:T(128)} %pad_add_fusion.place_ref, bf16[192,1024]{1,0:T(8,128)(2,1)} %bitcast.57, bf16[64,1024]{1,0:T(8,128)(2,1)} %bitcast.65, bf16[64,1024]{1,0:T(8,128)(2,1)} %copy-done.15, bf16[64,1024]{1,0:T(8,128)(2,1)} %copy-done.16, bf16[64,1024]{1,0:T(8,128)(2,1)} %copy-done.17, ...), custom_call_target="tpu_custom_call" | custom-call | tf_op jit(solution)/shard_map/pallas_call | solution.py:425
  203.2 4.2 %all-to-all-start.8 = ((f32[4,4,48,128]{3,2,1,0:T(8,128)}), f32[4,4,48,128]{3,2,1,0:T(8,128)S(1)}, u32[]{:S(2)}, u32[]{:S(2)}) async-start(f32[4,4,48,128]{3,2,1,0:T(8,128)} %shard_map.118), calls=%async_computation.8 | async-start | bytes 786432 | tf_op jit(solution)/shard_map/all_to_all | solution.py:34
  207.4 0.7 fusion.6
  208.1 5.5 %all-to-all-done.8.parts_ref = f32[4,4,48,128]{3,2,1,0:T(8,128)S(1)} async-done(((f32[4,4,48,128]{3,2,1,0:T(8,128)}), f32[4,4,48,128]{3,2,1,0:T(8,128)S(1)}, u32[]{:S(2)}, u32[]{:S(2)}) %all-to-all-start.8) | async-done | bytes 393248 | tf_op jit(solution)/shard_map/all_to_all | solution.py:34
  213.6 0.7 copy-done.2
  214.4 1.9 shard_map.119
  216.2 7.5 %all-to-all-start.9 = ((bf16[32,24,128]{2,1,0:T(8,128)(2,1)}), bf16[32,24,128]{2,1,0:T(8,128)(2,1)S(1)}, u32[]{:S(2)}, u32[]{:S(2)}) async-start(bf16[32,24,128]{2,1,0:T(8,128)(2,1)} %bitcast.59), calls=%async_computation.9 | async-start | bytes 393216 | tf_op jit(solution)/shard_map/all_to_all | solution.py:34
  223.8 0.7 fusion.7
  225.1 6.9 %all-to-all-done.9 = bf16[32,24,128]{2,1,0:T(8,128)(2,1)S(1)} async-done(((bf16[32,24,128]{2,1,0:T(8,128)(2,1)}), bf16[32,24,128]{2,1,0:T(8,128)(2,1)S(1)}, u32[]{:S(2)}, u32[]{:S(2)}) %all-to-all-start.9) | async-done | bytes 196640 | tf_op jit(solution)/shard_map/all_to_all | solution.py:34
  232.3 0.8 copy.126
  (138 shorter events, 13.0 us)
Async XLA Ops:
  0.6 10.0 %copy-start.13 = (bf16[64,1024]{1,0:T(8,128)(2,1)S(1)}, bf16[64,1024]{1,0:T(8,128)(2,1)}, u32[]{:S(2)}) copy-start(bf16[64,1024]{1,0:T(8,128)(2,1)} %param.12) | copy-start | bytes 393220
  0.6 10.0 %copy-start.22 = (bf16[64,128]{1,0:T(8,128)(2,1)S(1)}, bf16[64,128]{1,0:T(8,128)(2,1)}, u32[]{:S(2)}) copy-start(bf16[64,128]{1,0:T(8,128)(2,1)} %param.13) | copy-start | bytes 49156
  0.7 10.0 %copy-start.23 = (bf16[64,128]{1,0:T(8,128)(2,1)S(1)}, bf16[64,128]{1,0:T(8,128)(2,1)}, u32[]{:S(2)}) copy-start(bf16[64,128]{1,0:T(8,128)(2,1)} %param.14) | copy-start | bytes 49156
  4.1 20.7 %all-to-all-start = ((bf16[8,104,128]{2,1,0:T(8,128)(2,1)}), bf16[8,104,128]{2,1,0:T(8,128)(2,1)S(1)}, u32[]{:S(2)}, u32[]{:S(2)}) async-start(bf16[8,104,128]{2,1,0:T(8,128)(2,1)} %pad_maximum_fusion), calls=%async_computation | async-start | bytes 425984 | tf_op jit(solution)/shard_map/all_to_all | solution.py:34
  10.7 24.4 %copy-start.4 = (bf16[64,1280]{1,0:T(8,128)(2,1)}, bf16[64,1280]{1,0:T(8,128)(2,1)S(1)}, u32[]{:S(2)}) copy-start(bf16[64,1280]{1,0:T(8,128)(2,1)S(1)} %constant_dynamic-update-slice_fusion.rest_0_) | copy-start | bytes 491524
  10.7 9.5 %collective-permute-start = (bf16[64,1280]{1,0:T(8,128)(2,1)S(1)}, bf16[64,1280]{1,0:T(8,128)(2,1)S(1)}, u32[]{:S(2)}, u32[]{:S(2)}) collective-permute-start(bf16[64,1280]{1,0:T(8,128)(2,1)S(1)} %constant_dynamic-update-slice_fusion.rest_0_), channel_id=1, source_target_pairs={{0,2},{2,4},{4,6},{6,0},{1,3},{3,5},{5,7},{7,1},{8,10},{10,12},{12... | collective-permute-start | bytes 491528 | tf_op jit(solution)/shard_map/ppermute | solution.py:44
  12.2 11.6 %collective-permute-start.1 = (bf16[64,1280]{1,0:T(8,128)(2,1)S(1)}, bf16[64,1280]{1,0:T(8,128)(2,1)S(1)}, u32[]{:S(2)}, u32[]{:S(2)}) collective-permute-start(bf16[64,1280]{1,0:T(8,128)(2,1)S(1)} %constant_dynamic-update-slice_fusion.rest_0_), channel_id=1, source_target_pairs={{0,4},{2,6},{4,0},{6,2},{1,5},{3,7},{5,1},{7,3},{8,12},{10,14},{12... | collective-permute-start | bytes 491528 | tf_op jit(solution)/shard_map/ppermute | solution.py:44
  14.6 10.1 %collective-permute-start.2 = (bf16[64,1280]{1,0:T(8,128)(2,1)S(1)}, bf16[64,1280]{1,0:T(8,128)(2,1)S(1)}, u32[]{:S(2)}, u32[]{:S(2)}) collective-permute-start(bf16[64,1280]{1,0:T(8,128)(2,1)S(1)} %constant_dynamic-update-slice_fusion.rest_0_), channel_id=1, source_target_pairs={{0,6},{2,0},{4,2},{6,4},{1,7},{3,1},{5,3},{7,5},{8,14},{10,8},{12,... | collective-permute-start | bytes 491528 | tf_op jit(solution)/shard_map/ppermute | solution.py:44
  15.8 25.0 %collective-permute-start.3 = (bf16[64,1280]{1,0:T(8,128)(2,1)S(1)}, bf16[64,1280]{1,0:T(8,128)(2,1)S(1)}, u32[]{:S(2)}, u32[]{:S(2)}) collective-permute-start(bf16[64,1280]{1,0:T(8,128)(2,1)S(1)} %constant_dynamic-update-slice_fusion.rest_0_), channel_id=1, source_target_pairs={{0,1},{1,0},{2,3},{3,2},{4,5},{5,4},{6,7},{7,6},{8,9},{9,8},{10,11... | collective-permute-start | bytes 491528 | tf_op jit(solution)/shard_map/ppermute | solution.py:45
  20.2 14.9 %copy-start.5 = (bf16[64,1280]{1,0:T(8,128)(2,1)}, bf16[64,1280]{1,0:T(8,128)(2,1)S(1)}, u32[]{:S(2)}) copy-start(bf16[64,1280]{1,0:T(8,128)(2,1)S(1)} %collective-permute-done.rest_1_) | copy-start | bytes 491524
  20.2 20.6 %collective-permute-start.4 = (bf16[64,1280]{1,0:T(8,128)(2,1)S(1)}, bf16[64,1280]{1,0:T(8,128)(2,1)S(1)}, u32[]{:S(2)}, u32[]{:S(2)}) collective-permute-start(bf16[64,1280]{1,0:T(8,128)(2,1)S(1)} %collective-permute-done.rest_1_), channel_id=1, source_target_pairs={{0,1},{1,0},{2,3},{3,2},{4,5},{5,4},{6,7},{7,6},{8,9},{9,8},{10,11... | collective-permute-start | bytes 491528 | tf_op jit(solution)/shard_map/ppermute | solution.py:45
  23.8 11.3 %copy-start.6 = (bf16[64,1280]{1,0:T(8,128)(2,1)}, bf16[64,1280]{1,0:T(8,128)(2,1)S(1)}, u32[]{:S(2)}) copy-start(bf16[64,1280]{1,0:T(8,128)(2,1)S(1)} %collective-permute-done.1.rest_2_) | copy-start | bytes 491524
  23.8 17.0 %collective-permute-start.5 = (bf16[64,1280]{1,0:T(8,128)(2,1)S(1)}, bf16[64,1280]{1,0:T(8,128)(2,1)S(1)}, u32[]{:S(2)}, u32[]{:S(2)}) collective-permute-start(bf16[64,1280]{1,0:T(8,128)(2,1)S(1)} %collective-permute-done.1.rest_2_), channel_id=1, source_target_pairs={{0,1},{1,0},{2,3},{3,2},{4,5},{5,4},{6,7},{7,6},{8,9},{9,8},{10,11... | collective-permute-start | bytes 491528 | tf_op jit(solution)/shard_map/ppermute | solution.py:45
  24.7 10.4 %copy-start.7 = (bf16[64,1280]{1,0:T(8,128)(2,1)}, bf16[64,1280]{1,0:T(8,128)(2,1)S(1)}, u32[]{:S(2)}) copy-start(bf16[64,1280]{1,0:T(8,128)(2,1)S(1)} %collective-permute-done.2.rest_3_) | copy-start | bytes 491524
  24.7 16.1 %collective-permute-start.6 = (bf16[64,1280]{1,0:T(8,128)(2,1)S(1)}, bf16[64,1280]{1,0:T(8,128)(2,1)S(1)}, u32[]{:S(2)}, u32[]{:S(2)}) collective-permute-start(bf16[64,1280]{1,0:T(8,128)(2,1)S(1)} %collective-permute-done.2.rest_3_), channel_id=1, source_target_pairs={{0,1},{1,0},{2,3},{3,2},{4,5},{5,4},{6,7},{7,6},{8,9},{9,8},{10,11... | collective-permute-start | bytes 491528 | tf_op jit(solution)/shard_map/ppermute | solution.py:45
  25.9 14.0 %all-to-all-start.1 = ((f32[8,2,128]{2,1,0:T(2,128)}), f32[8,2,128]{2,1,0:T(2,128)S(1)}, u32[]{:S(2)}, u32[]{:S(2)}) async-start(f32[8,2,128]{2,1,0:T(2,128)} %broadcast_in_dim.117), calls=%async_computation.1 | async-start | bytes 16384 | tf_op jit(solution)/shard_map/all_to_all | solution.py:34
  35.1 10.3 %copy-start.1 = (f32[4,192,128]{2,1,0:T(8,128)}, f32[4,192,128]{2,1,0:T(8,128)S(1)}, u32[]{:S(2)}) copy-start(f32[4,192,128]{2,1,0:T(8,128)S(1)} %reshape.183.stream_ref) | copy-start | bytes 1179652
  40.8 10.1 %copy-start.25 = (s32[3,512]{1,0:T(4,128)S(1)}, s32[3,512]{1,0:T(4,128)}, u32[]{:S(2)}) copy-start(s32[3,512]{1,0:T(4,128)} %param.19) | copy-start | bytes 18436
  40.8 10.6 %copy-start.24 = (s32[512]{0:T(512)S(1)}, s32[512]{0:T(512)}, u32[]{:S(2)}) copy-start(s32[512]{0:T(512)} %param.17) | copy-start | bytes 6148
  40.8 0.7 copy-start.9
  40.8 0.8 copy-start.10
  41.6 0.7 copy-start.11
  45.4 31.3 %all-to-all-start.2 = ((f32[8,24,1280]{2,1,0:T(8,128)}), f32[8,24,1280]{2,1,0:T(8,128)S(1)}, u32[]{:S(2)}, u32[]{:S(2)}) async-start(f32[8,24,1280]{2,1,0:T(8,128)} %bitcast.52), calls=%async_computation.2 | async-start | bytes 1966080 | tf_op jit(solution)/shard_map/all_to_all | solution.py:34
  49.0 59.0 %collective-permute-start.7 = (bf16[32,2,128,128]{3,2,1,0:T(8,128)(2,1)}, bf16[32,2,128,128]{3,2,1,0:T(8,128)(2,1)}, u32[]{:S(2)}, u32[]{:S(2)}) collective-permute-start(bf16[32,2,128,128]{3,2,1,0:T(8,128)(2,1)} %bitcast.26.own_ref), channel_id=1, source_target_pairs={{0,1},{1,0},{2,3},{3,2},{4,5},{5,4},{6,7},{7,6},{8,9},{9,8},{10,11... | collective-permute-start | bytes 6291464 | tf_op jit(solution)/shard_map/ppermute | solution.py:303
  76.7 1.0 copy-start
  79.7 18.5 %all-to-all-start.3 = ((bf16[8,192,128]{2,1,0:T(8,128)(2,1)}), bf16[8,192,128]{2,1,0:T(8,128)(2,1)S(1)}, u32[]{:S(2)}, u32[]{:S(2)}) async-start(bf16[8,192,128]{2,1,0:T(8,128)(2,1)} %get-tuple-element.6), calls=%async_computation.3 | async-start | bytes 786432 | tf_op jit(solution)/shard_map/all_to_all | solution.py:34
  99.6 4.2 %copy-start.12 = (s32[512,64]{0,1:T(8,128)S(1)}, s32[512,64]{0,1:T(8,128)}, u32[]{:S(2)}) copy-start(s32[512,64]{0,1:T(8,128)} %param.18) | copy-start | bytes 393220
  99.6 24.0 %all-to-all-start.4 = ((bf16[4,1536,128]{2,1,0:T(8,128)(2,1)}), bf16[4,1536,128]{2,1,0:T(8,128)(2,1)S(1)}, u32[]{:S(2)}, u32[]{:S(2)}) async-start(bf16[4,1536,128]{2,1,0:T(8,128)(2,1)} %broadcast_in_dim.126), calls=%async_computation.4 | async-start | bytes 3145728 | tf_op jit(solution)/shard_map/all_to_all | solution.py:34
  157.3 27.4 %copy-start.14 = (bf16[1024,64]{0,1:T(8,128)(2,1)S(1)}, bf16[1024,64]{0,1:T(8,128)(2,1)}, u32[]{:S(2)}) copy-start(bf16[1024,64]{0,1:T(8,128)(2,1)} %param.15) | copy-start | bytes 393220
  181.2 18.4 %all-to-all-start.7 = ((bf16[8,24,1024]{2,1,0:T(8,128)(2,1)}), bf16[8,24,1024]{2,1,0:T(8,128)(2,1)S(1)}, u32[]{:S(2)}, u32[]{:S(2)}) async-start(bf16[8,24,1024]{2,1,0:T(8,128)(2,1)} %shard_map.117), calls=%async_computation.7 | async-start | bytes 786432 | tf_op jit(solution)/shard_map/all_to_all | solution.py:34
  184.7 9.1 %collective-permute-start.8 = (bf16[64,1024]{1,0:T(8,128)(2,1)S(1)}, bf16[64,1024]{1,0:T(8,128)(2,1)S(1)}, u32[]{:S(2)}, u32[]{:S(2)}) collective-permute-start(bf16[64,1024]{1,0:T(8,128)(2,1)S(1)} %bitcast.66), channel_id=1, source_target_pairs={{0,2},{2,4},{4,6},{6,0},{1,3},{3,5},{5,7},{7,1},{8,10},{10,12},{12... | collective-permute-start | bytes 393224 | tf_op jit(solution)/shard_map/ppermute | solution.py:44
  185.1 12.7 %collective-permute-start.9 = (bf16[64,1024]{1,0:T(8,128)(2,1)S(1)}, bf16[64,1024]{1,0:T(8,128)(2,1)S(1)}, u32[]{:S(2)}, u32[]{:S(2)}) collective-permute-start(bf16[64,1024]{1,0:T(8,128)(2,1)S(1)} %bitcast.67), channel_id=1, source_target_pairs={{0,4},{2,6},{4,0},{6,2},{1,5},{3,7},{5,1},{7,3},{8,12},{10,14},{12... | collective-permute-start | bytes 393224 | tf_op jit(solution)/shard_map/ppermute | solution.py:44
  186.8 11.0 %collective-permute-start.10 = (bf16[64,1024]{1,0:T(8,128)(2,1)S(1)}, bf16[64,1024]{1,0:T(8,128)(2,1)S(1)}, u32[]{:S(2)}, u32[]{:S(2)}) collective-permute-start(bf16[64,1024]{1,0:T(8,128)(2,1)S(1)} %bitcast.68), channel_id=1, source_target_pairs={{0,6},{2,0},{4,2},{6,4},{1,7},{3,1},{5,3},{7,5},{8,14},{10,8},{12,... | collective-permute-start | bytes 393224 | tf_op jit(solution)/shard_map/ppermute | solution.py:44
  187.5 11.0 %collective-permute-start.11 = (bf16[64,1024]{1,0:T(8,128)(2,1)S(1)}, bf16[64,1024]{1,0:T(8,128)(2,1)S(1)}, u32[]{:S(2)}, u32[]{:S(2)}) collective-permute-start(bf16[64,1024]{1,0:T(8,128)(2,1)S(1)} %bitcast.69), channel_id=1, source_target_pairs={{0,1},{1,0},{2,3},{3,2},{4,5},{5,4},{6,7},{7,6},{8,9},{9,8},{10,11... | collective-permute-start | bytes 393224 | tf_op jit(solution)/shard_map/ppermute | solution.py:45
  193.8 5.8 %copy-start.15 = (bf16[64,1024]{1,0:T(8,128)(2,1)}, bf16[64,1024]{1,0:T(8,128)(2,1)S(1)}, u32[]{:S(2)}) copy-start(bf16[64,1024]{1,0:T(8,128)(2,1)S(1)} %collective-permute-done.8.rest_1_) | copy-start | bytes 393220
  193.8 4.9 %collective-permute-start.12 = (bf16[64,1024]{1,0:T(8,128)(2,1)S(1)}, bf16[64,1024]{1,0:T(8,128)(2,1)S(1)}, u32[]{:S(2)}, u32[]{:S(2)}) collective-permute-start(bf16[64,1024]{1,0:T(8,128)(2,1)S(1)} %collective-permute-done.8.rest_1_), channel_id=1, source_target_pairs={{0,1},{1,0},{2,3},{3,2},{4,5},{5,4},{6,7},{7,6},{8,9},{9,8},{10,11... | collective-permute-start | bytes 393224 | tf_op jit(solution)/shard_map/ppermute | solution.py:45
  197.7 1.9 copy-start.16
  197.7 1.3 collective-permute-start.13
  197.8 1.8 copy-start.17
  197.8 1.7 collective-permute-start.14
  198.6 1.0 copy-start.18
  198.7 0.9 copy-start.19
  199.1 0.7 copy-start.20
  199.6 0.7 copy-start.21
  199.6 0.8 copy-start.3
  203.2 10.4 %all-to-all-start.8 = ((f32[4,4,48,128]{3,2,1,0:T(8,128)}), f32[4,4,48,128]{3,2,1,0:T(8,128)S(1)}, u32[]{:S(2)}, u32[]{:S(2)}) async-start(f32[4,4,48,128]{3,2,1,0:T(8,128)} %shard_map.118), calls=%async_computation.8 | async-start | bytes 786432 | tf_op jit(solution)/shard_map/all_to_all | solution.py:34
  213.6 0.7 copy-start.2
  216.2 15.8 %all-to-all-start.9 = ((bf16[32,24,128]{2,1,0:T(8,128)(2,1)}), bf16[32,24,128]{2,1,0:T(8,128)(2,1)S(1)}, u32[]{:S(2)}, u32[]{:S(2)}) async-start(bf16[32,24,128]{2,1,0:T(8,128)(2,1)} %bitcast.59), calls=%async_computation.9 | async-start | bytes 393216 | tf_op jit(solution)/shard_map/all_to_all | solution.py:34
  (1 other events, 0.7 us)

commit v3 on v2

--- a/solution.py
+++ b/solution.py
@@ -23,7 +23,7 @@
 JN = XN * CN
 KN = 4
 PART = 64
-QUARTER = ZN * SB // KN
+PAIR = GROUP // KN
 PAIRS = [(s, u) for s in range(STEPS) for u in range(s + 1)]
 SCALE = 1.0 / math.sqrt(HD)
 XC = ("x", "core")
@@ -67,30 +67,31 @@
         )
 
 
-def deliver(place_ref, rows_ref, *rest):
-    chunks, out_ref, wide = rest[: 2 * XN], rest[2 * XN], rest[2 * XN + 1]
-    join(place_ref, chunks, wide)
+def collect(place_ref, *rest):
+    join(place_ref, rest[: 2 * XN], rest[2 * XN + 1])
     x = place_ref[0]
     for hop in range(XN):
-        result = lax.dot_general(
-            rows_ref[...],
-            wide[hop],
-            (((1,), (1,)), ((), ())),
-            preferred_element_type=jnp.float32,
+        start = pl.multiple_of((x + XN - hop) % XN * 2 * PART, 2 * PART)
+        rest[2 * XN][pl.ds(start, 2 * PART), :] = rest[2 * XN + 1][hop]
+
+
+def deliver(place_ref, parts_ref, stream_ref, *rest):
+    wides, out_ref = rest[:KN], rest[KN]
+    kv = place_ref[2]
+    count = ZN * GROUP
+    lanes = lax.broadcasted_iota(jnp.int32, (count // 2, 2 * PART), 1)
+    for x in range(XN):
+        columns = slice(x * 2 * PART, (x + 1) * 2 * PART)
+        total = stream_ref[x] + sum(
+            lax.dot_general(
+                parts_ref[(kv + KN - hop) % KN],
+                wides[hop][columns, :],
+                (((1,), (1,)), ((), ())),
+                preferred_element_type=jnp.float32,
+            )
+            for hop in range(KN)
         )
-        for kv in range(KN):
-            out_ref[kv, (x + XN - hop) % XN] = result[kv * QUARTER : (kv + 1) * QUARTER]
-
-
-def settle(place_ref, parts_ref, stream_ref, out_ref):
-    kv = place_ref[2]
-    lanes = lax.broadcasted_iota(jnp.int32, (SB, 2 * PART), 1)
-    for x in range(XN):
-        total = parts_ref[0, x]
-        for source in range(1, KN):
-            total = total + parts_ref[source, x]
-        total = stream_ref[x, pl.ds(pl.multiple_of(kv * QUARTER, 8), QUARTER), :] + total
-        upper, lower = total[:SB], total[SB:]
+        upper, lower = total[: count // 2], total[count // 2 :]
         first = jnp.where(lanes < PART, upper, pltpu.roll(lower, PART, 1)).astype(jnp.bfloat16)
         second = jnp.where(lanes < PART, pltpu.roll(upper, PART, 1), lower).astype(jnp.bfloat16)
         for target in range(KN):
@@ -232,7 +233,7 @@
     out_ref[0] = seal(merged, stat)
 
 
-def finish(parts_ref, q_ref, k_ref, v_ref, out_ref, hold):
+def finish(parts_ref, q_ref, k_ref, v_ref, out_ref, hold, shares):
     count = parts_ref.shape[0]
     sums, stats = zip(*[unseal(parts_ref[source]) for source in range(count)])
     cached_top = functools.reduce(jnp.maximum, stats)
@@ -268,9 +269,15 @@
                     PAIRS.index((step, token))
                 ]
             hold[step * GROUP : (step + 1) * GROUP, head * HD : (head + 1) * HD] = above / below
-    attended = hold[...].astype(jnp.bfloat16)
-    for target in range(ZN):
-        out_ref[target] = attended
+    shares[...] = jnp.zeros_like(shares)
+    for kv in range(KN):
+        for step in range(STEPS):
+            row = step * GROUP + kv * PAIR
+            shares[kv, step * PAIR : (step + 1) * PAIR, :] = hold[row : row + PAIR, :]
+    for kv in range(KN):
+        share = shares[kv].astype(jnp.bfloat16)
+        for target in range(ZN):
+            out_ref[kv, target] = share
 
 
 def compose(parents_near):
@@ -296,7 +303,8 @@
 
     weights = ring(jnp.concatenate([w_query, w_key, w_value], axis=1))
     turned = ring(w_out.T)
-    place = jnp.stack([x, core, lax.axis_index("kv")]).astype(jnp.int32)
+    kv = lax.axis_index("kv")
+    place = jnp.stack([x, core, kv]).astype(jnp.int32)
     vmem = pl.BlockSpec(memory_space=pltpu.VMEM)
     smem = pl.BlockSpec(memory_space=pltpu.SMEM)
     cache = cache_kv[:, 0]
@@ -351,15 +359,18 @@
     ).astype(jnp.bfloat16)
     gain_rows = jnp.concatenate([gain_rows, jnp.zeros((6, HD), jnp.bfloat16)])
     packed = jnp.concatenate([by_row, jnp.broadcast_to(gain_rows[None], (JN, 8, HD))], axis=1)
+    squares = jnp.sum(jnp.square(embeds.astype(jnp.float32)), axis=2)
+    squares = squares.reshape(STEPS, ZN, JN, GROUP).transpose(2, 1, 0, 3).reshape(JN, rows)
+    squares = jnp.pad(squares, ((0, 0), (0, 256 - rows))).reshape(JN, 2, 128)
+    squares = jnp.broadcast_to(squares[None], (ZN, JN, 2, 128)).reshape(groups, 2, 128)
+    squares = exchange(squares, BLK)
     packed = exchange(packed, XC)
     stream = packed[:, :half].reshape(XN, CN, ZN // 2, SB, 2, PART).transpose(0, 2, 4, 3, 1, 5)
     stream = stream.reshape(XN, rows, 2 * PART).astype(jnp.float32)
     tails = packed[:, half : half + 2].astype(jnp.float32)
     gain = tails[:, 0, :PART] + tails[:, 0, PART:] + tails[:, 1, :PART]
     gain = gain.reshape(XN, 1, 2 * PART)
-    squares = jnp.sum(stream * stream, axis=(0, 2))
-    squares = jnp.pad(squares, (0, 256 - rows)).reshape(2, 128)
-    squares = jnp.sum(spread(squares, "z", ZN), axis=0).reshape(256)[:rows]
+    squares = jnp.sum(squares, axis=0).reshape(256)[:rows]
     inverse = lax.rsqrt(squares / width + EPSILON)
     normed = (stream * inverse[None, :, None] * gain).astype(jnp.bfloat16)
     columns = weights[0].shape[1]
@@ -371,6 +382,23 @@
         scratch_shapes=[pltpu.VMEM((XN, 2 * PART, columns), jnp.bfloat16)],
     )(place, normed, *weights)
     projected = exchange(projected.reshape(ZN, SB, columns), "z")
+    projected, turned = lax.optimization_barrier((projected, turned))
+    wide = pl.pallas_call(
+        collect,
+        out_shape=jax.ShapeDtypeStruct((2 * PART * XN, HEADS * HD), jnp.bfloat16),
+        in_specs=[smem] + [vmem] * (2 * XN),
+        out_specs=vmem,
+        scratch_shapes=[pltpu.VMEM((XN, 2 * PART, HEADS * HD), jnp.bfloat16)],
+    )(place, *turned)
+    wides = [wide] + [
+        lax.ppermute(wide, "kv", [(i, (i + hop) % KN) for i in range(KN)])
+        for hop in range(1, KN)
+    ]
+    shares = stream.reshape(XN, ZN, STEPS, KN, PAIR, 2 * PART)
+    shares = lax.dynamic_index_in_dim(shares, kv, 3, keepdims=False)
+    shares = shares.reshape(XN, ZN, STEPS * PAIR, 2 * PART)
+    shares = jnp.pad(shares, ((0, 0), (0, 0), (0, GROUP - STEPS * PAIR), (0, 0)))
+    shares = shares.reshape(XN, ZN * GROUP, 2 * PART)
 
     small = jax.ShapeDtypeStruct((len(PAIRS), GROUP, HD), jnp.float32)
     queries, everyone, key_chain, value_chain = pl.pallas_call(
@@ -405,6 +433,7 @@
     )(owner, group, count, everyone, root_tiles, cache, other_cache)
 
     partial = exchange(partial.reshape(XN, ZN * BLOCK, HD), "x").reshape(XN, ZN, BLOCK, HD)
+    partial, wides = lax.optimization_barrier((partial, wides))
     partial = pl.pallas_call(
         merge,
         grid=(ZN,),
@@ -415,29 +444,26 @@
     partial = exchange(partial, "z")
     attended = pl.pallas_call(
         finish,
-        out_shape=jax.ShapeDtypeStruct((ZN, SB, HEADS * HD), jnp.bfloat16),
+        out_shape=jax.ShapeDtypeStruct((KN, ZN, GROUP, HEADS * HD), jnp.bfloat16),
         in_specs=[vmem] * 4,
         out_specs=vmem,
-        scratch_shapes=[pltpu.VMEM((SB, HEADS * HD), jnp.float32)],
+        scratch_shapes=[
+            pltpu.VMEM((SB, HEADS * HD), jnp.float32),
+            pltpu.VMEM((KN, GROUP, HEADS * HD), jnp.float32),
+        ],
     )(partial, queries, key_chain, value_chain)
 
-    attended = exchange(attended, "z").reshape(rows, HEADS * HD)
+    attended = exchange(attended.reshape(KN * ZN, GROUP, HEADS * HD), ("kv", "z"))
+    attended = attended.reshape(KN, ZN * GROUP, HEADS * HD)
     result = pl.pallas_call(
         deliver,
-        out_shape=jax.ShapeDtypeStruct((KN, XN, QUARTER, 2 * PART), jnp.float32),
-        in_specs=[smem] + [vmem] * (1 + 2 * XN),
+        out_shape=jax.ShapeDtypeStruct((KN, XN, CN, ZN * GROUP // 2, 2 * PART), jnp.bfloat16),
+        in_specs=[smem] + [vmem] * (2 + KN),
         out_specs=vmem,
-        scratch_shapes=[pltpu.VMEM((XN, 2 * PART, HEADS * HD), jnp.bfloat16)],
-    )(place, attended, *turned)
-    result = exchange(result, "kv")
-    result = pl.pallas_call(
-        settle,
-        out_shape=jax.ShapeDtypeStruct((KN, XN, CN, SB, 2 * PART), jnp.bfloat16),
-        in_specs=[smem, vmem, vmem],
-        out_specs=vmem,
-    )(place, result, stream)
-    result = exchange(result.reshape(KN * JN, SB, 2 * PART), ("kv",) + XC)
-    result = result.reshape(KN, JN, STEPS, GROUP, 2, PART).transpose(2, 0, 4, 1, 3, 5)
+    )(place, attended, shares, *wides)
+    result = exchange(result.reshape(KN * JN, ZN * GROUP // 2, 2 * PART), ("kv",) + XC)
+    result = result.reshape(KN, JN, ZN // 2, GROUP, 2, PART)[:, :, :, : STEPS * PAIR]
+    result = result.reshape(KN, JN, ZN // 2, STEPS, PAIR, 2, PART).transpose(3, 5, 2, 1, 0, 4, 6)
     return (result.reshape(STEPS, beams, PART), appended)
 
 

time: 236 us -> 262 us (1.11)
  waiting for transfers between devices: 76.9 us -> 112 us
  blocking collectives: 38.1 us -> 18.2 us
  starting transfers between devices: 63.9 us -> 68.9 us
  local copies, waits for them, and re-layouts: 15.1 us -> 19.4 us
    ppermute x0 -> x3, waiting for transfers between devices: none -> 43.7 us  [body(): lax.ppermute(wide, 'kv', [(i, (i + hop) % KN) for i in range(KN)])]
    all_to_all x2 -> x1, blocking collectives: 38.1 us -> 18.2 us  [exchange(): return lax.all_to_all(value, axis, 0, 0, tiled=True)]
    all_to_all x8, starting transfers between devices: 40 us -> 47.7 us  [exchange(): return lax.all_to_all(value, axis, 0, 0, tiled=True)]
    ppermute x8, starting transfers between devices: 14.1 us -> 7.72 us  [ring(): return own + [lax.ppermute(part, 'core', [(0, 1), (1, 0)]) for part in own]]
    ppermute x0 -> x3, starting transfers between devices: none -> 4.99 us  [body(): lax.ppermute(wide, 'kv', [(i, (i + hop) % KN) for i in range(KN)])]
    ppermute x6, waiting for transfers between devices: 5.3 us -> 1.06 us  [ring(): lax.ppermute(value, 'x', [(i, (i + hop) % XN) for i in range(XN)])]
    all_to_all x8, waiting for transfers between devices: 70.6 us -> 66.9 us  [exchange(): return lax.all_to_all(value, axis, 0, 0, tiled=True)]
    pallas_call x3, Pallas kernels: 7.03 us -> 9.7 us  [the longest x1 4.76 us: body(): pl.pallas_call(deliver, out_shape=jax.ShapeDtypeStruct((KN, XN, CN, ZN *...]
  transfers between devices with their start and end apart: 23 -> 26, of which waited for: 11 -> 11; matrix products, arithmetic and copies ran while one was open for 6% -> 8% of each run, Pallas kernels for 1% -> 2%
where the time goes in v3:
time: 262 us; the launch traced here: 260 us
  waiting for transfers between devices  112 us (43%)
  starting transfers between devices  68.9 us (26%)
  Pallas kernels  31 us (12%)
  local copies, waits for them, and re-layouts  19.4 us (7%)
  blocking collectives  18.2 us (7%)
  other arithmetic  9.3 us (4%)
    all_to_all x8, waiting for transfers between devices, exchange(): return lax.all_to_all(value, axis, 0, 0, tiled=True)  66.9 us
    all_to_all x8, starting transfers between devices, exchange(): return lax.all_to_all(value, axis, 0, 0, tiled=True)  47.7 us
    ppermute x3, waiting for transfers between devices, body(): lax.ppermute(wide, 'kv', [(i, (i + hop) % KN) for i in range(KN)])  43.7 us
    all_to_all x1, blocking collectives, exchange(): return lax.all_to_all(value, axis, 0, 0, tiled=True)  18.2 us
    pallas_call x1, Pallas kernels, body(): pl.pallas_call(attention, out_shape=jax.ShapeDtypeStruct((XN * ZN, BLOCK,...  9.97 us
    ppermute x6, starting transfers between devices, ring(): lax.ppermute(value, 'x', [(i, (i + hop) % XN) for i in range(XN)])  8.52 us
    ppermute x8, starting transfers between devices, ring(): return own + [lax.ppermute(part, 'core', [(0, 1), (1, 0)]) for part in own]  7.72 us
    unnamed x51, local copies, waits for them, and re-layouts  7.63 us
  transfers between devices with their start and end apart: 26, of which 11 were waited for; matrix products, arithmetic and copies ran while one was open for 8% of the time, Pallas kernels for 2%

profile of v3, /device:TPU:1, one launch (start us, length us, event | category | flops | bytes accessed | tf_op | source)
XLA Modules:
  0.0 259.8 jit_solution(14581436201249880454)
XLA Ops:
  0.6 0.9 constant_dynamic-update-slice_fusion.2
  1.5 0.7 constant_dynamic-update-slice_fusion.1
  3.0 2.0 collective-permute-start
  5.0 2.5 collective-permute-start.1
  7.5 1.2 collective-permute-start.2
  8.7 1.5 collective-permute-start.3
  10.2 1.0 multiply_reduce_fusion
  12.2 9.2 %all-to-all-start.1 = ((f32[64,2,128]{2,1,0:T(2,128)}), f32[64,2,128]{2,1,0:T(2,128)S(1)}, u32[]{:S(2)}, u32[]{:S(2)}) async-start(f32[64,2,128]{2,1,0:T(2,128)} %bitcast.11), calls=%async_computation.1 | async-start | bytes 131072 | tf_op jit(solution)/shard_map/all_to_all | solution.py:34
  22.7 1.1 copy.115
  25.3 6.1 %all-to-all-done.1 = f32[64,2,128]{2,1,0:T(2,128)S(1)} async-done(((f32[64,2,128]{2,1,0:T(2,128)}), f32[64,2,128]{2,1,0:T(2,128)S(1)}, u32[]{:S(2)}, u32[]{:S(2)}) %all-to-all-start.1) | async-done | bytes 65568 | tf_op jit(solution)/shard_map/all_to_all | solution.py:34
  31.4 3.7 %all-to-all-start = ((bf16[8,104,128]{2,1,0:T(8,128)(2,1)}), bf16[8,104,128]{2,1,0:T(8,128)(2,1)S(1)}, u32[]{:S(2)}, u32[]{:S(2)}) async-start(bf16[8,104,128]{2,1,0:T(8,128)(2,1)} %pad_maximum_fusion), calls=%async_computation | async-start | bytes 425984 | tf_op jit(solution)/shard_map/all_to_all | solution.py:34
  35.9 5.2 %all-to-all-done = bf16[8,104,128]{2,1,0:T(8,128)(2,1)S(1)} async-done(((bf16[8,104,128]{2,1,0:T(8,128)(2,1)}), bf16[8,104,128]{2,1,0:T(8,128)(2,1)S(1)}, u32[]{:S(2)}, u32[]{:S(2)}) %all-to-all-start) | async-done | bytes 213024 | tf_op jit(solution)/shard_map/all_to_all | solution.py:34
  43.0 0.8 multiply_convert_fusion.rows_ref
  45.3 3.1 %shard_map.113 = f32[192,1280]{1,0:T(8,128)} custom-call(s32[3]{0:T(128)} %pad_add_fusion.place_ref, bf16[4,192,128]{2,1,0:T(8,128)(2,1)} %multiply_convert_fusion.rows_ref, bf16[64,1280]{1,0:T(8,128)(2,1)} %copy-done.3, bf16[64,1280]{1,0:T(8,128)(2,1)} %copy-done.4, bf16[64,1280]{1,0:T(8,128)(2,1)} %copy-done.5, bf16[64,1280]{1,0:T(8,128)(2,1)} %copy-done.6, ...), custom_call_target="tpu_custom_call" | custom-call | tf_op jit(solution)/shard_map/pallas_call | solution.py:377
  48.4 3.6 %all-to-all-start.2 = ((f32[8,24,1280]{2,1,0:T(8,128)}), f32[8,24,1280]{2,1,0:T(8,128)S(1)}, u32[]{:S(2)}, u32[]{:S(2)}) async-start(f32[8,24,1280]{2,1,0:T(8,128)} %bitcast.61), calls=%async_computation.2 | async-start | bytes 1966080 | tf_op jit(solution)/shard_map/all_to_all | solution.py:34
  52.4 1.8 collective-permute-start.8
  54.1 0.7 collective-permute-start.9
  54.8 1.5 collective-permute-start.10
  57.6 1.1 collective-permute-done.7.rest_1_
  58.6 3.4 %collective-permute-start.11 = (bf16[64,1024]{1,0:T(8,128)(2,1)S(1)}, bf16[64,1024]{1,0:T(8,128)(2,1)S(1)}, u32[]{:S(2)}, u32[]{:S(2)}) collective-permute-start(bf16[64,1024]{1,0:T(8,128)(2,1)S(1)} %collective-permute-done.7.rest_1_), channel_id=1, source_target_pairs={{0,1},{1,0},{2,3},{3,2},{4,5},{5,4},{6,7},{7,6},{8,9},{9,8},{10,11... | collective-permute-start | bytes 393224 | tf_op jit(solution)/shard_map/ppermute | solution.py:45
  64.2 13.3 %all-to-all-done.2.parts_ref = f32[8,24,1280]{2,1,0:T(8,128)S(1)} async-done(((f32[8,24,1280]{2,1,0:T(8,128)}), f32[8,24,1280]{2,1,0:T(8,128)S(1)}, u32[]{:S(2)}, u32[]{:S(2)}) %all-to-all-start.2) | async-done | bytes 983072 | tf_op jit(solution)/shard_map/all_to_all | solution.py:34
  77.5 0.9 copy-done
  78.4 2.1 shard_map.114
  80.6 3.5 %all-to-all-start.3 = ((bf16[8,192,128]{2,1,0:T(8,128)(2,1)}), bf16[8,192,128]{2,1,0:T(8,128)(2,1)S(1)}, u32[]{:S(2)}, u32[]{:S(2)}) async-start(bf16[8,192,128]{2,1,0:T(8,128)(2,1)} %get-tuple-element.21), calls=%async_computation.3 | async-start | bytes 786432 | tf_op jit(solution)/shard_map/all_to_all | solution.py:34
  84.4 11.5 %all-to-all-done.3 = bf16[8,192,128]{2,1,0:T(8,128)(2,1)S(1)} async-done(((bf16[8,192,128]{2,1,0:T(8,128)(2,1)}), bf16[8,192,128]{2,1,0:T(8,128)(2,1)S(1)}, u32[]{:S(2)}, u32[]{:S(2)}) %all-to-all-start.3) | async-done | bytes 393248 | tf_op jit(solution)/shard_map/all_to_all | solution.py:34
  95.9 1.4 broadcast_in_dim.126
  97.3 3.7 %all-to-all-start.4 = ((bf16[4,1536,128]{2,1,0:T(8,128)(2,1)}), bf16[4,1536,128]{2,1,0:T(8,128)(2,1)S(1)}, u32[]{:S(2)}, u32[]{:S(2)}) async-start(bf16[4,1536,128]{2,1,0:T(8,128)(2,1)} %broadcast_in_dim.126), calls=%async_computation.4 | async-start | bytes 3145728 | tf_op jit(solution)/shard_map/all_to_all | solution.py:34
  101.9 3.6 %fusion.1 = (s32[64]{0:T(128)S(1)}, s32[64]{0:T(128)S(1)}) fusion(s32[256,128]{1,0:T(8,128)S(1)} %copy.114, s32[256,128]{1,0:T(8,128)S(1)} %eq.77, s32[64]{0:T(128)S(1)} %pad_add_fusion.1, s32[256,128]{1,0:T(8,128)S(1)} %multiply_add_fusion), kind=kLoop, calls=%fused_computation.3 | loop fusion | flops 10485632 | bytes 393984 | tf_op jit(solution)/shard_map/reduce_max | solution.py:339
  105.5 12.1 %all-to-all-done.4 = bf16[4,1536,128]{2,1,0:T(8,128)(2,1)S(1)} async-done(((bf16[4,1536,128]{2,1,0:T(8,128)(2,1)}), bf16[4,1536,128]{2,1,0:T(8,128)(2,1)S(1)}, u32[]{:S(2)}, u32[]{:S(2)}) %all-to-all-start.4) | async-done | bytes 1572896 | tf_op jit(solution)/shard_map/all_to_all | solution.py:34
  117.8 10.0 %shard_map.115 = bf16[32,216,128]{2,1,0:T(8,128)(2,1)} custom-call(s32[64]{0:T(128)S(1)} %get-tuple-element.57.owner_ref, s32[64]{0:T(128)S(1)} %fusion.17.group_ref, s32[64]{0:T(128)S(1)} %get-tuple-element.54.count_ref, bf16[32,192,128]{2,1,0:T(8,128)(2,1)S(1)} %bitcast.58, s32[32,24,128]{2,1,0:T(8,128)S(1)} %broadcast_in_dim.128.root_ref, ...), custom_call_target="tpu_custom_call" | custom-call | tf_op jit(solution)/shard_map/pallas_call | solution.py:422
  127.8 5.9 %all-to-all-start.5 = ((bf16[4,1728,128]{2,1,0:T(8,128)(2,1)}), bf16[4,1728,128]{2,1,0:T(8,128)(2,1)}, u32[]{:S(2)}, u32[]{:S(2)}) async-start(bf16[4,1728,128]{2,1,0:T(8,128)(2,1)} %bitcast.29), calls=%async_computation.5 | async-start | bytes 3538944 | tf_op jit(solution)/shard_map/all_to_all | solution.py:34
  133.7 2.5 shard_map.116.rest_0_
  136.2 1.3 collective-permute-start.15
  137.4 2.6 %collective-permute-start.16 = (bf16[512,1024]{1,0:T(8,128)(2,1)}, bf16[512,1024]{1,0:T(8,128)(2,1)}, u32[]{:S(2)}, u32[]{:S(2)}) collective-permute-start(bf16[512,1024]{1,0:T(8,128)(2,1)} %shard_map.116.rest_0_), channel_id=1, source_target_pairs={{0,128},{64,192},{128,0},{192,64},{1,129},{65,193},{129,1},{193,65... | collective-permute-start | bytes 3145736 | tf_op jit(solution)/shard_map/ppermute | solution.py:394
  140.1 1.1 collective-permute-start.17
  141.1 12.9 %collective-permute-done.15.rest_1_ = bf16[512,1024]{1,0:T(8,128)(2,1)S(1)} collective-permute-done((bf16[512,1024]{1,0:T(8,128)(2,1)}, bf16[512,1024]{1,0:T(8,128)(2,1)S(1)}, u32[]{:S(2)}, u32[]{:S(2)}) %collective-permute-start.15) | collective-permute-done | bytes 1048608 | tf_op jit(solution)/shard_map/ppermute | solution.py:394
  154.1 23.6 %collective-permute-done.16.rest_2_ = bf16[512,1024]{1,0:T(8,128)(2,1)} collective-permute-done((bf16[512,1024]{1,0:T(8,128)(2,1)}, bf16[512,1024]{1,0:T(8,128)(2,1)}, u32[]{:S(2)}, u32[]{:S(2)}) %collective-permute-start.16) | collective-permute-done | bytes 1048608 | tf_op jit(solution)/shard_map/ppermute | solution.py:394
  177.7 7.2 %collective-permute-done.17.rest_3_ = bf16[512,1024]{1,0:T(8,128)(2,1)} collective-permute-done((bf16[512,1024]{1,0:T(8,128)(2,1)}, bf16[512,1024]{1,0:T(8,128)(2,1)}, u32[]{:S(2)}, u32[]{:S(2)}) %collective-permute-start.17) | collective-permute-done | bytes 1048608 | tf_op jit(solution)/shard_map/ppermute | solution.py:394
  184.9 6.0 %shard_map.117 = bf16[8,216,128]{2,1,0:T(8,128)(2,1)} custom-call(bf16[4,8,216,128]{3,2,1,0:T(8,128)(2,1)} %bitcast.30.parts_ref), custom_call_target="tpu_custom_call" | custom-call | tf_op jit(solution)/shard_map/pallas_call | solution.py:437
  190.9 18.2 %all_to_all.45.parts_ref = bf16[8,216,128]{2,1,0:T(8,128)(2,1)} all-to-all(bf16[8,216,128]{2,1,0:T(8,128)(2,1)} %shard_map.117), channel_id=1, replica_groups=mesh['kv'=4,'z'=8,'x'=4,'core'=2] {'z'}, dimensions={0} | all-to-all | bytes 884736 | tf_op jit(solution)/shard_map/all_to_all | solution.py:34
  209.1 2.5 shard_map.118
  211.6 8.5 %all-to-all-start.7 = ((bf16[32,8,1024]{2,1,0:T(8,128)(2,1)}), bf16[32,8,1024]{2,1,0:T(8,128)(2,1)S(1)}, u32[]{:S(2)}, u32[]{:S(2)}) async-start(bf16[32,8,1024]{2,1,0:T(8,128)(2,1)} %bitcast.62), calls=%async_computation.7 | async-start | bytes 1048576 | tf_op jit(solution)/shard_map/all_to_all | solution.py:34
  222.6 11.1 %all-to-all-done.7 = bf16[32,8,1024]{2,1,0:T(8,128)(2,1)S(1)} async-done(((bf16[32,8,1024]{2,1,0:T(8,128)(2,1)}), bf16[32,8,1024]{2,1,0:T(8,128)(2,1)S(1)}, u32[]{:S(2)}, u32[]{:S(2)}) %all-to-all-start.7) | async-done | bytes 524320 | tf_op jit(solution)/shard_map/all_to_all | solution.py:34
  233.6 0.8 copy-done.1
  234.4 4.8 %shard_map.119 = bf16[4,4,2,32,128]{4,3,2,1,0:T(8,128)(2,1)} custom-call(s32[3]{0:T(128)} %pad_add_fusion.place_ref, bf16[4,64,1024]{2,1,0:T(8,128)(2,1)} %bitcast.63, f32[4,64,128]{2,1,0:T(8,128)} %pad_bitcast_fusion.stream_ref, bf16[512,1024]{1,0:T(8,128)(2,1)} %shard_map.116.rest_0_, bf16[512,1024]{1,0:T(8,128)(2,1)} %copy-done.2, ...), custom_call_target="tpu_custom_call" | custom-call | tf_op jit(solution)/shard_map/pallas_call | solution.py:458
  239.2 9.7 %all-to-all-start.8 = ((bf16[32,32,128]{2,1,0:T(8,128)(2,1)}), bf16[32,32,128]{2,1,0:T(8,128)(2,1)S(1)}, u32[]{:S(2)}, u32[]{:S(2)}) async-start(bf16[32,32,128]{2,1,0:T(8,128)(2,1)} %bitcast.68), calls=%async_computation.8 | async-start | bytes 524288 | tf_op jit(solution)/shard_map/all_to_all | solution.py:34
  250.3 7.6 %all-to-all-done.8 = bf16[32,32,128]{2,1,0:T(8,128)(2,1)S(1)} async-done(((bf16[32,32,128]{2,1,0:T(8,128)(2,1)}), bf16[32,32,128]{2,1,0:T(8,128)(2,1)S(1)}, u32[]{:S(2)}, u32[]{:S(2)}) %all-to-all-start.8) | async-done | bytes 262176 | tf_op jit(solution)/shard_map/all_to_all | solution.py:34
  258.9 0.8 copy.134
  (142 shorter events, 18.3 us)
Async XLA Ops:
  3.0 38.2 %copy-start.3 = (bf16[64,1280]{1,0:T(8,128)(2,1)}, bf16[64,1280]{1,0:T(8,128)(2,1)S(1)}, u32[]{:S(2)}) copy-start(bf16[64,1280]{1,0:T(8,128)(2,1)S(1)} %constant_dynamic-update-slice_fusion.rest_0_) | copy-start | bytes 491524
  3.0 32.2 %collective-permute-start = (bf16[64,1280]{1,0:T(8,128)(2,1)S(1)}, bf16[64,1280]{1,0:T(8,128)(2,1)S(1)}, u32[]{:S(2)}, u32[]{:S(2)}) collective-permute-start(bf16[64,1280]{1,0:T(8,128)(2,1)S(1)} %constant_dynamic-update-slice_fusion.rest_0_), channel_id=1, source_target_pairs={{0,2},{2,4},{4,6},{6,0},{1,3},{3,5},{5,7},{7,1},{8,10},{10,12},{12... | collective-permute-start | bytes 491528 | tf_op jit(solution)/shard_map/ppermute | solution.py:44
  5.0 30.4 %collective-permute-start.1 = (bf16[64,1280]{1,0:T(8,128)(2,1)S(1)}, bf16[64,1280]{1,0:T(8,128)(2,1)S(1)}, u32[]{:S(2)}, u32[]{:S(2)}) collective-permute-start(bf16[64,1280]{1,0:T(8,128)(2,1)S(1)} %constant_dynamic-update-slice_fusion.rest_0_), channel_id=1, source_target_pairs={{0,4},{2,6},{4,0},{6,2},{1,5},{3,7},{5,1},{7,3},{8,12},{10,14},{12... | collective-permute-start | bytes 491528 | tf_op jit(solution)/shard_map/ppermute | solution.py:44
  7.5 28.3 %collective-permute-start.2 = (bf16[64,1280]{1,0:T(8,128)(2,1)S(1)}, bf16[64,1280]{1,0:T(8,128)(2,1)S(1)}, u32[]{:S(2)}, u32[]{:S(2)}) collective-permute-start(bf16[64,1280]{1,0:T(8,128)(2,1)S(1)} %constant_dynamic-update-slice_fusion.rest_0_), channel_id=1, source_target_pairs={{0,6},{2,0},{4,2},{6,4},{1,7},{3,1},{5,3},{7,5},{8,14},{10,8},{12,... | collective-permute-start | bytes 491528 | tf_op jit(solution)/shard_map/ppermute | solution.py:44
  8.7 35.1 %collective-permute-start.3 = (bf16[64,1280]{1,0:T(8,128)(2,1)S(1)}, bf16[64,1280]{1,0:T(8,128)(2,1)S(1)}, u32[]{:S(2)}, u32[]{:S(2)}) collective-permute-start(bf16[64,1280]{1,0:T(8,128)(2,1)S(1)} %constant_dynamic-update-slice_fusion.rest_0_), channel_id=1, source_target_pairs={{0,1},{1,0},{2,3},{3,2},{4,5},{5,4},{6,7},{7,6},{8,9},{9,8},{10,11... | collective-permute-start | bytes 491528 | tf_op jit(solution)/shard_map/ppermute | solution.py:45
  12.2 19.3 %all-to-all-start.1 = ((f32[64,2,128]{2,1,0:T(2,128)}), f32[64,2,128]{2,1,0:T(2,128)S(1)}, u32[]{:S(2)}, u32[]{:S(2)}) async-start(f32[64,2,128]{2,1,0:T(2,128)} %bitcast.11), calls=%async_computation.1 | async-start | bytes 131072 | tf_op jit(solution)/shard_map/all_to_all | solution.py:34
  31.4 9.8 %all-to-all-start = ((bf16[8,104,128]{2,1,0:T(8,128)(2,1)}), bf16[8,104,128]{2,1,0:T(8,128)(2,1)S(1)}, u32[]{:S(2)}, u32[]{:S(2)}) async-start(bf16[8,104,128]{2,1,0:T(8,128)(2,1)} %pad_maximum_fusion), calls=%async_computation | async-start | bytes 425984 | tf_op jit(solution)/shard_map/all_to_all | solution.py:34
  35.2 7.6 %copy-start.4 = (bf16[64,1280]{1,0:T(8,128)(2,1)}, bf16[64,1280]{1,0:T(8,128)(2,1)S(1)}, u32[]{:S(2)}) copy-start(bf16[64,1280]{1,0:T(8,128)(2,1)S(1)} %collective-permute-done.rest_1_) | copy-start | bytes 491524
  35.2 8.6 %collective-permute-start.4 = (bf16[64,1280]{1,0:T(8,128)(2,1)S(1)}, bf16[64,1280]{1,0:T(8,128)(2,1)S(1)}, u32[]{:S(2)}, u32[]{:S(2)}) collective-permute-start(bf16[64,1280]{1,0:T(8,128)(2,1)S(1)} %collective-permute-done.rest_1_), channel_id=1, source_target_pairs={{0,1},{1,0},{2,3},{3,2},{4,5},{5,4},{6,7},{7,6},{8,9},{9,8},{10,11... | collective-permute-start | bytes 491528 | tf_op jit(solution)/shard_map/ppermute | solution.py:45
  35.4 7.4 %copy-start.5 = (bf16[64,1280]{1,0:T(8,128)(2,1)}, bf16[64,1280]{1,0:T(8,128)(2,1)S(1)}, u32[]{:S(2)}) copy-start(bf16[64,1280]{1,0:T(8,128)(2,1)S(1)} %collective-permute-done.1.rest_2_) | copy-start | bytes 491524
  35.4 8.4 %collective-permute-start.5 = (bf16[64,1280]{1,0:T(8,128)(2,1)S(1)}, bf16[64,1280]{1,0:T(8,128)(2,1)S(1)}, u32[]{:S(2)}, u32[]{:S(2)}) collective-permute-start(bf16[64,1280]{1,0:T(8,128)(2,1)S(1)} %collective-permute-done.1.rest_2_), channel_id=1, source_target_pairs={{0,1},{1,0},{2,3},{3,2},{4,5},{5,4},{6,7},{7,6},{8,9},{9,8},{10,11... | collective-permute-start | bytes 491528 | tf_op jit(solution)/shard_map/ppermute | solution.py:45
  35.8 7.0 %copy-start.6 = (bf16[64,1280]{1,0:T(8,128)(2,1)}, bf16[64,1280]{1,0:T(8,128)(2,1)S(1)}, u32[]{:S(2)}) copy-start(bf16[64,1280]{1,0:T(8,128)(2,1)S(1)} %collective-permute-done.2.rest_3_) | copy-start | bytes 491524
  35.8 8.0 %collective-permute-start.6 = (bf16[64,1280]{1,0:T(8,128)(2,1)S(1)}, bf16[64,1280]{1,0:T(8,128)(2,1)S(1)}, u32[]{:S(2)}, u32[]{:S(2)}) collective-permute-start(bf16[64,1280]{1,0:T(8,128)(2,1)S(1)} %collective-permute-done.2.rest_3_), channel_id=1, source_target_pairs={{0,1},{1,0},{2,3},{3,2},{4,5},{5,4},{6,7},{7,6},{8,9},{9,8},{10,11... | collective-permute-start | bytes 491528 | tf_op jit(solution)/shard_map/ppermute | solution.py:45
  43.8 8.2 %copy-start.12 = (bf16[1024,64]{0,1:T(8,128)(2,1)S(1)}, bf16[1024,64]{0,1:T(8,128)(2,1)}, u32[]{:S(2)}) copy-start(bf16[1024,64]{0,1:T(8,128)(2,1)} %param.15) | copy-start | bytes 393220
  43.8 12.6 %copy-start.21 = (s32[3,512]{1,0:T(4,128)S(1)}, s32[3,512]{1,0:T(4,128)}, u32[]{:S(2)}) copy-start(s32[3,512]{1,0:T(4,128)} %param.19) | copy-start | bytes 18436
  43.8 12.7 %copy-start.20 = (s32[512]{0:T(512)S(1)}, s32[512]{0:T(512)}, u32[]{:S(2)}) copy-start(s32[512]{0:T(512)} %param.17) | copy-start | bytes 6148
  43.8 0.7 copy-start.7
  43.8 0.7 copy-start.8
  43.8 0.8 copy-start.9
  44.6 0.7 copy-start.10
  48.4 29.1 %all-to-all-start.2 = ((f32[8,24,1280]{2,1,0:T(8,128)}), f32[8,24,1280]{2,1,0:T(8,128)S(1)}, u32[]{:S(2)}, u32[]{:S(2)}) async-start(f32[8,24,1280]{2,1,0:T(8,128)} %bitcast.61), calls=%async_computation.2 | async-start | bytes 1966080 | tf_op jit(solution)/shard_map/all_to_all | solution.py:34
  52.0 6.7 %collective-permute-start.7 = (bf16[64,1024]{1,0:T(8,128)(2,1)S(1)}, bf16[64,1024]{1,0:T(8,128)(2,1)S(1)}, u32[]{:S(2)}, u32[]{:S(2)}) collective-permute-start(bf16[64,1024]{1,0:T(8,128)(2,1)S(1)} %bitcast.75), channel_id=1, source_target_pairs={{0,2},{2,4},{4,6},{6,0},{1,3},{3,5},{5,7},{7,1},{8,10},{10,12},{12... | collective-permute-start | bytes 393224 | tf_op jit(solution)/shard_map/ppermute | solution.py:44
  52.4 9.6 %collective-permute-start.8 = (bf16[64,1024]{1,0:T(8,128)(2,1)S(1)}, bf16[64,1024]{1,0:T(8,128)(2,1)S(1)}, u32[]{:S(2)}, u32[]{:S(2)}) collective-permute-start(bf16[64,1024]{1,0:T(8,128)(2,1)S(1)} %bitcast.76), channel_id=1, source_target_pairs={{0,4},{2,6},{4,0},{6,2},{1,5},{3,7},{5,1},{7,3},{8,12},{10,14},{12... | collective-permute-start | bytes 393224 | tf_op jit(solution)/shard_map/ppermute | solution.py:44
  54.1 8.0 %collective-permute-start.9 = (bf16[64,1024]{1,0:T(8,128)(2,1)S(1)}, bf16[64,1024]{1,0:T(8,128)(2,1)S(1)}, u32[]{:S(2)}, u32[]{:S(2)}) collective-permute-start(bf16[64,1024]{1,0:T(8,128)(2,1)S(1)} %bitcast.77), channel_id=1, source_target_pairs={{0,6},{2,0},{4,2},{6,4},{1,7},{3,1},{5,3},{7,5},{8,14},{10,8},{12,... | collective-permute-start | bytes 393224 | tf_op jit(solution)/shard_map/ppermute | solution.py:44
  54.8 9.3 %collective-permute-start.10 = (bf16[64,1024]{1,0:T(8,128)(2,1)S(1)}, bf16[64,1024]{1,0:T(8,128)(2,1)S(1)}, u32[]{:S(2)}, u32[]{:S(2)}) collective-permute-start(bf16[64,1024]{1,0:T(8,128)(2,1)S(1)} %bitcast.78), channel_id=1, source_target_pairs={{0,1},{1,0},{2,3},{3,2},{4,5},{5,4},{6,7},{7,6},{8,9},{9,8},{10,11... | collective-permute-start | bytes 393224 | tf_op jit(solution)/shard_map/ppermute | solution.py:45
  56.4 49.2 %collective-permute-start.14 = (bf16[32,2,128,128]{3,2,1,0:T(8,128)(2,1)}, bf16[32,2,128,128]{3,2,1,0:T(8,128)(2,1)}, u32[]{:S(2)}, u32[]{:S(2)}) collective-permute-start(bf16[32,2,128,128]{3,2,1,0:T(8,128)(2,1)} %bitcast.28.own_ref), channel_id=1, source_target_pairs={{0,1},{1,0},{2,3},{3,2},{4,5},{5,4},{6,7},{7,6},{8,9},{9,8},{10,11... | collective-permute-start | bytes 6291464 | tf_op jit(solution)/shard_map/ppermute | solution.py:311
  58.6 69.2 %copy-start.13 = (bf16[64,1024]{1,0:T(8,128)(2,1)}, bf16[64,1024]{1,0:T(8,128)(2,1)S(1)}, u32[]{:S(2)}) copy-start(bf16[64,1024]{1,0:T(8,128)(2,1)S(1)} %collective-permute-done.7.rest_1_) | copy-start | bytes 393220
  58.6 5.5 %collective-permute-start.11 = (bf16[64,1024]{1,0:T(8,128)(2,1)S(1)}, bf16[64,1024]{1,0:T(8,128)(2,1)S(1)}, u32[]{:S(2)}, u32[]{:S(2)}) collective-permute-start(bf16[64,1024]{1,0:T(8,128)(2,1)S(1)} %collective-permute-done.7.rest_1_), channel_id=1, source_target_pairs={{0,1},{1,0},{2,3},{3,2},{4,5},{5,4},{6,7},{7,6},{8,9},{9,8},{10,11... | collective-permute-start | bytes 393224 | tf_op jit(solution)/shard_map/ppermute | solution.py:45
  62.0 65.8 %copy-start.14 = (bf16[64,1024]{1,0:T(8,128)(2,1)}, bf16[64,1024]{1,0:T(8,128)(2,1)S(1)}, u32[]{:S(2)}) copy-start(bf16[64,1024]{1,0:T(8,128)(2,1)S(1)} %collective-permute-done.8.rest_2_) | copy-start | bytes 393220
  62.0 2.1 collective-permute-start.12
  62.1 65.7 %copy-start.15 = (bf16[64,1024]{1,0:T(8,128)(2,1)}, bf16[64,1024]{1,0:T(8,128)(2,1)S(1)}, u32[]{:S(2)}) copy-start(bf16[64,1024]{1,0:T(8,128)(2,1)S(1)} %collective-permute-done.9.rest_3_) | copy-start | bytes 393220
  62.1 2.0 collective-permute-start.13
  64.1 63.7 %copy-start.16 = (bf16[64,1024]{1,0:T(8,128)(2,1)}, bf16[64,1024]{1,0:T(8,128)(2,1)S(1)}, u32[]{:S(2)}) copy-start(bf16[64,1024]{1,0:T(8,128)(2,1)S(1)} %collective-permute-done.10.rest_4_) | copy-start | bytes 393220
  64.1 33.2 %copy-start.17 = (bf16[64,1024]{1,0:T(8,128)(2,1)}, bf16[64,1024]{1,0:T(8,128)(2,1)S(1)}, u32[]{:S(2)}) copy-start(bf16[64,1024]{1,0:T(8,128)(2,1)S(1)} %collective-permute-done.11.rest_5_) | copy-start | bytes 393220
  64.1 33.2 %copy-start.18 = (bf16[64,1024]{1,0:T(8,128)(2,1)}, bf16[64,1024]{1,0:T(8,128)(2,1)S(1)}, u32[]{:S(2)}) copy-start(bf16[64,1024]{1,0:T(8,128)(2,1)S(1)} %collective-permute-done.12.rest_6_) | copy-start | bytes 393220
  64.1 36.9 %copy-start.19 = (bf16[64,1024]{1,0:T(8,128)(2,1)}, bf16[64,1024]{1,0:T(8,128)(2,1)S(1)}, u32[]{:S(2)}) copy-start(bf16[64,1024]{1,0:T(8,128)(2,1)S(1)} %collective-permute-done.13.rest_7_) | copy-start | bytes 393220
  77.5 0.9 copy-start
  80.6 15.4 %all-to-all-start.3 = ((bf16[8,192,128]{2,1,0:T(8,128)(2,1)}), bf16[8,192,128]{2,1,0:T(8,128)(2,1)S(1)}, u32[]{:S(2)}, u32[]{:S(2)}) async-start(bf16[8,192,128]{2,1,0:T(8,128)(2,1)} %get-tuple-element.21), calls=%async_computation.3 | async-start | bytes 786432 | tf_op jit(solution)/shard_map/all_to_all | solution.py:34
  97.3 4.1 %copy-start.11 = (s32[512,64]{0,1:T(8,128)S(1)}, s32[512,64]{0,1:T(8,128)}, u32[]{:S(2)}) copy-start(s32[512,64]{0,1:T(8,128)} %param.18) | copy-start | bytes 393220
  97.3 20.3 %all-to-all-start.4 = ((bf16[4,1536,128]{2,1,0:T(8,128)(2,1)}), bf16[4,1536,128]{2,1,0:T(8,128)(2,1)S(1)}, u32[]{:S(2)}, u32[]{:S(2)}) async-start(bf16[4,1536,128]{2,1,0:T(8,128)(2,1)} %broadcast_in_dim.126), calls=%async_computation.4 | async-start | bytes 3145728 | tf_op jit(solution)/shard_map/all_to_all | solution.py:34
  127.8 57.0 %all-to-all-start.5 = ((bf16[4,1728,128]{2,1,0:T(8,128)(2,1)}), bf16[4,1728,128]{2,1,0:T(8,128)(2,1)}, u32[]{:S(2)}, u32[]{:S(2)}) async-start(bf16[4,1728,128]{2,1,0:T(8,128)(2,1)} %bitcast.29), calls=%async_computation.5 | async-start | bytes 3538944 | tf_op jit(solution)/shard_map/all_to_all | solution.py:34
  136.2 17.9 %collective-permute-start.15 = (bf16[512,1024]{1,0:T(8,128)(2,1)}, bf16[512,1024]{1,0:T(8,128)(2,1)S(1)}, u32[]{:S(2)}, u32[]{:S(2)}) collective-permute-start(bf16[512,1024]{1,0:T(8,128)(2,1)} %shard_map.116.rest_0_), channel_id=1, source_target_pairs={{0,64},{64,128},{128,192},{192,0},{1,65},{65,129},{129,193},{193,1... | collective-permute-start | bytes 3145736 | tf_op jit(solution)/shard_map/ppermute | solution.py:394
  137.4 40.2 %collective-permute-start.16 = (bf16[512,1024]{1,0:T(8,128)(2,1)}, bf16[512,1024]{1,0:T(8,128)(2,1)}, u32[]{:S(2)}, u32[]{:S(2)}) collective-permute-start(bf16[512,1024]{1,0:T(8,128)(2,1)} %shard_map.116.rest_0_), channel_id=1, source_target_pairs={{0,128},{64,192},{128,0},{192,64},{1,129},{65,193},{129,1},{193,65... | collective-permute-start | bytes 3145736 | tf_op jit(solution)/shard_map/ppermute | solution.py:394
  140.1 44.8 %collective-permute-start.17 = (bf16[512,1024]{1,0:T(8,128)(2,1)}, bf16[512,1024]{1,0:T(8,128)(2,1)}, u32[]{:S(2)}, u32[]{:S(2)}) collective-permute-start(bf16[512,1024]{1,0:T(8,128)(2,1)} %shard_map.116.rest_0_), channel_id=1, source_target_pairs={{0,192},{64,0},{128,64},{192,128},{1,193},{65,1},{129,65},{193,129... | collective-permute-start | bytes 3145736 | tf_op jit(solution)/shard_map/ppermute | solution.py:394
  154.1 57.5 %copy-start.2 = (bf16[512,1024]{1,0:T(8,128)(2,1)}, bf16[512,1024]{1,0:T(8,128)(2,1)S(1)}, u32[]{:S(2)}) copy-start(bf16[512,1024]{1,0:T(8,128)(2,1)S(1)} %collective-permute-done.15.rest_1_) | copy-start | bytes 3145732
  211.6 22.0 %all-to-all-start.7 = ((bf16[32,8,1024]{2,1,0:T(8,128)(2,1)}), bf16[32,8,1024]{2,1,0:T(8,128)(2,1)S(1)}, u32[]{:S(2)}, u32[]{:S(2)}) async-start(bf16[32,8,1024]{2,1,0:T(8,128)(2,1)} %bitcast.62), calls=%async_computation.7 | async-start | bytes 1048576 | tf_op jit(solution)/shard_map/all_to_all | solution.py:34
  233.6 0.8 copy-start.1
  239.2 18.6 %all-to-all-start.8 = ((bf16[32,32,128]{2,1,0:T(8,128)(2,1)}), bf16[32,32,128]{2,1,0:T(8,128)(2,1)S(1)}, u32[]{:S(2)}, u32[]{:S(2)}) async-start(bf16[32,32,128]{2,1,0:T(8,128)(2,1)} %bitcast.68), calls=%async_computation.8 | async-start | bytes 524288 | tf_op jit(solution)/shard_map/all_to_all | solution.py:34

commit v4 on v2

--- a/solution.py
+++ b/solution.py
@@ -23,6 +23,8 @@
 JN = XN * CN
 KN = 4
 PART = 64
+SEGMENTS = 5
+DEPTH = 12
 QUARTER = ZN * SB // KN
 PAIRS = [(s, u) for s in range(STEPS) for u in range(s + 1)]
 SCALE = 1.0 / math.sqrt(HD)
@@ -38,22 +40,29 @@
     return exchange(jnp.broadcast_to(value[None], (count,) + value.shape), axis)
 
 
+def swap(value):
+    return lax.ppermute(value, "core", [(0, 1), (1, 0)])
+
+
+def shift(value, hop):
+    return lax.ppermute(value, "x", [(i, (i + hop) % XN) for i in range(XN)])
+
+
 def ring(value):
-    own = [value]
-    for hop in range(1, XN):
-        own.append(lax.ppermute(value, "x", [(i, (i + hop) % XN) for i in range(XN)]))
-    return own + [lax.ppermute(part, "core", [(0, 1), (1, 0)]) for part in own]
+    both = jnp.concatenate([value, swap(value)], axis=0)
+    return [both] + [shift(both, hop) for hop in range(1, XN)]
 
 
 def join(place_ref, chunks, wide):
     core = place_ref[1]
     for hop in range(XN):
-        wide[hop, pl.ds(pl.multiple_of(core * PART, PART), PART), :] = chunks[hop][...]
-        wide[hop, pl.ds(pl.multiple_of((1 - core) * PART, PART), PART), :] = chunks[XN + hop][...]
+        for side, start in ((0, core * PART), (1, (1 - core) * PART)):
+            rows = pl.ds(pl.multiple_of(start, PART), PART)
+            wide[hop, rows, :] = chunks[hop][side * PART : (side + 1) * PART, :]
 
 
 def project(place_ref, rows_ref, *rest):
-    chunks, out_ref, wide = rest[: 2 * XN], rest[2 * XN], rest[2 * XN + 1]
+    chunks, out_ref, wide = rest[:XN], rest[XN], rest[XN + 1]
     join(place_ref, chunks, wide)
     x = place_ref[0]
     for start in range(0, out_ref.shape[1], 256):
@@ -68,7 +77,7 @@
 
 
 def deliver(place_ref, rows_ref, *rest):
-    chunks, out_ref, wide = rest[: 2 * XN], rest[2 * XN], rest[2 * XN + 1]
+    chunks, out_ref, wide = rest[:XN], rest[XN], rest[XN + 1]
     join(place_ref, chunks, wide)
     x = place_ref[0]
     for hop in range(XN):
@@ -130,64 +139,97 @@
                     ref[index, pl.ds(beam, 1), :] = ref[before, pl.ds(parent, 1), :]
 
 
-def attention(
-    owner_ref,
-    group_ref,
-    count_ref,
-    q_ref,
-    root_ref,
-    own_ref,
-    other_ref,
-    out_ref,
-    top_ref,
-    sum_ref,
-    hold,
-):
-    groups = ZN * XN
+def attention(place_ref, table_ref, length_ref, q_ref, root_ref, *rest):
+    caches, rest = rest[: 2 * SEGMENTS], rest[2 * SEGMENTS :]
+    out_ref, top_ref, sum_ref, hold, pages, arrived, beam_list, block_list = rest
+    x, core, z = place_ref[0], place_ref[1], place_ref[3]
+    blocks = table_ref.shape[0] // (ZN * GROUP)
+    slots = caches[0].shape[0]
     top_ref[...] = jnp.full_like(top_ref, NEGATIVE)
     sum_ref[...] = jnp.zeros_like(sum_ref)
     hold[...] = jnp.zeros_like(hold)
+
+    def scan_beam(beam, found):
+        used = (length_ref[beam] + HD - 1) // HD
+
+        def scan_block(block, found):
+            slot = table_ref[beam * blocks + block]
+            near = slot // (slots * JN) == z
+
+            @pl.when(near)
+            def _():
+                beam_list[found] = beam
+                block_list[found] = block
+
+            return found + near.astype(jnp.int32)
+
+        return lax.fori_loop(0, used, scan_block, found)
+
+    found = lax.fori_loop(0, ZN * GROUP, scan_beam, 0)
+
+    def fetch(item):
+        slot = table_ref[beam_list[item] * blocks + block_list[item]]
+        lane = item % DEPTH
+        offset = slot % slots
+        source = slot // slots % JN
+        far = (source // CN + XN - x) % XN
+        foreign = jnp.where(source % CN == core, 0, 1)
+        half = slots // 2
+        segment = jnp.where(far == 0, 0, jnp.where(far == 3, 1, jnp.where(far == 1, 2, 3)))
+        late = (segment == 3) & (offset >= half)
+        segment = jnp.where(late, 4, segment) + foreign * SEGMENTS
+        offset = jnp.where(late, offset - half, offset)
+        for index in range(2 * SEGMENTS):
+
+            @pl.when(segment == index)
+            def _(index=index):
+                pltpu.make_async_copy(
+                    caches[index].at[offset], pages.at[lane], arrived.at[lane]
+                ).start()
+
+    for item in range(DEPTH):
+
+        @pl.when(item < found)
+        def _(item=item):
+            fetch(item)
+
     tokens = lax.broadcasted_iota(jnp.int32, (SB, HD), 1)
-    slots = own_ref.shape[0]
-
-    def visit(cache_ref, offset):
-        def step(slot, carry):
-            count = count_ref[offset + slot]
-
-            @pl.when(count > 0)
-            def _():
-                group = group_ref[offset + slot]
-                owner = owner_ref[offset + slot]
-                keys = cache_ref[slot, 0]
-                values = cache_ref[slot, 1]
-                live = (root_ref[group] == owner) & (tokens < count)
-                live = jnp.concatenate([live] * HEADS, axis=0)
-                scores = (
-                    lax.dot_general(
-                        q_ref[group],
-                        keys,
-                        (((1,), (1,)), ((), ())),
-                        preferred_element_type=jnp.float32,
-                    )
-                    * SCALE
-                )
-                scores = jnp.where(live, scores, NEGATIVE)
-                old = top_ref[group]
-                new = jnp.maximum(old, jnp.max(scores, axis=1, keepdims=True))
-                weights = jnp.where(live, jnp.exp(scores - new), 0.0)
-                fade = jnp.exp(old - new)
-                top_ref[group] = new
-                sum_ref[group] = sum_ref[group] * fade + jnp.sum(weights, axis=1, keepdims=True)
-                hold[group] = hold[group] * fade + jnp.dot(
-                    weights.astype(jnp.bfloat16), values, preferred_element_type=jnp.float32
-                )
-
-            return carry
-
-        lax.fori_loop(0, slots, step, 0)
-
-    visit(own_ref, 0)
-    visit(other_ref, slots)
+
+    def visit(item, carry):
+        lane = item % DEPTH
+        beam = beam_list[item]
+        group = beam // GROUP
+        count = length_ref[beam] - block_list[item] * HD
+        live = (root_ref[group] == beam % GROUP) & (tokens < count)
+        live = jnp.concatenate([live] * HEADS, axis=0)
+        pltpu.make_async_copy(caches[0].at[0], pages.at[lane], arrived.at[lane]).wait()
+        scores = (
+            lax.dot_general(
+                q_ref[group],
+                pages[lane, 0],
+                (((1,), (1,)), ((), ())),
+                preferred_element_type=jnp.float32,
+            )
+            * SCALE
+        )
+        scores = jnp.where(live, scores, NEGATIVE)
+        old = top_ref[group]
+        new = jnp.maximum(old, jnp.max(scores, axis=1, keepdims=True))
+        weights = jnp.where(live, jnp.exp(scores - new), 0.0)
+        fade = jnp.exp(old - new)
+        top_ref[group] = new
+        sum_ref[group] = sum_ref[group] * fade + jnp.sum(weights, axis=1, keepdims=True)
+        hold[group] = hold[group] * fade + jnp.dot(
+            weights.astype(jnp.bfloat16), pages[lane, 1], preferred_element_type=jnp.float32
+        )
+
+        @pl.when(item + DEPTH < found)
+        def _():
+            fetch(item + DEPTH)
+
+        return carry
+
+    lax.fori_loop(0, found, visit, 0)
     lanes = lax.broadcasted_iota(jnp.int32, (GROUP, HD), 1)
 
     def pack(group, carry):
@@ -199,7 +241,7 @@
         out_ref[group] = seal([hold[group]], tile)
         return carry
 
-    lax.fori_loop(0, groups, pack, 0)
+    lax.fori_loop(0, ZN, pack, 0)
 
 
 def seal(sums, stat):
@@ -213,23 +255,6 @@
     block = block.astype(jnp.float32)
     stat = block[ROWS : ROWS + GROUP] + block[ROWS + GROUP : ROWS + 2 * GROUP]
     return block[:ROWS], stat + block[ROWS + 2 * GROUP :]
-
-
-def merge(parts_ref, out_ref):
-    count = parts_ref.shape[0]
-    sums, stats = zip(*[unseal(parts_ref[source, 0]) for source in range(count)])
-    top = functools.reduce(jnp.maximum, stats)
-    fades = [jnp.exp(stat - top) for stat in stats]
-    total = sum(fade * pltpu.roll(stat, HD // 2, 1) for fade, stat in zip(fades, stats))
-    lanes = lax.broadcasted_iota(jnp.int32, (GROUP, HD), 1)
-    stat = jnp.where(lanes < HD // 2, top, pltpu.roll(total, HD // 2, 1))
-    merged = []
-    for part in range(HEADS * STEPS):
-        rows = slice(part * GROUP, (part + 1) * GROUP)
-        merged.append(
-            sum(fades[source][:, part : part + 1] * sums[source][rows] for source in range(count))
-        )
-    out_ref[0] = seal(merged, stat)
 
 
 def finish(parts_ref, q_ref, k_ref, v_ref, out_ref, hold):
@@ -291,21 +316,19 @@
     here = (z * XN + x) * CN + core
     groups = ZN * JN
     beams = groups * GROUP
-    slots = cache_kv.shape[0]
+    half_slots = cache_kv.shape[0] // 2
     width = PART * groups
 
     weights = ring(jnp.concatenate([w_query, w_key, w_value], axis=1))
     turned = ring(w_out.T)
-    place = jnp.stack([x, core, lax.axis_index("kv")]).astype(jnp.int32)
+    place = jnp.stack([x, core, lax.axis_index("kv"), z]).astype(jnp.int32)
     vmem = pl.BlockSpec(memory_space=pltpu.VMEM)
     smem = pl.BlockSpec(memory_space=pltpu.SMEM)
     cache = cache_kv[:, 0]
-    other_cache = lax.ppermute(cache, "core", [(0, 1), (1, 0)])
 
     base = jnp.arange(groups, dtype=jnp.int32)[None, :, None] * GROUP
     parents_near = parents.reshape(STEPS, groups, GROUP) - base
     roots_near = compose(parents_near)
-    roots = roots_near + base
     length_of = lengths.reshape(groups, GROUP)
     own_roots = lax.dynamic_slice_in_dim(roots_near, here, 1, 1)[:, 0]
     own_parents = lax.dynamic_slice_in_dim(parents_near, here, 1, 1)[:, 0]
@@ -321,23 +344,16 @@
     sines = jnp.sin(angles)
     cosines = jnp.concatenate([cosines, cosines], axis=1)
     sines = jnp.concatenate([-sines, sines], axis=1)
-    own_ids = here * slots + jnp.arange(slots, dtype=jnp.int32)
-    other_ids = (here + 1 - 2 * core) * slots + jnp.arange(slots, dtype=jnp.int32)
-    ids = jnp.concatenate([own_ids, other_ids])
-    table = block_table.reshape(-1, 128)
-    codes = jnp.arange(table.size, dtype=jnp.int32).reshape(table.shape)
-    code = jnp.max(jnp.where(table[None] == ids[:, None, None], codes[None], -1), axis=(1, 2))
-    spans = jnp.broadcast_to(lengths[:, None], block_table.shape).reshape(table.shape)
-    span = jnp.max(jnp.where(table[None] == ids[:, None, None], spans[None], 0), axis=(1, 2))
-    owner = code // block_table.shape[1]
-    count = span - (code % block_table.shape[1]) * HD
-    group = owner // GROUP
-    mine = (code >= 0) & (group % CN == core)
-    count = jnp.where(mine, count, 0)
-    group = jnp.where(mine, (group // CN % XN) * ZN + group // JN, 0)
-    root_tiles = lax.dynamic_slice_in_dim(roots.reshape(STEPS, ZN, XN, CN, GROUP), core, 1, 3)
-    root_tiles = root_tiles[:, :, :, 0].transpose(2, 1, 0, 3).reshape(ZN * XN, SB)
-    root_tiles = jnp.broadcast_to(root_tiles[:, :, None], (ZN * XN, SB, HD))
+    lead = x * CN + core
+    table = lax.dynamic_index_in_dim(
+        block_table.reshape(ZN, JN, GROUP * block_table.shape[1]), lead, 1, keepdims=False
+    ).reshape(-1)
+    spans = lax.dynamic_index_in_dim(lengths.reshape(ZN, JN, GROUP), lead, 1, keepdims=False)
+    root_tiles = lax.dynamic_index_in_dim(
+        roots_near.reshape(STEPS, ZN, JN, GROUP), lead, 2, keepdims=False
+    )
+    root_tiles = root_tiles.transpose(1, 0, 2).reshape(ZN, SB)
+    root_tiles = jnp.broadcast_to(root_tiles[:, :, None], (ZN, SB, HD))
 
     rows = ZN * SB
     half = rows // 2
@@ -359,6 +375,10 @@
     gain = gain.reshape(XN, 1, 2 * PART)
     squares = jnp.sum(stream * stream, axis=(0, 2))
     squares = jnp.pad(squares, (0, 256 - rows)).reshape(2, 128)
+    cache, squares = lax.optimization_barrier((cache, squares))
+    left = shift(cache, 1)
+    right = shift(cache, -1)
+    across = [shift(left[:half_slots], 1), shift(right[half_slots:], -1)]
     squares = jnp.sum(spread(squares, "z", ZN), axis=0).reshape(256)[:rows]
     inverse = lax.rsqrt(squares / width + EPSILON)
     normed = (stream * inverse[None, :, None] * gain).astype(jnp.bfloat16)
@@ -366,7 +386,7 @@
     projected = pl.pallas_call(
         project,
         out_shape=jax.ShapeDtypeStruct((rows, columns), jnp.float32),
-        in_specs=[smem] + [vmem] * (1 + 2 * XN),
+        in_specs=[smem] + [vmem] * (1 + XN),
         out_specs=vmem,
         scratch_shapes=[pltpu.VMEM((XN, 2 * PART, columns), jnp.bfloat16)],
     )(place, normed, *weights)
@@ -385,33 +405,33 @@
         out_specs=(vmem,) * 4,
         scratch_shapes=[pltpu.VMEM((ROWS, HD), jnp.float32)],
     )(own_parents.reshape(SB), projected, cosines, sines)
+    caches = [cache, left, right, None, None]
+    caches = caches + [swap(part) for part in caches[:3]]
     last = PAIRS.index((STEPS - 1, 0))
     appended = jnp.stack([key_chain[last:], value_chain[last:]], axis=2)
     appended = appended[:, :, None].astype(jnp.bfloat16)
 
     everyone = exchange(everyone, "z")
-    everyone = spread(everyone.reshape(ZN * ROWS, HD), "x", XN).reshape(XN * ZN, ROWS, HD)
+    everyone, across = lax.optimization_barrier((everyone, across))
+    caches[3:5] = across
+    caches = caches + [swap(part) for part in across]
     partial = pl.pallas_call(
         attention,
-        out_shape=jax.ShapeDtypeStruct((XN * ZN, BLOCK, HD), jnp.bfloat16),
-        in_specs=[smem, smem, smem, vmem, vmem, vmem, vmem],
+        out_shape=jax.ShapeDtypeStruct((ZN, BLOCK, HD), jnp.bfloat16),
+        in_specs=[smem, smem, smem, vmem, vmem]
+        + [pl.BlockSpec(memory_space=pl.ANY)] * (2 * SEGMENTS),
         out_specs=vmem,
         scratch_shapes=[
-            pltpu.VMEM((XN * ZN, ROWS, HD), jnp.float32),
-            pltpu.VMEM((XN * ZN, ROWS, HD), jnp.float32),
-            pltpu.VMEM((XN * ZN, ROWS, HD), jnp.float32),
+            pltpu.VMEM((ZN, ROWS, HD), jnp.float32),
+            pltpu.VMEM((ZN, ROWS, HD), jnp.float32),
+            pltpu.VMEM((ZN, ROWS, HD), jnp.float32),
+            pltpu.VMEM((DEPTH,) + cache.shape[1:], jnp.bfloat16),
+            pltpu.SemaphoreType.DMA((DEPTH,)),
+            pltpu.SMEM((2 * half_slots * JN,), jnp.int32),
+            pltpu.SMEM((2 * half_slots * JN,), jnp.int32),
         ],
-        compiler_params=pltpu.CompilerParams(vmem_limit_bytes=40 << 20),
-    )(owner, group, count, everyone, root_tiles, cache, other_cache)
-
-    partial = exchange(partial.reshape(XN, ZN * BLOCK, HD), "x").reshape(XN, ZN, BLOCK, HD)
-    partial = pl.pallas_call(
-        merge,
-        grid=(ZN,),
-        out_shape=jax.ShapeDtypeStruct((ZN, BLOCK, HD), jnp.bfloat16),
-        in_specs=[pl.BlockSpec((XN, 1, BLOCK, HD), lambda i: (0, i, 0, 0))],
-        out_specs=pl.BlockSpec((1, BLOCK, HD), lambda i: (i, 0, 0)),
-    )(partial)
+    )(place, table, spans.reshape(-1), everyone, root_tiles, *caches)
+
     partial = exchange(partial, "z")
     attended = pl.pallas_call(
         finish,
@@ -425,7 +445,7 @@
     result = pl.pallas_call(
         deliver,
         out_shape=jax.ShapeDtypeStruct((KN, XN, QUARTER, 2 * PART), jnp.float32),
-        in_specs=[smem] + [vmem] * (1 + 2 * XN),
+        in_specs=[smem] + [vmem] * (1 + XN),
         out_specs=vmem,
         scratch_shapes=[pltpu.VMEM((XN, 2 * PART, HEADS * HD), jnp.bfloat16)],
     )(place, attended, *turned)

time: 236 us -> 210 us (0.89)
  waiting for transfers between devices: 76.9 us -> 55.5 us
  local copies, waits for them, and re-layouts: 15.1 us -> 23.5 us
  starting transfers between devices: 63.9 us -> 56.1 us
  Pallas kernels: 29.3 us -> 23.3 us
  blocking collectives: 38.1 us -> 43.5 us
  other arithmetic: 8.58 us -> 5.43 us
    all_to_all x8 -> x6, waiting for transfers between devices: 70.6 us -> 15.3 us  [exchange(): return lax.all_to_all(value, axis, 0, 0, tiled=True)]
    ppermute x15 -> x17, waiting for transfers between devices: 6.3 us -> 40.2 us  [the longest x10 38.8 us: shift(): return lax.ppermute(value, 'x', [(i, (i + hop) % XN) for i in range(XN)])]
    all_to_all x8 -> x6, starting transfers between devices: 40 us -> 30.7 us  [exchange(): return lax.all_to_all(value, axis, 0, 0, tiled=True)]
    pallas_call x2 -> x1, Pallas kernels: 17 us -> 11.2 us  [body(): pl.pallas_call(attention, out_shape=jax.ShapeDtypeStruct((ZN, BLOCK, HD),...]
    all_to_all x2, blocking collectives: 38.1 us -> 43.5 us  [exchange(): return lax.all_to_all(value, axis, 0, 0, tiled=True)]
    reduce_max x1 -> x0, other arithmetic: 3.59 us -> none  [body(): jnp.max(jnp.where(table[None] == ids[:, None, None], spans[None], 0), axi...]
    slice x0 -> x2, local copies, waits for them, and re-layouts: none -> 3.53 us  [body(): across = [shift(left[:half_slots], 1), shift(right[half_slots:], -1)]]
    ppermute x15 -> x17, starting transfers between devices: 23.9 us -> 25.4 us  [the longest x10 15.2 us: shift(): return lax.ppermute(value, 'x', [(i, (i + hop) % XN) for i in range(XN)])]
  transfers between devices with their start and end apart: 23 -> 23, of which waited for: 11 -> 8; matrix products, arithmetic and copies ran while one was open for 6% -> 11% of each run, Pallas kernels for 1% -> 2%
where the time goes in v4:
time: 210 us; the launch traced here: 208 us
  starting transfers between devices  56.1 us (27%)
  waiting for transfers between devices  55.5 us (26%)
  blocking collectives  43.5 us (21%)
  local copies, waits for them, and re-layouts  23.5 us (11%)
  Pallas kernels  23.3 us (11%)
  other arithmetic  5.43 us (3%)
    all_to_all x2, blocking collectives, exchange(): return lax.all_to_all(value, axis, 0, 0, tiled=True)  43.5 us
    ppermute x10, waiting for transfers between devices, shift(): return lax.ppermute(value, 'x', [(i, (i + hop) % XN) for i in range(XN)])  38.8 us
    all_to_all x6, starting transfers between devices, exchange(): return lax.all_to_all(value, axis, 0, 0, tiled=True)  30.7 us
    all_to_all x6, waiting for transfers between devices, exchange(): return lax.all_to_all(value, axis, 0, 0, tiled=True)  15.3 us
    ppermute x10, starting transfers between devices, shift(): return lax.ppermute(value, 'x', [(i, (i + hop) % XN) for i in range(XN)])  15.2 us
    pallas_call x1, Pallas kernels, body(): pl.pallas_call(attention, out_shape=jax.ShapeDtypeStruct((ZN, BLOCK, HD),...  11.2 us
    ppermute x7, starting transfers between devices, swap(): return lax.ppermute(value, 'core', [(0, 1), (1, 0)])  10.2 us
    unnamed x35, local copies, waits for them, and re-layouts  7.11 us
  transfers between devices with their start and end apart: 23, of which 8 were waited for; matrix products, arithmetic and copies ran while one was open for 11% of the time, Pallas kernels for 2%

profile of v4, /device:TPU:1, one launch (start us, length us, event | category | flops | bytes accessed | tf_op | source)
XLA Modules:
  0.0 208.4 jit_solution(17601040732036611321)
XLA Ops:
  0.6 0.9 constant_dynamic-update-slice_fusion.2
  1.5 0.7 constant_dynamic-update-slice_fusion.1
  2.3 0.7 constant_dynamic-update-slice_fusion
  3.0 3.2 %collective-permute-start = (bf16[64,1280]{1,0:T(8,128)(2,1)S(1)}, bf16[64,1280]{1,0:T(8,128)(2,1)S(1)}, u32[]{:S(2)}, u32[]{:S(2)}) collective-permute-start(bf16[64,1280]{1,0:T(8,128)(2,1)S(1)} %constant_dynamic-update-slice_fusion), channel_id=1, source_target_pairs={{0,1},{1,0},{2,3},{3,2},{4,5},{5,4},{6,7},{7,6},{8,9},{9,8},{10,11... | collective-permute-start | bytes 491528 | tf_op jit(solution)/shard_map/ppermute | solution.py:44
  6.9 1.1 copy.89
  9.6 3.3 %all-to-all-start = ((bf16[8,104,128]{2,1,0:T(8,128)(2,1)}), bf16[8,104,128]{2,1,0:T(8,128)(2,1)S(1)}, u32[]{:S(2)}, u32[]{:S(2)}) async-start(bf16[8,104,128]{2,1,0:T(8,128)(2,1)} %pad_maximum_fusion.2), calls=%async_computation | async-start | bytes 425984 | tf_op jit(solution)/shard_map/all_to_all | solution.py:36
  13.6 0.7 pad_maximum_fusion.rest_0_
  14.3 1.3 collective-permute-start.1
  15.6 2.4 %collective-permute-start.2 = (bf16[128,1280]{1,0:T(8,128)(2,1)}, bf16[128,1280]{1,0:T(8,128)(2,1)}, u32[]{:S(2)}, u32[]{:S(2)}) collective-permute-start(bf16[128,1280]{1,0:T(8,128)(2,1)} %pad_maximum_fusion.rest_0_), channel_id=1, source_target_pairs={{0,4},{2,6},{4,0},{6,2},{1,5},{3,7},{5,1},{7,3},{8,12},{10,14},{12... | collective-permute-start | bytes 983048 | tf_op jit(solution)/shard_map/ppermute | solution.py:48
  18.0 1.2 collective-permute-start.3
  20.1 2.4 %collective-permute-start.6 = (bf16[32,2,128,128]{3,2,1,0:T(8,128)(2,1)}, bf16[32,2,128,128]{3,2,1,0:T(8,128)(2,1)}, u32[]{:S(2)}, u32[]{:S(2)}) collective-permute-start(bf16[32,2,128,128]{3,2,1,0:T(8,128)(2,1)} %bitcast.50), channel_id=1, source_target_pairs={{0,6},{2,0},{4,2},{6,4},{1,7},{3,1},{5,3},{7,5},{8,14},{10,8},{12,... | collective-permute-start | bytes 6291464 | tf_op jit(solution)/shard_map/ppermute | solution.py:48
  23.1 7.5 %all-to-all-start.1 = ((f32[8,2,128]{2,1,0:T(2,128)}), f32[8,2,128]{2,1,0:T(2,128)S(1)}, u32[]{:S(2)}, u32[]{:S(2)}) async-start(f32[8,2,128]{2,1,0:T(2,128)} %broadcast_in_dim.66), calls=%async_computation.1 | async-start | bytes 16384 | tf_op jit(solution)/shard_map/all_to_all | solution.py:36
  31.3 1.5 copy.91
  32.8 1.6 reshape.169.stream_ref
  34.4 2.8 %all-to-all-done.1 = f32[8,2,128]{2,1,0:T(2,128)S(1)} async-done(((f32[8,2,128]{2,1,0:T(2,128)}), f32[8,2,128]{2,1,0:T(2,128)S(1)}, u32[]{:S(2)}, u32[]{:S(2)}) %all-to-all-start.1) | async-done | bytes 8224 | tf_op jit(solution)/shard_map/all_to_all | solution.py:36
  37.3 0.8 multiply_convert_fusion.rows_ref
  38.1 3.1 %shard_map.113 = f32[192,1280]{1,0:T(8,128)} custom-call(s32[4]{0:T(128)} %pad_add_fusion.place_ref, bf16[4,192,128]{2,1,0:T(8,128)(2,1)} %multiply_convert_fusion.rows_ref, bf16[128,1280]{1,0:T(8,128)(2,1)} %pad_maximum_fusion.rest_0_, bf16[128,1280]{1,0:T(8,128)(2,1)} %collective-permute-done.1.rest_1_, bf16[128,1280]{1,0:T(8,128)(2,1)} %collective-permute-done.2.rest_2_, ...), custom_call_target="tpu_custom_call" | custom-call | tf_op jit(solution)/shard_map/pallas_call | solution.py:386
  41.1 3.8 %all-to-all-start.2 = ((f32[8,24,1280]{2,1,0:T(8,128)}), f32[8,24,1280]{2,1,0:T(8,128)S(1)}, u32[]{:S(2)}, u32[]{:S(2)}) async-start(f32[8,24,1280]{2,1,0:T(8,128)} %bitcast.47), calls=%async_computation.2 | async-start | bytes 1966080 | tf_op jit(solution)/shard_map/all_to_all | solution.py:36
  46.1 3.0 %collective-permute-start.8 = (bf16[32,2,128,128]{3,2,1,0:T(8,128)(2,1)}, bf16[32,2,128,128]{3,2,1,0:T(8,128)(2,1)}, u32[]{:S(2)}, u32[]{:S(2)}) collective-permute-start(bf16[32,2,128,128]{3,2,1,0:T(8,128)(2,1)} %bitcast.51), channel_id=1, source_target_pairs={{0,1},{1,0},{2,3},{3,2},{4,5},{5,4},{6,7},{7,6},{8,9},{9,8},{10,11... | collective-permute-start | bytes 6291464 | tf_op jit(solution)/shard_map/ppermute | solution.py:44
  49.1 28.9 %collective-permute-done.4.rest_1_ = bf16[32,2,128,128]{3,2,1,0:T(8,128)(2,1)S(1)} collective-permute-done((bf16[32,2,128,128]{3,2,1,0:T(8,128)(2,1)}, bf16[32,2,128,128]{3,2,1,0:T(8,128)(2,1)S(1)}, u32[]{:S(2)}, u32[]{:S(2)}) %collective-permute-start.4) | collective-permute-done | bytes 2097184 | tf_op jit(solution)/shard_map/ppermute | solution.py:48
  78.0 1.2 slice.62
  79.2 2.3 %slice.63 = bf16[16,2,128,128]{3,2,1,0:T(8,128)(2,1)} slice(bf16[32,2,128,128]{3,2,1,0:T(8,128)(2,1)} %collective-permute-done.6.rest_2_), slice={[16:32], [0:2], [0:128], [0:128]} | slice | bytes 2097152 | tf_op jit(solution)/shard_map/slice | solution.py:381
  81.5 2.6 %collective-permute-start.7 = (bf16[16,2,128,128]{3,2,1,0:T(8,128)(2,1)}, bf16[16,2,128,128]{3,2,1,0:T(8,128)(2,1)}, u32[]{:S(2)}, u32[]{:S(2)}) collective-permute-start(bf16[16,2,128,128]{3,2,1,0:T(8,128)(2,1)} %slice.63), channel_id=1, source_target_pairs={{0,6},{2,0},{4,2},{6,4},{1,7},{3,1},{5,3},{7,5},{8,14},{10,8},{12,... | collective-permute-start | bytes 3145736 | tf_op jit(solution)/shard_map/ppermute | solution.py:48
  84.2 1.2 collective-permute-start.10
  87.0 1.0 copy-done.1
  87.9 2.2 %shard_map.114 = (bf16[192,128]{1,0:T(8,128)(2,1)}, bf16[8,192,128]{2,1,0:T(8,128)(2,1)}, f32[6,8,128]{2,1,0:T(8,128)}, f32[6,8,128]{2,1,0:T(8,128)}) custom-call(s32[24]{0:T(128)} %reshape_squeeze.3.parent_ref, f32[8,24,1280]{2,1,0:T(8,128)} %copy-done.1, f32[24,128]{1,0:T(8,128)} %get-tuple-element.49.cos_ref, f32[24,128]{1,0:T(8,128)} %get-tuple-element.50.sin_ref), custom_call_target="tpu_custom_call" | custom-call | tf_op jit(solution)/shard_map/pallas_call | solution.py:396
  90.1 21.1 %all_to_all.40.q_ref = bf16[8,192,128]{2,1,0:T(8,128)(2,1)} all-to-all(bf16[8,192,128]{2,1,0:T(8,128)(2,1)} %get-tuple-element.12), channel_id=1, replica_groups=mesh['kv'=4,'z'=8,'x'=4,'core'=2] {'z'}, dimensions={0} | all-to-all | bytes 786432 | tf_op jit(solution)/shard_map/all_to_all | solution.py:36
  111.2 2.2 %collective-permute-start.11 = (bf16[16,2,128,128]{3,2,1,0:T(8,128)(2,1)}, bf16[16,2,128,128]{3,2,1,0:T(8,128)(2,1)S(1)}, u32[]{:S(2)}, u32[]{:S(2)}) collective-permute-start(bf16[16,2,128,128]{3,2,1,0:T(8,128)(2,1)} %collective-permute-done.5.rest_3_), channel_id=1, source_target_pairs={{0,1},{1,0},{2,3},{3,2},{4,5},{5,4},{6,7},{7,6},{8,9},{9,8},{10,11... | collective-permute-start | bytes 3145736 | tf_op jit(solution)/shard_map/ppermute | solution.py:44
  113.6 0.7 reshape.156
  115.0 0.8 dynamic-slice_reduce_fusion
  117.5 0.7 broadcast_in_dim.75.root_ref
  118.2 11.2 %shard_map.115 = bf16[8,216,128]{2,1,0:T(8,128)(2,1)} custom-call(s32[4]{0:T(128)} %pad_add_fusion.place_ref, s32[4096]{0:T(1024)} %bitcast.60, s32[64]{0:T(128)} %reshape.157.length_ref, bf16[8,192,128]{2,1,0:T(8,128)(2,1)} %all_to_all.40.q_ref, s32[8,24,128]{2,1,0:T(8,128)} %broadcast_in_dim.75.root_ref, bf16[32,2,128,128]{3,2,1,0:T(8,128)(2,1)} %bitcast.52, ...), custom_call_target="tpu_custom_call" | custom-call | tf_op jit(solution)/shard_map/pallas_call | solution.py:418
  129.4 22.5 %all_to_all.41.parts_ref = bf16[8,216,128]{2,1,0:T(8,128)(2,1)} all-to-all(bf16[8,216,128]{2,1,0:T(8,128)(2,1)} %shard_map.115), channel_id=1, replica_groups=mesh['kv'=4,'z'=8,'x'=4,'core'=2] {'z'}, dimensions={0} | all-to-all | bytes 884736 | tf_op jit(solution)/shard_map/all_to_all | solution.py:36
  151.9 2.3 %shard_map.116 = bf16[8,24,1024]{2,1,0:T(8,128)(2,1)} custom-call(bf16[8,216,128]{2,1,0:T(8,128)(2,1)} %all_to_all.41.parts_ref, bf16[192,128]{1,0:T(8,128)(2,1)} %get-tuple-element.17.q_ref, f32[6,8,128]{2,1,0:T(8,128)} %get-tuple-element.18.k_ref, f32[6,8,128]{2,1,0:T(8,128)} %get-tuple-element.19.v_ref), custom_call_target="tpu_custom_call" | custom-call | tf_op jit(solution)/shard_map/pallas_call | solution.py:436
  154.2 3.5 %all-to-all-start.5 = ((bf16[8,24,1024]{2,1,0:T(8,128)(2,1)}), bf16[8,24,1024]{2,1,0:T(8,128)(2,1)S(1)}, u32[]{:S(2)}, u32[]{:S(2)}) async-start(bf16[8,24,1024]{2,1,0:T(8,128)(2,1)} %shard_map.116), calls=%async_computation.5 | async-start | bytes 786432 | tf_op jit(solution)/shard_map/all_to_all | solution.py:36
  158.2 1.0 collective-permute-done.13
  159.3 2.8 %collective-permute-start.15 = (bf16[128,1024]{1,0:T(8,128)(2,1)S(1)}, bf16[128,1024]{1,0:T(8,128)(2,1)S(1)}, u32[]{:S(2)}, u32[]{:S(2)}) collective-permute-start(bf16[128,1024]{1,0:T(8,128)(2,1)S(1)} %pad_maximum_fusion.1.rest_0_), channel_id=1, source_target_pairs={{0,4},{2,6},{4,0},{6,2},{1,5},{3,7},{5,1},{7,3},{8,12},{10,14},{12... | collective-permute-start | bytes 786440 | tf_op jit(solution)/shard_map/ppermute | solution.py:48
  162.1 2.0 collective-permute-start.16
  164.1 3.9 %collective-permute-done.14.rest_1_ = bf16[128,1024]{1,0:T(8,128)(2,1)S(1)} collective-permute-done((bf16[128,1024]{1,0:T(8,128)(2,1)S(1)}, bf16[128,1024]{1,0:T(8,128)(2,1)S(1)}, u32[]{:S(2)}, u32[]{:S(2)}) %collective-permute-start.14) | collective-permute-done | bytes 262176 | tf_op jit(solution)/shard_map/ppermute | solution.py:48
  168.0 5.9 %collective-permute-done.15.rest_2_ = bf16[128,1024]{1,0:T(8,128)(2,1)S(1)} collective-permute-done((bf16[128,1024]{1,0:T(8,128)(2,1)S(1)}, bf16[128,1024]{1,0:T(8,128)(2,1)S(1)}, u32[]{:S(2)}, u32[]{:S(2)}) %collective-permute-start.15) | collective-permute-done | bytes 262176 | tf_op jit(solution)/shard_map/ppermute | solution.py:48
  174.9 2.7 %shard_map.117 = f32[4,4,48,128]{3,2,1,0:T(8,128)} custom-call(s32[4]{0:T(128)} %pad_add_fusion.place_ref, bf16[192,1024]{1,0:T(8,128)(2,1)} %bitcast.56, bf16[128,1024]{1,0:T(8,128)(2,1)} %copy-done.6, bf16[128,1024]{1,0:T(8,128)(2,1)} %copy-done.7, bf16[128,1024]{1,0:T(8,128)(2,1)} %copy-done.8, bf16[128,1024]{1,0:T(8,128)(2,1)} %copy-done.9), custom_call_target="tpu_custom_call" | custom-call | tf_op jit(solution)/shard_map/pallas_call | solution.py:445
  177.6 4.2 %all-to-all-start.6 = ((f32[4,4,48,128]{3,2,1,0:T(8,128)}), f32[4,4,48,128]{3,2,1,0:T(8,128)S(1)}, u32[]{:S(2)}, u32[]{:S(2)}) async-start(f32[4,4,48,128]{3,2,1,0:T(8,128)} %shard_map.117), calls=%async_computation.6 | async-start | bytes 786432 | tf_op jit(solution)/shard_map/all_to_all | solution.py:36
  182.5 5.5 %all-to-all-done.6.parts_ref = f32[4,4,48,128]{3,2,1,0:T(8,128)S(1)} async-done(((f32[4,4,48,128]{3,2,1,0:T(8,128)}), f32[4,4,48,128]{3,2,1,0:T(8,128)S(1)}, u32[]{:S(2)}, u32[]{:S(2)}) %all-to-all-start.6) | async-done | bytes 393248 | tf_op jit(solution)/shard_map/all_to_all | solution.py:36
  188.0 0.7 copy-done.3
  188.8 1.9 shard_map.118
  190.7 8.3 %all-to-all-start.7 = ((bf16[32,24,128]{2,1,0:T(8,128)(2,1)}), bf16[32,24,128]{2,1,0:T(8,128)(2,1)S(1)}, u32[]{:S(2)}, u32[]{:S(2)}) async-start(bf16[32,24,128]{2,1,0:T(8,128)(2,1)} %bitcast.57), calls=%async_computation.7 | async-start | bytes 393216 | tf_op jit(solution)/shard_map/all_to_all | solution.py:36
  200.3 6.9 %all-to-all-done.7 = bf16[32,24,128]{2,1,0:T(8,128)(2,1)S(1)} async-done(((bf16[32,24,128]{2,1,0:T(8,128)(2,1)}), bf16[32,24,128]{2,1,0:T(8,128)(2,1)S(1)}, u32[]{:S(2)}, u32[]{:S(2)}) %all-to-all-start.7) | async-done | bytes 196640 | tf_op jit(solution)/shard_map/all_to_all | solution.py:36
  207.5 0.8 copy.102
  (109 shorter events, 14.0 us)
Async XLA Ops:
  3.0 10.5 %collective-permute-start = (bf16[64,1280]{1,0:T(8,128)(2,1)S(1)}, bf16[64,1280]{1,0:T(8,128)(2,1)S(1)}, u32[]{:S(2)}, u32[]{:S(2)}) collective-permute-start(bf16[64,1280]{1,0:T(8,128)(2,1)S(1)} %constant_dynamic-update-slice_fusion), channel_id=1, source_target_pairs={{0,1},{1,0},{2,3},{3,2},{4,5},{5,4},{6,7},{7,6},{8,9},{9,8},{10,11... | collective-permute-start | bytes 491528 | tf_op jit(solution)/shard_map/ppermute | solution.py:44
  9.6 9.6 %all-to-all-start = ((bf16[8,104,128]{2,1,0:T(8,128)(2,1)}), bf16[8,104,128]{2,1,0:T(8,128)(2,1)S(1)}, u32[]{:S(2)}, u32[]{:S(2)}) async-start(bf16[8,104,128]{2,1,0:T(8,128)(2,1)} %pad_maximum_fusion.2), calls=%async_computation | async-start | bytes 425984 | tf_op jit(solution)/shard_map/all_to_all | solution.py:36
  14.3 23.8 %collective-permute-start.1 = (bf16[128,1280]{1,0:T(8,128)(2,1)}, bf16[128,1280]{1,0:T(8,128)(2,1)}, u32[]{:S(2)}, u32[]{:S(2)}) collective-permute-start(bf16[128,1280]{1,0:T(8,128)(2,1)} %pad_maximum_fusion.rest_0_), channel_id=1, source_target_pairs={{0,2},{2,4},{4,6},{6,0},{1,3},{3,5},{5,7},{7,1},{8,10},{10,12},{12... | collective-permute-start | bytes 983048 | tf_op jit(solution)/shard_map/ppermute | solution.py:48
  15.6 22.4 %collective-permute-start.2 = (bf16[128,1280]{1,0:T(8,128)(2,1)}, bf16[128,1280]{1,0:T(8,128)(2,1)}, u32[]{:S(2)}, u32[]{:S(2)}) collective-permute-start(bf16[128,1280]{1,0:T(8,128)(2,1)} %pad_maximum_fusion.rest_0_), channel_id=1, source_target_pairs={{0,4},{2,6},{4,0},{6,2},{1,5},{3,7},{5,1},{7,3},{8,12},{10,14},{12... | collective-permute-start | bytes 983048 | tf_op jit(solution)/shard_map/ppermute | solution.py:48
  18.0 20.0 %collective-permute-start.3 = (bf16[128,1280]{1,0:T(8,128)(2,1)}, bf16[128,1280]{1,0:T(8,128)(2,1)}, u32[]{:S(2)}, u32[]{:S(2)}) collective-permute-start(bf16[128,1280]{1,0:T(8,128)(2,1)} %pad_maximum_fusion.rest_0_), channel_id=1, source_target_pairs={{0,6},{2,0},{4,2},{6,4},{1,7},{3,1},{5,3},{7,5},{8,14},{10,8},{12,... | collective-permute-start | bytes 983048 | tf_op jit(solution)/shard_map/ppermute | solution.py:48
  19.8 58.2 %collective-permute-start.4 = (bf16[32,2,128,128]{3,2,1,0:T(8,128)(2,1)}, bf16[32,2,128,128]{3,2,1,0:T(8,128)(2,1)S(1)}, u32[]{:S(2)}, u32[]{:S(2)}) collective-permute-start(bf16[32,2,128,128]{3,2,1,0:T(8,128)(2,1)} %bitcast.49), channel_id=1, source_target_pairs={{0,2},{2,4},{4,6},{6,0},{1,3},{3,5},{5,7},{7,1},{8,10},{10,12},{12... | collective-permute-start | bytes 6291464 | tf_op jit(solution)/shard_map/ppermute | solution.py:48
  20.1 59.1 %collective-permute-start.6 = (bf16[32,2,128,128]{3,2,1,0:T(8,128)(2,1)}, bf16[32,2,128,128]{3,2,1,0:T(8,128)(2,1)}, u32[]{:S(2)}, u32[]{:S(2)}) collective-permute-start(bf16[32,2,128,128]{3,2,1,0:T(8,128)(2,1)} %bitcast.50), channel_id=1, source_target_pairs={{0,6},{2,0},{4,2},{6,4},{1,7},{3,1},{5,3},{7,5},{8,14},{10,8},{12,... | collective-permute-start | bytes 6291464 | tf_op jit(solution)/shard_map/ppermute | solution.py:48
  23.1 14.1 %all-to-all-start.1 = ((f32[8,2,128]{2,1,0:T(2,128)}), f32[8,2,128]{2,1,0:T(2,128)S(1)}, u32[]{:S(2)}, u32[]{:S(2)}) async-start(f32[8,2,128]{2,1,0:T(2,128)} %broadcast_in_dim.66), calls=%async_computation.1 | async-start | bytes 16384 | tf_op jit(solution)/shard_map/all_to_all | solution.py:36
  34.4 6.8 %copy-start.2 = (f32[4,192,128]{2,1,0:T(8,128)}, f32[4,192,128]{2,1,0:T(8,128)S(1)}, u32[]{:S(2)}) copy-start(f32[4,192,128]{2,1,0:T(8,128)S(1)} %reshape.169.stream_ref) | copy-start | bytes 1179652
  38.1 6.9 %copy-start.13 = (s32[3,512]{1,0:T(4,128)S(1)}, s32[3,512]{1,0:T(4,128)}, u32[]{:S(2)}) copy-start(s32[3,512]{1,0:T(4,128)} %param.19) | copy-start | bytes 18436
  38.1 7.4 %copy-start.12 = (s32[512]{0:T(512)S(1)}, s32[512]{0:T(512)}, u32[]{:S(2)}) copy-start(s32[512]{0:T(512)} %param.17) | copy-start | bytes 6148
  41.1 45.8 %all-to-all-start.2 = ((f32[8,24,1280]{2,1,0:T(8,128)}), f32[8,24,1280]{2,1,0:T(8,128)S(1)}, u32[]{:S(2)}, u32[]{:S(2)}) async-start(f32[8,24,1280]{2,1,0:T(8,128)} %bitcast.47), calls=%async_computation.2 | async-start | bytes 1966080 | tf_op jit(solution)/shard_map/all_to_all | solution.py:36
  46.1 70.9 %collective-permute-start.8 = (bf16[32,2,128,128]{3,2,1,0:T(8,128)(2,1)}, bf16[32,2,128,128]{3,2,1,0:T(8,128)(2,1)}, u32[]{:S(2)}, u32[]{:S(2)}) collective-permute-start(bf16[32,2,128,128]{3,2,1,0:T(8,128)(2,1)} %bitcast.51), channel_id=1, source_target_pairs={{0,1},{1,0},{2,3},{3,2},{4,5},{5,4},{6,7},{7,6},{8,9},{9,8},{10,11... | collective-permute-start | bytes 6291464 | tf_op jit(solution)/shard_map/ppermute | solution.py:44
  78.0 7.4 %copy-start = (bf16[32,2,128,128]{3,2,1,0:T(8,128)(2,1)}, bf16[32,2,128,128]{3,2,1,0:T(8,128)(2,1)S(1)}, u32[]{:S(2)}) copy-start(bf16[32,2,128,128]{3,2,1,0:T(8,128)(2,1)S(1)} %collective-permute-done.4.rest_1_) | copy-start | bytes 6291460
  79.2 35.6 %copy-start.10 = (s32[512,64]{0,1:T(8,128)S(1)}, s32[512,64]{0,1:T(8,128)}, u32[]{:S(2)}) copy-start(s32[512,64]{0,1:T(8,128)} %param.18) | copy-start | bytes 393220
  79.2 32.0 %collective-permute-start.5 = (bf16[16,2,128,128]{3,2,1,0:T(8,128)(2,1)}, bf16[16,2,128,128]{3,2,1,0:T(8,128)(2,1)}, u32[]{:S(2)}, u32[]{:S(2)}) collective-permute-start(bf16[16,2,128,128]{3,2,1,0:T(8,128)(2,1)} %slice.62), channel_id=1, source_target_pairs={{0,2},{2,4},{4,6},{6,0},{1,3},{3,5},{5,7},{7,1},{8,10},{10,12},{12... | collective-permute-start | bytes 3145736 | tf_op jit(solution)/shard_map/ppermute | solution.py:48
  81.5 29.6 %collective-permute-start.7 = (bf16[16,2,128,128]{3,2,1,0:T(8,128)(2,1)}, bf16[16,2,128,128]{3,2,1,0:T(8,128)(2,1)}, u32[]{:S(2)}, u32[]{:S(2)}) collective-permute-start(bf16[16,2,128,128]{3,2,1,0:T(8,128)(2,1)} %slice.63), channel_id=1, source_target_pairs={{0,6},{2,0},{4,2},{6,4},{1,7},{3,1},{5,3},{7,5},{8,14},{10,8},{12,... | collective-permute-start | bytes 3145736 | tf_op jit(solution)/shard_map/ppermute | solution.py:48
  84.2 33.3 %collective-permute-start.10 = (bf16[32,2,128,128]{3,2,1,0:T(8,128)(2,1)}, bf16[32,2,128,128]{3,2,1,0:T(8,128)(2,1)}, u32[]{:S(2)}, u32[]{:S(2)}) collective-permute-start(bf16[32,2,128,128]{3,2,1,0:T(8,128)(2,1)} %collective-permute-done.6.rest_2_), channel_id=1, source_target_pairs={{0,1},{1,0},{2,3},{3,2},{4,5},{5,4},{6,7},{7,6},{8,9},{9,8},{10,11... | collective-permute-start | bytes 6291464 | tf_op jit(solution)/shard_map/ppermute | solution.py:44
  85.4 32.1 %collective-permute-start.9 = (bf16[32,2,128,128]{3,2,1,0:T(8,128)(2,1)S(1)}, bf16[32,2,128,128]{3,2,1,0:T(8,128)(2,1)}, u32[]{:S(2)}, u32[]{:S(2)}) collective-permute-start(bf16[32,2,128,128]{3,2,1,0:T(8,128)(2,1)S(1)} %collective-permute-done.4.rest_1_), channel_id=1, source_target_pairs={{0,1},{1,0},{2,3},{3,2},{4,5},{5,4},{6,7},{7,6},{8,9},{9,8},{10,11... | collective-permute-start | bytes 6291464 | tf_op jit(solution)/shard_map/ppermute | solution.py:44
  87.0 1.0 copy-start.1
  111.2 5.9 %collective-permute-start.11 = (bf16[16,2,128,128]{3,2,1,0:T(8,128)(2,1)}, bf16[16,2,128,128]{3,2,1,0:T(8,128)(2,1)S(1)}, u32[]{:S(2)}, u32[]{:S(2)}) collective-permute-start(bf16[16,2,128,128]{3,2,1,0:T(8,128)(2,1)} %collective-permute-done.5.rest_3_), channel_id=1, source_target_pairs={{0,1},{1,0},{2,3},{3,2},{4,5},{5,4},{6,7},{7,6},{8,9},{9,8},{10,11... | collective-permute-start | bytes 3145736 | tf_op jit(solution)/shard_map/ppermute | solution.py:44
  113.3 4.1 %collective-permute-start.12 = (bf16[16,2,128,128]{3,2,1,0:T(8,128)(2,1)}, bf16[16,2,128,128]{3,2,1,0:T(8,128)(2,1)}, u32[]{:S(2)}, u32[]{:S(2)}) collective-permute-start(bf16[16,2,128,128]{3,2,1,0:T(8,128)(2,1)} %collective-permute-done.7.rest_4_), channel_id=1, source_target_pairs={{0,1},{1,0},{2,3},{3,2},{4,5},{5,4},{6,7},{7,6},{8,9},{9,8},{10,11... | collective-permute-start | bytes 3145736 | tf_op jit(solution)/shard_map/ppermute | solution.py:44
  117.0 1.2 copy-start.5
  129.4 28.3 %copy-start.11 = (bf16[1024,64]{0,1:T(8,128)(2,1)S(1)}, bf16[1024,64]{0,1:T(8,128)(2,1)}, u32[]{:S(2)}) copy-start(bf16[1024,64]{0,1:T(8,128)(2,1)} %param.15) | copy-start | bytes 393220
  154.2 19.7 %all-to-all-start.5 = ((bf16[8,24,1024]{2,1,0:T(8,128)(2,1)}), bf16[8,24,1024]{2,1,0:T(8,128)(2,1)S(1)}, u32[]{:S(2)}, u32[]{:S(2)}) async-start(bf16[8,24,1024]{2,1,0:T(8,128)(2,1)} %shard_map.116), calls=%async_computation.5 | async-start | bytes 786432 | tf_op jit(solution)/shard_map/all_to_all | solution.py:36
  157.7 1.5 collective-permute-start.13
  159.2 14.8 %copy-start.6 = (bf16[128,1024]{1,0:T(8,128)(2,1)}, bf16[128,1024]{1,0:T(8,128)(2,1)S(1)}, u32[]{:S(2)}) copy-start(bf16[128,1024]{1,0:T(8,128)(2,1)S(1)} %pad_maximum_fusion.1.rest_0_) | copy-start | bytes 786436
  159.2 8.8 %collective-permute-start.14 = (bf16[128,1024]{1,0:T(8,128)(2,1)S(1)}, bf16[128,1024]{1,0:T(8,128)(2,1)S(1)}, u32[]{:S(2)}, u32[]{:S(2)}) collective-permute-start(bf16[128,1024]{1,0:T(8,128)(2,1)S(1)} %pad_maximum_fusion.1.rest_0_), channel_id=1, source_target_pairs={{0,2},{2,4},{4,6},{6,0},{1,3},{3,5},{5,7},{7,1},{8,10},{10,12},{12... | collective-permute-start | bytes 786440 | tf_op jit(solution)/shard_map/ppermute | solution.py:48
  159.3 14.7 %collective-permute-start.15 = (bf16[128,1024]{1,0:T(8,128)(2,1)S(1)}, bf16[128,1024]{1,0:T(8,128)(2,1)S(1)}, u32[]{:S(2)}, u32[]{:S(2)}) collective-permute-start(bf16[128,1024]{1,0:T(8,128)(2,1)S(1)} %pad_maximum_fusion.1.rest_0_), channel_id=1, source_target_pairs={{0,4},{2,6},{4,0},{6,2},{1,5},{3,7},{5,1},{7,3},{8,12},{10,14},{12... | collective-permute-start | bytes 786440 | tf_op jit(solution)/shard_map/ppermute | solution.py:48
  162.1 11.9 %collective-permute-start.16 = (bf16[128,1024]{1,0:T(8,128)(2,1)S(1)}, bf16[128,1024]{1,0:T(8,128)(2,1)S(1)}, u32[]{:S(2)}, u32[]{:S(2)}) collective-permute-start(bf16[128,1024]{1,0:T(8,128)(2,1)S(1)} %pad_maximum_fusion.1.rest_0_), channel_id=1, source_target_pairs={{0,6},{2,0},{4,2},{6,4},{1,7},{3,1},{5,3},{7,5},{8,14},{10,8},{12,... | collective-permute-start | bytes 786440 | tf_op jit(solution)/shard_map/ppermute | solution.py:48
  168.0 6.0 %copy-start.7 = (bf16[128,1024]{1,0:T(8,128)(2,1)}, bf16[128,1024]{1,0:T(8,128)(2,1)S(1)}, u32[]{:S(2)}) copy-start(bf16[128,1024]{1,0:T(8,128)(2,1)S(1)} %collective-permute-done.14.rest_1_) | copy-start | bytes 786436
  173.9 0.7 copy-start.8
  173.9 0.8 copy-start.9
  174.0 0.9 copy-start.4
  177.6 10.4 %all-to-all-start.6 = ((f32[4,4,48,128]{3,2,1,0:T(8,128)}), f32[4,4,48,128]{3,2,1,0:T(8,128)S(1)}, u32[]{:S(2)}, u32[]{:S(2)}) async-start(f32[4,4,48,128]{3,2,1,0:T(8,128)} %shard_map.117), calls=%async_computation.6 | async-start | bytes 786432 | tf_op jit(solution)/shard_map/all_to_all | solution.py:36
  188.0 0.7 copy-start.3
  190.7 16.6 %all-to-all-start.7 = ((bf16[32,24,128]{2,1,0:T(8,128)(2,1)}), bf16[32,24,128]{2,1,0:T(8,128)(2,1)S(1)}, u32[]{:S(2)}, u32[]{:S(2)}) async-start(bf16[32,24,128]{2,1,0:T(8,128)(2,1)} %bitcast.57), calls=%async_computation.7 | async-start | bytes 393216 | tf_op jit(solution)/shard_map/all_to_all | solution.py:36

commit v5 on v4

--- a/solution.py
+++ b/solution.py
@@ -23,7 +23,7 @@
 JN = XN * CN
 KN = 4
 PART = 64
-SEGMENTS = 5
+SLOTS = 32
 DEPTH = 12
 QUARTER = ZN * SB // KN
 PAIRS = [(s, u) for s in range(STEPS) for u in range(s + 1)]
@@ -139,52 +139,61 @@
                     ref[index, pl.ds(beam, 1), :] = ref[before, pl.ds(parent, 1), :]
 
 
-def attention(place_ref, table_ref, length_ref, q_ref, root_ref, *rest):
-    caches, rest = rest[: 2 * SEGMENTS], rest[2 * SEGMENTS :]
-    out_ref, top_ref, sum_ref, hold, pages, arrived, beam_list, block_list = rest
+def scan(place_ref, table_ref, length_ref, near_list, far_list, count_ref):
     x, core, z = place_ref[0], place_ref[1], place_ref[3]
     blocks = table_ref.shape[0] // (ZN * GROUP)
-    slots = caches[0].shape[0]
-    top_ref[...] = jnp.full_like(top_ref, NEGATIVE)
-    sum_ref[...] = jnp.zeros_like(sum_ref)
-    hold[...] = jnp.zeros_like(hold)
+    half = SLOTS // 2
 
     def scan_beam(beam, found):
-        used = (length_ref[beam] + HD - 1) // HD
+        used = lax.shift_right_logical(length_ref[beam] + (HD - 1), 7)
 
         def scan_block(block, found):
             slot = table_ref[beam * blocks + block]
-            near = slot // (slots * JN) == z
-
-            @pl.when(near)
+            near, far = found
+            hit = lax.shift_right_logical(slot, 8) == z
+            hops = jnp.bitwise_and(lax.shift_right_logical(slot, 6) - x, XN - 1)
+            opposite = hops == 2
+            offset = jnp.bitwise_and(slot, half - 1)
+            upper = jnp.bitwise_and(lax.shift_right_logical(slot, 4), 1)
+            foreign = jnp.bitwise_xor(jnp.bitwise_and(lax.shift_right_logical(slot, 5), 1), core)
+            chip = jnp.where(hops == 0, 0, jnp.where(hops == 3, 1, 2))
+            segment = jnp.where(opposite, upper + 2 * foreign, chip * 4 + upper + 2 * foreign)
+            code = ((beam * blocks + block) * SLOTS + segment) * SLOTS + offset
+
+            @pl.when(hit & opposite)
             def _():
-                beam_list[found] = beam
-                block_list[found] = block
-
-            return found + near.astype(jnp.int32)
+                far_list[far] = code
+
+            @pl.when(hit & jnp.logical_not(opposite))
+            def _():
+                near_list[near] = code
+
+            return (
+                near + (hit & jnp.logical_not(opposite)).astype(jnp.int32),
+                far + (hit & opposite).astype(jnp.int32),
+            )
 
         return lax.fori_loop(0, used, scan_block, found)
 
-    found = lax.fori_loop(0, ZN * GROUP, scan_beam, 0)
+    near, far = lax.fori_loop(0, ZN * GROUP, scan_beam, (0, 0))
+    count_ref[0] = near
+    count_ref[1] = far
+
+
+def attend(list_ref, found, length_ref, q_ref, root_ref, sources, state, pages, arrived):
+    top_ref, sum_ref, hold = state
 
     def fetch(item):
-        slot = table_ref[beam_list[item] * blocks + block_list[item]]
-        lane = item % DEPTH
-        offset = slot % slots
-        source = slot // slots % JN
-        far = (source // CN + XN - x) % XN
-        foreign = jnp.where(source % CN == core, 0, 1)
-        half = slots // 2
-        segment = jnp.where(far == 0, 0, jnp.where(far == 3, 1, jnp.where(far == 1, 2, 3)))
-        late = (segment == 3) & (offset >= half)
-        segment = jnp.where(late, 4, segment) + foreign * SEGMENTS
-        offset = jnp.where(late, offset - half, offset)
-        for index in range(2 * SEGMENTS):
+        code = list_ref[item]
+        lane = lax.rem(item, DEPTH)
+        offset = jnp.bitwise_and(code, SLOTS - 1)
+        segment = jnp.bitwise_and(lax.shift_right_logical(code, 5), SLOTS - 1)
+        for index, (ref, base) in enumerate(sources):
 
             @pl.when(segment == index)
-            def _(index=index):
+            def _(ref=ref, base=base):
                 pltpu.make_async_copy(
-                    caches[index].at[offset], pages.at[lane], arrived.at[lane]
+                    ref.at[base + offset], pages.at[lane], arrived.at[lane]
                 ).start()
 
     for item in range(DEPTH):
@@ -196,13 +205,14 @@
     tokens = lax.broadcasted_iota(jnp.int32, (SB, HD), 1)
 
     def visit(item, carry):
-        lane = item % DEPTH
-        beam = beam_list[item]
-        group = beam // GROUP
-        count = length_ref[beam] - block_list[item] * HD
-        live = (root_ref[group] == beam % GROUP) & (tokens < count)
+        lane = lax.rem(item, DEPTH)
+        place = lax.shift_right_logical(list_ref[item], 10)
+        beam = lax.shift_right_logical(place, 6)
+        group = lax.shift_right_logical(beam, 3)
+        count = length_ref[beam] - jnp.bitwise_and(place, 63) * HD
+        live = (root_ref[group] == jnp.bitwise_and(beam, 7)) & (tokens < count)
         live = jnp.concatenate([live] * HEADS, axis=0)
-        pltpu.make_async_copy(caches[0].at[0], pages.at[lane], arrived.at[lane]).wait()
+        pltpu.make_async_copy(sources[0][0].at[0], pages.at[lane], arrived.at[lane]).wait()
         scores = (
             lax.dot_general(
                 q_ref[group],
@@ -230,6 +240,31 @@
         return carry
 
     lax.fori_loop(0, found, visit, 0)
+
+
+def attend_near(list_ref, count_ref, length_ref, q_ref, root_ref, *rest):
+    wholes = rest[:6]
+    top_ref, sum_ref, hold, pages, arrived = rest[6:]
+    sources = [(whole, base) for whole in wholes for base in (0, SLOTS // 2)]
+    top_ref[...] = jnp.full_like(top_ref, NEGATIVE)
+    sum_ref[...] = jnp.zeros_like(sum_ref)
+    hold[...] = jnp.zeros_like(hold)
+    state = (top_ref, sum_ref, hold)
+    attend(
+        list_ref, count_ref[0], length_ref, q_ref, root_ref, sources, state, pages, arrived
+    )
+
+
+def attend_far(list_ref, count_ref, length_ref, q_ref, root_ref, *rest):
+    parts, before, out_ref, state = rest[:4], rest[4:7], rest[7], rest[8:11]
+    pages, arrived = rest[11:]
+    for ref, start in zip(state, before):
+        ref[...] = start[...]
+    sources = [(part, 0) for part in parts]
+    attend(
+        list_ref, count_ref[1], length_ref, q_ref, root_ref, sources, state, pages, arrived
+    )
+    top_ref, sum_ref, hold = state
     lanes = lax.broadcasted_iota(jnp.int32, (GROUP, HD), 1)
 
     def pack(group, carry):
@@ -316,11 +351,9 @@
     here = (z * XN + x) * CN + core
     groups = ZN * JN
     beams = groups * GROUP
-    half_slots = cache_kv.shape[0] // 2
+    half_slots = SLOTS // 2
     width = PART * groups
 
-    weights = ring(jnp.concatenate([w_query, w_key, w_value], axis=1))
-    turned = ring(w_out.T)
     place = jnp.stack([x, core, lax.axis_index("kv"), z]).astype(jnp.int32)
     vmem = pl.BlockSpec(memory_space=pltpu.VMEM)
     smem = pl.BlockSpec(memory_space=pltpu.SMEM)
@@ -349,6 +382,14 @@
         block_table.reshape(ZN, JN, GROUP * block_table.shape[1]), lead, 1, keepdims=False
     ).reshape(-1)
     spans = lax.dynamic_index_in_dim(lengths.reshape(ZN, JN, GROUP), lead, 1, keepdims=False)
+    spans = spans.reshape(-1)
+    listing = jax.ShapeDtypeStruct((SLOTS * JN,), jnp.int32)
+    near_list, far_list, counts = pl.pallas_call(
+        scan,
+        out_shape=(listing, listing, jax.ShapeDtypeStruct((2,), jnp.int32)),
+        in_specs=[smem] * 3,
+        out_specs=(smem,) * 3,
+    )(place, table, spans)
     root_tiles = lax.dynamic_index_in_dim(
         roots_near.reshape(STEPS, ZN, JN, GROUP), lead, 2, keepdims=False
     )
@@ -367,6 +408,8 @@
     ).astype(jnp.bfloat16)
     gain_rows = jnp.concatenate([gain_rows, jnp.zeros((6, HD), jnp.bfloat16)])
     packed = jnp.concatenate([by_row, jnp.broadcast_to(gain_rows[None], (JN, 8, HD))], axis=1)
+    packed, w_query, w_key, w_value = lax.optimization_barrier((packed, w_query, w_key, w_value))
+    weights = ring(jnp.concatenate([w_query, w_key, w_value], axis=1))
     packed = exchange(packed, XC)
     stream = packed[:, :half].reshape(XN, CN, ZN // 2, SB, 2, PART).transpose(0, 2, 4, 3, 1, 5)
     stream = stream.reshape(XN, rows, 2 * PART).astype(jnp.float32)
@@ -405,34 +448,41 @@
         out_specs=(vmem,) * 4,
         scratch_shapes=[pltpu.VMEM((ROWS, HD), jnp.float32)],
     )(own_parents.reshape(SB), projected, cosines, sines)
-    caches = [cache, left, right, None, None]
-    caches = caches + [swap(part) for part in caches[:3]]
+    queries, cache, left, right = lax.optimization_barrier((queries, cache, left, right))
+    near = [part for whole in (cache, left, right) for part in (whole, swap(whole))]
     last = PAIRS.index((STEPS - 1, 0))
     appended = jnp.stack([key_chain[last:], value_chain[last:]], axis=2)
     appended = appended[:, :, None].astype(jnp.bfloat16)
 
     everyone = exchange(everyone, "z")
-    everyone, across = lax.optimization_barrier((everyone, across))
-    caches[3:5] = across
-    caches = caches + [swap(part) for part in across]
+    everyone, turned = lax.optimization_barrier((everyone, w_out.T))
+    turned = ring(turned)
+    state = (jax.ShapeDtypeStruct((ZN, ROWS, HD), jnp.float32),) * 3
+    ring_buffers = [
+        pltpu.VMEM((DEPTH,) + cache.shape[1:], jnp.bfloat16),
+        pltpu.SemaphoreType.DMA((DEPTH,)),
+    ]
+    anywhere = pl.BlockSpec(memory_space=pl.ANY)
+    before = pl.pallas_call(
+        attend_near,
+        out_shape=state,
+        in_specs=[smem, smem, smem, vmem, vmem] + [anywhere] * 6,
+        out_specs=(vmem,) * 3,
+        scratch_shapes=ring_buffers,
+        cost_estimate=pl.CostEstimate(flops=1, bytes_accessed=1, transcendentals=0),
+    )(near_list, counts, spans, everyone, root_tiles, *near)
+    across, before = lax.optimization_barrier((across, before))
+    across = across + [swap(part) for part in across]
     partial = pl.pallas_call(
-        attention,
+        attend_far,
         out_shape=jax.ShapeDtypeStruct((ZN, BLOCK, HD), jnp.bfloat16),
-        in_specs=[smem, smem, smem, vmem, vmem]
-        + [pl.BlockSpec(memory_space=pl.ANY)] * (2 * SEGMENTS),
+        in_specs=[smem, smem, smem, vmem, vmem] + [anywhere] * 4 + [vmem] * 3,
         out_specs=vmem,
-        scratch_shapes=[
-            pltpu.VMEM((ZN, ROWS, HD), jnp.float32),
-            pltpu.VMEM((ZN, ROWS, HD), jnp.float32),
-            pltpu.VMEM((ZN, ROWS, HD), jnp.float32),
-            pltpu.VMEM((DEPTH,) + cache.shape[1:], jnp.bfloat16),
-            pltpu.SemaphoreType.DMA((DEPTH,)),
-            pltpu.SMEM((2 * half_slots * JN,), jnp.int32),
-            pltpu.SMEM((2 * half_slots * JN,), jnp.int32),
-        ],
-    )(place, table, spans.reshape(-1), everyone, root_tiles, *caches)
+        scratch_shapes=[pltpu.VMEM(part.shape, part.dtype) for part in state] + ring_buffers,
+    )(far_list, counts, spans, everyone, root_tiles, *across, *before)
 
     partial = exchange(partial, "z")
+    partial, turned = lax.optimization_barrier((partial, turned))
     attended = pl.pallas_call(
         finish,
         out_shape=jax.ShapeDtypeStruct((ZN, SB, HEADS * HD), jnp.bfloat16),

time: 210 us -> 208 us (level)
  blocking collectives: 43.5 us -> 19.1 us
  waiting for transfers between devices: 55.5 us -> 67.5 us
  starting transfers between devices: 56.1 us -> 64.1 us
  Pallas kernels: 23.3 us -> 29.7 us
  local copies, waits for them, and re-layouts: 23.5 us -> 20.7 us
    all_to_all x6 -> x7, waiting for transfers between devices: 15.3 us -> 45.8 us  [exchange(): return lax.all_to_all(value, axis, 0, 0, tiled=True)]
    all_to_all x2 -> x1, blocking collectives: 43.5 us -> 19.1 us  [exchange(): return lax.all_to_all(value, axis, 0, 0, tiled=True)]
    ppermute x10, waiting for transfers between devices: 38.8 us -> 16.5 us  [shift(): return lax.ppermute(value, 'x', [(i, (i + hop) % XN) for i in range(XN)])]
    all_to_all x6 -> x7, starting transfers between devices: 30.7 us -> 39.3 us  [exchange(): return lax.all_to_all(value, axis, 0, 0, tiled=True)]
    pallas_call x1 -> x3, Pallas kernels: 11.2 us -> 17.5 us  [the longest x1 6.59 us: body(): pl.pallas_call(attend_far, out_shape=jax.ShapeDtypeStruct((ZN, BLOCK, HD)...]
    ppermute x7, waiting for transfers between devices: 1.43 us -> 5.22 us  [swap(): return lax.ppermute(value, 'core', [(0, 1), (1, 0)])]
    unnamed x35 -> x46, local copies, waits for them, and re-layouts: 7.11 us -> 6.4 us
  transfers between devices with their start and end apart: 23 -> 24, of which waited for: 8 -> 11; matrix products, arithmetic and copies ran while one was open for 11% -> 9% of each run, Pallas kernels for 2% -> 8%
where the time goes in v5:
time: 208 us
  waiting for transfers between devices  67.5 us (32%)
  starting transfers between devices  64.1 us (31%)
  Pallas kernels  29.7 us (14%)
  local copies, waits for them, and re-layouts  20.7 us (10%)
  blocking collectives  19.1 us (9%)
  other arithmetic  5.48 us (3%)
    all_to_all x7, waiting for transfers between devices, exchange(): return lax.all_to_all(value, axis, 0, 0, tiled=True)  45.8 us
    all_to_all x7, starting transfers between devices, exchange(): return lax.all_to_all(value, axis, 0, 0, tiled=True)  39.3 us
    all_to_all x1, blocking collectives, exchange(): return lax.all_to_all(value, axis, 0, 0, tiled=True)  19.1 us
    ppermute x10, waiting for transfers between devices, shift(): return lax.ppermute(value, 'x', [(i, (i + hop) % XN) for i in range(XN)])  16.5 us
    ppermute x10, starting transfers between devices, shift(): return lax.ppermute(value, 'x', [(i, (i + hop) % XN) for i in range(XN)])  13.1 us
    ppermute x7, starting transfers between devices, swap(): return lax.ppermute(value, 'core', [(0, 1), (1, 0)])  11.7 us
    pallas_call x1, Pallas kernels, body(): pl.pallas_call(attend_far, out_shape=jax.ShapeDtypeStruct((ZN, BLOCK, HD)...  6.59 us
    pallas_call x1, Pallas kernels, body(): pl.pallas_call(attend_near, out_shape=state, in_specs=[smem, smem, smem,...  6.49 us
  transfers between devices with their start and end apart: 24, of which 11 were waited for; matrix products, arithmetic and copies ran while one was open for 9% of the time, Pallas kernels for 8%

profile of v5, /device:TPU:1, one launch (start us, length us, event | category | flops | bytes accessed | tf_op | source)
XLA Modules:
  0.0 207.7 jit_solution(7559606855764305371)
XLA Ops:
  1.4 1.1 copy.89
  4.2 3.3 %collective-permute-start = (bf16[64,1280]{1,0:T(8,128)(2,1)S(1)}, bf16[64,1280]{1,0:T(8,128)(2,1)S(1)}, u32[]{:S(2)}, u32[]{:S(2)}) collective-permute-start(bf16[64,1280]{1,0:T(8,128)(2,1)S(1)} %constant_dynamic-update-slice_fusion), channel_id=1, source_target_pairs={{0,1},{1,0},{2,3},{3,2},{4,5},{5,4},{6,7},{7,6},{8,9},{9,8},{10,11... | collective-permute-start | bytes 491528 | tf_op jit(solution)/shard_map/ppermute | solution.py:44
  7.5 3.3 %all-to-all-start = ((bf16[8,104,128]{2,1,0:T(8,128)(2,1)}), bf16[8,104,128]{2,1,0:T(8,128)(2,1)S(1)}, u32[]{:S(2)}, u32[]{:S(2)}) async-start(bf16[8,104,128]{2,1,0:T(8,128)(2,1)} %pad_maximum_fusion.1), calls=%async_computation | async-start | bytes 425984 | tf_op jit(solution)/shard_map/all_to_all | solution.py:36
  11.4 0.8 pad_maximum_fusion.rest_0_
  12.2 1.4 collective-permute-start.1
  13.5 2.4 %collective-permute-start.2 = (bf16[128,1280]{1,0:T(8,128)(2,1)}, bf16[128,1280]{1,0:T(8,128)(2,1)}, u32[]{:S(2)}, u32[]{:S(2)}) collective-permute-start(bf16[128,1280]{1,0:T(8,128)(2,1)} %pad_maximum_fusion.rest_0_), channel_id=1, source_target_pairs={{0,4},{2,6},{4,0},{6,2},{1,5},{3,7},{5,1},{7,3},{8,12},{10,14},{12... | collective-permute-start | bytes 983048 | tf_op jit(solution)/shard_map/ppermute | solution.py:48
  15.9 1.2 collective-permute-start.3
  18.0 2.4 %collective-permute-start.6 = (bf16[32,2,128,128]{3,2,1,0:T(8,128)(2,1)}, bf16[32,2,128,128]{3,2,1,0:T(8,128)(2,1)}, u32[]{:S(2)}, u32[]{:S(2)}) collective-permute-start(bf16[32,2,128,128]{3,2,1,0:T(8,128)(2,1)} %bitcast.50), channel_id=1, source_target_pairs={{0,6},{2,0},{4,2},{6,4},{1,7},{3,1},{5,3},{7,5},{8,14},{10,8},{12,... | collective-permute-start | bytes 6291464 | tf_op jit(solution)/shard_map/ppermute | solution.py:48
  21.0 7.5 %all-to-all-start.1 = ((f32[8,2,128]{2,1,0:T(2,128)}), f32[8,2,128]{2,1,0:T(2,128)S(1)}, u32[]{:S(2)}, u32[]{:S(2)}) async-start(f32[8,2,128]{2,1,0:T(2,128)} %broadcast_in_dim.66), calls=%async_computation.1 | async-start | bytes 16384 | tf_op jit(solution)/shard_map/all_to_all | solution.py:36
  29.1 1.5 copy.91
  30.6 1.6 reshape.169.stream_ref
  32.3 2.8 %all-to-all-done.1 = f32[8,2,128]{2,1,0:T(2,128)S(1)} async-done(((f32[8,2,128]{2,1,0:T(2,128)}), f32[8,2,128]{2,1,0:T(2,128)S(1)}, u32[]{:S(2)}, u32[]{:S(2)}) %all-to-all-start.1) | async-done | bytes 8224 | tf_op jit(solution)/shard_map/all_to_all | solution.py:36
  35.1 0.8 multiply_convert_fusion.rows_ref
  36.0 3.1 %shard_map.114 = f32[192,1280]{1,0:T(8,128)} custom-call(s32[4]{0:T(128)} %pad_add_fusion.place_ref, bf16[4,192,128]{2,1,0:T(8,128)(2,1)} %multiply_convert_fusion.rows_ref, bf16[128,1280]{1,0:T(8,128)(2,1)} %pad_maximum_fusion.rest_0_, bf16[128,1280]{1,0:T(8,128)(2,1)} %collective-permute-done.1.rest_1_, bf16[128,1280]{1,0:T(8,128)(2,1)} %collective-permute-done.2.rest_2_, ...), custom_call_target="tpu_custom_call" | custom-call | tf_op jit(solution)/shard_map/pallas_call | solution.py:429
  39.0 3.8 %all-to-all-start.2 = ((f32[8,24,1280]{2,1,0:T(8,128)}), f32[8,24,1280]{2,1,0:T(8,128)S(1)}, u32[]{:S(2)}, u32[]{:S(2)}) async-start(f32[8,24,1280]{2,1,0:T(8,128)} %bitcast.47), calls=%async_computation.2 | async-start | bytes 1966080 | tf_op jit(solution)/shard_map/all_to_all | solution.py:36
  45.6 22.9 %all-to-all-done.2.parts_ref = f32[8,24,1280]{2,1,0:T(8,128)S(1)} async-done(((f32[8,24,1280]{2,1,0:T(8,128)}), f32[8,24,1280]{2,1,0:T(8,128)S(1)}, u32[]{:S(2)}, u32[]{:S(2)}) %all-to-all-start.2) | async-done | bytes 983072 | tf_op jit(solution)/shard_map/all_to_all | solution.py:36
  68.5 1.0 copy-done.1
  69.5 2.2 %shard_map.115 = (bf16[192,128]{1,0:T(8,128)(2,1)}, bf16[8,192,128]{2,1,0:T(8,128)(2,1)}, f32[6,8,128]{2,1,0:T(8,128)}, f32[6,8,128]{2,1,0:T(8,128)}) custom-call(s32[24]{0:T(128)} %reshape_squeeze.3.parent_ref, f32[8,24,1280]{2,1,0:T(8,128)} %copy-done.1, f32[24,128]{1,0:T(8,128)} %get-tuple-element.95.cos_ref, f32[24,128]{1,0:T(8,128)} %get-tuple-element.96.sin_ref), custom_call_target="tpu_custom_call" | custom-call | tf_op jit(solution)/shard_map/pallas_call | solution.py:439
  71.6 4.3 %collective-permute-done.4.rest_2_ = bf16[32,2,128,128]{3,2,1,0:T(8,128)(2,1)S(1)} collective-permute-done((bf16[32,2,128,128]{3,2,1,0:T(8,128)(2,1)}, bf16[32,2,128,128]{3,2,1,0:T(8,128)(2,1)S(1)}, u32[]{:S(2)}, u32[]{:S(2)}) %collective-permute-start.4) | collective-permute-done | bytes 2097184 | tf_op jit(solution)/shard_map/ppermute | solution.py:48
  75.9 0.8 collective-permute-start.10
  77.2 1.1 slice.62
  78.2 1.2 collective-permute-start.5
  79.4 2.3 %slice.63 = bf16[16,2,128,128]{3,2,1,0:T(8,128)(2,1)} slice(bf16[32,2,128,128]{3,2,1,0:T(8,128)(2,1)} %collective-permute-done.6.rest_4_), slice={[16:32], [0:2], [0:128], [0:128]} | slice | bytes 2097152 | tf_op jit(solution)/shard_map/slice | solution.py:424
  81.7 1.5 collective-permute-start.7
  83.3 7.5 %all-to-all-start.3 = ((bf16[8,192,128]{2,1,0:T(8,128)(2,1)}), bf16[8,192,128]{2,1,0:T(8,128)(2,1)S(1)}, u32[]{:S(2)}, u32[]{:S(2)}) async-start(bf16[8,192,128]{2,1,0:T(8,128)(2,1)} %get-tuple-element.41), calls=%async_computation.3 | async-start | bytes 786432 | tf_op jit(solution)/shard_map/all_to_all | solution.py:36
  93.1 4.4 %shard_map.113 = (s32[256]{0:T(256)}, s32[256]{0:T(256)}, s32[2]{0:T(128)}) custom-call(s32[4]{0:T(128)} %pad_add_fusion.place_ref, s32[4096]{0:T(1024)} %bitcast.61, s32[64]{0:T(128)} %reshape.157.length_ref), custom_call_target="tpu_custom_call" | custom-call | tf_op jit(solution)/shard_map/pallas_call | solution.py:387
  97.5 7.6 %all-to-all-done.3.q_ref = bf16[8,192,128]{2,1,0:T(8,128)(2,1)S(1)} async-done(((bf16[8,192,128]{2,1,0:T(8,128)(2,1)}), bf16[8,192,128]{2,1,0:T(8,128)(2,1)S(1)}, u32[]{:S(2)}, u32[]{:S(2)}) %all-to-all-start.3) | async-done | bytes 393248 | tf_op jit(solution)/shard_map/all_to_all | solution.py:36
  105.9 6.5 %shard_map.116 = (f32[8,192,128]{2,1,0:T(8,128)}, f32[8,192,128]{2,1,0:T(8,128)}, f32[8,192,128]{2,1,0:T(8,128)}) custom-call(s32[256]{0:T(256)} %get-tuple-element.44.list_ref, s32[2]{0:T(128)} %get-tuple-element.35.count_ref, s32[64]{0:T(128)} %reshape.157.length_ref, bf16[8,192,128]{2,1,0:T(8,128)(2,1)} %copy-done.2, ...), custom_call_target="tpu_custom_call" | custom-call | flops 1 | bytes 1 | tf_op jit(solution)/shard_map/pallas_call | solution.py:466
  112.4 6.9 %collective-permute-start.11 = (bf16[16,2,128,128]{3,2,1,0:T(8,128)(2,1)}, bf16[16,2,128,128]{3,2,1,0:T(8,128)(2,1)S(1)}, u32[]{:S(2)}, u32[]{:S(2)}) collective-permute-start(bf16[16,2,128,128]{3,2,1,0:T(8,128)(2,1)} %collective-permute-done.5.rest_0_), channel_id=1, source_target_pairs={{0,1},{1,0},{2,3},{3,2},{4,5},{5,4},{6,7},{7,6},{8,9},{9,8},{10,11... | collective-permute-start | bytes 3145736 | tf_op jit(solution)/shard_map/ppermute | solution.py:44
  119.4 2.4 %collective-permute-done.11.rest_2_ = bf16[16,2,128,128]{3,2,1,0:T(8,128)(2,1)S(1)} collective-permute-done((bf16[16,2,128,128]{3,2,1,0:T(8,128)(2,1)}, bf16[16,2,128,128]{3,2,1,0:T(8,128)(2,1)S(1)}, u32[]{:S(2)}, u32[]{:S(2)}) %collective-permute-start.11) | collective-permute-done | bytes 1048608 | tf_op jit(solution)/shard_map/ppermute | solution.py:44
  121.8 1.5 collective-permute-done.12.rest_3_
  123.3 1.0 copy-done.7
  124.3 6.6 %shard_map.117 = bf16[8,216,128]{2,1,0:T(8,128)(2,1)} custom-call(s32[256]{0:T(256)} %get-tuple-element.34.list_ref, s32[2]{0:T(128)} %get-tuple-element.35.count_ref, s32[64]{0:T(128)} %reshape.157.length_ref, bf16[8,192,128]{2,1,0:T(8,128)(2,1)} %copy-done.2, s32[8,24,128]{2,1,0:T(8,128)} %broadcast_in_dim.75.root_ref, ...), custom_call_target="tpu_custom_call" | custom-call | tf_op jit(solution)/shard_map/pallas_call | solution.py:476
  130.9 3.5 %all-to-all-start.4 = ((bf16[8,216,128]{2,1,0:T(8,128)(2,1)}), bf16[8,216,128]{2,1,0:T(8,128)(2,1)S(1)}, u32[]{:S(2)}, u32[]{:S(2)}) async-start(bf16[8,216,128]{2,1,0:T(8,128)(2,1)} %shard_map.117), calls=%async_computation.4 | async-start | bytes 884736 | tf_op jit(solution)/shard_map/all_to_all | solution.py:36
  134.5 1.3 collective-permute-done.13
  136.1 2.6 %collective-permute-start.16 = (bf16[128,1024]{1,0:T(8,128)(2,1)S(1)}, bf16[128,1024]{1,0:T(8,128)(2,1)S(1)}, u32[]{:S(2)}, u32[]{:S(2)}) collective-permute-start(bf16[128,1024]{1,0:T(8,128)(2,1)S(1)} %constant_dynamic-update-slice_fusion.3.rest_0_), channel_id=1, source_target_pairs={{0,6},{2,0},{4,2},{6,4},{1,7},{3,1},{5,3},{7,5},{8,14},{10,8},{12,... | collective-permute-start | bytes 786440 | tf_op jit(solution)/shard_map/ppermute | solution.py:48
  138.6 12.0 %collective-permute-done.14.rest_1_ = bf16[128,1024]{1,0:T(8,128)(2,1)S(1)} collective-permute-done((bf16[128,1024]{1,0:T(8,128)(2,1)S(1)}, bf16[128,1024]{1,0:T(8,128)(2,1)S(1)}, u32[]{:S(2)}, u32[]{:S(2)}) %collective-permute-start.14) | collective-permute-done | bytes 262176 | tf_op jit(solution)/shard_map/ppermute | solution.py:48
  150.8 0.8 copy-done.4
  151.6 2.3 %shard_map.118 = bf16[8,24,1024]{2,1,0:T(8,128)(2,1)} custom-call(bf16[8,216,128]{2,1,0:T(8,128)(2,1)} %copy-done.4, bf16[192,128]{1,0:T(8,128)(2,1)} %get-tuple-element.59.q_ref, f32[6,8,128]{2,1,0:T(8,128)} %get-tuple-element.60.k_ref, f32[6,8,128]{2,1,0:T(8,128)} %get-tuple-element.61.v_ref), custom_call_target="tpu_custom_call" | custom-call | tf_op jit(solution)/shard_map/pallas_call | solution.py:486
  154.0 19.1 %all_to_all.40 = bf16[8,24,1024]{2,1,0:T(8,128)(2,1)} all-to-all(bf16[8,24,1024]{2,1,0:T(8,128)(2,1)} %shard_map.118), channel_id=1, replica_groups=mesh['kv'=4,'z'=8,'x'=4,'core'=2] {'z'}, dimensions={0} | all-to-all | bytes 786432 | tf_op jit(solution)/shard_map/all_to_all | solution.py:36
  173.1 2.7 %shard_map.119 = f32[4,4,48,128]{3,2,1,0:T(8,128)} custom-call(s32[4]{0:T(128)} %pad_add_fusion.place_ref, bf16[192,1024]{1,0:T(8,128)(2,1)} %bitcast.56, bf16[128,1024]{1,0:T(8,128)(2,1)} %copy-done.8, bf16[128,1024]{1,0:T(8,128)(2,1)} %copy-done.9, bf16[128,1024]{1,0:T(8,128)(2,1)} %copy-done.10, bf16[128,1024]{1,0:T(8,128)(2,1)} %copy-done.11), custom_call_target="tpu_custom_call" | custom-call | tf_op jit(solution)/shard_map/pallas_call | solution.py:495
  175.8 4.2 %all-to-all-start.6 = ((f32[4,4,48,128]{3,2,1,0:T(8,128)}), f32[4,4,48,128]{3,2,1,0:T(8,128)S(1)}, u32[]{:S(2)}, u32[]{:S(2)}) async-start(f32[4,4,48,128]{3,2,1,0:T(8,128)} %shard_map.119), calls=%async_computation.6 | async-start | bytes 786432 | tf_op jit(solution)/shard_map/all_to_all | solution.py:36
  180.7 5.5 %all-to-all-done.6.parts_ref = f32[4,4,48,128]{3,2,1,0:T(8,128)S(1)} async-done(((f32[4,4,48,128]{3,2,1,0:T(8,128)}), f32[4,4,48,128]{3,2,1,0:T(8,128)S(1)}, u32[]{:S(2)}, u32[]{:S(2)}) %all-to-all-start.6) | async-done | bytes 393248 | tf_op jit(solution)/shard_map/all_to_all | solution.py:36
  186.3 0.8 copy-done.5
  187.0 1.9 shard_map.120
  188.9 9.4 %all-to-all-start.7 = ((bf16[32,24,128]{2,1,0:T(8,128)(2,1)}), bf16[32,24,128]{2,1,0:T(8,128)(2,1)S(1)}, u32[]{:S(2)}, u32[]{:S(2)}) async-start(bf16[32,24,128]{2,1,0:T(8,128)(2,1)} %bitcast.57), calls=%async_computation.7 | async-start | bytes 393216 | tf_op jit(solution)/shard_map/all_to_all | solution.py:36
  199.7 6.9 %all-to-all-done.7 = bf16[32,24,128]{2,1,0:T(8,128)(2,1)S(1)} async-done(((bf16[32,24,128]{2,1,0:T(8,128)(2,1)}), bf16[32,24,128]{2,1,0:T(8,128)(2,1)S(1)}, u32[]{:S(2)}, u32[]{:S(2)}) %all-to-all-start.7) | async-done | bytes 196640 | tf_op jit(solution)/shard_map/all_to_all | solution.py:36
  206.9 0.8 copy.102
  (123 shorter events, 14.1 us)
Async XLA Ops:
  0.6 3.5 %copy-start.13 = (bf16[64,1024]{1,0:T(8,128)(2,1)S(1)}, bf16[64,1024]{1,0:T(8,128)(2,1)}, u32[]{:S(2)}) copy-start(bf16[64,1024]{1,0:T(8,128)(2,1)} %param.12) | copy-start | bytes 393220
  0.6 3.5 %copy-start.15 = (bf16[64,128]{1,0:T(8,128)(2,1)S(1)}, bf16[64,128]{1,0:T(8,128)(2,1)}, u32[]{:S(2)}) copy-start(bf16[64,128]{1,0:T(8,128)(2,1)} %param.13) | copy-start | bytes 49156
  0.7 3.5 %copy-start.16 = (bf16[64,128]{1,0:T(8,128)(2,1)S(1)}, bf16[64,128]{1,0:T(8,128)(2,1)}, u32[]{:S(2)}) copy-start(bf16[64,128]{1,0:T(8,128)(2,1)} %param.14) | copy-start | bytes 49156
  4.2 7.2 %collective-permute-start = (bf16[64,1280]{1,0:T(8,128)(2,1)S(1)}, bf16[64,1280]{1,0:T(8,128)(2,1)S(1)}, u32[]{:S(2)}, u32[]{:S(2)}) collective-permute-start(bf16[64,1280]{1,0:T(8,128)(2,1)S(1)} %constant_dynamic-update-slice_fusion), channel_id=1, source_target_pairs={{0,1},{1,0},{2,3},{3,2},{4,5},{5,4},{6,7},{7,6},{8,9},{9,8},{10,11... | collective-permute-start | bytes 491528 | tf_op jit(solution)/shard_map/ppermute | solution.py:44
  7.5 9.6 %all-to-all-start = ((bf16[8,104,128]{2,1,0:T(8,128)(2,1)}), bf16[8,104,128]{2,1,0:T(8,128)(2,1)S(1)}, u32[]{:S(2)}, u32[]{:S(2)}) async-start(bf16[8,104,128]{2,1,0:T(8,128)(2,1)} %pad_maximum_fusion.1), calls=%async_computation | async-start | bytes 425984 | tf_op jit(solution)/shard_map/all_to_all | solution.py:36
  12.2 23.8 %collective-permute-start.1 = (bf16[128,1280]{1,0:T(8,128)(2,1)}, bf16[128,1280]{1,0:T(8,128)(2,1)}, u32[]{:S(2)}, u32[]{:S(2)}) collective-permute-start(bf16[128,1280]{1,0:T(8,128)(2,1)} %pad_maximum_fusion.rest_0_), channel_id=1, source_target_pairs={{0,2},{2,4},{4,6},{6,0},{1,3},{3,5},{5,7},{7,1},{8,10},{10,12},{12... | collective-permute-start | bytes 983048 | tf_op jit(solution)/shard_map/ppermute | solution.py:48
  13.5 22.4 %collective-permute-start.2 = (bf16[128,1280]{1,0:T(8,128)(2,1)}, bf16[128,1280]{1,0:T(8,128)(2,1)}, u32[]{:S(2)}, u32[]{:S(2)}) collective-permute-start(bf16[128,1280]{1,0:T(8,128)(2,1)} %pad_maximum_fusion.rest_0_), channel_id=1, source_target_pairs={{0,4},{2,6},{4,0},{6,2},{1,5},{3,7},{5,1},{7,3},{8,12},{10,14},{12... | collective-permute-start | bytes 983048 | tf_op jit(solution)/shard_map/ppermute | solution.py:48
  15.9 20.0 %collective-permute-start.3 = (bf16[128,1280]{1,0:T(8,128)(2,1)}, bf16[128,1280]{1,0:T(8,128)(2,1)}, u32[]{:S(2)}, u32[]{:S(2)}) collective-permute-start(bf16[128,1280]{1,0:T(8,128)(2,1)} %pad_maximum_fusion.rest_0_), channel_id=1, source_target_pairs={{0,6},{2,0},{4,2},{6,4},{1,7},{3,1},{5,3},{7,5},{8,14},{10,8},{12,... | collective-permute-start | bytes 983048 | tf_op jit(solution)/shard_map/ppermute | solution.py:48
  17.7 58.2 %collective-permute-start.4 = (bf16[32,2,128,128]{3,2,1,0:T(8,128)(2,1)}, bf16[32,2,128,128]{3,2,1,0:T(8,128)(2,1)S(1)}, u32[]{:S(2)}, u32[]{:S(2)}) collective-permute-start(bf16[32,2,128,128]{3,2,1,0:T(8,128)(2,1)} %bitcast.49), channel_id=1, source_target_pairs={{0,2},{2,4},{4,6},{6,0},{1,3},{3,5},{5,7},{7,1},{8,10},{10,12},{12... | collective-permute-start | bytes 6291464 | tf_op jit(solution)/shard_map/ppermute | solution.py:48
  18.0 57.9 %collective-permute-start.6 = (bf16[32,2,128,128]{3,2,1,0:T(8,128)(2,1)}, bf16[32,2,128,128]{3,2,1,0:T(8,128)(2,1)}, u32[]{:S(2)}, u32[]{:S(2)}) collective-permute-start(bf16[32,2,128,128]{3,2,1,0:T(8,128)(2,1)} %bitcast.50), channel_id=1, source_target_pairs={{0,6},{2,0},{4,2},{6,4},{1,7},{3,1},{5,3},{7,5},{8,14},{10,8},{12,... | collective-permute-start | bytes 6291464 | tf_op jit(solution)/shard_map/ppermute | solution.py:48
  21.0 14.1 %all-to-all-start.1 = ((f32[8,2,128]{2,1,0:T(2,128)}), f32[8,2,128]{2,1,0:T(2,128)S(1)}, u32[]{:S(2)}, u32[]{:S(2)}) async-start(f32[8,2,128]{2,1,0:T(2,128)} %broadcast_in_dim.66), calls=%async_computation.1 | async-start | bytes 16384 | tf_op jit(solution)/shard_map/all_to_all | solution.py:36
  32.2 6.8 %copy-start.3 = (f32[4,192,128]{2,1,0:T(8,128)}, f32[4,192,128]{2,1,0:T(8,128)S(1)}, u32[]{:S(2)}) copy-start(f32[4,192,128]{2,1,0:T(8,128)S(1)} %reshape.169.stream_ref) | copy-start | bytes 1179652
  35.9 6.9 %copy-start.18 = (s32[3,512]{1,0:T(4,128)S(1)}, s32[3,512]{1,0:T(4,128)}, u32[]{:S(2)}) copy-start(s32[3,512]{1,0:T(4,128)} %param.19) | copy-start | bytes 18436
  35.9 7.4 %copy-start.17 = (s32[512]{0:T(512)S(1)}, s32[512]{0:T(512)}, u32[]{:S(2)}) copy-start(s32[512]{0:T(512)} %param.17) | copy-start | bytes 6148
  39.0 29.5 %all-to-all-start.2 = ((f32[8,24,1280]{2,1,0:T(8,128)}), f32[8,24,1280]{2,1,0:T(8,128)S(1)}, u32[]{:S(2)}, u32[]{:S(2)}) async-start(f32[8,24,1280]{2,1,0:T(8,128)} %bitcast.47), calls=%async_computation.2 | async-start | bytes 1966080 | tf_op jit(solution)/shard_map/all_to_all | solution.py:36
  68.5 1.0 copy-start.1
  75.9 5.9 %copy-start = (bf16[32,2,128,128]{3,2,1,0:T(8,128)(2,1)}, bf16[32,2,128,128]{3,2,1,0:T(8,128)(2,1)S(1)}, u32[]{:S(2)}) copy-start(bf16[32,2,128,128]{3,2,1,0:T(8,128)(2,1)S(1)} %collective-permute-done.4.rest_2_) | copy-start | bytes 6291460
  75.9 15.8 %copy-start.12 = (s32[512,64]{0,1:T(8,128)S(1)}, s32[512,64]{0,1:T(8,128)}, u32[]{:S(2)}) copy-start(s32[512,64]{0,1:T(8,128)} %param.18) | copy-start | bytes 393220
  75.9 29.3 %collective-permute-start.10 = (bf16[32,2,128,128]{3,2,1,0:T(8,128)(2,1)}, bf16[32,2,128,128]{3,2,1,0:T(8,128)(2,1)}, u32[]{:S(2)}, u32[]{:S(2)}) collective-permute-start(bf16[32,2,128,128]{3,2,1,0:T(8,128)(2,1)} %collective-permute-done.6.rest_4_), channel_id=1, source_target_pairs={{0,1},{1,0},{2,3},{3,2},{4,5},{5,4},{6,7},{7,6},{8,9},{9,8},{10,11... | collective-permute-start | bytes 6291464 | tf_op jit(solution)/shard_map/ppermute | solution.py:44
  76.6 28.5 %collective-permute-start.8 = (bf16[32,2,128,128]{3,2,1,0:T(8,128)(2,1)}, bf16[32,2,128,128]{3,2,1,0:T(8,128)(2,1)}, u32[]{:S(2)}, u32[]{:S(2)}) collective-permute-start(bf16[32,2,128,128]{3,2,1,0:T(8,128)(2,1)} %bitcast.51), channel_id=1, source_target_pairs={{0,1},{1,0},{2,3},{3,2},{4,5},{5,4},{6,7},{7,6},{8,9},{9,8},{10,11... | collective-permute-start | bytes 6291464 | tf_op jit(solution)/shard_map/ppermute | solution.py:44
  76.7 28.4 %collective-permute-start.9 = (bf16[32,2,128,128]{3,2,1,0:T(8,128)(2,1)S(1)}, bf16[32,2,128,128]{3,2,1,0:T(8,128)(2,1)}, u32[]{:S(2)}, u32[]{:S(2)}) collective-permute-start(bf16[32,2,128,128]{3,2,1,0:T(8,128)(2,1)S(1)} %collective-permute-done.4.rest_2_), channel_id=1, source_target_pairs={{0,1},{1,0},{2,3},{3,2},{4,5},{5,4},{6,7},{7,6},{8,9},{9,8},{10,11... | collective-permute-start | bytes 6291464 | tf_op jit(solution)/shard_map/ppermute | solution.py:44
  78.2 34.2 %collective-permute-start.5 = (bf16[16,2,128,128]{3,2,1,0:T(8,128)(2,1)}, bf16[16,2,128,128]{3,2,1,0:T(8,128)(2,1)}, u32[]{:S(2)}, u32[]{:S(2)}) collective-permute-start(bf16[16,2,128,128]{3,2,1,0:T(8,128)(2,1)} %slice.62), channel_id=1, source_target_pairs={{0,2},{2,4},{4,6},{6,0},{1,3},{3,5},{5,7},{7,1},{8,10},{10,12},{12... | collective-permute-start | bytes 3145736 | tf_op jit(solution)/shard_map/ppermute | solution.py:48
  81.7 30.7 %collective-permute-start.7 = (bf16[16,2,128,128]{3,2,1,0:T(8,128)(2,1)}, bf16[16,2,128,128]{3,2,1,0:T(8,128)(2,1)}, u32[]{:S(2)}, u32[]{:S(2)}) collective-permute-start(bf16[16,2,128,128]{3,2,1,0:T(8,128)(2,1)} %slice.63), channel_id=1, source_target_pairs={{0,6},{2,0},{4,2},{6,4},{1,7},{3,1},{5,3},{7,5},{8,14},{10,8},{12,... | collective-permute-start | bytes 3145736 | tf_op jit(solution)/shard_map/ppermute | solution.py:48
  83.3 21.9 %all-to-all-start.3 = ((bf16[8,192,128]{2,1,0:T(8,128)(2,1)}), bf16[8,192,128]{2,1,0:T(8,128)(2,1)S(1)}, u32[]{:S(2)}, u32[]{:S(2)}) async-start(bf16[8,192,128]{2,1,0:T(8,128)(2,1)} %get-tuple-element.41), calls=%async_computation.3 | async-start | bytes 786432 | tf_op jit(solution)/shard_map/all_to_all | solution.py:36
  105.1 0.8 copy-start.2
  112.4 9.4 %collective-permute-start.11 = (bf16[16,2,128,128]{3,2,1,0:T(8,128)(2,1)}, bf16[16,2,128,128]{3,2,1,0:T(8,128)(2,1)S(1)}, u32[]{:S(2)}, u32[]{:S(2)}) collective-permute-start(bf16[16,2,128,128]{3,2,1,0:T(8,128)(2,1)} %collective-permute-done.5.rest_0_), channel_id=1, source_target_pairs={{0,1},{1,0},{2,3},{3,2},{4,5},{5,4},{6,7},{7,6},{8,9},{9,8},{10,11... | collective-permute-start | bytes 3145736 | tf_op jit(solution)/shard_map/ppermute | solution.py:44
  119.3 4.0 %collective-permute-start.12 = (bf16[16,2,128,128]{3,2,1,0:T(8,128)(2,1)}, bf16[16,2,128,128]{3,2,1,0:T(8,128)(2,1)S(1)}, u32[]{:S(2)}, u32[]{:S(2)}) collective-permute-start(bf16[16,2,128,128]{3,2,1,0:T(8,128)(2,1)} %collective-permute-done.7.rest_1_), channel_id=1, source_target_pairs={{0,1},{1,0},{2,3},{3,2},{4,5},{5,4},{6,7},{7,6},{8,9},{9,8},{10,11... | collective-permute-start | bytes 3145736 | tf_op jit(solution)/shard_map/ppermute | solution.py:44
  121.8 1.5 copy-start.6
  123.3 1.0 copy-start.7
  124.3 10.1 %copy-start.14 = (bf16[1024,64]{0,1:T(8,128)(2,1)S(1)}, bf16[1024,64]{0,1:T(8,128)(2,1)}, u32[]{:S(2)}) copy-start(bf16[1024,64]{0,1:T(8,128)(2,1)} %param.15) | copy-start | bytes 393220
  130.9 19.9 %all-to-all-start.4 = ((bf16[8,216,128]{2,1,0:T(8,128)(2,1)}), bf16[8,216,128]{2,1,0:T(8,128)(2,1)S(1)}, u32[]{:S(2)}, u32[]{:S(2)}) async-start(bf16[8,216,128]{2,1,0:T(8,128)(2,1)} %shard_map.117), calls=%async_computation.4 | async-start | bytes 884736 | tf_op jit(solution)/shard_map/all_to_all | solution.py:36
  134.4 1.4 collective-permute-start.13
  135.8 37.2 %copy-start.8 = (bf16[128,1024]{1,0:T(8,128)(2,1)}, bf16[128,1024]{1,0:T(8,128)(2,1)S(1)}, u32[]{:S(2)}) copy-start(bf16[128,1024]{1,0:T(8,128)(2,1)S(1)} %constant_dynamic-update-slice_fusion.3.rest_0_) | copy-start | bytes 786436
  135.9 14.8 %collective-permute-start.14 = (bf16[128,1024]{1,0:T(8,128)(2,1)S(1)}, bf16[128,1024]{1,0:T(8,128)(2,1)S(1)}, u32[]{:S(2)}, u32[]{:S(2)}) collective-permute-start(bf16[128,1024]{1,0:T(8,128)(2,1)S(1)} %constant_dynamic-update-slice_fusion.3.rest_0_), channel_id=1, source_target_pairs={{0,2},{2,4},{4,6},{6,0},{1,3},{3,5},{5,7},{7,1},{8,10},{10,12},{12... | collective-permute-start | bytes 786440 | tf_op jit(solution)/shard_map/ppermute | solution.py:48
  136.0 14.7 %collective-permute-start.15 = (bf16[128,1024]{1,0:T(8,128)(2,1)S(1)}, bf16[128,1024]{1,0:T(8,128)(2,1)S(1)}, u32[]{:S(2)}, u32[]{:S(2)}) collective-permute-start(bf16[128,1024]{1,0:T(8,128)(2,1)S(1)} %constant_dynamic-update-slice_fusion.3.rest_0_), channel_id=1, source_target_pairs={{0,4},{2,6},{4,0},{6,2},{1,5},{3,7},{5,1},{7,3},{8,12},{10,14},{12... | collective-permute-start | bytes 786440 | tf_op jit(solution)/shard_map/ppermute | solution.py:48
  136.1 14.8 %collective-permute-start.16 = (bf16[128,1024]{1,0:T(8,128)(2,1)S(1)}, bf16[128,1024]{1,0:T(8,128)(2,1)S(1)}, u32[]{:S(2)}, u32[]{:S(2)}) collective-permute-start(bf16[128,1024]{1,0:T(8,128)(2,1)S(1)} %constant_dynamic-update-slice_fusion.3.rest_0_), channel_id=1, source_target_pairs={{0,6},{2,0},{4,2},{6,4},{1,7},{3,1},{5,3},{7,5},{8,14},{10,8},{12,... | collective-permute-start | bytes 786440 | tf_op jit(solution)/shard_map/ppermute | solution.py:48
  150.7 22.4 %copy-start.9 = (bf16[128,1024]{1,0:T(8,128)(2,1)}, bf16[128,1024]{1,0:T(8,128)(2,1)S(1)}, u32[]{:S(2)}) copy-start(bf16[128,1024]{1,0:T(8,128)(2,1)S(1)} %collective-permute-done.14.rest_1_) | copy-start | bytes 786436
  150.7 22.4 %copy-start.10 = (bf16[128,1024]{1,0:T(8,128)(2,1)}, bf16[128,1024]{1,0:T(8,128)(2,1)S(1)}, u32[]{:S(2)}) copy-start(bf16[128,1024]{1,0:T(8,128)(2,1)S(1)} %collective-permute-done.15.rest_2_) | copy-start | bytes 786436
  150.8 22.3 %copy-start.11 = (bf16[128,1024]{1,0:T(8,128)(2,1)}, bf16[128,1024]{1,0:T(8,128)(2,1)S(1)}, u32[]{:S(2)}) copy-start(bf16[128,1024]{1,0:T(8,128)(2,1)S(1)} %collective-permute-done.16.rest_3_) | copy-start | bytes 786436
  150.8 0.8 copy-start.4
  175.8 10.4 %all-to-all-start.6 = ((f32[4,4,48,128]{3,2,1,0:T(8,128)}), f32[4,4,48,128]{3,2,1,0:T(8,128)S(1)}, u32[]{:S(2)}, u32[]{:S(2)}) async-start(f32[4,4,48,128]{3,2,1,0:T(8,128)} %shard_map.119), calls=%async_computation.6 | async-start | bytes 786432 | tf_op jit(solution)/shard_map/all_to_all | solution.py:36
  186.3 0.8 copy-start.5
  188.9 17.7 %all-to-all-start.7 = ((bf16[32,24,128]{2,1,0:T(8,128)(2,1)}), bf16[32,24,128]{2,1,0:T(8,128)(2,1)S(1)}, u32[]{:S(2)}, u32[]{:S(2)}) async-start(bf16[32,24,128]{2,1,0:T(8,128)(2,1)} %bitcast.57), calls=%async_computation.7 | async-start | bytes 393216 | tf_op jit(solution)/shard_map/all_to_all | solution.py:36

commit v6 on v5

--- a/solution.py
+++ b/solution.py
@@ -26,6 +26,7 @@
 SLOTS = 32
 DEPTH = 12
 QUARTER = ZN * SB // KN
+SMALL = pltpu.CompilerParams(vmem_limit_bytes=16 << 20)
 PAIRS = [(s, u) for s in range(STEPS) for u in range(s + 1)]
 SCALE = 1.0 / math.sqrt(HD)
 XC = ("x", "core")
@@ -49,20 +50,18 @@
 
 
 def ring(value):
-    both = jnp.concatenate([value, swap(value)], axis=0)
-    return [both] + [shift(both, hop) for hop in range(1, XN)]
+    return [value] + [shift(value, hop) for hop in range(1, XN)]
 
 
 def join(place_ref, chunks, wide):
     core = place_ref[1]
     for hop in range(XN):
-        for side, start in ((0, core * PART), (1, (1 - core) * PART)):
-            rows = pl.ds(pl.multiple_of(start, PART), PART)
-            wide[hop, rows, :] = chunks[hop][side * PART : (side + 1) * PART, :]
+        wide[hop, pl.ds(pl.multiple_of(core * PART, PART), PART), :] = chunks[hop][...]
+        wide[hop, pl.ds(pl.multiple_of((1 - core) * PART, PART), PART), :] = chunks[XN + hop][...]
 
 
 def project(place_ref, rows_ref, *rest):
-    chunks, out_ref, wide = rest[:XN], rest[XN], rest[XN + 1]
+    chunks, out_ref, wide = rest[: 2 * XN], rest[2 * XN], rest[2 * XN + 1]
     join(place_ref, chunks, wide)
     x = place_ref[0]
     for start in range(0, out_ref.shape[1], 256):
@@ -77,27 +76,30 @@
 
 
 def deliver(place_ref, rows_ref, *rest):
-    chunks, out_ref, wide = rest[:XN], rest[XN], rest[XN + 1]
+    chunks, outs, wide = rest[: 2 * XN], rest[2 * XN : 2 * XN + KN], rest[2 * XN + KN]
+    hold = rest[2 * XN + KN + 1]
     join(place_ref, chunks, wide)
-    x = place_ref[0]
+    x, kv = place_ref[0], place_ref[2]
     for hop in range(XN):
-        result = lax.dot_general(
+        hold[...] = lax.dot_general(
             rows_ref[...],
             wide[hop],
             (((1,), (1,)), ((), ())),
             preferred_element_type=jnp.float32,
         )
-        for kv in range(KN):
-            out_ref[kv, (x + XN - hop) % XN] = result[kv * QUARTER : (kv + 1) * QUARTER]
-
-
-def settle(place_ref, parts_ref, stream_ref, out_ref):
+        for far in range(KN):
+            start = pl.multiple_of(lax.rem(kv + far, KN) * QUARTER, 8)
+            outs[far][lax.rem(x + XN - hop, XN)] = hold[pl.ds(start, QUARTER), :]
+
+
+def settle(place_ref, *rest):
+    parts, stream_ref, out_ref = rest[:KN], rest[KN], rest[KN + 1]
     kv = place_ref[2]
     lanes = lax.broadcasted_iota(jnp.int32, (SB, 2 * PART), 1)
     for x in range(XN):
-        total = parts_ref[0, x]
-        for source in range(1, KN):
-            total = total + parts_ref[source, x]
+        total = parts[0][x]
+        for part in parts[1:]:
+            total = total + part[x]
         total = stream_ref[x, pl.ds(pl.multiple_of(kv * QUARTER, 8), QUARTER), :] + total
         upper, lower = total[:SB], total[SB:]
         first = jnp.where(lanes < PART, upper, pltpu.roll(lower, PART, 1)).astype(jnp.bfloat16)
@@ -386,6 +388,7 @@
     listing = jax.ShapeDtypeStruct((SLOTS * JN,), jnp.int32)
     near_list, far_list, counts = pl.pallas_call(
         scan,
+        compiler_params=SMALL,
         out_shape=(listing, listing, jax.ShapeDtypeStruct((2,), jnp.int32)),
         in_specs=[smem] * 3,
         out_specs=(smem,) * 3,
@@ -394,7 +397,6 @@
         roots_near.reshape(STEPS, ZN, JN, GROUP), lead, 2, keepdims=False
     )
     root_tiles = root_tiles.transpose(1, 0, 2).reshape(ZN, SB)
-    root_tiles = jnp.broadcast_to(root_tiles[:, :, None], (ZN, SB, HD))
 
     rows = ZN * SB
     half = rows // 2
@@ -408,9 +410,15 @@
     ).astype(jnp.bfloat16)
     gain_rows = jnp.concatenate([gain_rows, jnp.zeros((6, HD), jnp.bfloat16)])
     packed = jnp.concatenate([by_row, jnp.broadcast_to(gain_rows[None], (JN, 8, HD))], axis=1)
-    packed, w_query, w_key, w_value = lax.optimization_barrier((packed, w_query, w_key, w_value))
-    weights = ring(jnp.concatenate([w_query, w_key, w_value], axis=1))
+    weights = jnp.concatenate([w_query, w_key, w_value], axis=1)
+    cache, weights = lax.optimization_barrier((cache, weights))
+    weights = ring(weights)
+    left = shift(cache, 1)
+    right = shift(cache, -1)
+    across = [shift(left[:half_slots], 1), shift(right[half_slots:], -1)]
     packed = exchange(packed, XC)
+    packed, weights = lax.optimization_barrier((packed, weights))
+    weights = weights + [swap(part) for part in weights]
     stream = packed[:, :half].reshape(XN, CN, ZN // 2, SB, 2, PART).transpose(0, 2, 4, 3, 1, 5)
     stream = stream.reshape(XN, rows, 2 * PART).astype(jnp.float32)
     tails = packed[:, half : half + 2].astype(jnp.float32)
@@ -418,26 +426,25 @@
     gain = gain.reshape(XN, 1, 2 * PART)
     squares = jnp.sum(stream * stream, axis=(0, 2))
     squares = jnp.pad(squares, (0, 256 - rows)).reshape(2, 128)
-    cache, squares = lax.optimization_barrier((cache, squares))
-    left = shift(cache, 1)
-    right = shift(cache, -1)
-    across = [shift(left[:half_slots], 1), shift(right[half_slots:], -1)]
     squares = jnp.sum(spread(squares, "z", ZN), axis=0).reshape(256)[:rows]
     inverse = lax.rsqrt(squares / width + EPSILON)
     normed = (stream * inverse[None, :, None] * gain).astype(jnp.bfloat16)
     columns = weights[0].shape[1]
     projected = pl.pallas_call(
         project,
+        compiler_params=SMALL,
         out_shape=jax.ShapeDtypeStruct((rows, columns), jnp.float32),
-        in_specs=[smem] + [vmem] * (1 + XN),
+        in_specs=[smem] + [vmem] * (1 + 2 * XN),
         out_specs=vmem,
         scratch_shapes=[pltpu.VMEM((XN, 2 * PART, columns), jnp.bfloat16)],
     )(place, normed, *weights)
     projected = exchange(projected.reshape(ZN, SB, columns), "z")
+    projected, near_list = lax.optimization_barrier((projected, near_list))
 
     small = jax.ShapeDtypeStruct((len(PAIRS), GROUP, HD), jnp.float32)
     queries, everyone, key_chain, value_chain = pl.pallas_call(
         after_projection,
+        compiler_params=SMALL,
         out_shape=(
             jax.ShapeDtypeStruct((ROWS, HD), jnp.bfloat16),
             jax.ShapeDtypeStruct((ZN, ROWS, HD), jnp.bfloat16),
@@ -448,15 +455,17 @@
         out_specs=(vmem,) * 4,
         scratch_shapes=[pltpu.VMEM((ROWS, HD), jnp.float32)],
     )(own_parents.reshape(SB), projected, cosines, sines)
-    queries, cache, left, right = lax.optimization_barrier((queries, cache, left, right))
+    root_tiles = jnp.broadcast_to(root_tiles[:, :, None], (ZN, SB, HD))
     near = [part for whole in (cache, left, right) for part in (whole, swap(whole))]
     last = PAIRS.index((STEPS - 1, 0))
     appended = jnp.stack([key_chain[last:], value_chain[last:]], axis=2)
     appended = appended[:, :, None].astype(jnp.bfloat16)
 
     everyone = exchange(everyone, "z")
-    everyone, turned = lax.optimization_barrier((everyone, w_out.T))
+    everyone, turned, across = lax.optimization_barrier((everyone, w_out.T, across))
+    across = across + [swap(part) for part in across]
     turned = ring(turned)
+    turned = turned + [swap(part) for part in turned]
     state = (jax.ShapeDtypeStruct((ZN, ROWS, HD), jnp.float32),) * 3
     ring_buffers = [
         pltpu.VMEM((DEPTH,) + cache.shape[1:], jnp.bfloat16),
@@ -465,16 +474,16 @@
     anywhere = pl.BlockSpec(memory_space=pl.ANY)
     before = pl.pallas_call(
         attend_near,
+        compiler_params=SMALL,
         out_shape=state,
         in_specs=[smem, smem, smem, vmem, vmem] + [anywhere] * 6,
         out_specs=(vmem,) * 3,
         scratch_shapes=ring_buffers,
         cost_estimate=pl.CostEstimate(flops=1, bytes_accessed=1, transcendentals=0),
     )(near_list, counts, spans, everyone, root_tiles, *near)
-    across, before = lax.optimization_barrier((across, before))
-    across = across + [swap(part) for part in across]
     partial = pl.pallas_call(
         attend_far,
+        compiler_params=SMALL,
         out_shape=jax.ShapeDtypeStruct((ZN, BLOCK, HD), jnp.bfloat16),
         in_specs=[smem, smem, smem, vmem, vmem] + [anywhere] * 4 + [vmem] * 3,
         out_specs=vmem,
@@ -485,6 +494,7 @@
     partial, turned = lax.optimization_barrier((partial, turned))
     attended = pl.pallas_call(
         finish,
+        compiler_params=SMALL,
         out_shape=jax.ShapeDtypeStruct((ZN, SB, HEADS * HD), jnp.bfloat16),
         in_specs=[vmem] * 4,
         out_specs=vmem,
@@ -492,20 +502,29 @@
     )(partial, queries, key_chain, value_chain)
 
     attended = exchange(attended, "z").reshape(rows, HEADS * HD)
-    result = pl.pallas_call(
+    share = jax.ShapeDtypeStruct((XN, QUARTER, 2 * PART), jnp.float32)
+    shares = pl.pallas_call(
         deliver,
-        out_shape=jax.ShapeDtypeStruct((KN, XN, QUARTER, 2 * PART), jnp.float32),
-        in_specs=[smem] + [vmem] * (1 + XN),
-        out_specs=vmem,
-        scratch_shapes=[pltpu.VMEM((XN, 2 * PART, HEADS * HD), jnp.bfloat16)],
+        compiler_params=SMALL,
+        out_shape=(share,) * KN,
+        in_specs=[smem] + [vmem] * (1 + 2 * XN),
+        out_specs=(vmem,) * KN,
+        scratch_shapes=[
+            pltpu.VMEM((XN, 2 * PART, HEADS * HD), jnp.bfloat16),
+            pltpu.VMEM((rows, 2 * PART), jnp.float32),
+        ],
     )(place, attended, *turned)
-    result = exchange(result, "kv")
+    shares = [shares[0]] + [
+        lax.ppermute(shares[far], "kv", [(i, (i + far) % KN) for i in range(KN)])
+        for far in range(1, KN)
+    ]
     result = pl.pallas_call(
         settle,
+        compiler_params=SMALL,
         out_shape=jax.ShapeDtypeStruct((KN, XN, CN, SB, 2 * PART), jnp.bfloat16),
-        in_specs=[smem, vmem, vmem],
+        in_specs=[smem] + [vmem] * (KN + 1),
         out_specs=vmem,
-    )(place, result, stream)
+    )(place, *shares, stream)
     result = exchange(result.reshape(KN * JN, SB, 2 * PART), ("kv",) + XC)
     result = result.reshape(KN, JN, STEPS, GROUP, 2, PART).transpose(2, 0, 4, 1, 3, 5)
     return (result.reshape(STEPS, beams, PART), appended)

time: 208 us -> 193 us (0.928)
  waiting for transfers between devices: 67.5 us -> 25.4 us
  blocking collectives: 19.1 us -> 43.4 us
  local copies, waits for them, and re-layouts: 20.7 us -> 31.8 us
  Pallas kernels: 29.7 us -> 21.7 us
    all_to_all x7 -> x5, waiting for transfers between devices: 45.8 us -> 7.64 us  [exchange(): return lax.all_to_all(value, axis, 0, 0, tiled=True)]
    all_to_all x1 -> x2, blocking collectives: 19.1 us -> 43.4 us  [exchange(): return lax.all_to_all(value, axis, 0, 0, tiled=True)]
    pallas_call x8, Pallas kernels: 29.7 us -> 21.7 us  [the longest x1 7.7 us: body(): pl.pallas_call(attend_near, compiler_params=SMALL, out_shape=state, in_sp...]
    all_to_all x7 -> x5, starting transfers between devices: 39.3 us -> 32.2 us  [exchange(): return lax.all_to_all(value, axis, 0, 0, tiled=True)]
    ppermute x0 -> x3, starting transfers between devices: none -> 5.07 us  [body(): lax.ppermute(shares[far], 'kv', [(i, (i + far) % KN) for i in range(KN)])]
    ppermute x10, waiting for transfers between devices: 16.5 us -> 11.5 us  [shift(): return lax.ppermute(value, 'x', [(i, (i + hop) % XN) for i in range(XN)])]
    ppermute x7 -> x13, starting transfers between devices: 11.7 us -> 15.5 us  [swap(): return lax.ppermute(value, 'core', [(0, 1), (1, 0)])]
    unnamed x46 -> x51, local copies, waits for them, and re-layouts: 6.4 us -> 10 us
  transfers between devices with their start and end apart: 24 -> 31, of which waited for: 11 -> 10; matrix products, arithmetic and copies ran while one was open for 9% -> 13% of each run, Pallas kernels for 8% -> 8%
where the time goes in v6:
time: 193 us
  starting transfers between devices  65.4 us (34%)
  blocking collectives  43.4 us (22%)
  local copies, waits for them, and re-layouts  31.8 us (16%)
  waiting for transfers between devices  25.4 us (13%)
  Pallas kernels  21.7 us (11%)
  other arithmetic  3.83 us (2%)
    all_to_all x2, blocking collectives, exchange(): return lax.all_to_all(value, axis, 0, 0, tiled=True)  43.4 us
    all_to_all x5, starting transfers between devices, exchange(): return lax.all_to_all(value, axis, 0, 0, tiled=True)  32.2 us
    ppermute x13, starting transfers between devices, swap(): return lax.ppermute(value, 'core', [(0, 1), (1, 0)])  15.5 us
    ppermute x10, starting transfers between devices, shift(): return lax.ppermute(value, 'x', [(i, (i + hop) % XN) for i in range(XN)])  12.7 us
    ppermute x10, waiting for transfers between devices, shift(): return lax.ppermute(value, 'x', [(i, (i + hop) % XN) for i in range(XN)])  11.5 us
    unnamed x51, local copies, waits for them, and re-layouts  10 us
    pallas_call x1, Pallas kernels, body(): pl.pallas_call(attend_near, compiler_params=SMALL, out_shape=state, in_sp...  7.7 us
    all_to_all x5, waiting for transfers between devices, exchange(): return lax.all_to_all(value, axis, 0, 0, tiled=True)  7.64 us
  transfers between devices with their start and end apart: 31, of which 10 were waited for; matrix products, arithmetic and copies ran while one was open for 13% of the time, Pallas kernels for 8%

profile of v6, /device:TPU:1, one launch (start us, length us, event | category | flops | bytes accessed | tf_op | source)
XLA Modules:
  0.0 192.9 jit_solution(10811539983808739405)
XLA Ops:
  1.4 1.1 copy.89
  4.1 6.5 %all-to-all-start = ((bf16[8,104,128]{2,1,0:T(8,128)(2,1)}), bf16[8,104,128]{2,1,0:T(8,128)(2,1)S(1)}, u32[]{:S(2)}, u32[]{:S(2)}) async-start(bf16[8,104,128]{2,1,0:T(8,128)(2,1)} %pad_maximum_fusion), calls=%async_computation | async-start | bytes 425984 | tf_op jit(solution)/shard_map/all_to_all | solution.py:37
  10.7 1.5 collective-permute-start
  12.1 2.4 %collective-permute-start.1 = (bf16[64,1280]{1,0:T(8,128)(2,1)S(1)}, bf16[64,1280]{1,0:T(8,128)(2,1)S(1)}, u32[]{:S(2)}, u32[]{:S(2)}) collective-permute-start(bf16[64,1280]{1,0:T(8,128)(2,1)S(1)} %pad_maximum_fusion.1.rest_0_), channel_id=1, source_target_pairs={{0,4},{2,6},{4,0},{6,2},{1,5},{3,7},{5,1},{7,3},{8,12},{10,14},{12... | collective-permute-start | bytes 491528 | tf_op jit(solution)/shard_map/ppermute | solution.py:49
  14.6 1.2 collective-permute-start.2
  15.8 1.4 collective-permute-start.7
  17.3 2.9 %collective-permute-done.rest_1_ = bf16[64,1280]{1,0:T(8,128)(2,1)S(1)} collective-permute-done((bf16[64,1280]{1,0:T(8,128)(2,1)S(1)}, bf16[64,1280]{1,0:T(8,128)(2,1)S(1)}, u32[]{:S(2)}, u32[]{:S(2)}) %collective-permute-start) | collective-permute-done | bytes 163872 | tf_op jit(solution)/shard_map/ppermute | solution.py:49
  20.2 3.7 %collective-permute-done.1.rest_2_ = bf16[64,1280]{1,0:T(8,128)(2,1)S(1)} collective-permute-done((bf16[64,1280]{1,0:T(8,128)(2,1)S(1)}, bf16[64,1280]{1,0:T(8,128)(2,1)S(1)}, u32[]{:S(2)}, u32[]{:S(2)}) %collective-permute-start.1) | collective-permute-done | bytes 163872 | tf_op jit(solution)/shard_map/ppermute | solution.py:49
  25.0 7.4 %all-to-all-start.1 = ((f32[8,2,128]{2,1,0:T(2,128)}), f32[8,2,128]{2,1,0:T(2,128)S(1)}, u32[]{:S(2)}, u32[]{:S(2)}) async-start(f32[8,2,128]{2,1,0:T(2,128)} %broadcast_in_dim.68), calls=%async_computation.1 | async-start | bytes 16384 | tf_op jit(solution)/shard_map/all_to_all | solution.py:37
  32.6 1.4 reshape.166
  33.9 2.6 %copy.91 = f32[4,4,2,24,2,64]{5,4,3,2,1,0:T(2,128)} copy(f32[4,4,2,24,2,64]{5,2,3,1,4,0:T(2,128)} %bitcast.59) | data formatting | bytes 786432 | tf_op jit(solution)/shard_map/convert_element_type | solution.py:423
  36.6 1.6 reshape.165.rest_4_
  38.2 1.6 collective-permute-start.3
  40.9 1.0 collective-permute-start.6
  43.0 1.7 shard_map.114
  44.7 1.0 copy-done
  45.6 6.3 %all-to-all-start.2 = ((f32[8,24,1280]{2,1,0:T(8,128)}), f32[8,24,1280]{2,1,0:T(8,128)S(1)}, u32[]{:S(2)}, u32[]{:S(2)}) async-start(f32[8,24,1280]{2,1,0:T(8,128)} %bitcast.47), calls=%async_computation.2 | async-start | bytes 1966080 | tf_op jit(solution)/shard_map/all_to_all | solution.py:37
  51.9 1.8 copy.88
  53.7 1.7 reshape.151
  56.1 1.0 broadcast_subtract_fusion
  59.2 0.8 copy.95
  61.3 0.9 constant_dynamic-slice_fusion.2
  62.5 4.9 %collective-permute-done.9.rest_4_ = bf16[32,2,128,128]{3,2,1,0:T(8,128)(2,1)S(1)} collective-permute-done((bf16[32,2,128,128]{3,2,1,0:T(8,128)(2,1)}, bf16[32,2,128,128]{3,2,1,0:T(8,128)(2,1)S(1)}, u32[]{:S(2)}, u32[]{:S(2)}) %collective-permute-start.9) | collective-permute-done | bytes 2097184 | tf_op jit(solution)/shard_map/ppermute | solution.py:49
  67.4 1.0 slice.61
  68.4 2.6 %collective-permute-start.10 = (bf16[16,2,128,128]{3,2,1,0:T(8,128)(2,1)}, bf16[16,2,128,128]{3,2,1,0:T(8,128)(2,1)}, u32[]{:S(2)}, u32[]{:S(2)}) collective-permute-start(bf16[16,2,128,128]{3,2,1,0:T(8,128)(2,1)} %slice.61), channel_id=1, source_target_pairs={{0,6},{2,0},{4,2},{6,4},{1,7},{3,1},{5,3},{7,5},{8,14},{10,8},{12,... | collective-permute-start | bytes 3145736 | tf_op jit(solution)/shard_map/ppermute | solution.py:49
  71.1 2.3 %slice.60 = bf16[16,2,128,128]{3,2,1,0:T(8,128)(2,1)} slice(bf16[32,2,128,128]{3,2,1,0:T(8,128)(2,1)} %collective-permute-done.7.rest_2_), slice={[0:16], [0:2], [0:128], [0:128]} | slice | bytes 2097152 | tf_op jit(solution)/shard_map/slice | solution.py:418
  75.8 4.8 %shard_map.113 = (s32[256]{0:T(256)S(1)}, s32[256]{0:T(256)S(1)}, s32[2]{0:T(128)S(1)}) custom-call(s32[4]{0:T(128)S(1)} %pad_add_fusion.place_ref, s32[4096]{0:T(1024)S(1)} %bitcast.58, s32[64]{0:T(128)S(1)} %reshape.154.length_ref), custom_call_target="tpu_custom_call" | custom-call | tf_op jit(solution)/shard_map/pallas_call | solution.py:389
  82.7 22.4 %all_to_all.35.q_ref = bf16[8,192,128]{2,1,0:T(8,128)(2,1)S(1)} all-to-all(bf16[8,192,128]{2,1,0:T(8,128)(2,1)S(1)} %get-tuple-element.48), channel_id=1, replica_groups=mesh['kv'=4,'z'=8,'x'=4,'core'=2] {'z'}, dimensions={0} | all-to-all | bytes 786432 | tf_op jit(solution)/shard_map/all_to_all | solution.py:37
  107.3 0.8 copy.98
  108.6 1.6 copy-done.1
  111.5 7.7 %shard_map.116 = (f32[8,192,128]{2,1,0:T(8,128)S(1)}, f32[8,192,128]{2,1,0:T(8,128)S(1)}, f32[8,192,128]{2,1,0:T(8,128)S(1)}) custom-call(s32[256]{0:T(256)S(1)} %copy-done.14, s32[2]{0:T(128)S(1)} %copy-done.9, s32[64]{0:T(128)S(1)} %reshape.154.length_ref, bf16[8,192,128]{2,1,0:T(8,128)(2,1)S(1)} %all_to_all.35.q_ref, ...), custom_call_target="tpu_custom_call" | custom-call | flops 1 | bytes 1 | tf_op jit(solution)/shard_map/pallas_call | solution.py:475
  119.3 3.7 %shard_map.117 = bf16[8,216,128]{2,1,0:T(8,128)(2,1)} custom-call(s32[256]{0:T(256)S(1)} %copy-done.12, s32[2]{0:T(128)S(1)} %copy-done.10, s32[64]{0:T(128)S(1)} %reshape.154.length_ref, bf16[8,192,128]{2,1,0:T(8,128)(2,1)S(1)} %all_to_all.35.q_ref, s32[8,24,128]{2,1,0:T(8,128)S(1)} %broadcast_in_dim.77.root_ref, ...), custom_call_target="tpu_custom_call" | custom-call | tf_op jit(solution)/shard_map/pallas_call | solution.py:484
  123.0 4.7 %all-to-all-start.4 = ((bf16[8,216,128]{2,1,0:T(8,128)(2,1)}), bf16[8,216,128]{2,1,0:T(8,128)(2,1)S(1)}, u32[]{:S(2)}, u32[]{:S(2)}) async-start(bf16[8,216,128]{2,1,0:T(8,128)(2,1)} %shard_map.117), calls=%async_computation.4 | async-start | bytes 884736 | tf_op jit(solution)/shard_map/all_to_all | solution.py:37
  127.9 2.6 %collective-permute-start.17 = (bf16[64,1024]{1,0:T(8,128)(2,1)S(1)}, bf16[64,1024]{1,0:T(8,128)(2,1)S(1)}, u32[]{:S(2)}, u32[]{:S(2)}) collective-permute-start(bf16[64,1024]{1,0:T(8,128)(2,1)S(1)} %bitcast.54), channel_id=1, source_target_pairs={{0,4},{2,6},{4,0},{6,2},{1,5},{3,7},{5,1},{7,3},{8,12},{10,14},{12... | collective-permute-start | bytes 393224 | tf_op jit(solution)/shard_map/ppermute | solution.py:49
  131.3 7.1 %collective-permute-start.19 = (bf16[64,1024]{1,0:T(8,128)(2,1)S(1)}, bf16[64,1024]{1,0:T(8,128)(2,1)S(1)}, u32[]{:S(2)}, u32[]{:S(2)}) collective-permute-start(bf16[64,1024]{1,0:T(8,128)(2,1)S(1)} %bitcast.56), channel_id=1, source_target_pairs={{0,1},{1,0},{2,3},{3,2},{4,5},{5,4},{6,7},{7,6},{8,9},{9,8},{10,11... | collective-permute-start | bytes 393224 | tf_op jit(solution)/shard_map/ppermute | solution.py:45
  138.3 3.7 %collective-permute-start.21 = (bf16[64,1024]{1,0:T(8,128)(2,1)S(1)}, bf16[64,1024]{1,0:T(8,128)(2,1)S(1)}, u32[]{:S(2)}, u32[]{:S(2)}) collective-permute-start(bf16[64,1024]{1,0:T(8,128)(2,1)S(1)} %collective-permute-done.17.rest_2_), channel_id=1, source_target_pairs={{0,1},{1,0},{2,3},{3,2},{4,5},{5,4},{6,7},{7,6},{8,9},{9,8},{10,11... | collective-permute-start | bytes 393224 | tf_op jit(solution)/shard_map/ppermute | solution.py:45
  142.0 1.0 collective-permute-done.21.rest_6_
  143.9 21.0 %all_to_all.36 = bf16[8,24,1024]{2,1,0:T(8,128)(2,1)S(1)} all-to-all(bf16[8,24,1024]{2,1,0:T(8,128)(2,1)S(1)} %shard_map.118), channel_id=1, replica_groups=mesh['kv'=4,'z'=8,'x'=4,'core'=2] {'z'}, dimensions={0} | all-to-all | bytes 786432 | tf_op jit(solution)/shard_map/all_to_all | solution.py:37
  164.9 1.2 shard_map.119
  166.2 1.4 collective-permute-start.23
  167.6 2.6 %collective-permute-start.24 = (f32[4,48,128]{2,1,0:T(8,128)S(1)}, f32[4,48,128]{2,1,0:T(8,128)S(1)}, u32[]{:S(2)}, u32[]{:S(2)}) collective-permute-start(f32[4,48,128]{2,1,0:T(8,128)S(1)} %get-tuple-element.72), channel_id=1, source_target_pairs={{0,128},{64,192},{128,0},{192,64},{1,129},{65,193},{129,1},{193,65... | collective-permute-start | bytes 294920 | tf_op jit(solution)/shard_map/ppermute | solution.py:518
  170.2 1.1 collective-permute-start.25
  171.3 2.3 %collective-permute-done.24.rest_2_ = f32[4,48,128]{2,1,0:T(8,128)S(1)} collective-permute-done((f32[4,48,128]{2,1,0:T(8,128)S(1)}, f32[4,48,128]{2,1,0:T(8,128)S(1)}, u32[]{:S(2)}, u32[]{:S(2)}) %collective-permute-start.24) | collective-permute-done | bytes 98336 | tf_op jit(solution)/shard_map/ppermute | solution.py:518
  173.5 1.3 collective-permute-done.25.rest_3_
  174.9 1.3 shard_map.120
  176.2 7.3 %all-to-all-start.6 = ((bf16[32,24,128]{2,1,0:T(8,128)(2,1)}), bf16[32,24,128]{2,1,0:T(8,128)(2,1)S(1)}, u32[]{:S(2)}, u32[]{:S(2)}) async-start(bf16[32,24,128]{2,1,0:T(8,128)(2,1)} %bitcast.26), calls=%async_computation.6 | async-start | bytes 393216 | tf_op jit(solution)/shard_map/all_to_all | solution.py:37
  184.1 7.6 %all-to-all-done.6 = bf16[32,24,128]{2,1,0:T(8,128)(2,1)S(1)} async-done(((bf16[32,24,128]{2,1,0:T(8,128)(2,1)}), bf16[32,24,128]{2,1,0:T(8,128)(2,1)S(1)}, u32[]{:S(2)}, u32[]{:S(2)}) %all-to-all-start.6) | async-done | bytes 196640 | tf_op jit(solution)/shard_map/all_to_all | solution.py:37
  192.0 0.8 copy.102
  (141 shorter events, 21.1 us)
Async XLA Ops:
  0.6 10.0 %copy-start.16 = (bf16[64,1024]{1,0:T(8,128)(2,1)S(1)}, bf16[64,1024]{1,0:T(8,128)(2,1)}, u32[]{:S(2)}) copy-start(bf16[64,1024]{1,0:T(8,128)(2,1)} %param.12) | copy-start | bytes 393220
  0.6 10.0 %copy-start.20 = (bf16[64,128]{1,0:T(8,128)(2,1)S(1)}, bf16[64,128]{1,0:T(8,128)(2,1)}, u32[]{:S(2)}) copy-start(bf16[64,128]{1,0:T(8,128)(2,1)} %param.13) | copy-start | bytes 49156
  0.7 10.0 %copy-start.19 = (bf16[64,128]{1,0:T(8,128)(2,1)S(1)}, bf16[64,128]{1,0:T(8,128)(2,1)}, u32[]{:S(2)}) copy-start(bf16[64,128]{1,0:T(8,128)(2,1)} %param.14) | copy-start | bytes 49156
  4.1 19.8 %all-to-all-start = ((bf16[8,104,128]{2,1,0:T(8,128)(2,1)}), bf16[8,104,128]{2,1,0:T(8,128)(2,1)S(1)}, u32[]{:S(2)}, u32[]{:S(2)}) async-start(bf16[8,104,128]{2,1,0:T(8,128)(2,1)} %pad_maximum_fusion), calls=%async_computation | async-start | bytes 425984 | tf_op jit(solution)/shard_map/all_to_all | solution.py:37
  10.7 9.5 %collective-permute-start = (bf16[64,1280]{1,0:T(8,128)(2,1)S(1)}, bf16[64,1280]{1,0:T(8,128)(2,1)S(1)}, u32[]{:S(2)}, u32[]{:S(2)}) collective-permute-start(bf16[64,1280]{1,0:T(8,128)(2,1)S(1)} %pad_maximum_fusion.1.rest_0_), channel_id=1, source_target_pairs={{0,2},{2,4},{4,6},{6,0},{1,3},{3,5},{5,7},{7,1},{8,10},{10,12},{12... | collective-permute-start | bytes 491528 | tf_op jit(solution)/shard_map/ppermute | solution.py:49
  12.1 11.7 %collective-permute-start.1 = (bf16[64,1280]{1,0:T(8,128)(2,1)S(1)}, bf16[64,1280]{1,0:T(8,128)(2,1)S(1)}, u32[]{:S(2)}, u32[]{:S(2)}) collective-permute-start(bf16[64,1280]{1,0:T(8,128)(2,1)S(1)} %pad_maximum_fusion.1.rest_0_), channel_id=1, source_target_pairs={{0,4},{2,6},{4,0},{6,2},{1,5},{3,7},{5,1},{7,3},{8,12},{10,14},{12... | collective-permute-start | bytes 491528 | tf_op jit(solution)/shard_map/ppermute | solution.py:49
  14.6 9.3 %collective-permute-start.2 = (bf16[64,1280]{1,0:T(8,128)(2,1)S(1)}, bf16[64,1280]{1,0:T(8,128)(2,1)S(1)}, u32[]{:S(2)}, u32[]{:S(2)}) collective-permute-start(bf16[64,1280]{1,0:T(8,128)(2,1)S(1)} %pad_maximum_fusion.1.rest_0_), channel_id=1, source_target_pairs={{0,6},{2,0},{4,2},{6,4},{1,7},{3,1},{5,3},{7,5},{8,14},{10,8},{12,... | collective-permute-start | bytes 491528 | tf_op jit(solution)/shard_map/ppermute | solution.py:49
  15.7 51.7 %collective-permute-start.9 = (bf16[32,2,128,128]{3,2,1,0:T(8,128)(2,1)}, bf16[32,2,128,128]{3,2,1,0:T(8,128)(2,1)S(1)}, u32[]{:S(2)}, u32[]{:S(2)}) collective-permute-start(bf16[32,2,128,128]{3,2,1,0:T(8,128)(2,1)} %bitcast.48), channel_id=1, source_target_pairs={{0,6},{2,0},{4,2},{6,4},{1,7},{3,1},{5,3},{7,5},{8,14},{10,8},{12,... | collective-permute-start | bytes 6291464 | tf_op jit(solution)/shard_map/ppermute | solution.py:49
  15.8 55.3 %collective-permute-start.7 = (bf16[32,2,128,128]{3,2,1,0:T(8,128)(2,1)}, bf16[32,2,128,128]{3,2,1,0:T(8,128)(2,1)}, u32[]{:S(2)}, u32[]{:S(2)}) collective-permute-start(bf16[32,2,128,128]{3,2,1,0:T(8,128)(2,1)} %bitcast.49), channel_id=1, source_target_pairs={{0,2},{2,4},{4,6},{6,0},{1,3},{3,5},{5,7},{7,1},{8,10},{10,12},{12... | collective-permute-start | bytes 6291464 | tf_op jit(solution)/shard_map/ppermute | solution.py:49
  25.0 15.4 %all-to-all-start.1 = ((f32[8,2,128]{2,1,0:T(2,128)}), f32[8,2,128]{2,1,0:T(2,128)S(1)}, u32[]{:S(2)}, u32[]{:S(2)}) async-start(f32[8,2,128]{2,1,0:T(2,128)} %broadcast_in_dim.68), calls=%async_computation.1 | async-start | bytes 16384 | tf_op jit(solution)/shard_map/all_to_all | solution.py:37
  38.2 2.7 %collective-permute-start.3 = (bf16[64,1280]{1,0:T(8,128)(2,1)S(1)}, bf16[64,1280]{1,0:T(8,128)(2,1)S(1)}, u32[]{:S(2)}, u32[]{:S(2)}) collective-permute-start(bf16[64,1280]{1,0:T(8,128)(2,1)S(1)} %pad_maximum_fusion.1.rest_0_), channel_id=1, source_target_pairs={{0,1},{1,0},{2,3},{3,2},{4,5},{5,4},{6,7},{7,6},{8,9},{9,8},{10,11... | collective-permute-start | bytes 491528 | tf_op jit(solution)/shard_map/ppermute | solution.py:45
  39.9 2.2 %collective-permute-start.4 = (bf16[64,1280]{1,0:T(8,128)(2,1)S(1)}, bf16[64,1280]{1,0:T(8,128)(2,1)S(1)}, u32[]{:S(2)}, u32[]{:S(2)}) collective-permute-start(bf16[64,1280]{1,0:T(8,128)(2,1)S(1)} %collective-permute-done.rest_1_), channel_id=1, source_target_pairs={{0,1},{1,0},{2,3},{3,2},{4,5},{5,4},{6,7},{7,6},{8,9},{9,8},{10,11... | collective-permute-start | bytes 491528 | tf_op jit(solution)/shard_map/ppermute | solution.py:45
  40.0 2.2 %collective-permute-start.5 = (bf16[64,1280]{1,0:T(8,128)(2,1)S(1)}, bf16[64,1280]{1,0:T(8,128)(2,1)}, u32[]{:S(2)}, u32[]{:S(2)}) collective-permute-start(bf16[64,1280]{1,0:T(8,128)(2,1)S(1)} %collective-permute-done.1.rest_2_), channel_id=1, source_target_pairs={{0,1},{1,0},{2,3},{3,2},{4,5},{5,4},{6,7},{7,6},{8,9},{9,8},{10,11... | collective-permute-start | bytes 491528 | tf_op jit(solution)/shard_map/ppermute | solution.py:45
  40.9 2.1 %collective-permute-start.6 = (bf16[64,1280]{1,0:T(8,128)(2,1)S(1)}, bf16[64,1280]{1,0:T(8,128)(2,1)S(1)}, u32[]{:S(2)}, u32[]{:S(2)}) collective-permute-start(bf16[64,1280]{1,0:T(8,128)(2,1)S(1)} %collective-permute-done.2.rest_3_), channel_id=1, source_target_pairs={{0,1},{1,0},{2,3},{3,2},{4,5},{5,4},{6,7},{7,6},{8,9},{9,8},{10,11... | collective-permute-start | bytes 491528 | tf_op jit(solution)/shard_map/ppermute | solution.py:45
  42.1 13.3 %copy-start.22 = (s32[3,512]{1,0:T(4,128)S(1)}, s32[3,512]{1,0:T(4,128)}, u32[]{:S(2)}) copy-start(s32[3,512]{1,0:T(4,128)} %param.19) | copy-start | bytes 18436
  42.1 66.4 %collective-permute-start.13 = (bf16[32,2,128,128]{3,2,1,0:T(8,128)(2,1)}, bf16[32,2,128,128]{3,2,1,0:T(8,128)(2,1)}, u32[]{:S(2)}, u32[]{:S(2)}) collective-permute-start(bf16[32,2,128,128]{3,2,1,0:T(8,128)(2,1)} %bitcast.50), channel_id=1, source_target_pairs={{0,1},{1,0},{2,3},{3,2},{4,5},{5,4},{6,7},{7,6},{8,9},{9,8},{10,11... | collective-permute-start | bytes 6291464 | tf_op jit(solution)/shard_map/ppermute | solution.py:45
  44.7 1.0 copy-start
  45.6 35.7 %all-to-all-start.2 = ((f32[8,24,1280]{2,1,0:T(8,128)}), f32[8,24,1280]{2,1,0:T(8,128)S(1)}, u32[]{:S(2)}, u32[]{:S(2)}) async-start(f32[8,24,1280]{2,1,0:T(8,128)} %bitcast.47), calls=%async_computation.2 | async-start | bytes 1966080 | tf_op jit(solution)/shard_map/all_to_all | solution.py:37
  61.0 1.4 copy-start.17
  61.0 1.4 copy-start.18
  62.4 11.8 %copy-start.21 = (s32[512]{0:T(512)S(1)}, s32[512]{0:T(512)}, u32[]{:S(2)}) copy-start(s32[512]{0:T(512)} %param.17) | copy-start | bytes 6148
  68.4 36.6 %collective-permute-start.10 = (bf16[16,2,128,128]{3,2,1,0:T(8,128)(2,1)}, bf16[16,2,128,128]{3,2,1,0:T(8,128)(2,1)}, u32[]{:S(2)}, u32[]{:S(2)}) collective-permute-start(bf16[16,2,128,128]{3,2,1,0:T(8,128)(2,1)} %slice.61), channel_id=1, source_target_pairs={{0,6},{2,0},{4,2},{6,4},{1,7},{3,1},{5,3},{7,5},{8,14},{10,8},{12,... | collective-permute-start | bytes 3145736 | tf_op jit(solution)/shard_map/ppermute | solution.py:49
  73.4 31.7 %collective-permute-start.8 = (bf16[16,2,128,128]{3,2,1,0:T(8,128)(2,1)}, bf16[16,2,128,128]{3,2,1,0:T(8,128)(2,1)}, u32[]{:S(2)}, u32[]{:S(2)}) collective-permute-start(bf16[16,2,128,128]{3,2,1,0:T(8,128)(2,1)} %slice.60), channel_id=1, source_target_pairs={{0,2},{2,4},{4,6},{6,0},{1,3},{3,5},{5,7},{7,1},{8,10},{10,12},{12... | collective-permute-start | bytes 3145736 | tf_op jit(solution)/shard_map/ppermute | solution.py:49
  73.4 35.1 %collective-permute-start.14 = (bf16[32,2,128,128]{3,2,1,0:T(8,128)(2,1)}, bf16[32,2,128,128]{3,2,1,0:T(8,128)(2,1)}, u32[]{:S(2)}, u32[]{:S(2)}) collective-permute-start(bf16[32,2,128,128]{3,2,1,0:T(8,128)(2,1)} %collective-permute-done.7.rest_2_), channel_id=1, source_target_pairs={{0,1},{1,0},{2,3},{3,2},{4,5},{5,4},{6,7},{7,6},{8,9},{9,8},{10,11... | collective-permute-start | bytes 6291464 | tf_op jit(solution)/shard_map/ppermute | solution.py:45
  74.2 34.4 %collective-permute-start.15 = (bf16[32,2,128,128]{3,2,1,0:T(8,128)(2,1)S(1)}, bf16[32,2,128,128]{3,2,1,0:T(8,128)(2,1)}, u32[]{:S(2)}, u32[]{:S(2)}) collective-permute-start(bf16[32,2,128,128]{3,2,1,0:T(8,128)(2,1)S(1)} %collective-permute-done.9.rest_4_), channel_id=1, source_target_pairs={{0,1},{1,0},{2,3},{3,2},{4,5},{5,4},{6,7},{7,6},{8,9},{9,8},{10,11... | collective-permute-start | bytes 6291464 | tf_op jit(solution)/shard_map/ppermute | solution.py:45
  81.3 0.7 copy-start.7
  82.6 22.4 %copy-start.3 = (f32[6,8,128]{2,1,0:T(8,128)}, f32[6,8,128]{2,1,0:T(8,128)S(1)}, u32[]{:S(2)}) copy-start(f32[6,8,128]{2,1,0:T(8,128)S(1)} %get-tuple-element.61.v_ref) | copy-start | bytes 73732
  82.7 22.4 %copy-start.5 = (f32[6,8,128]{2,1,0:T(8,128)}, f32[6,8,128]{2,1,0:T(8,128)S(1)}, u32[]{:S(2)}) copy-start(f32[6,8,128]{2,1,0:T(8,128)S(1)} %get-tuple-element.60.k_ref) | copy-start | bytes 73732
  105.1 14.1 %collective-permute-start.11 = (bf16[16,2,128,128]{3,2,1,0:T(8,128)(2,1)}, bf16[16,2,128,128]{3,2,1,0:T(8,128)(2,1)}, u32[]{:S(2)}, u32[]{:S(2)}) collective-permute-start(bf16[16,2,128,128]{3,2,1,0:T(8,128)(2,1)} %collective-permute-done.8.rest_0_), channel_id=1, source_target_pairs={{0,1},{1,0},{2,3},{3,2},{4,5},{5,4},{6,7},{7,6},{8,9},{9,8},{10,11... | collective-permute-start | bytes 3145736 | tf_op jit(solution)/shard_map/ppermute | solution.py:45
  105.7 13.5 %collective-permute-start.12 = (bf16[16,2,128,128]{3,2,1,0:T(8,128)(2,1)}, bf16[16,2,128,128]{3,2,1,0:T(8,128)(2,1)}, u32[]{:S(2)}, u32[]{:S(2)}) collective-permute-start(bf16[16,2,128,128]{3,2,1,0:T(8,128)(2,1)} %collective-permute-done.10.rest_1_), channel_id=1, source_target_pairs={{0,1},{1,0},{2,3},{3,2},{4,5},{5,4},{6,7},{7,6},{8,9},{9,8},{10,11... | collective-permute-start | bytes 3145736 | tf_op jit(solution)/shard_map/ppermute | solution.py:45
  108.6 1.6 copy-start.1
  111.5 7.7 %copy-start.10 = (s32[2]{0:T(128)S(1)}, s32[2]{0:T(128)}, u32[]{:S(2)}) copy-start(s32[2]{0:T(128)} %copy-done.8) | copy-start | bytes 28
  111.5 7.7 %copy-start.12 = (s32[256]{0:T(256)S(1)}, s32[256]{0:T(256)}, u32[]{:S(2)}) copy-start(s32[256]{0:T(256)} %copy-done.11) | copy-start | bytes 3076
  119.2 8.5 %copy-start.2 = (bf16[1024,64]{0,1:T(8,128)(2,1)S(1)}, bf16[1024,64]{0,1:T(8,128)(2,1)}, u32[]{:S(2)}) copy-start(bf16[1024,64]{0,1:T(8,128)(2,1)} %param.15) | copy-start | bytes 393220
  119.2 24.1 %copy-start.4 = (f32[6,8,128]{2,1,0:T(8,128)S(1)}, f32[6,8,128]{2,1,0:T(8,128)}, u32[]{:S(2)}) copy-start(f32[6,8,128]{2,1,0:T(8,128)} %copy-done.3) | copy-start | bytes 73732
  119.2 24.1 %copy-start.6 = (f32[6,8,128]{2,1,0:T(8,128)S(1)}, f32[6,8,128]{2,1,0:T(8,128)}, u32[]{:S(2)}) copy-start(f32[6,8,128]{2,1,0:T(8,128)} %copy-done.5) | copy-start | bytes 73732
  123.0 20.4 %all-to-all-start.4 = ((bf16[8,216,128]{2,1,0:T(8,128)(2,1)}), bf16[8,216,128]{2,1,0:T(8,128)(2,1)S(1)}, u32[]{:S(2)}, u32[]{:S(2)}) async-start(bf16[8,216,128]{2,1,0:T(8,128)(2,1)} %shard_map.117), calls=%async_computation.4 | async-start | bytes 884736 | tf_op jit(solution)/shard_map/all_to_all | solution.py:37
  127.7 10.6 %collective-permute-start.16 = (bf16[64,1024]{1,0:T(8,128)(2,1)S(1)}, bf16[64,1024]{1,0:T(8,128)(2,1)S(1)}, u32[]{:S(2)}, u32[]{:S(2)}) collective-permute-start(bf16[64,1024]{1,0:T(8,128)(2,1)S(1)} %bitcast.53), channel_id=1, source_target_pairs={{0,2},{2,4},{4,6},{6,0},{1,3},{3,5},{5,7},{7,1},{8,10},{10,12},{12... | collective-permute-start | bytes 393224 | tf_op jit(solution)/shard_map/ppermute | solution.py:49
  127.9 10.4 %collective-permute-start.17 = (bf16[64,1024]{1,0:T(8,128)(2,1)S(1)}, bf16[64,1024]{1,0:T(8,128)(2,1)S(1)}, u32[]{:S(2)}, u32[]{:S(2)}) collective-permute-start(bf16[64,1024]{1,0:T(8,128)(2,1)S(1)} %bitcast.54), channel_id=1, source_target_pairs={{0,4},{2,6},{4,0},{6,2},{1,5},{3,7},{5,1},{7,3},{8,12},{10,14},{12... | collective-permute-start | bytes 393224 | tf_op jit(solution)/shard_map/ppermute | solution.py:49
  130.5 11.5 %collective-permute-start.18 = (bf16[64,1024]{1,0:T(8,128)(2,1)S(1)}, bf16[64,1024]{1,0:T(8,128)(2,1)S(1)}, u32[]{:S(2)}, u32[]{:S(2)}) collective-permute-start(bf16[64,1024]{1,0:T(8,128)(2,1)S(1)} %bitcast.55), channel_id=1, source_target_pairs={{0,6},{2,0},{4,2},{6,4},{1,7},{3,1},{5,3},{7,5},{8,14},{10,8},{12,... | collective-permute-start | bytes 393224 | tf_op jit(solution)/shard_map/ppermute | solution.py:49
  131.3 10.8 %collective-permute-start.19 = (bf16[64,1024]{1,0:T(8,128)(2,1)S(1)}, bf16[64,1024]{1,0:T(8,128)(2,1)S(1)}, u32[]{:S(2)}, u32[]{:S(2)}) collective-permute-start(bf16[64,1024]{1,0:T(8,128)(2,1)S(1)} %bitcast.56), channel_id=1, source_target_pairs={{0,1},{1,0},{2,3},{3,2},{4,5},{5,4},{6,7},{7,6},{8,9},{9,8},{10,11... | collective-permute-start | bytes 393224 | tf_op jit(solution)/shard_map/ppermute | solution.py:45
  138.3 3.7 %collective-permute-start.20 = (bf16[64,1024]{1,0:T(8,128)(2,1)S(1)}, bf16[64,1024]{1,0:T(8,128)(2,1)S(1)}, u32[]{:S(2)}, u32[]{:S(2)}) collective-permute-start(bf16[64,1024]{1,0:T(8,128)(2,1)S(1)} %collective-permute-done.16.rest_1_), channel_id=1, source_target_pairs={{0,1},{1,0},{2,3},{3,2},{4,5},{5,4},{6,7},{7,6},{8,9},{9,8},{10,11... | collective-permute-start | bytes 393224 | tf_op jit(solution)/shard_map/ppermute | solution.py:45
  138.3 4.7 %collective-permute-start.21 = (bf16[64,1024]{1,0:T(8,128)(2,1)S(1)}, bf16[64,1024]{1,0:T(8,128)(2,1)S(1)}, u32[]{:S(2)}, u32[]{:S(2)}) collective-permute-start(bf16[64,1024]{1,0:T(8,128)(2,1)S(1)} %collective-permute-done.17.rest_2_), channel_id=1, source_target_pairs={{0,1},{1,0},{2,3},{3,2},{4,5},{5,4},{6,7},{7,6},{8,9},{9,8},{10,11... | collective-permute-start | bytes 393224 | tf_op jit(solution)/shard_map/ppermute | solution.py:45
  142.0 1.3 collective-permute-start.22
  166.2 5.1 %collective-permute-start.23 = (f32[4,48,128]{2,1,0:T(8,128)S(1)}, f32[4,48,128]{2,1,0:T(8,128)S(1)}, u32[]{:S(2)}, u32[]{:S(2)}) collective-permute-start(f32[4,48,128]{2,1,0:T(8,128)S(1)} %get-tuple-element.71), channel_id=1, source_target_pairs={{0,64},{64,128},{128,192},{192,0},{1,65},{65,129},{129,193},{193,1... | collective-permute-start | bytes 294920 | tf_op jit(solution)/shard_map/ppermute | solution.py:518
  167.6 6.0 %collective-permute-start.24 = (f32[4,48,128]{2,1,0:T(8,128)S(1)}, f32[4,48,128]{2,1,0:T(8,128)S(1)}, u32[]{:S(2)}, u32[]{:S(2)}) collective-permute-start(f32[4,48,128]{2,1,0:T(8,128)S(1)} %get-tuple-element.72), channel_id=1, source_target_pairs={{0,128},{64,192},{128,0},{192,64},{1,129},{65,193},{129,1},{193,65... | collective-permute-start | bytes 294920 | tf_op jit(solution)/shard_map/ppermute | solution.py:518
  170.2 4.7 %collective-permute-start.25 = (f32[4,48,128]{2,1,0:T(8,128)S(1)}, f32[4,48,128]{2,1,0:T(8,128)S(1)}, u32[]{:S(2)}, u32[]{:S(2)}) collective-permute-start(f32[4,48,128]{2,1,0:T(8,128)S(1)} %get-tuple-element.73), channel_id=1, source_target_pairs={{0,192},{64,0},{128,64},{192,128},{1,193},{65,1},{129,65},{193,129... | collective-permute-start | bytes 294920 | tf_op jit(solution)/shard_map/ppermute | solution.py:518
  176.2 15.6 %all-to-all-start.6 = ((bf16[32,24,128]{2,1,0:T(8,128)(2,1)}), bf16[32,24,128]{2,1,0:T(8,128)(2,1)S(1)}, u32[]{:S(2)}, u32[]{:S(2)}) async-start(bf16[32,24,128]{2,1,0:T(8,128)(2,1)} %bitcast.26), calls=%async_computation.6 | async-start | bytes 393216 | tf_op jit(solution)/shard_map/all_to_all | solution.py:37
  (6 other events, 3.5 us)

commit v7 on v6

--- a/solution.py
+++ b/solution.py
@@ -384,7 +384,11 @@
         block_table.reshape(ZN, JN, GROUP * block_table.shape[1]), lead, 1, keepdims=False
     ).reshape(-1)
     spans = lax.dynamic_index_in_dim(lengths.reshape(ZN, JN, GROUP), lead, 1, keepdims=False)
-    spans = spans.reshape(-1)
+    root_tiles = lax.dynamic_index_in_dim(
+        roots_near.reshape(STEPS, ZN, JN, GROUP), lead, 2, keepdims=False
+    )
+    alive = jnp.any(root_tiles[0][:, :, None] == digits, axis=1)
+    spans = jnp.where(alive, spans, 0).reshape(-1)
     listing = jax.ShapeDtypeStruct((SLOTS * JN,), jnp.int32)
     near_list, far_list, counts = pl.pallas_call(
         scan,
@@ -393,9 +397,6 @@
         in_specs=[smem] * 3,
         out_specs=(smem,) * 3,
     )(place, table, spans)
-    root_tiles = lax.dynamic_index_in_dim(
-        roots_near.reshape(STEPS, ZN, JN, GROUP), lead, 2, keepdims=False
-    )
     root_tiles = root_tiles.transpose(1, 0, 2).reshape(ZN, SB)
 
     rows = ZN * SB
@@ -417,8 +418,6 @@
     right = shift(cache, -1)
     across = [shift(left[:half_slots], 1), shift(right[half_slots:], -1)]
     packed = exchange(packed, XC)
-    packed, weights = lax.optimization_barrier((packed, weights))
-    weights = weights + [swap(part) for part in weights]
     stream = packed[:, :half].reshape(XN, CN, ZN // 2, SB, 2, PART).transpose(0, 2, 4, 3, 1, 5)
     stream = stream.reshape(XN, rows, 2 * PART).astype(jnp.float32)
     tails = packed[:, half : half + 2].astype(jnp.float32)
@@ -427,6 +426,8 @@
     squares = jnp.sum(stream * stream, axis=(0, 2))
     squares = jnp.pad(squares, (0, 256 - rows)).reshape(2, 128)
     squares = jnp.sum(spread(squares, "z", ZN), axis=0).reshape(256)[:rows]
+    stream, weights = lax.optimization_barrier((stream, weights))
+    weights = weights + [swap(part) for part in weights]
     inverse = lax.rsqrt(squares / width + EPSILON)
     normed = (stream * inverse[None, :, None] * gain).astype(jnp.bfloat16)
     columns = weights[0].shape[1]
@@ -439,7 +440,10 @@
         scratch_shapes=[pltpu.VMEM((XN, 2 * PART, columns), jnp.bfloat16)],
     )(place, normed, *weights)
     projected = exchange(projected.reshape(ZN, SB, columns), "z")
-    projected, near_list = lax.optimization_barrier((projected, near_list))
+    root_tiles = jnp.broadcast_to(root_tiles[:, :, None], (ZN, SB, HD))
+    projected, near_list, root_tiles = lax.optimization_barrier(
+        (projected, near_list, root_tiles)
+    )
 
     small = jax.ShapeDtypeStruct((len(PAIRS), GROUP, HD), jnp.float32)
     queries, everyone, key_chain, value_chain = pl.pallas_call(
@@ -455,7 +459,6 @@
         out_specs=(vmem,) * 4,
         scratch_shapes=[pltpu.VMEM((ROWS, HD), jnp.float32)],
     )(own_parents.reshape(SB), projected, cosines, sines)
-    root_tiles = jnp.broadcast_to(root_tiles[:, :, None], (ZN, SB, HD))
     near = [part for whole in (cache, left, right) for part in (whole, swap(whole))]
     last = PAIRS.index((STEPS - 1, 0))
     appended = jnp.stack([key_chain[last:], value_chain[last:]], axis=2)
@@ -471,7 +474,7 @@
         pltpu.VMEM((DEPTH,) + cache.shape[1:], jnp.bfloat16),
         pltpu.SemaphoreType.DMA((DEPTH,)),
     ]
-    anywhere = pl.BlockSpec(memory_space=pl.ANY)
+    anywhere = pl.BlockSpec(memory_space=pltpu.HBM)
     before = pl.pallas_call(
         attend_near,
         compiler_params=SMALL,

time: 193 us -> 224 us (1.16)
  waiting for transfers between devices: 25.4 us -> 65.4 us
  starting transfers between devices: 65.4 us -> 53.2 us
  blocking collectives: 43.4 us -> 39.5 us
  local copies, waits for them, and re-layouts: 31.8 us -> 35.4 us
  other arithmetic: 3.83 us -> 7.18 us
    all_to_all x5, waiting for transfers between devices: 7.64 us -> 53.4 us  [exchange(): return lax.all_to_all(value, axis, 0, 0, tiled=True)]
    ppermute x13, starting transfers between devices: 15.5 us -> 4.93 us  [swap(): return lax.ppermute(value, 'core', [(0, 1), (1, 0)])]
    ppermute x10, waiting for transfers between devices: 11.5 us -> 6.07 us  [shift(): return lax.ppermute(value, 'x', [(i, (i + hop) % XN) for i in range(XN)])]
    all_to_all x2, blocking collectives: 43.4 us -> 39.5 us  [exchange(): return lax.all_to_all(value, axis, 0, 0, tiled=True)]
    unnamed x51 -> x39, local copies, waits for them, and re-layouts: 10 us -> 10 us
  transfers between devices with their start and end apart: 31 -> 31, of which waited for: 10 -> 12; matrix products, arithmetic and copies ran while one was open for 13% -> 16% of each run, Pallas kernels for 8% -> 6%
where the time goes in v7:
time: 224 us; the launch traced here: 223 us
  waiting for transfers between devices  65.4 us (29%)
  starting transfers between devices  53.2 us (24%)
  blocking collectives  39.5 us (18%)
  local copies, waits for them, and re-layouts  35.4 us (16%)
  Pallas kernels  20.7 us (9%)
  other arithmetic  7.18 us (3%)
    all_to_all x5, waiting for transfers between devices, exchange(): return lax.all_to_all(value, axis, 0, 0, tiled=True)  53.4 us
    all_to_all x2, blocking collectives, exchange(): return lax.all_to_all(value, axis, 0, 0, tiled=True)  39.5 us
    all_to_all x5, starting transfers between devices, exchange(): return lax.all_to_all(value, axis, 0, 0, tiled=True)  31.3 us
    ppermute x10, starting transfers between devices, shift(): return lax.ppermute(value, 'x', [(i, (i + hop) % XN) for i in range(XN)])  11.9 us
    unnamed x39, local copies, waits for them, and re-layouts  10 us
    pallas_call x1, Pallas kernels, body(): pl.pallas_call(attend_near, compiler_params=SMALL, out_shape=state, in_sp...  6.77 us
    ppermute x10, waiting for transfers between devices, shift(): return lax.ppermute(value, 'x', [(i, (i + hop) % XN) for i in range(XN)])  6.07 us
    convert_element_type x3, local copies, waits for them, and re-layouts, body(): stream = stream.reshape(XN, rows, 2 * PART).astype(jnp.float32)  5.58 us
  transfers between devices with their start and end apart: 31, of which 12 were waited for; matrix products, arithmetic and copies ran while one was open for 16% of the time, Pallas kernels for 6%

profile of v7, /device:TPU:1, one launch (start us, length us, event | category | flops | bytes accessed | tf_op | source)
XLA Modules:
  0.0 222.5 jit_solution(2856604077833936796)
XLA Ops:
  0.6 1.0 pad_maximum_fusion.1.rest_0_
  1.6 2.1 collective-permute-start
  3.7 2.5 %collective-permute-start.1 = (bf16[64,1280]{1,0:T(8,128)(2,1)S(1)}, bf16[64,1280]{1,0:T(8,128)(2,1)S(1)}, u32[]{:S(2)}, u32[]{:S(2)}) collective-permute-start(bf16[64,1280]{1,0:T(8,128)(2,1)S(1)} %pad_maximum_fusion.1.rest_0_), channel_id=1, source_target_pairs={{0,4},{2,6},{4,0},{6,2},{1,5},{3,7},{5,1},{7,3},{8,12},{10,14},{12... | collective-permute-start | bytes 491528 | tf_op jit(solution)/shard_map/ppermute | solution.py:49
  6.2 1.2 collective-permute-start.2
  7.4 1.4 collective-permute-start.7
  8.8 1.2 reduce-precision_convert_fusion.1
  10.0 1.1 copy.103
  13.3 5.6 %all-to-all-start = ((bf16[8,104,128]{2,1,0:T(8,128)(2,1)}), bf16[8,104,128]{2,1,0:T(8,128)(2,1)S(1)}, u32[]{:S(2)}, u32[]{:S(2)}) async-start(bf16[8,104,128]{2,1,0:T(8,128)(2,1)} %pad_maximum_fusion), calls=%async_computation | async-start | bytes 425984 | tf_op jit(solution)/shard_map/all_to_all | solution.py:37
  19.8 41.4 %all-to-all-done = bf16[8,104,128]{2,1,0:T(8,128)(2,1)S(1)} async-done(((bf16[8,104,128]{2,1,0:T(8,128)(2,1)}), bf16[8,104,128]{2,1,0:T(8,128)(2,1)S(1)}, u32[]{:S(2)}, u32[]{:S(2)}) %all-to-all-start) | async-done | bytes 213024 | tf_op jit(solution)/shard_map/all_to_all | solution.py:37
  62.4 8.1 %all-to-all-start.1 = ((f32[8,2,128]{2,1,0:T(2,128)}), f32[8,2,128]{2,1,0:T(2,128)S(1)}, u32[]{:S(2)}, u32[]{:S(2)}) async-start(f32[8,2,128]{2,1,0:T(2,128)} %broadcast_in_dim.78), calls=%async_computation.1 | async-start | bytes 16384 | tf_op jit(solution)/shard_map/all_to_all | solution.py:37
  70.6 1.4 reshape.167
  72.0 2.6 %copy.105 = f32[4,4,2,24,2,64]{5,4,3,2,1,0:T(2,128)} copy(f32[4,4,2,24,2,64]{5,2,3,1,4,0:T(2,128)} %bitcast.60) | data formatting | bytes 786432 | tf_op jit(solution)/shard_map/convert_element_type | solution.py:422
  74.6 1.6 reshape.166.rest_4_
  76.3 1.3 collective-permute-start.3
  78.6 1.0 collective-permute-start.6
  80.6 1.7 shard_map.114
  82.3 1.0 copy-done
  83.3 6.3 %all-to-all-start.2 = ((f32[8,24,1280]{2,1,0:T(8,128)}), f32[8,24,1280]{2,1,0:T(8,128)S(1)}, u32[]{:S(2)}, u32[]{:S(2)}) async-start(f32[8,24,1280]{2,1,0:T(8,128)} %bitcast.48), calls=%async_computation.2 | async-start | bytes 1966080 | tf_op jit(solution)/shard_map/all_to_all | solution.py:37
  89.6 1.4 fusion.12
  93.2 1.4 copy.99
  96.4 0.9 dynamic-slice_add_fusion
  99.1 1.7 copy.97
  100.8 1.7 reshape.153
  103.4 0.9 constant_dynamic-slice_fusion.2
  104.6 1.1 slice.69
  105.7 1.9 collective-permute-start.10
  107.6 2.3 %slice.68 = bf16[16,2,128,128]{3,2,1,0:T(8,128)(2,1)} slice(bf16[32,2,128,128]{3,2,1,0:T(8,128)(2,1)} %collective-permute-done.7.rest_2_), slice={[0:16], [0:2], [0:128], [0:128]} | slice | bytes 2097152 | tf_op jit(solution)/shard_map/slice | solution.py:419
  109.9 0.9 collective-permute-start.14
  110.9 1.1 copy.108
  114.1 4.7 %shard_map.113 = (s32[256]{0:T(256)S(1)}, s32[256]{0:T(256)S(1)}, s32[2]{0:T(128)S(1)}) custom-call(s32[4]{0:T(128)S(1)} %pad_add_fusion.place_ref, s32[4096]{0:T(1024)S(1)} %bitcast.59, s32[64]{0:T(128)S(1)} %broadcast_select_fusion.length_ref), custom_call_target="tpu_custom_call" | custom-call | tf_op jit(solution)/shard_map/pallas_call | solution.py:393
  121.6 22.0 %all_to_all.35.q_ref = bf16[8,192,128]{2,1,0:T(8,128)(2,1)S(1)} all-to-all(bf16[8,192,128]{2,1,0:T(8,128)(2,1)S(1)} %get-tuple-element.49), channel_id=1, replica_groups=mesh['kv'=4,'z'=8,'x'=4,'core'=2] {'z'}, dimensions={0} | all-to-all | bytes 786432 | tf_op jit(solution)/shard_map/all_to_all | solution.py:37
  144.1 1.6 copy-done.1
  147.0 6.8 %shard_map.116 = (f32[8,192,128]{2,1,0:T(8,128)S(1)}, f32[8,192,128]{2,1,0:T(8,128)S(1)}, f32[8,192,128]{2,1,0:T(8,128)S(1)}) custom-call(s32[256]{0:T(256)S(1)} %copy-done.13, s32[2]{0:T(128)S(1)} %copy-done.9, s32[64]{0:T(128)S(1)} %broadcast_select_fusion.length_ref, bf16[8,192,128]{2,1,0:T(8,128)(2,1)S(1)} %all_to_all.35.q_ref, ...), custom_call_target="tpu_custom_call" | custom-call | flops 1 | bytes 1 | tf_op jit(solution)/shard_map/pallas_call | solution.py:478
  153.8 3.8 %shard_map.117 = bf16[8,216,128]{2,1,0:T(8,128)(2,1)} custom-call(s32[256]{0:T(256)S(1)} %copy-done.11, s32[2]{0:T(128)S(1)} %copy-done.9, s32[64]{0:T(128)S(1)} %broadcast_select_fusion.length_ref, bf16[8,192,128]{2,1,0:T(8,128)(2,1)S(1)} %all_to_all.35.q_ref, s32[8,24,128]{2,1,0:T(8,128)S(1)} %broadcast_in_dim.80.root_ref, ...), custom_call_target="tpu_custom_call" | custom-call | tf_op jit(solution)/shard_map/pallas_call | solution.py:487
  157.7 4.5 %all-to-all-start.4 = ((bf16[8,216,128]{2,1,0:T(8,128)(2,1)}), bf16[8,216,128]{2,1,0:T(8,128)(2,1)S(1)}, u32[]{:S(2)}, u32[]{:S(2)}) async-start(bf16[8,216,128]{2,1,0:T(8,128)(2,1)} %shard_map.117), calls=%async_computation.4 | async-start | bytes 884736 | tf_op jit(solution)/shard_map/all_to_all | solution.py:37
  162.4 2.6 %collective-permute-start.18 = (bf16[64,1024]{1,0:T(8,128)(2,1)S(1)}, bf16[64,1024]{1,0:T(8,128)(2,1)S(1)}, u32[]{:S(2)}, u32[]{:S(2)}) collective-permute-start(bf16[64,1024]{1,0:T(8,128)(2,1)S(1)} %bitcast.56), channel_id=1, source_target_pairs={{0,6},{2,0},{4,2},{6,4},{1,7},{3,1},{5,3},{7,5},{8,14},{10,8},{12,... | collective-permute-start | bytes 393224 | tf_op jit(solution)/shard_map/ppermute | solution.py:49
  165.0 5.7 %collective-permute-done.16.rest_1_ = bf16[64,1024]{1,0:T(8,128)(2,1)S(1)} collective-permute-done((bf16[64,1024]{1,0:T(8,128)(2,1)S(1)}, bf16[64,1024]{1,0:T(8,128)(2,1)S(1)}, u32[]{:S(2)}, u32[]{:S(2)}) %collective-permute-start.16) | collective-permute-done | bytes 131104 | tf_op jit(solution)/shard_map/ppermute | solution.py:49
  172.9 4.4 %all-to-all-done.4.parts_ref = bf16[8,216,128]{2,1,0:T(8,128)(2,1)S(1)} async-done(((bf16[8,216,128]{2,1,0:T(8,128)(2,1)}), bf16[8,216,128]{2,1,0:T(8,128)(2,1)S(1)}, u32[]{:S(2)}, u32[]{:S(2)}) %all-to-all-start.4) | async-done | bytes 442400 | tf_op jit(solution)/shard_map/all_to_all | solution.py:37
  177.9 17.5 %all_to_all.36 = bf16[8,24,1024]{2,1,0:T(8,128)(2,1)S(1)} all-to-all(bf16[8,24,1024]{2,1,0:T(8,128)(2,1)S(1)} %shard_map.118), channel_id=1, replica_groups=mesh['kv'=4,'z'=8,'x'=4,'core'=2] {'z'}, dimensions={0} | all-to-all | bytes 786432 | tf_op jit(solution)/shard_map/all_to_all | solution.py:37
  195.4 1.2 shard_map.119
  196.6 1.4 collective-permute-start.23
  198.0 2.6 %collective-permute-start.24 = (f32[4,48,128]{2,1,0:T(8,128)S(1)}, f32[4,48,128]{2,1,0:T(8,128)S(1)}, u32[]{:S(2)}, u32[]{:S(2)}) collective-permute-start(f32[4,48,128]{2,1,0:T(8,128)S(1)} %get-tuple-element.74), channel_id=1, source_target_pairs={{0,128},{64,192},{128,0},{192,64},{1,129},{65,193},{129,1},{193,65... | collective-permute-start | bytes 294920 | tf_op jit(solution)/shard_map/ppermute | solution.py:521
  200.6 1.1 collective-permute-start.25
  201.8 3.2 %collective-permute-done.24.rest_2_ = f32[4,48,128]{2,1,0:T(8,128)S(1)} collective-permute-done((f32[4,48,128]{2,1,0:T(8,128)S(1)}, f32[4,48,128]{2,1,0:T(8,128)S(1)}, u32[]{:S(2)}, u32[]{:S(2)}) %collective-permute-start.24) | collective-permute-done | bytes 98336 | tf_op jit(solution)/shard_map/ppermute | solution.py:521
  205.0 1.3 shard_map.120
  206.3 6.8 %all-to-all-start.6 = ((bf16[32,24,128]{2,1,0:T(8,128)(2,1)}), bf16[32,24,128]{2,1,0:T(8,128)(2,1)S(1)}, u32[]{:S(2)}, u32[]{:S(2)}) async-start(bf16[32,24,128]{2,1,0:T(8,128)(2,1)} %bitcast.26), calls=%async_computation.6 | async-start | bytes 393216 | tf_op jit(solution)/shard_map/all_to_all | solution.py:37
  213.8 7.6 %all-to-all-done.6 = bf16[32,24,128]{2,1,0:T(8,128)(2,1)S(1)} async-done(((bf16[32,24,128]{2,1,0:T(8,128)(2,1)}), bf16[32,24,128]{2,1,0:T(8,128)(2,1)S(1)}, u32[]{:S(2)}, u32[]{:S(2)}) %all-to-all-start.6) | async-done | bytes 196640 | tf_op jit(solution)/shard_map/all_to_all | solution.py:37
  221.7 0.8 copy.112
  (134 shorter events, 24.0 us)
Async XLA Ops:
  0.6 18.3 %copy-start.16 = (s32[3,512]{1,0:T(4,128)S(1)}, s32[3,512]{1,0:T(4,128)}, u32[]{:S(2)}) copy-start(s32[3,512]{1,0:T(4,128)} %param.19) | copy-start | bytes 18436
  1.6 74.6 %collective-permute-start = (bf16[64,1280]{1,0:T(8,128)(2,1)S(1)}, bf16[64,1280]{1,0:T(8,128)(2,1)S(1)}, u32[]{:S(2)}, u32[]{:S(2)}) collective-permute-start(bf16[64,1280]{1,0:T(8,128)(2,1)S(1)} %pad_maximum_fusion.1.rest_0_), channel_id=1, source_target_pairs={{0,2},{2,4},{4,6},{6,0},{1,3},{3,5},{5,7},{7,1},{8,10},{10,12},{12... | collective-permute-start | bytes 491528 | tf_op jit(solution)/shard_map/ppermute | solution.py:49
  3.7 72.5 %collective-permute-start.1 = (bf16[64,1280]{1,0:T(8,128)(2,1)S(1)}, bf16[64,1280]{1,0:T(8,128)(2,1)S(1)}, u32[]{:S(2)}, u32[]{:S(2)}) collective-permute-start(bf16[64,1280]{1,0:T(8,128)(2,1)S(1)} %pad_maximum_fusion.1.rest_0_), channel_id=1, source_target_pairs={{0,4},{2,6},{4,0},{6,2},{1,5},{3,7},{5,1},{7,3},{8,12},{10,14},{12... | collective-permute-start | bytes 491528 | tf_op jit(solution)/shard_map/ppermute | solution.py:49
  6.2 70.0 %collective-permute-start.2 = (bf16[64,1280]{1,0:T(8,128)(2,1)S(1)}, bf16[64,1280]{1,0:T(8,128)(2,1)S(1)}, u32[]{:S(2)}, u32[]{:S(2)}) collective-permute-start(bf16[64,1280]{1,0:T(8,128)(2,1)S(1)} %pad_maximum_fusion.1.rest_0_), channel_id=1, source_target_pairs={{0,6},{2,0},{4,2},{6,4},{1,7},{3,1},{5,3},{7,5},{8,14},{10,8},{12,... | collective-permute-start | bytes 491528 | tf_op jit(solution)/shard_map/ppermute | solution.py:49
  7.3 97.2 %collective-permute-start.9 = (bf16[32,2,128,128]{3,2,1,0:T(8,128)(2,1)}, bf16[32,2,128,128]{3,2,1,0:T(8,128)(2,1)S(1)}, u32[]{:S(2)}, u32[]{:S(2)}) collective-permute-start(bf16[32,2,128,128]{3,2,1,0:T(8,128)(2,1)} %bitcast.49), channel_id=1, source_target_pairs={{0,6},{2,0},{4,2},{6,4},{1,7},{3,1},{5,3},{7,5},{8,14},{10,8},{12,... | collective-permute-start | bytes 6291464 | tf_op jit(solution)/shard_map/ppermute | solution.py:49
  7.4 100.2 %collective-permute-start.7 = (bf16[32,2,128,128]{3,2,1,0:T(8,128)(2,1)}, bf16[32,2,128,128]{3,2,1,0:T(8,128)(2,1)}, u32[]{:S(2)}, u32[]{:S(2)}) collective-permute-start(bf16[32,2,128,128]{3,2,1,0:T(8,128)(2,1)} %bitcast.50), channel_id=1, source_target_pairs={{0,2},{2,4},{4,6},{6,0},{1,3},{3,5},{5,7},{7,1},{8,10},{10,12},{12... | collective-permute-start | bytes 6291464 | tf_op jit(solution)/shard_map/ppermute | solution.py:49
  13.3 47.9 %all-to-all-start = ((bf16[8,104,128]{2,1,0:T(8,128)(2,1)}), bf16[8,104,128]{2,1,0:T(8,128)(2,1)S(1)}, u32[]{:S(2)}, u32[]{:S(2)}) async-start(bf16[8,104,128]{2,1,0:T(8,128)(2,1)} %pad_maximum_fusion), calls=%async_computation | async-start | bytes 425984 | tf_op jit(solution)/shard_map/all_to_all | solution.py:37
  62.4 15.7 %all-to-all-start.1 = ((f32[8,2,128]{2,1,0:T(2,128)}), f32[8,2,128]{2,1,0:T(2,128)S(1)}, u32[]{:S(2)}, u32[]{:S(2)}) async-start(f32[8,2,128]{2,1,0:T(2,128)} %broadcast_in_dim.78), calls=%async_computation.1 | async-start | bytes 16384 | tf_op jit(solution)/shard_map/all_to_all | solution.py:37
  76.3 2.3 %collective-permute-start.3 = (bf16[64,1280]{1,0:T(8,128)(2,1)S(1)}, bf16[64,1280]{1,0:T(8,128)(2,1)S(1)}, u32[]{:S(2)}, u32[]{:S(2)}) collective-permute-start(bf16[64,1280]{1,0:T(8,128)(2,1)S(1)} %pad_maximum_fusion.1.rest_0_), channel_id=1, source_target_pairs={{0,1},{1,0},{2,3},{3,2},{4,5},{5,4},{6,7},{7,6},{8,9},{9,8},{10,11... | collective-permute-start | bytes 491528 | tf_op jit(solution)/shard_map/ppermute | solution.py:45
  77.6 2.1 collective-permute-start.4
  77.7 2.1 collective-permute-start.5
  78.6 2.0 collective-permute-start.6
  79.7 11.3 %copy-start.15 = (s32[512]{0:T(512)S(1)}, s32[512]{0:T(512)}, u32[]{:S(2)}) copy-start(s32[512]{0:T(512)} %param.17) | copy-start | bytes 6148
  79.7 64.4 %collective-permute-start.13 = (bf16[32,2,128,128]{3,2,1,0:T(8,128)(2,1)}, bf16[32,2,128,128]{3,2,1,0:T(8,128)(2,1)}, u32[]{:S(2)}, u32[]{:S(2)}) collective-permute-start(bf16[32,2,128,128]{3,2,1,0:T(8,128)(2,1)} %bitcast.51), channel_id=1, source_target_pairs={{0,1},{1,0},{2,3},{3,2},{4,5},{5,4},{6,7},{7,6},{8,9},{9,8},{10,11... | collective-permute-start | bytes 6291464 | tf_op jit(solution)/shard_map/ppermute | solution.py:45
  82.3 1.0 copy-start
  83.3 36.1 %all-to-all-start.2 = ((f32[8,24,1280]{2,1,0:T(8,128)}), f32[8,24,1280]{2,1,0:T(8,128)S(1)}, u32[]{:S(2)}, u32[]{:S(2)}) async-start(f32[8,24,1280]{2,1,0:T(8,128)} %bitcast.48), calls=%async_computation.2 | async-start | bytes 1966080 | tf_op jit(solution)/shard_map/all_to_all | solution.py:37
  97.2 0.6 copy-start.14
  105.7 37.9 %collective-permute-start.10 = (bf16[16,2,128,128]{3,2,1,0:T(8,128)(2,1)}, bf16[16,2,128,128]{3,2,1,0:T(8,128)(2,1)}, u32[]{:S(2)}, u32[]{:S(2)}) collective-permute-start(bf16[16,2,128,128]{3,2,1,0:T(8,128)(2,1)} %slice.69), channel_id=1, source_target_pairs={{0,6},{2,0},{4,2},{6,4},{1,7},{3,1},{5,3},{7,5},{8,14},{10,8},{12,... | collective-permute-start | bytes 3145736 | tf_op jit(solution)/shard_map/ppermute | solution.py:49
  109.9 33.6 %collective-permute-start.8 = (bf16[16,2,128,128]{3,2,1,0:T(8,128)(2,1)}, bf16[16,2,128,128]{3,2,1,0:T(8,128)(2,1)}, u32[]{:S(2)}, u32[]{:S(2)}) collective-permute-start(bf16[16,2,128,128]{3,2,1,0:T(8,128)(2,1)} %slice.68), channel_id=1, source_target_pairs={{0,2},{2,4},{4,6},{6,0},{1,3},{3,5},{5,7},{7,1},{8,10},{10,12},{12... | collective-permute-start | bytes 3145736 | tf_op jit(solution)/shard_map/ppermute | solution.py:49
  109.9 34.1 %collective-permute-start.14 = (bf16[32,2,128,128]{3,2,1,0:T(8,128)(2,1)}, bf16[32,2,128,128]{3,2,1,0:T(8,128)(2,1)}, u32[]{:S(2)}, u32[]{:S(2)}) collective-permute-start(bf16[32,2,128,128]{3,2,1,0:T(8,128)(2,1)} %collective-permute-done.7.rest_2_), channel_id=1, source_target_pairs={{0,1},{1,0},{2,3},{3,2},{4,5},{5,4},{6,7},{7,6},{8,9},{9,8},{10,11... | collective-permute-start | bytes 6291464 | tf_op jit(solution)/shard_map/ppermute | solution.py:45
  110.9 33.2 %collective-permute-start.15 = (bf16[32,2,128,128]{3,2,1,0:T(8,128)(2,1)S(1)}, bf16[32,2,128,128]{3,2,1,0:T(8,128)(2,1)}, u32[]{:S(2)}, u32[]{:S(2)}) collective-permute-start(bf16[32,2,128,128]{3,2,1,0:T(8,128)(2,1)S(1)} %collective-permute-done.9.rest_4_), channel_id=1, source_target_pairs={{0,1},{1,0},{2,3},{3,2},{4,5},{5,4},{6,7},{7,6},{8,9},{9,8},{10,11... | collective-permute-start | bytes 6291464 | tf_op jit(solution)/shard_map/ppermute | solution.py:45
  118.8 0.5 copy-start.12
  118.8 0.6 copy-start.8
  118.8 0.6 copy-start.10
  120.2 0.7 copy-start.7
  121.6 22.5 %copy-start.3 = (f32[6,8,128]{2,1,0:T(8,128)}, f32[6,8,128]{2,1,0:T(8,128)S(1)}, u32[]{:S(2)}) copy-start(f32[6,8,128]{2,1,0:T(8,128)S(1)} %get-tuple-element.63.v_ref) | copy-start | bytes 73732
  121.6 22.5 %copy-start.5 = (f32[6,8,128]{2,1,0:T(8,128)}, f32[6,8,128]{2,1,0:T(8,128)S(1)}, u32[]{:S(2)}) copy-start(f32[6,8,128]{2,1,0:T(8,128)S(1)} %get-tuple-element.62.k_ref) | copy-start | bytes 73732
  143.6 10.2 %collective-permute-start.11 = (bf16[16,2,128,128]{3,2,1,0:T(8,128)(2,1)}, bf16[16,2,128,128]{3,2,1,0:T(8,128)(2,1)S(1)}, u32[]{:S(2)}, u32[]{:S(2)}) collective-permute-start(bf16[16,2,128,128]{3,2,1,0:T(8,128)(2,1)} %collective-permute-done.8.rest_0_), channel_id=1, source_target_pairs={{0,1},{1,0},{2,3},{3,2},{4,5},{5,4},{6,7},{7,6},{8,9},{9,8},{10,11... | collective-permute-start | bytes 3145736 | tf_op jit(solution)/shard_map/ppermute | solution.py:45
  144.0 9.8 %collective-permute-start.12 = (bf16[16,2,128,128]{3,2,1,0:T(8,128)(2,1)}, bf16[16,2,128,128]{3,2,1,0:T(8,128)(2,1)S(1)}, u32[]{:S(2)}, u32[]{:S(2)}) collective-permute-start(bf16[16,2,128,128]{3,2,1,0:T(8,128)(2,1)} %collective-permute-done.10.rest_1_), channel_id=1, source_target_pairs={{0,1},{1,0},{2,3},{3,2},{4,5},{5,4},{6,7},{7,6},{8,9},{9,8},{10,11... | collective-permute-start | bytes 3145736 | tf_op jit(solution)/shard_map/ppermute | solution.py:45
  144.1 1.6 copy-start.1
  145.7 0.7 copy-start.9
  146.4 0.6 copy-start.13
  147.0 6.8 %copy-start.11 = (s32[256]{0:T(256)S(1)}, s32[256]{0:T(256)}, u32[]{:S(2)}) copy-start(s32[256]{0:T(256)} %copy-done.10) | copy-start | bytes 3076
  153.8 8.4 %copy-start.2 = (bf16[1024,64]{0,1:T(8,128)(2,1)S(1)}, bf16[1024,64]{0,1:T(8,128)(2,1)}, u32[]{:S(2)}) copy-start(bf16[1024,64]{0,1:T(8,128)(2,1)} %param.15) | copy-start | bytes 393220
  153.8 23.5 %copy-start.4 = (f32[6,8,128]{2,1,0:T(8,128)S(1)}, f32[6,8,128]{2,1,0:T(8,128)}, u32[]{:S(2)}) copy-start(f32[6,8,128]{2,1,0:T(8,128)} %copy-done.3) | copy-start | bytes 73732
  153.8 23.5 %copy-start.6 = (f32[6,8,128]{2,1,0:T(8,128)S(1)}, f32[6,8,128]{2,1,0:T(8,128)}, u32[]{:S(2)}) copy-start(f32[6,8,128]{2,1,0:T(8,128)} %copy-done.5) | copy-start | bytes 73732
  157.7 19.7 %all-to-all-start.4 = ((bf16[8,216,128]{2,1,0:T(8,128)(2,1)}), bf16[8,216,128]{2,1,0:T(8,128)(2,1)S(1)}, u32[]{:S(2)}, u32[]{:S(2)}) async-start(bf16[8,216,128]{2,1,0:T(8,128)(2,1)} %shard_map.117), calls=%async_computation.4 | async-start | bytes 884736 | tf_op jit(solution)/shard_map/all_to_all | solution.py:37
  162.2 8.4 %collective-permute-start.16 = (bf16[64,1024]{1,0:T(8,128)(2,1)S(1)}, bf16[64,1024]{1,0:T(8,128)(2,1)S(1)}, u32[]{:S(2)}, u32[]{:S(2)}) collective-permute-start(bf16[64,1024]{1,0:T(8,128)(2,1)S(1)} %bitcast.54), channel_id=1, source_target_pairs={{0,2},{2,4},{4,6},{6,0},{1,3},{3,5},{5,7},{7,1},{8,10},{10,12},{12... | collective-permute-start | bytes 393224 | tf_op jit(solution)/shard_map/ppermute | solution.py:49
  162.3 8.3 %collective-permute-start.17 = (bf16[64,1024]{1,0:T(8,128)(2,1)S(1)}, bf16[64,1024]{1,0:T(8,128)(2,1)S(1)}, u32[]{:S(2)}, u32[]{:S(2)}) collective-permute-start(bf16[64,1024]{1,0:T(8,128)(2,1)S(1)} %bitcast.55), channel_id=1, source_target_pairs={{0,4},{2,6},{4,0},{6,2},{1,5},{3,7},{5,1},{7,3},{8,12},{10,14},{12... | collective-permute-start | bytes 393224 | tf_op jit(solution)/shard_map/ppermute | solution.py:49
  162.4 9.1 %collective-permute-start.18 = (bf16[64,1024]{1,0:T(8,128)(2,1)S(1)}, bf16[64,1024]{1,0:T(8,128)(2,1)S(1)}, u32[]{:S(2)}, u32[]{:S(2)}) collective-permute-start(bf16[64,1024]{1,0:T(8,128)(2,1)S(1)} %bitcast.56), channel_id=1, source_target_pairs={{0,6},{2,0},{4,2},{6,4},{1,7},{3,1},{5,3},{7,5},{8,14},{10,8},{12,... | collective-permute-start | bytes 393224 | tf_op jit(solution)/shard_map/ppermute | solution.py:49
  165.0 6.7 %collective-permute-start.19 = (bf16[64,1024]{1,0:T(8,128)(2,1)S(1)}, bf16[64,1024]{1,0:T(8,128)(2,1)S(1)}, u32[]{:S(2)}, u32[]{:S(2)}) collective-permute-start(bf16[64,1024]{1,0:T(8,128)(2,1)S(1)} %bitcast.57), channel_id=1, source_target_pairs={{0,1},{1,0},{2,3},{3,2},{4,5},{5,4},{6,7},{7,6},{8,9},{9,8},{10,11... | collective-permute-start | bytes 393224 | tf_op jit(solution)/shard_map/ppermute | solution.py:45
  170.6 1.3 collective-permute-start.20
  170.6 1.5 collective-permute-start.21
  171.5 1.3 collective-permute-start.22
  196.6 5.2 %collective-permute-start.23 = (f32[4,48,128]{2,1,0:T(8,128)S(1)}, f32[4,48,128]{2,1,0:T(8,128)S(1)}, u32[]{:S(2)}, u32[]{:S(2)}) collective-permute-start(f32[4,48,128]{2,1,0:T(8,128)S(1)} %get-tuple-element.73), channel_id=1, source_target_pairs={{0,64},{64,128},{128,192},{192,0},{1,65},{65,129},{129,193},{193,1... | collective-permute-start | bytes 294920 | tf_op jit(solution)/shard_map/ppermute | solution.py:521
  198.0 7.1 %collective-permute-start.24 = (f32[4,48,128]{2,1,0:T(8,128)S(1)}, f32[4,48,128]{2,1,0:T(8,128)S(1)}, u32[]{:S(2)}, u32[]{:S(2)}) collective-permute-start(f32[4,48,128]{2,1,0:T(8,128)S(1)} %get-tuple-element.74), channel_id=1, source_target_pairs={{0,128},{64,192},{128,0},{192,64},{1,129},{65,193},{129,1},{193,65... | collective-permute-start | bytes 294920 | tf_op jit(solution)/shard_map/ppermute | solution.py:521
  200.6 4.4 %collective-permute-start.25 = (f32[4,48,128]{2,1,0:T(8,128)S(1)}, f32[4,48,128]{2,1,0:T(8,128)S(1)}, u32[]{:S(2)}, u32[]{:S(2)}) collective-permute-start(f32[4,48,128]{2,1,0:T(8,128)S(1)} %get-tuple-element.75), channel_id=1, source_target_pairs={{0,192},{64,0},{128,64},{192,128},{1,193},{65,1},{129,65},{193,129... | collective-permute-start | bytes 294920 | tf_op jit(solution)/shard_map/ppermute | solution.py:521
  206.3 15.1 %all-to-all-start.6 = ((bf16[32,24,128]{2,1,0:T(8,128)(2,1)}), bf16[32,24,128]{2,1,0:T(8,128)(2,1)S(1)}, u32[]{:S(2)}, u32[]{:S(2)}) async-start(bf16[32,24,128]{2,1,0:T(8,128)(2,1)} %bitcast.26), calls=%async_computation.6 | async-start | bytes 393216 | tf_op jit(solution)/shard_map/all_to_all | solution.py:37

commit v8 on v7

--- a/solution.py
+++ b/solution.py
@@ -412,11 +412,7 @@
     gain_rows = jnp.concatenate([gain_rows, jnp.zeros((6, HD), jnp.bfloat16)])
     packed = jnp.concatenate([by_row, jnp.broadcast_to(gain_rows[None], (JN, 8, HD))], axis=1)
     weights = jnp.concatenate([w_query, w_key, w_value], axis=1)
-    cache, weights = lax.optimization_barrier((cache, weights))
     weights = ring(weights)
-    left = shift(cache, 1)
-    right = shift(cache, -1)
-    across = [shift(left[:half_slots], 1), shift(right[half_slots:], -1)]
     packed = exchange(packed, XC)
     stream = packed[:, :half].reshape(XN, CN, ZN // 2, SB, 2, PART).transpose(0, 2, 4, 3, 1, 5)
     stream = stream.reshape(XN, rows, 2 * PART).astype(jnp.float32)
@@ -425,6 +421,10 @@
     gain = gain.reshape(XN, 1, 2 * PART)
     squares = jnp.sum(stream * stream, axis=(0, 2))
     squares = jnp.pad(squares, (0, 256 - rows)).reshape(2, 128)
+    cache, squares = lax.optimization_barrier((cache, squares))
+    left = shift(cache, 1)
+    right = shift(cache, -1)
+    across = [shift(left[:half_slots], 1), shift(right[half_slots:], -1)]
     squares = jnp.sum(spread(squares, "z", ZN), axis=0).reshape(256)[:rows]
     stream, weights = lax.optimization_barrier((stream, weights))
     weights = weights + [swap(part) for part in weights]

time: 224 us -> 191 us (0.85)
  waiting for transfers between devices: 65.4 us -> 19.7 us
  starting transfers between devices: 53.2 us -> 70.1 us
  Pallas kernels: 20.7 us -> 13.8 us
  local copies, waits for them, and re-layouts: 35.4 us -> 37.7 us
    all_to_all x5, waiting for transfers between devices: 53.4 us -> 12.8 us  [exchange(): return lax.all_to_all(value, axis, 0, 0, tiled=True)]
    ppermute x13, starting transfers between devices: 4.93 us -> 15.6 us  [swap(): return lax.ppermute(value, 'core', [(0, 1), (1, 0)])]
    ppermute x10, waiting for transfers between devices: 6.07 us -> 1.04 us  [shift(): return lax.ppermute(value, 'x', [(i, (i + hop) % XN) for i in range(XN)])]
    pallas_call x1, Pallas kernels: 6.77 us -> 2.72 us  [body(): pl.pallas_call(attend_near, compiler_params=SMALL, out_shape=state, in_sp...]
    all_to_all x5, starting transfers between devices: 31.3 us -> 34.6 us  [exchange(): return lax.all_to_all(value, axis, 0, 0, tiled=True)]
    ppermute x10, starting transfers between devices: 11.9 us -> 14.7 us  [shift(): return lax.ppermute(value, 'x', [(i, (i + hop) % XN) for i in range(XN)])]
    unnamed x39 -> x41, local copies, waits for them, and re-layouts: 10 us -> 11.7 us
  transfers between devices with their start and end apart: 31 -> 31, of which waited for: 12 -> 9; matrix products, arithmetic and copies ran while one was open for 16% -> 18% of each run, Pallas kernels for 6% -> 5%
where the time goes in v8:
time: 191 us; the launch traced here: 189 us
  starting transfers between devices  70.1 us (37%)
  blocking collectives  41.7 us (22%)
  local copies, waits for them, and re-layouts  37.7 us (20%)
  waiting for transfers between devices  19.7 us (10%)
  Pallas kernels  13.8 us (7%)
  other arithmetic  5.07 us (3%)
    all_to_all x2, blocking collectives, exchange(): return lax.all_to_all(value, axis, 0, 0, tiled=True)  41.7 us
    all_to_all x5, starting transfers between devices, exchange(): return lax.all_to_all(value, axis, 0, 0, tiled=True)  34.6 us
    ppermute x13, starting transfers between devices, swap(): return lax.ppermute(value, 'core', [(0, 1), (1, 0)])  15.6 us
    ppermute x10, starting transfers between devices, shift(): return lax.ppermute(value, 'x', [(i, (i + hop) % XN) for i in range(XN)])  14.7 us
    all_to_all x5, waiting for transfers between devices, exchange(): return lax.all_to_all(value, axis, 0, 0, tiled=True)  12.8 us
    unnamed x41, local copies, waits for them, and re-layouts  11.7 us
    convert_element_type x3, local copies, waits for them, and re-layouts, body(): stream = stream.reshape(XN, rows, 2 * PART).astype(jnp.float32)  5.58 us
    ppermute x3, starting transfers between devices, body(): lax.ppermute(shares[far], 'kv', [(i, (i + far) % KN) for i in range(KN)])  5.06 us
  transfers between devices with their start and end apart: 31, of which 9 were waited for; matrix products, arithmetic and copies ran while one was open for 18% of the time, Pallas kernels for 5%

profile of v8, /device:TPU:1, one launch (start us, length us, event | category | flops | bytes accessed | tf_op | source)
XLA Modules:
  0.0 189.1 jit_solution(17764409352997665556)
XLA Ops:
  3.0 2.0 %collective-permute-start = (bf16[64,1280]{1,0:T(8,128)(2,1)S(1)}, bf16[64,1280]{1,0:T(8,128)(2,1)S(1)}, u32[]{:S(2)}, u32[]{:S(2)}) collective-permute-start(bf16[64,1280]{1,0:T(8,128)(2,1)S(1)} %constant_dynamic-update-slice_fusion.rest_0_), channel_id=1, source_target_pairs={{0,2},{2,4},{4,6},{6,0},{1,3},{3,5},{5,7},{7,1},{8,10},{10,12},{12... | collective-permute-start | bytes 491528 | tf_op jit(solution)/shard_map/ppermute | solution.py:49
  5.1 2.5 %collective-permute-start.1 = (bf16[64,1280]{1,0:T(8,128)(2,1)S(1)}, bf16[64,1280]{1,0:T(8,128)(2,1)S(1)}, u32[]{:S(2)}, u32[]{:S(2)}) collective-permute-start(bf16[64,1280]{1,0:T(8,128)(2,1)S(1)} %constant_dynamic-update-slice_fusion.rest_0_), channel_id=1, source_target_pairs={{0,4},{2,6},{4,0},{6,2},{1,5},{3,7},{5,1},{7,3},{8,12},{10,14},{12... | collective-permute-start | bytes 491528 | tf_op jit(solution)/shard_map/ppermute | solution.py:49
  7.5 1.2 collective-permute-start.2
  9.3 1.1 copy.103
  12.0 5.0 %all-to-all-start = ((bf16[8,104,128]{2,1,0:T(8,128)(2,1)}), bf16[8,104,128]{2,1,0:T(8,128)(2,1)S(1)}, u32[]{:S(2)}, u32[]{:S(2)}) async-start(bf16[8,104,128]{2,1,0:T(8,128)(2,1)} %pad_maximum_fusion), calls=%async_computation | async-start | bytes 425984 | tf_op jit(solution)/shard_map/all_to_all | solution.py:37
  18.0 5.1 %all-to-all-done = bf16[8,104,128]{2,1,0:T(8,128)(2,1)S(1)} async-done(((bf16[8,104,128]{2,1,0:T(8,128)(2,1)}), bf16[8,104,128]{2,1,0:T(8,128)(2,1)S(1)}, u32[]{:S(2)}, u32[]{:S(2)}) %all-to-all-start) | async-done | bytes 213024 | tf_op jit(solution)/shard_map/all_to_all | solution.py:37
  23.7 1.0 collective-permute-start.9
  25.8 8.0 %all-to-all-start.1 = ((f32[8,2,128]{2,1,0:T(2,128)}), f32[8,2,128]{2,1,0:T(2,128)S(1)}, u32[]{:S(2)}, u32[]{:S(2)}) async-start(f32[8,2,128]{2,1,0:T(2,128)} %broadcast_in_dim.76), calls=%async_computation.1 | async-start | bytes 16384 | tf_op jit(solution)/shard_map/all_to_all | solution.py:37
  33.9 1.4 reshape.171
  35.3 2.6 %copy.105 = f32[4,4,2,24,2,64]{5,4,3,2,1,0:T(2,128)} copy(f32[4,4,2,24,2,64]{5,2,3,1,4,0:T(2,128)} %bitcast.60) | data formatting | bytes 786432 | tf_op jit(solution)/shard_map/convert_element_type | solution.py:418
  37.9 1.6 reshape.170.rest_4_
  39.6 1.8 collective-permute-start.3
  42.5 1.0 collective-permute-start.6
  44.5 1.7 shard_map.114
  46.2 1.0 copy-done
  47.2 6.3 %all-to-all-start.2 = ((f32[8,24,1280]{2,1,0:T(8,128)}), f32[8,24,1280]{2,1,0:T(8,128)S(1)}, u32[]{:S(2)}, u32[]{:S(2)}) async-start(f32[8,24,1280]{2,1,0:T(8,128)} %bitcast.48), calls=%async_computation.2 | async-start | bytes 1966080 | tf_op jit(solution)/shard_map/all_to_all | solution.py:37
  53.5 1.4 fusion.12
  57.1 1.4 copy.99
  62.9 1.7 copy.97
  64.7 1.7 reshape.156
  69.2 1.0 collective-permute-done.9.rest_4_
  70.2 1.0 slice.69
  71.2 2.0 %collective-permute-start.10 = (bf16[16,2,128,128]{3,2,1,0:T(8,128)(2,1)}, bf16[16,2,128,128]{3,2,1,0:T(8,128)(2,1)}, u32[]{:S(2)}, u32[]{:S(2)}) collective-permute-start(bf16[16,2,128,128]{3,2,1,0:T(8,128)(2,1)} %slice.69), channel_id=1, source_target_pairs={{0,6},{2,0},{4,2},{6,4},{1,7},{3,1},{5,3},{7,5},{8,14},{10,8},{12,... | collective-permute-start | bytes 3145736 | tf_op jit(solution)/shard_map/ppermute | solution.py:49
  73.2 2.3 %slice.68 = bf16[16,2,128,128]{3,2,1,0:T(8,128)(2,1)} slice(bf16[32,2,128,128]{3,2,1,0:T(8,128)(2,1)} %collective-permute-done.7.rest_2_), slice={[0:16], [0:2], [0:128], [0:128]} | slice | bytes 2097152 | tf_op jit(solution)/shard_map/slice | solution.py:427
  75.6 2.2 %collective-permute-start.14 = (bf16[32,2,128,128]{3,2,1,0:T(8,128)(2,1)}, bf16[32,2,128,128]{3,2,1,0:T(8,128)(2,1)}, u32[]{:S(2)}, u32[]{:S(2)}) collective-permute-start(bf16[32,2,128,128]{3,2,1,0:T(8,128)(2,1)} %collective-permute-done.7.rest_2_), channel_id=1, source_target_pairs={{0,1},{1,0},{2,3},{3,2},{4,5},{5,4},{6,7},{7,6},{8,9},{9,8},{10,11... | collective-permute-start | bytes 6291464 | tf_op jit(solution)/shard_map/ppermute | solution.py:45
  77.8 1.1 copy.108
  81.0 3.7 %shard_map.113 = (s32[256]{0:T(256)S(1)}, s32[256]{0:T(256)S(1)}, s32[2]{0:T(128)S(1)}) custom-call(s32[4]{0:T(128)S(1)} %pad_add_fusion.place_ref, s32[4096]{0:T(1024)S(1)} %bitcast.59, s32[64]{0:T(128)S(1)} %broadcast_select_fusion.length_ref), custom_call_target="tpu_custom_call" | custom-call | tf_op jit(solution)/shard_map/pallas_call | solution.py:393
  87.4 21.2 %all_to_all.35.q_ref = bf16[8,192,128]{2,1,0:T(8,128)(2,1)S(1)} all-to-all(bf16[8,192,128]{2,1,0:T(8,128)(2,1)S(1)} %get-tuple-element.49), channel_id=1, replica_groups=mesh['kv'=4,'z'=8,'x'=4,'core'=2] {'z'}, dimensions={0} | all-to-all | bytes 786432 | tf_op jit(solution)/shard_map/all_to_all | solution.py:37
  108.7 2.2 %collective-permute-start.11 = (bf16[16,2,128,128]{3,2,1,0:T(8,128)(2,1)}, bf16[16,2,128,128]{3,2,1,0:T(8,128)(2,1)S(1)}, u32[]{:S(2)}, u32[]{:S(2)}) collective-permute-start(bf16[16,2,128,128]{3,2,1,0:T(8,128)(2,1)} %collective-permute-done.8.rest_0_), channel_id=1, source_target_pairs={{0,1},{1,0},{2,3},{3,2},{4,5},{5,4},{6,7},{7,6},{8,9},{9,8},{10,11... | collective-permute-start | bytes 3145736 | tf_op jit(solution)/shard_map/ppermute | solution.py:45
  111.0 1.6 copy-done.1
  113.9 2.7 %shard_map.116 = (f32[8,192,128]{2,1,0:T(8,128)S(1)}, f32[8,192,128]{2,1,0:T(8,128)S(1)}, f32[8,192,128]{2,1,0:T(8,128)S(1)}) custom-call(s32[256]{0:T(256)S(1)} %copy-done.13, s32[2]{0:T(128)S(1)} %copy-done.9, s32[64]{0:T(128)S(1)} %broadcast_select_fusion.length_ref, bf16[8,192,128]{2,1,0:T(8,128)(2,1)S(1)} %all_to_all.35.q_ref, ...), custom_call_target="tpu_custom_call" | custom-call | flops 1 | bytes 1 | tf_op jit(solution)/shard_map/pallas_call | solution.py:478
  116.7 2.0 %shard_map.117 = bf16[8,216,128]{2,1,0:T(8,128)(2,1)} custom-call(s32[256]{0:T(256)S(1)} %copy-done.11, s32[2]{0:T(128)S(1)} %copy-done.9, s32[64]{0:T(128)S(1)} %broadcast_select_fusion.length_ref, bf16[8,192,128]{2,1,0:T(8,128)(2,1)S(1)} %all_to_all.35.q_ref, s32[8,24,128]{2,1,0:T(8,128)S(1)} %broadcast_in_dim.78.root_ref, ...), custom_call_target="tpu_custom_call" | custom-call | tf_op jit(solution)/shard_map/pallas_call | solution.py:487
  118.6 5.9 %all-to-all-start.4 = ((bf16[8,216,128]{2,1,0:T(8,128)(2,1)}), bf16[8,216,128]{2,1,0:T(8,128)(2,1)S(1)}, u32[]{:S(2)}, u32[]{:S(2)}) async-start(bf16[8,216,128]{2,1,0:T(8,128)(2,1)} %shard_map.117), calls=%async_computation.4 | async-start | bytes 884736 | tf_op jit(solution)/shard_map/all_to_all | solution.py:37
  124.5 2.9 %collective-permute-start.16 = (bf16[64,1024]{1,0:T(8,128)(2,1)S(1)}, bf16[64,1024]{1,0:T(8,128)(2,1)S(1)}, u32[]{:S(2)}, u32[]{:S(2)}) collective-permute-start(bf16[64,1024]{1,0:T(8,128)(2,1)S(1)} %bitcast.54), channel_id=1, source_target_pairs={{0,2},{2,4},{4,6},{6,0},{1,3},{3,5},{5,7},{7,1},{8,10},{10,12},{12... | collective-permute-start | bytes 393224 | tf_op jit(solution)/shard_map/ppermute | solution.py:49
  127.4 1.4 collective-permute-start.17
  128.9 1.2 collective-permute-start.18
  130.0 4.6 %collective-permute-start.19 = (bf16[64,1024]{1,0:T(8,128)(2,1)S(1)}, bf16[64,1024]{1,0:T(8,128)(2,1)S(1)}, u32[]{:S(2)}, u32[]{:S(2)}) collective-permute-start(bf16[64,1024]{1,0:T(8,128)(2,1)S(1)} %bitcast.57), channel_id=1, source_target_pairs={{0,1},{1,0},{2,3},{3,2},{4,5},{5,4},{6,7},{7,6},{8,9},{9,8},{10,11... | collective-permute-start | bytes 393224 | tf_op jit(solution)/shard_map/ppermute | solution.py:45
  134.8 1.5 collective-permute-start.21
  138.7 20.5 %all_to_all.36 = bf16[8,24,1024]{2,1,0:T(8,128)(2,1)S(1)} all-to-all(bf16[8,24,1024]{2,1,0:T(8,128)(2,1)S(1)} %shard_map.118), channel_id=1, replica_groups=mesh['kv'=4,'z'=8,'x'=4,'core'=2] {'z'}, dimensions={0} | all-to-all | bytes 786432 | tf_op jit(solution)/shard_map/all_to_all | solution.py:37
  159.1 1.2 shard_map.119
  160.4 1.4 collective-permute-start.23
  161.8 2.6 %collective-permute-start.24 = (f32[4,48,128]{2,1,0:T(8,128)S(1)}, f32[4,48,128]{2,1,0:T(8,128)S(1)}, u32[]{:S(2)}, u32[]{:S(2)}) collective-permute-start(f32[4,48,128]{2,1,0:T(8,128)S(1)} %get-tuple-element.74), channel_id=1, source_target_pairs={{0,128},{64,192},{128,0},{192,64},{1,129},{65,193},{129,1},{193,65... | collective-permute-start | bytes 294920 | tf_op jit(solution)/shard_map/ppermute | solution.py:521
  164.4 1.1 collective-permute-start.25
  165.5 2.1 %collective-permute-done.24.rest_2_ = f32[4,48,128]{2,1,0:T(8,128)S(1)} collective-permute-done((f32[4,48,128]{2,1,0:T(8,128)S(1)}, f32[4,48,128]{2,1,0:T(8,128)S(1)}, u32[]{:S(2)}, u32[]{:S(2)}) %collective-permute-start.24) | collective-permute-done | bytes 98336 | tf_op jit(solution)/shard_map/ppermute | solution.py:521
  167.5 1.4 collective-permute-done.25.rest_3_
  168.9 1.3 shard_map.120
  170.3 9.4 %all-to-all-start.6 = ((bf16[32,24,128]{2,1,0:T(8,128)(2,1)}), bf16[32,24,128]{2,1,0:T(8,128)(2,1)S(1)}, u32[]{:S(2)}, u32[]{:S(2)}) async-start(bf16[32,24,128]{2,1,0:T(8,128)(2,1)} %bitcast.26), calls=%async_computation.6 | async-start | bytes 393216 | tf_op jit(solution)/shard_map/all_to_all | solution.py:37
  180.3 7.6 %all-to-all-done.6 = bf16[32,24,128]{2,1,0:T(8,128)(2,1)S(1)} async-done(((bf16[32,24,128]{2,1,0:T(8,128)(2,1)}), bf16[32,24,128]{2,1,0:T(8,128)(2,1)S(1)}, u32[]{:S(2)}, u32[]{:S(2)}) %all-to-all-start.6) | async-done | bytes 196640 | tf_op jit(solution)/shard_map/all_to_all | solution.py:37
  (136 shorter events, 29.3 us)
Async XLA Ops:
  0.6 16.4 %copy-start.16 = (s32[3,512]{1,0:T(4,128)S(1)}, s32[3,512]{1,0:T(4,128)}, u32[]{:S(2)}) copy-start(s32[3,512]{1,0:T(4,128)} %param.19) | copy-start | bytes 18436
  3.0 36.5 %collective-permute-start = (bf16[64,1280]{1,0:T(8,128)(2,1)S(1)}, bf16[64,1280]{1,0:T(8,128)(2,1)S(1)}, u32[]{:S(2)}, u32[]{:S(2)}) collective-permute-start(bf16[64,1280]{1,0:T(8,128)(2,1)S(1)} %constant_dynamic-update-slice_fusion.rest_0_), channel_id=1, source_target_pairs={{0,2},{2,4},{4,6},{6,0},{1,3},{3,5},{5,7},{7,1},{8,10},{10,12},{12... | collective-permute-start | bytes 491528 | tf_op jit(solution)/shard_map/ppermute | solution.py:49
  5.1 34.5 %collective-permute-start.1 = (bf16[64,1280]{1,0:T(8,128)(2,1)S(1)}, bf16[64,1280]{1,0:T(8,128)(2,1)S(1)}, u32[]{:S(2)}, u32[]{:S(2)}) collective-permute-start(bf16[64,1280]{1,0:T(8,128)(2,1)S(1)} %constant_dynamic-update-slice_fusion.rest_0_), channel_id=1, source_target_pairs={{0,4},{2,6},{4,0},{6,2},{1,5},{3,7},{5,1},{7,3},{8,12},{10,14},{12... | collective-permute-start | bytes 491528 | tf_op jit(solution)/shard_map/ppermute | solution.py:49
  7.5 32.0 %collective-permute-start.2 = (bf16[64,1280]{1,0:T(8,128)(2,1)S(1)}, bf16[64,1280]{1,0:T(8,128)(2,1)S(1)}, u32[]{:S(2)}, u32[]{:S(2)}) collective-permute-start(bf16[64,1280]{1,0:T(8,128)(2,1)S(1)} %constant_dynamic-update-slice_fusion.rest_0_), channel_id=1, source_target_pairs={{0,6},{2,0},{4,2},{6,4},{1,7},{3,1},{5,3},{7,5},{8,14},{10,8},{12,... | collective-permute-start | bytes 491528 | tf_op jit(solution)/shard_map/ppermute | solution.py:49
  12.0 11.1 %all-to-all-start = ((bf16[8,104,128]{2,1,0:T(8,128)(2,1)}), bf16[8,104,128]{2,1,0:T(8,128)(2,1)S(1)}, u32[]{:S(2)}, u32[]{:S(2)}) async-start(bf16[8,104,128]{2,1,0:T(8,128)(2,1)} %pad_maximum_fusion), calls=%async_computation | async-start | bytes 425984 | tf_op jit(solution)/shard_map/all_to_all | solution.py:37
  23.7 46.5 %collective-permute-start.9 = (bf16[32,2,128,128]{3,2,1,0:T(8,128)(2,1)}, bf16[32,2,128,128]{3,2,1,0:T(8,128)(2,1)S(1)}, u32[]{:S(2)}, u32[]{:S(2)}) collective-permute-start(bf16[32,2,128,128]{3,2,1,0:T(8,128)(2,1)} %bitcast.49), channel_id=1, source_target_pairs={{0,6},{2,0},{4,2},{6,4},{1,7},{3,1},{5,3},{7,5},{8,14},{10,8},{12,... | collective-permute-start | bytes 6291464 | tf_op jit(solution)/shard_map/ppermute | solution.py:49
  24.6 48.6 %collective-permute-start.7 = (bf16[32,2,128,128]{3,2,1,0:T(8,128)(2,1)}, bf16[32,2,128,128]{3,2,1,0:T(8,128)(2,1)}, u32[]{:S(2)}, u32[]{:S(2)}) collective-permute-start(bf16[32,2,128,128]{3,2,1,0:T(8,128)(2,1)} %bitcast.50), channel_id=1, source_target_pairs={{0,2},{2,4},{4,6},{6,0},{1,3},{3,5},{5,7},{7,1},{8,10},{10,12},{12... | collective-permute-start | bytes 6291464 | tf_op jit(solution)/shard_map/ppermute | solution.py:49
  25.8 16.2 %all-to-all-start.1 = ((f32[8,2,128]{2,1,0:T(2,128)}), f32[8,2,128]{2,1,0:T(2,128)S(1)}, u32[]{:S(2)}, u32[]{:S(2)}) async-start(f32[8,2,128]{2,1,0:T(2,128)} %broadcast_in_dim.76), calls=%async_computation.1 | async-start | bytes 16384 | tf_op jit(solution)/shard_map/all_to_all | solution.py:37
  39.6 2.9 %collective-permute-start.3 = (bf16[64,1280]{1,0:T(8,128)(2,1)S(1)}, bf16[64,1280]{1,0:T(8,128)(2,1)S(1)}, u32[]{:S(2)}, u32[]{:S(2)}) collective-permute-start(bf16[64,1280]{1,0:T(8,128)(2,1)S(1)} %constant_dynamic-update-slice_fusion.rest_0_), channel_id=1, source_target_pairs={{0,1},{1,0},{2,3},{3,2},{4,5},{5,4},{6,7},{7,6},{8,9},{9,8},{10,11... | collective-permute-start | bytes 491528 | tf_op jit(solution)/shard_map/ppermute | solution.py:45
  41.5 2.1 %collective-permute-start.4 = (bf16[64,1280]{1,0:T(8,128)(2,1)S(1)}, bf16[64,1280]{1,0:T(8,128)(2,1)S(1)}, u32[]{:S(2)}, u32[]{:S(2)}) collective-permute-start(bf16[64,1280]{1,0:T(8,128)(2,1)S(1)} %collective-permute-done.rest_1_), channel_id=1, source_target_pairs={{0,1},{1,0},{2,3},{3,2},{4,5},{5,4},{6,7},{7,6},{8,9},{9,8},{10,11... | collective-permute-start | bytes 491528 | tf_op jit(solution)/shard_map/ppermute | solution.py:45
  41.6 2.0 %collective-permute-start.5 = (bf16[64,1280]{1,0:T(8,128)(2,1)S(1)}, bf16[64,1280]{1,0:T(8,128)(2,1)}, u32[]{:S(2)}, u32[]{:S(2)}) collective-permute-start(bf16[64,1280]{1,0:T(8,128)(2,1)S(1)} %collective-permute-done.1.rest_2_), channel_id=1, source_target_pairs={{0,1},{1,0},{2,3},{3,2},{4,5},{5,4},{6,7},{7,6},{8,9},{9,8},{10,11... | collective-permute-start | bytes 491528 | tf_op jit(solution)/shard_map/ppermute | solution.py:45
  42.5 2.0 %collective-permute-start.6 = (bf16[64,1280]{1,0:T(8,128)(2,1)S(1)}, bf16[64,1280]{1,0:T(8,128)(2,1)S(1)}, u32[]{:S(2)}, u32[]{:S(2)}) collective-permute-start(bf16[64,1280]{1,0:T(8,128)(2,1)S(1)} %collective-permute-done.2.rest_3_), channel_id=1, source_target_pairs={{0,1},{1,0},{2,3},{3,2},{4,5},{5,4},{6,7},{7,6},{8,9},{9,8},{10,11... | collective-permute-start | bytes 491528 | tf_op jit(solution)/shard_map/ppermute | solution.py:45
  43.6 11.3 %copy-start.15 = (s32[512]{0:T(512)S(1)}, s32[512]{0:T(512)}, u32[]{:S(2)}) copy-start(s32[512]{0:T(512)} %param.17) | copy-start | bytes 6148
  46.2 1.0 copy-start
  47.2 38.1 %all-to-all-start.2 = ((f32[8,24,1280]{2,1,0:T(8,128)}), f32[8,24,1280]{2,1,0:T(8,128)S(1)}, u32[]{:S(2)}, u32[]{:S(2)}) async-start(f32[8,24,1280]{2,1,0:T(8,128)} %bitcast.48), calls=%async_computation.2 | async-start | bytes 1966080 | tf_op jit(solution)/shard_map/all_to_all | solution.py:37
  61.1 0.6 copy-start.14
  68.4 42.5 %collective-permute-start.13 = (bf16[32,2,128,128]{3,2,1,0:T(8,128)(2,1)}, bf16[32,2,128,128]{3,2,1,0:T(8,128)(2,1)}, u32[]{:S(2)}, u32[]{:S(2)}) collective-permute-start(bf16[32,2,128,128]{3,2,1,0:T(8,128)(2,1)} %bitcast.51), channel_id=1, source_target_pairs={{0,1},{1,0},{2,3},{3,2},{4,5},{5,4},{6,7},{7,6},{8,9},{9,8},{10,11... | collective-permute-start | bytes 6291464 | tf_op jit(solution)/shard_map/ppermute | solution.py:45
  71.2 37.4 %collective-permute-start.10 = (bf16[16,2,128,128]{3,2,1,0:T(8,128)(2,1)}, bf16[16,2,128,128]{3,2,1,0:T(8,128)(2,1)}, u32[]{:S(2)}, u32[]{:S(2)}) collective-permute-start(bf16[16,2,128,128]{3,2,1,0:T(8,128)(2,1)} %slice.69), channel_id=1, source_target_pairs={{0,6},{2,0},{4,2},{6,4},{1,7},{3,1},{5,3},{7,5},{8,14},{10,8},{12,... | collective-permute-start | bytes 3145736 | tf_op jit(solution)/shard_map/ppermute | solution.py:49
  75.6 33.1 %collective-permute-start.8 = (bf16[16,2,128,128]{3,2,1,0:T(8,128)(2,1)}, bf16[16,2,128,128]{3,2,1,0:T(8,128)(2,1)}, u32[]{:S(2)}, u32[]{:S(2)}) collective-permute-start(bf16[16,2,128,128]{3,2,1,0:T(8,128)(2,1)} %slice.68), channel_id=1, source_target_pairs={{0,2},{2,4},{4,6},{6,0},{1,3},{3,5},{5,7},{7,1},{8,10},{10,12},{12... | collective-permute-start | bytes 3145736 | tf_op jit(solution)/shard_map/ppermute | solution.py:49
  75.6 35.4 %collective-permute-start.14 = (bf16[32,2,128,128]{3,2,1,0:T(8,128)(2,1)}, bf16[32,2,128,128]{3,2,1,0:T(8,128)(2,1)}, u32[]{:S(2)}, u32[]{:S(2)}) collective-permute-start(bf16[32,2,128,128]{3,2,1,0:T(8,128)(2,1)} %collective-permute-done.7.rest_2_), channel_id=1, source_target_pairs={{0,1},{1,0},{2,3},{3,2},{4,5},{5,4},{6,7},{7,6},{8,9},{9,8},{10,11... | collective-permute-start | bytes 6291464 | tf_op jit(solution)/shard_map/ppermute | solution.py:45
  77.7 33.2 %collective-permute-start.15 = (bf16[32,2,128,128]{3,2,1,0:T(8,128)(2,1)S(1)}, bf16[32,2,128,128]{3,2,1,0:T(8,128)(2,1)}, u32[]{:S(2)}, u32[]{:S(2)}) collective-permute-start(bf16[32,2,128,128]{3,2,1,0:T(8,128)(2,1)S(1)} %collective-permute-done.9.rest_4_), channel_id=1, source_target_pairs={{0,1},{1,0},{2,3},{3,2},{4,5},{5,4},{6,7},{7,6},{8,9},{9,8},{10,11... | collective-permute-start | bytes 6291464 | tf_op jit(solution)/shard_map/ppermute | solution.py:45
  84.6 0.5 copy-start.12
  84.6 0.6 copy-start.8
  84.6 0.6 copy-start.10
  86.1 0.7 copy-start.7
  87.4 23.6 %copy-start.3 = (f32[6,8,128]{2,1,0:T(8,128)}, f32[6,8,128]{2,1,0:T(8,128)S(1)}, u32[]{:S(2)}) copy-start(f32[6,8,128]{2,1,0:T(8,128)S(1)} %get-tuple-element.63.v_ref) | copy-start | bytes 73732
  87.4 23.6 %copy-start.5 = (f32[6,8,128]{2,1,0:T(8,128)}, f32[6,8,128]{2,1,0:T(8,128)S(1)}, u32[]{:S(2)}) copy-start(f32[6,8,128]{2,1,0:T(8,128)S(1)} %get-tuple-element.62.k_ref) | copy-start | bytes 73732
  108.7 7.9 %collective-permute-start.11 = (bf16[16,2,128,128]{3,2,1,0:T(8,128)(2,1)}, bf16[16,2,128,128]{3,2,1,0:T(8,128)(2,1)S(1)}, u32[]{:S(2)}, u32[]{:S(2)}) collective-permute-start(bf16[16,2,128,128]{3,2,1,0:T(8,128)(2,1)} %collective-permute-done.8.rest_0_), channel_id=1, source_target_pairs={{0,1},{1,0},{2,3},{3,2},{4,5},{5,4},{6,7},{7,6},{8,9},{9,8},{10,11... | collective-permute-start | bytes 3145736 | tf_op jit(solution)/shard_map/ppermute | solution.py:45
  110.9 5.7 %collective-permute-start.12 = (bf16[16,2,128,128]{3,2,1,0:T(8,128)(2,1)}, bf16[16,2,128,128]{3,2,1,0:T(8,128)(2,1)S(1)}, u32[]{:S(2)}, u32[]{:S(2)}) collective-permute-start(bf16[16,2,128,128]{3,2,1,0:T(8,128)(2,1)} %collective-permute-done.10.rest_1_), channel_id=1, source_target_pairs={{0,1},{1,0},{2,3},{3,2},{4,5},{5,4},{6,7},{7,6},{8,9},{9,8},{10,11... | collective-permute-start | bytes 3145736 | tf_op jit(solution)/shard_map/ppermute | solution.py:45
  111.0 1.6 copy-start.1
  112.6 0.7 copy-start.9
  113.2 0.6 copy-start.13
  113.9 2.8 %copy-start.11 = (s32[256]{0:T(256)S(1)}, s32[256]{0:T(256)}, u32[]{:S(2)}) copy-start(s32[256]{0:T(256)} %copy-done.10) | copy-start | bytes 3076
  116.6 7.9 %copy-start.2 = (bf16[1024,64]{0,1:T(8,128)(2,1)S(1)}, bf16[1024,64]{0,1:T(8,128)(2,1)}, u32[]{:S(2)}) copy-start(bf16[1024,64]{0,1:T(8,128)(2,1)} %param.15) | copy-start | bytes 393220
  116.6 21.5 %copy-start.4 = (f32[6,8,128]{2,1,0:T(8,128)S(1)}, f32[6,8,128]{2,1,0:T(8,128)}, u32[]{:S(2)}) copy-start(f32[6,8,128]{2,1,0:T(8,128)} %copy-done.3) | copy-start | bytes 73732
  116.6 21.5 %copy-start.6 = (f32[6,8,128]{2,1,0:T(8,128)S(1)}, f32[6,8,128]{2,1,0:T(8,128)}, u32[]{:S(2)}) copy-start(f32[6,8,128]{2,1,0:T(8,128)} %copy-done.5) | copy-start | bytes 73732
  118.6 19.5 %all-to-all-start.4 = ((bf16[8,216,128]{2,1,0:T(8,128)(2,1)}), bf16[8,216,128]{2,1,0:T(8,128)(2,1)S(1)}, u32[]{:S(2)}, u32[]{:S(2)}) async-start(bf16[8,216,128]{2,1,0:T(8,128)(2,1)} %shard_map.117), calls=%async_computation.4 | async-start | bytes 884736 | tf_op jit(solution)/shard_map/all_to_all | solution.py:37
  124.5 10.1 %collective-permute-start.16 = (bf16[64,1024]{1,0:T(8,128)(2,1)S(1)}, bf16[64,1024]{1,0:T(8,128)(2,1)S(1)}, u32[]{:S(2)}, u32[]{:S(2)}) collective-permute-start(bf16[64,1024]{1,0:T(8,128)(2,1)S(1)} %bitcast.54), channel_id=1, source_target_pairs={{0,2},{2,4},{4,6},{6,0},{1,3},{3,5},{5,7},{7,1},{8,10},{10,12},{12... | collective-permute-start | bytes 393224 | tf_op jit(solution)/shard_map/ppermute | solution.py:49
  127.4 7.4 %collective-permute-start.17 = (bf16[64,1024]{1,0:T(8,128)(2,1)S(1)}, bf16[64,1024]{1,0:T(8,128)(2,1)S(1)}, u32[]{:S(2)}, u32[]{:S(2)}) collective-permute-start(bf16[64,1024]{1,0:T(8,128)(2,1)S(1)} %bitcast.55), channel_id=1, source_target_pairs={{0,4},{2,6},{4,0},{6,2},{1,5},{3,7},{5,1},{7,3},{8,12},{10,14},{12... | collective-permute-start | bytes 393224 | tf_op jit(solution)/shard_map/ppermute | solution.py:49
  128.9 7.5 %collective-permute-start.18 = (bf16[64,1024]{1,0:T(8,128)(2,1)S(1)}, bf16[64,1024]{1,0:T(8,128)(2,1)S(1)}, u32[]{:S(2)}, u32[]{:S(2)}) collective-permute-start(bf16[64,1024]{1,0:T(8,128)(2,1)S(1)} %bitcast.56), channel_id=1, source_target_pairs={{0,6},{2,0},{4,2},{6,4},{1,7},{3,1},{5,3},{7,5},{8,14},{10,8},{12,... | collective-permute-start | bytes 393224 | tf_op jit(solution)/shard_map/ppermute | solution.py:49
  130.0 7.1 %collective-permute-start.19 = (bf16[64,1024]{1,0:T(8,128)(2,1)S(1)}, bf16[64,1024]{1,0:T(8,128)(2,1)S(1)}, u32[]{:S(2)}, u32[]{:S(2)}) collective-permute-start(bf16[64,1024]{1,0:T(8,128)(2,1)S(1)} %bitcast.57), channel_id=1, source_target_pairs={{0,1},{1,0},{2,3},{3,2},{4,5},{5,4},{6,7},{7,6},{8,9},{9,8},{10,11... | collective-permute-start | bytes 393224 | tf_op jit(solution)/shard_map/ppermute | solution.py:45
  134.6 2.5 %collective-permute-start.20 = (bf16[64,1024]{1,0:T(8,128)(2,1)S(1)}, bf16[64,1024]{1,0:T(8,128)(2,1)S(1)}, u32[]{:S(2)}, u32[]{:S(2)}) collective-permute-start(bf16[64,1024]{1,0:T(8,128)(2,1)S(1)} %collective-permute-done.16.rest_1_), channel_id=1, source_target_pairs={{0,1},{1,0},{2,3},{3,2},{4,5},{5,4},{6,7},{7,6},{8,9},{9,8},{10,11... | collective-permute-start | bytes 393224 | tf_op jit(solution)/shard_map/ppermute | solution.py:45
  134.8 2.5 %collective-permute-start.21 = (bf16[64,1024]{1,0:T(8,128)(2,1)S(1)}, bf16[64,1024]{1,0:T(8,128)(2,1)S(1)}, u32[]{:S(2)}, u32[]{:S(2)}) collective-permute-start(bf16[64,1024]{1,0:T(8,128)(2,1)S(1)} %collective-permute-done.17.rest_2_), channel_id=1, source_target_pairs={{0,1},{1,0},{2,3},{3,2},{4,5},{5,4},{6,7},{7,6},{8,9},{9,8},{10,11... | collective-permute-start | bytes 393224 | tf_op jit(solution)/shard_map/ppermute | solution.py:45
  136.3 1.8 collective-permute-start.22
  160.4 5.1 %collective-permute-start.23 = (f32[4,48,128]{2,1,0:T(8,128)S(1)}, f32[4,48,128]{2,1,0:T(8,128)S(1)}, u32[]{:S(2)}, u32[]{:S(2)}) collective-permute-start(f32[4,48,128]{2,1,0:T(8,128)S(1)} %get-tuple-element.73), channel_id=1, source_target_pairs={{0,64},{64,128},{128,192},{192,0},{1,65},{65,129},{129,193},{193,1... | collective-permute-start | bytes 294920 | tf_op jit(solution)/shard_map/ppermute | solution.py:521
  161.8 5.8 %collective-permute-start.24 = (f32[4,48,128]{2,1,0:T(8,128)S(1)}, f32[4,48,128]{2,1,0:T(8,128)S(1)}, u32[]{:S(2)}, u32[]{:S(2)}) collective-permute-start(f32[4,48,128]{2,1,0:T(8,128)S(1)} %get-tuple-element.74), channel_id=1, source_target_pairs={{0,128},{64,192},{128,0},{192,64},{1,129},{65,193},{129,1},{193,65... | collective-permute-start | bytes 294920 | tf_op jit(solution)/shard_map/ppermute | solution.py:521
  164.4 4.6 %collective-permute-start.25 = (f32[4,48,128]{2,1,0:T(8,128)S(1)}, f32[4,48,128]{2,1,0:T(8,128)S(1)}, u32[]{:S(2)}, u32[]{:S(2)}) collective-permute-start(f32[4,48,128]{2,1,0:T(8,128)S(1)} %get-tuple-element.75), channel_id=1, source_target_pairs={{0,192},{64,0},{128,64},{192,128},{1,193},{65,1},{129,65},{193,129... | collective-permute-start | bytes 294920 | tf_op jit(solution)/shard_map/ppermute | solution.py:521
  170.3 17.7 %all-to-all-start.6 = ((bf16[32,24,128]{2,1,0:T(8,128)(2,1)}), bf16[32,24,128]{2,1,0:T(8,128)(2,1)S(1)}, u32[]{:S(2)}, u32[]{:S(2)}) async-start(bf16[32,24,128]{2,1,0:T(8,128)(2,1)} %bitcast.26), calls=%async_computation.6 | async-start | bytes 393216 | tf_op jit(solution)/shard_map/all_to_all | solution.py:37

commit v9 on v8

--- a/solution.py
+++ b/solution.py
@@ -424,6 +424,10 @@
     cache, squares = lax.optimization_barrier((cache, squares))
     left = shift(cache, 1)
     right = shift(cache, -1)
+    root_tiles = jnp.broadcast_to(root_tiles[:, :, None], (ZN, SB, HD))
+    left, right, near_list, root_tiles, own_parents, cosines, sines = lax.optimization_barrier(
+        (left, right, near_list, root_tiles, own_parents, cosines, sines)
+    )
     across = [shift(left[:half_slots], 1), shift(right[half_slots:], -1)]
     squares = jnp.sum(spread(squares, "z", ZN), axis=0).reshape(256)[:rows]
     stream, weights = lax.optimization_barrier((stream, weights))
@@ -440,10 +444,6 @@
         scratch_shapes=[pltpu.VMEM((XN, 2 * PART, columns), jnp.bfloat16)],
     )(place, normed, *weights)
     projected = exchange(projected.reshape(ZN, SB, columns), "z")
-    root_tiles = jnp.broadcast_to(root_tiles[:, :, None], (ZN, SB, HD))
-    projected, near_list, root_tiles = lax.optimization_barrier(
-        (projected, near_list, root_tiles)
-    )
 
     small = jax.ShapeDtypeStruct((len(PAIRS), GROUP, HD), jnp.float32)
     queries, everyone, key_chain, value_chain = pl.pallas_call(

time: 191 us -> 191 us (level)
  waiting for transfers between devices: 19.7 us -> 31.2 us
  local copies, waits for them, and re-layouts: 37.7 us -> 32.4 us
  blocking collectives: 41.7 us -> 37.2 us
  starting transfers between devices: 70.1 us -> 65.6 us
  Pallas kernels: 13.8 us -> 17.2 us
    ppermute x10, waiting for transfers between devices: 1.04 us -> 7.42 us  [shift(): return lax.ppermute(value, 'x', [(i, (i + hop) % XN) for i in range(XN)])]
    ppermute x13, starting transfers between devices: 15.6 us -> 9.67 us  [swap(): return lax.ppermute(value, 'core', [(0, 1), (1, 0)])]
    all_to_all x5, waiting for transfers between devices: 12.8 us -> 18.5 us  [exchange(): return lax.all_to_all(value, axis, 0, 0, tiled=True)]
    all_to_all x2, blocking collectives: 41.7 us -> 37.2 us  [exchange(): return lax.all_to_all(value, axis, 0, 0, tiled=True)]
    all_to_all x5, starting transfers between devices: 34.6 us -> 36.9 us  [exchange(): return lax.all_to_all(value, axis, 0, 0, tiled=True)]
    unnamed x41 -> x46, local copies, waits for them, and re-layouts: 11.7 us -> 10.5 us
  transfers between devices with their start and end apart: 31 -> 31, of which waited for: 9 -> 13; matrix products, arithmetic and copies ran while one was open for 18% -> 16% of each run, Pallas kernels for 5% -> 6%
where the time goes in v9:
time: 191 us; the launch traced here: 190 us
  starting transfers between devices  65.6 us (34%)
  blocking collectives  37.2 us (19%)
  local copies, waits for them, and re-layouts  32.4 us (17%)
  waiting for transfers between devices  31.2 us (16%)
  Pallas kernels  17.2 us (9%)
  other arithmetic  5.57 us (3%)
    all_to_all x2, blocking collectives, exchange(): return lax.all_to_all(value, axis, 0, 0, tiled=True)  37.2 us
    all_to_all x5, starting transfers between devices, exchange(): return lax.all_to_all(value, axis, 0, 0, tiled=True)  36.9 us
    all_to_all x5, waiting for transfers between devices, exchange(): return lax.all_to_all(value, axis, 0, 0, tiled=True)  18.5 us
    ppermute x10, starting transfers between devices, shift(): return lax.ppermute(value, 'x', [(i, (i + hop) % XN) for i in range(XN)])  13.9 us
    unnamed x46, local copies, waits for them, and re-layouts  10.5 us
    ppermute x13, starting transfers between devices, swap(): return lax.ppermute(value, 'core', [(0, 1), (1, 0)])  9.67 us
    ppermute x10, waiting for transfers between devices, shift(): return lax.ppermute(value, 'x', [(i, (i + hop) % XN) for i in range(XN)])  7.42 us
    convert_element_type x3, local copies, waits for them, and re-layouts, body(): stream = stream.reshape(XN, rows, 2 * PART).astype(jnp.float32)  5.58 us
  transfers between devices with their start and end apart: 31, of which 13 were waited for; matrix products, arithmetic and copies ran while one was open for 16% of the time, Pallas kernels for 6%

profile of v9, /device:TPU:1, one launch (start us, length us, event | category | flops | bytes accessed | tf_op | source)
XLA Modules:
  0.0 190.3 jit_solution(5365796727976269138)
XLA Ops:
  0.7 0.9 constant_dynamic-update-slice_fusion.2
  3.0 2.0 %collective-permute-start.2 = (bf16[64,1280]{1,0:T(8,128)(2,1)S(1)}, bf16[64,1280]{1,0:T(8,128)(2,1)S(1)}, u32[]{:S(2)}, u32[]{:S(2)}) collective-permute-start(bf16[64,1280]{1,0:T(8,128)(2,1)S(1)} %constant_dynamic-update-slice_fusion.rest_0_), channel_id=1, source_target_pairs={{0,2},{2,4},{4,6},{6,0},{1,3},{3,5},{5,7},{7,1},{8,10},{10,12},{12... | collective-permute-start | bytes 491528 | tf_op jit(solution)/shard_map/ppermute | solution.py:49
  5.1 2.5 %collective-permute-start.3 = (bf16[64,1280]{1,0:T(8,128)(2,1)S(1)}, bf16[64,1280]{1,0:T(8,128)(2,1)S(1)}, u32[]{:S(2)}, u32[]{:S(2)}) collective-permute-start(bf16[64,1280]{1,0:T(8,128)(2,1)S(1)} %constant_dynamic-update-slice_fusion.rest_0_), channel_id=1, source_target_pairs={{0,4},{2,6},{4,0},{6,2},{1,5},{3,7},{5,1},{7,3},{8,12},{10,14},{12... | collective-permute-start | bytes 491528 | tf_op jit(solution)/shard_map/ppermute | solution.py:49
  7.5 1.2 collective-permute-start.4
  9.3 1.1 copy.103
  12.0 5.0 %all-to-all-start = ((bf16[8,104,128]{2,1,0:T(8,128)(2,1)}), bf16[8,104,128]{2,1,0:T(8,128)(2,1)S(1)}, u32[]{:S(2)}, u32[]{:S(2)}) async-start(bf16[8,104,128]{2,1,0:T(8,128)(2,1)} %pad_maximum_fusion), calls=%async_computation | async-start | bytes 425984 | tf_op jit(solution)/shard_map/all_to_all | solution.py:37
  19.4 3.8 %all-to-all-done = bf16[8,104,128]{2,1,0:T(8,128)(2,1)S(1)} async-done(((bf16[8,104,128]{2,1,0:T(8,128)(2,1)}), bf16[8,104,128]{2,1,0:T(8,128)(2,1)S(1)}, u32[]{:S(2)}, u32[]{:S(2)}) %all-to-all-start) | async-done | bytes 213024 | tf_op jit(solution)/shard_map/all_to_all | solution.py:37
  24.0 2.4 %collective-permute-start.1 = (bf16[32,2,128,128]{3,2,1,0:T(8,128)(2,1)}, bf16[32,2,128,128]{3,2,1,0:T(8,128)(2,1)}, u32[]{:S(2)}, u32[]{:S(2)}) collective-permute-start(bf16[32,2,128,128]{3,2,1,0:T(8,128)(2,1)} %bitcast.52), channel_id=1, source_target_pairs={{0,6},{2,0},{4,2},{6,4},{1,7},{3,1},{5,3},{7,5},{8,14},{10,8},{12,... | collective-permute-start | bytes 6291464 | tf_op jit(solution)/shard_map/ppermute | solution.py:49
  27.0 8.0 %all-to-all-start.1 = ((f32[8,2,128]{2,1,0:T(2,128)}), f32[8,2,128]{2,1,0:T(2,128)}, u32[]{:S(2)}, u32[]{:S(2)}) async-start(f32[8,2,128]{2,1,0:T(2,128)} %broadcast_in_dim.81), calls=%async_computation.1 | async-start | bytes 16384 | tf_op jit(solution)/shard_map/all_to_all | solution.py:37
  35.7 1.4 reshape.175
  37.1 2.6 %copy.109 = f32[4,4,2,24,2,64]{5,4,3,2,1,0:T(2,128)} copy(f32[4,4,2,24,2,64]{5,2,3,1,4,0:T(2,128)} %bitcast.62) | data formatting | bytes 786432 | tf_op jit(solution)/shard_map/convert_element_type | solution.py:418
  39.7 1.6 reshape.174.rest_4_
  41.4 1.8 collective-permute-start.5
  44.5 0.9 collective-permute-start.8
  45.6 0.9 collective-permute-done.8.rest_7_
  46.5 2.7 %shard_map.114 = f32[192,1280]{1,0:T(8,128)} custom-call(s32[4]{0:T(128)S(1)} %pad_add_fusion.place_ref, bf16[4,192,128]{2,1,0:T(8,128)(2,1)S(1)} %multiply_convert_fusion.rows_ref, bf16[64,1280]{1,0:T(8,128)(2,1)S(1)} %constant_dynamic-update-slice_fusion.rest_0_, bf16[64,1280]{1,0:T(8,128)(2,1)S(1)} %collective-permute-done.2.rest_1_, ...), custom_call_target="tpu_custom_call" | custom-call | tf_op jit(solution)/shard_map/pallas_call | solution.py:438
  49.1 6.4 %all-to-all-start.2 = ((f32[8,24,1280]{2,1,0:T(8,128)}), f32[8,24,1280]{2,1,0:T(8,128)S(1)}, u32[]{:S(2)}, u32[]{:S(2)}) async-start(f32[8,24,1280]{2,1,0:T(8,128)} %bitcast.23), calls=%async_computation.2 | async-start | bytes 1966080 | tf_op jit(solution)/shard_map/all_to_all | solution.py:37
  57.0 1.1 copy.106
  60.3 1.7 copy.97
  62.1 1.7 reshape.159
  64.6 0.9 constant_dynamic-slice_fusion.2
  65.5 3.9 %shard_map.113 = (s32[256]{0:T(256)S(1)}, s32[256]{0:T(256)S(1)}, s32[2]{0:T(128)S(1)}) custom-call(s32[4]{0:T(128)S(1)} %pad_add_fusion.place_ref, s32[4096]{0:T(1024)S(1)} %bitcast.61, s32[64]{0:T(128)S(1)} %broadcast_select_fusion.length_ref), custom_call_target="tpu_custom_call" | custom-call | tf_op jit(solution)/shard_map/pallas_call | solution.py:393
  72.0 1.1 slice.55
  73.1 1.9 collective-permute-start.14
  75.0 2.3 %slice.56 = bf16[16,2,128,128]{3,2,1,0:T(8,128)(2,1)} slice(bf16[32,2,128,128]{3,2,1,0:T(8,128)(2,1)} %collective-permute-done.1.rest_4_), slice={[16:32], [0:2], [0:128], [0:128]} | slice | bytes 2097152 | tf_op jit(solution)/shard_map/slice | solution.py:431
  77.3 2.8 %collective-permute-start.10 = (bf16[16,2,128,128]{3,2,1,0:T(8,128)(2,1)}, bf16[16,2,128,128]{3,2,1,0:T(8,128)(2,1)}, u32[]{:S(2)}, u32[]{:S(2)}) collective-permute-start(bf16[16,2,128,128]{3,2,1,0:T(8,128)(2,1)} %slice.56), channel_id=1, source_target_pairs={{0,6},{2,0},{4,2},{6,4},{1,7},{3,1},{5,3},{7,5},{8,14},{10,8},{12,... | collective-permute-start | bytes 3145736 | tf_op jit(solution)/shard_map/ppermute | solution.py:49
  81.0 2.3 %all-to-all-done.2.parts_ref = f32[8,24,1280]{2,1,0:T(8,128)S(1)} async-done(((f32[8,24,1280]{2,1,0:T(8,128)}), f32[8,24,1280]{2,1,0:T(8,128)S(1)}, u32[]{:S(2)}, u32[]{:S(2)}) %all-to-all-start.2) | async-done | bytes 983072 | tf_op jit(solution)/shard_map/all_to_all | solution.py:37
  84.7 19.7 %all_to_all.35.q_ref = bf16[8,192,128]{2,1,0:T(8,128)(2,1)S(1)} all-to-all(bf16[8,192,128]{2,1,0:T(8,128)(2,1)S(1)} %get-tuple-element.56), channel_id=1, replica_groups=mesh['kv'=4,'z'=8,'x'=4,'core'=2] {'z'}, dimensions={0} | all-to-all | bytes 786432 | tf_op jit(solution)/shard_map/all_to_all | solution.py:37
  104.5 1.6 collective-permute-done.9.rest_0_
  106.1 1.1 collective-permute-start.11
  107.3 1.6 copy-done
  108.8 0.9 copy-done.1
  111.0 4.5 %shard_map.116 = (f32[8,192,128]{2,1,0:T(8,128)S(1)}, f32[8,192,128]{2,1,0:T(8,128)S(1)}, f32[8,192,128]{2,1,0:T(8,128)S(1)}) custom-call(s32[256]{0:T(256)S(1)} %copy-done.13, s32[2]{0:T(128)S(1)} %copy-done.9, s32[64]{0:T(128)S(1)} %broadcast_select_fusion.length_ref, bf16[8,192,128]{2,1,0:T(8,128)(2,1)S(1)} %all_to_all.35.q_ref, ...), custom_call_target="tpu_custom_call" | custom-call | flops 1 | bytes 1 | tf_op jit(solution)/shard_map/pallas_call | solution.py:478
  115.6 2.4 %shard_map.117 = bf16[8,216,128]{2,1,0:T(8,128)(2,1)} custom-call(s32[256]{0:T(256)S(1)} %copy-done.11, s32[2]{0:T(128)S(1)} %copy-done.9, s32[64]{0:T(128)S(1)} %broadcast_select_fusion.length_ref, bf16[8,192,128]{2,1,0:T(8,128)(2,1)S(1)} %all_to_all.35.q_ref, s32[8,24,128]{2,1,0:T(8,128)S(1)} %copy-done.1, ...), custom_call_target="tpu_custom_call" | custom-call | tf_op jit(solution)/shard_map/pallas_call | solution.py:487
  118.0 11.2 %all-to-all-start.4 = ((bf16[8,216,128]{2,1,0:T(8,128)(2,1)}), bf16[8,216,128]{2,1,0:T(8,128)(2,1)S(1)}, u32[]{:S(2)}, u32[]{:S(2)}) async-start(bf16[8,216,128]{2,1,0:T(8,128)(2,1)} %shard_map.117), calls=%async_computation.4 | async-start | bytes 884736 | tf_op jit(solution)/shard_map/all_to_all | solution.py:37
  129.4 2.6 %collective-permute-start.18 = (bf16[64,1024]{1,0:T(8,128)(2,1)S(1)}, bf16[64,1024]{1,0:T(8,128)(2,1)S(1)}, u32[]{:S(2)}, u32[]{:S(2)}) collective-permute-start(bf16[64,1024]{1,0:T(8,128)(2,1)S(1)} %bitcast.58), channel_id=1, source_target_pairs={{0,6},{2,0},{4,2},{6,4},{1,7},{3,1},{5,3},{7,5},{8,14},{10,8},{12,... | collective-permute-start | bytes 393224 | tf_op jit(solution)/shard_map/ppermute | solution.py:49
  132.0 1.6 collective-permute-start.19
  133.6 5.1 %collective-permute-done.16.rest_1_ = bf16[64,1024]{1,0:T(8,128)(2,1)S(1)} collective-permute-done((bf16[64,1024]{1,0:T(8,128)(2,1)S(1)}, bf16[64,1024]{1,0:T(8,128)(2,1)S(1)}, u32[]{:S(2)}, u32[]{:S(2)}) %collective-permute-start.16) | collective-permute-done | bytes 131104 | tf_op jit(solution)/shard_map/ppermute | solution.py:49
  140.9 4.7 %all-to-all-done.4.parts_ref = bf16[8,216,128]{2,1,0:T(8,128)(2,1)S(1)} async-done(((bf16[8,216,128]{2,1,0:T(8,128)(2,1)}), bf16[8,216,128]{2,1,0:T(8,128)(2,1)S(1)}, u32[]{:S(2)}, u32[]{:S(2)}) %all-to-all-start.4) | async-done | bytes 442400 | tf_op jit(solution)/shard_map/all_to_all | solution.py:37
  146.1 17.5 %all_to_all.36 = bf16[8,24,1024]{2,1,0:T(8,128)(2,1)S(1)} all-to-all(bf16[8,24,1024]{2,1,0:T(8,128)(2,1)S(1)} %shard_map.118), channel_id=1, replica_groups=mesh['kv'=4,'z'=8,'x'=4,'core'=2] {'z'}, dimensions={0} | all-to-all | bytes 786432 | tf_op jit(solution)/shard_map/all_to_all | solution.py:37
  163.6 1.2 shard_map.119
  164.9 1.4 collective-permute-start.23
  166.3 2.6 %collective-permute-start.24 = (f32[4,48,128]{2,1,0:T(8,128)S(1)}, f32[4,48,128]{2,1,0:T(8,128)S(1)}, u32[]{:S(2)}, u32[]{:S(2)}) collective-permute-start(f32[4,48,128]{2,1,0:T(8,128)S(1)} %get-tuple-element.82), channel_id=1, source_target_pairs={{0,128},{64,192},{128,0},{192,64},{1,129},{65,193},{129,1},{193,65... | collective-permute-start | bytes 294920 | tf_op jit(solution)/shard_map/ppermute | solution.py:521
  168.9 1.1 collective-permute-start.25
  170.2 3.2 %collective-permute-done.24.rest_2_ = f32[4,48,128]{2,1,0:T(8,128)S(1)} collective-permute-done((f32[4,48,128]{2,1,0:T(8,128)S(1)}, f32[4,48,128]{2,1,0:T(8,128)S(1)}, u32[]{:S(2)}, u32[]{:S(2)}) %collective-permute-start.24) | collective-permute-done | bytes 98336 | tf_op jit(solution)/shard_map/ppermute | solution.py:521
  173.4 1.3 shard_map.120
  174.7 6.2 %all-to-all-start.6 = ((bf16[32,24,128]{2,1,0:T(8,128)(2,1)}), bf16[32,24,128]{2,1,0:T(8,128)(2,1)S(1)}, u32[]{:S(2)}, u32[]{:S(2)}) async-start(bf16[32,24,128]{2,1,0:T(8,128)(2,1)} %bitcast.26), calls=%async_computation.6 | async-start | bytes 393216 | tf_op jit(solution)/shard_map/all_to_all | solution.py:37
  181.6 7.6 %all-to-all-done.6 = bf16[32,24,128]{2,1,0:T(8,128)(2,1)S(1)} async-done(((bf16[32,24,128]{2,1,0:T(8,128)(2,1)}), bf16[32,24,128]{2,1,0:T(8,128)(2,1)S(1)}, u32[]{:S(2)}, u32[]{:S(2)}) %all-to-all-start.6) | async-done | bytes 196640 | tf_op jit(solution)/shard_map/all_to_all | solution.py:37
  (142 shorter events, 24.9 us)
Async XLA Ops:
  0.6 16.4 %copy-start.18 = (s32[3,512]{1,0:T(4,128)S(1)}, s32[3,512]{1,0:T(4,128)}, u32[]{:S(2)}) copy-start(s32[3,512]{1,0:T(4,128)} %param.19) | copy-start | bytes 18436
  0.6 17.0 %copy-start.16 = (s32[512]{0:T(512)S(1)}, s32[512]{0:T(512)}, u32[]{:S(2)}) copy-start(s32[512]{0:T(512)} %param.17) | copy-start | bytes 6148
  3.0 38.3 %collective-permute-start.2 = (bf16[64,1280]{1,0:T(8,128)(2,1)S(1)}, bf16[64,1280]{1,0:T(8,128)(2,1)S(1)}, u32[]{:S(2)}, u32[]{:S(2)}) collective-permute-start(bf16[64,1280]{1,0:T(8,128)(2,1)S(1)} %constant_dynamic-update-slice_fusion.rest_0_), channel_id=1, source_target_pairs={{0,2},{2,4},{4,6},{6,0},{1,3},{3,5},{5,7},{7,1},{8,10},{10,12},{12... | collective-permute-start | bytes 491528 | tf_op jit(solution)/shard_map/ppermute | solution.py:49
  5.1 36.3 %collective-permute-start.3 = (bf16[64,1280]{1,0:T(8,128)(2,1)S(1)}, bf16[64,1280]{1,0:T(8,128)(2,1)S(1)}, u32[]{:S(2)}, u32[]{:S(2)}) collective-permute-start(bf16[64,1280]{1,0:T(8,128)(2,1)S(1)} %constant_dynamic-update-slice_fusion.rest_0_), channel_id=1, source_target_pairs={{0,4},{2,6},{4,0},{6,2},{1,5},{3,7},{5,1},{7,3},{8,12},{10,14},{12... | collective-permute-start | bytes 491528 | tf_op jit(solution)/shard_map/ppermute | solution.py:49
  7.5 33.8 %collective-permute-start.4 = (bf16[64,1280]{1,0:T(8,128)(2,1)S(1)}, bf16[64,1280]{1,0:T(8,128)(2,1)S(1)}, u32[]{:S(2)}, u32[]{:S(2)}) collective-permute-start(bf16[64,1280]{1,0:T(8,128)(2,1)S(1)} %constant_dynamic-update-slice_fusion.rest_0_), channel_id=1, source_target_pairs={{0,6},{2,0},{4,2},{6,4},{1,7},{3,1},{5,3},{7,5},{8,14},{10,8},{12,... | collective-permute-start | bytes 491528 | tf_op jit(solution)/shard_map/ppermute | solution.py:49
  12.0 11.1 %all-to-all-start = ((bf16[8,104,128]{2,1,0:T(8,128)(2,1)}), bf16[8,104,128]{2,1,0:T(8,128)(2,1)S(1)}, u32[]{:S(2)}, u32[]{:S(2)}) async-start(bf16[8,104,128]{2,1,0:T(8,128)(2,1)} %pad_maximum_fusion), calls=%async_computation | async-start | bytes 425984 | tf_op jit(solution)/shard_map/all_to_all | solution.py:37
  17.3 19.8 %copy-start.14 = (s32[3,64,8]{2,1,0:T(8,128)}, s32[3,64,8]{2,1,0:T(8,128)S(1)}, u32[]{:S(2)}) copy-start(s32[3,64,8]{2,1,0:T(8,128)S(1)} %broadcast_subtract_fusion) | copy-start | bytes 18436
  23.7 47.7 %collective-permute-start = (bf16[32,2,128,128]{3,2,1,0:T(8,128)(2,1)}, bf16[32,2,128,128]{3,2,1,0:T(8,128)(2,1)S(1)}, u32[]{:S(2)}, u32[]{:S(2)}) collective-permute-start(bf16[32,2,128,128]{3,2,1,0:T(8,128)(2,1)} %bitcast.51), channel_id=1, source_target_pairs={{0,2},{2,4},{4,6},{6,0},{1,3},{3,5},{5,7},{7,1},{8,10},{10,12},{12... | collective-permute-start | bytes 6291464 | tf_op jit(solution)/shard_map/ppermute | solution.py:49
  24.0 47.3 %collective-permute-start.1 = (bf16[32,2,128,128]{3,2,1,0:T(8,128)(2,1)}, bf16[32,2,128,128]{3,2,1,0:T(8,128)(2,1)}, u32[]{:S(2)}, u32[]{:S(2)}) collective-permute-start(bf16[32,2,128,128]{3,2,1,0:T(8,128)(2,1)} %bitcast.52), channel_id=1, source_target_pairs={{0,6},{2,0},{4,2},{6,4},{1,7},{3,1},{5,3},{7,5},{8,14},{10,8},{12,... | collective-permute-start | bytes 6291464 | tf_op jit(solution)/shard_map/ppermute | solution.py:49
  27.0 16.8 %all-to-all-start.1 = ((f32[8,2,128]{2,1,0:T(2,128)}), f32[8,2,128]{2,1,0:T(2,128)}, u32[]{:S(2)}, u32[]{:S(2)}) async-start(f32[8,2,128]{2,1,0:T(2,128)} %broadcast_in_dim.81), calls=%async_computation.1 | async-start | bytes 16384 | tf_op jit(solution)/shard_map/all_to_all | solution.py:37
  37.1 4.3 %copy-start.15 = (f32[8,64]{1,0:T(8,128)S(1)}, f32[8,64]{1,0:T(8,128)}, u32[]{:S(2)}) copy-start(f32[8,64]{1,0:T(8,128)} %fusion.4) | copy-start | bytes 6148
  41.4 3.1 %collective-permute-start.5 = (bf16[64,1280]{1,0:T(8,128)(2,1)S(1)}, bf16[64,1280]{1,0:T(8,128)(2,1)S(1)}, u32[]{:S(2)}, u32[]{:S(2)}) collective-permute-start(bf16[64,1280]{1,0:T(8,128)(2,1)S(1)} %constant_dynamic-update-slice_fusion.rest_0_), channel_id=1, source_target_pairs={{0,1},{1,0},{2,3},{3,2},{4,5},{5,4},{6,7},{7,6},{8,9},{9,8},{10,11... | collective-permute-start | bytes 491528 | tf_op jit(solution)/shard_map/ppermute | solution.py:45
  43.3 2.3 %collective-permute-start.6 = (bf16[64,1280]{1,0:T(8,128)(2,1)S(1)}, bf16[64,1280]{1,0:T(8,128)(2,1)S(1)}, u32[]{:S(2)}, u32[]{:S(2)}) collective-permute-start(bf16[64,1280]{1,0:T(8,128)(2,1)S(1)} %collective-permute-done.2.rest_1_), channel_id=1, source_target_pairs={{0,1},{1,0},{2,3},{3,2},{4,5},{5,4},{6,7},{7,6},{8,9},{9,8},{10,11... | collective-permute-start | bytes 491528 | tf_op jit(solution)/shard_map/ppermute | solution.py:45
  43.4 2.2 %collective-permute-start.7 = (bf16[64,1280]{1,0:T(8,128)(2,1)S(1)}, bf16[64,1280]{1,0:T(8,128)(2,1)}, u32[]{:S(2)}, u32[]{:S(2)}) collective-permute-start(bf16[64,1280]{1,0:T(8,128)(2,1)S(1)} %collective-permute-done.3.rest_2_), channel_id=1, source_target_pairs={{0,1},{1,0},{2,3},{3,2},{4,5},{5,4},{6,7},{7,6},{8,9},{9,8},{10,11... | collective-permute-start | bytes 491528 | tf_op jit(solution)/shard_map/ppermute | solution.py:45
  44.5 2.0 %collective-permute-start.8 = (bf16[64,1280]{1,0:T(8,128)(2,1)S(1)}, bf16[64,1280]{1,0:T(8,128)(2,1)S(1)}, u32[]{:S(2)}, u32[]{:S(2)}) collective-permute-start(bf16[64,1280]{1,0:T(8,128)(2,1)S(1)} %collective-permute-done.4.rest_3_), channel_id=1, source_target_pairs={{0,1},{1,0},{2,3},{3,2},{4,5},{5,4},{6,7},{7,6},{8,9},{9,8},{10,11... | collective-permute-start | bytes 491528 | tf_op jit(solution)/shard_map/ppermute | solution.py:45
  45.6 10.7 %copy-start.17 = (s32[512]{0:T(512)S(1)}, s32[512]{0:T(512)}, u32[]{:S(2)}) copy-start(s32[512]{0:T(512)} %param.17) | copy-start | bytes 6148
  45.6 13.6 %slice-start = ((s32[3,8,1,8]{2,1,3,0:T(8,128)}), s32[1,8,1,8]{2,1,3,0:T(8,128)S(1)}, s32[]{:S(2)}) async-start(s32[3,8,1,8]{2,1,3,0:T(8,128)} %dynamic-slice_add_fusion), calls=%async_computation.7 | async-start | bytes 65536 | tf_op jit(solution)/shard_map/slice | solution.py:390
  49.1 34.2 %all-to-all-start.2 = ((f32[8,24,1280]{2,1,0:T(8,128)}), f32[8,24,1280]{2,1,0:T(8,128)S(1)}, u32[]{:S(2)}, u32[]{:S(2)}) async-start(f32[8,24,1280]{2,1,0:T(8,128)} %bitcast.23), calls=%async_computation.2 | async-start | bytes 1966080 | tf_op jit(solution)/shard_map/all_to_all | solution.py:37
  69.4 0.8 copy-start.8
  69.4 0.8 copy-start.10
  69.4 0.8 copy-start.12
  70.3 36.9 %collective-permute-start.13 = (bf16[32,2,128,128]{3,2,1,0:T(8,128)(2,1)}, bf16[32,2,128,128]{3,2,1,0:T(8,128)(2,1)}, u32[]{:S(2)}, u32[]{:S(2)}) collective-permute-start(bf16[32,2,128,128]{3,2,1,0:T(8,128)(2,1)} %bitcast.53), channel_id=1, source_target_pairs={{0,1},{1,0},{2,3},{3,2},{4,5},{5,4},{6,7},{7,6},{8,9},{9,8},{10,11... | collective-permute-start | bytes 6291464 | tf_op jit(solution)/shard_map/ppermute | solution.py:45
  73.1 34.1 %collective-permute-start.14 = (bf16[32,2,128,128]{3,2,1,0:T(8,128)(2,1)S(1)}, bf16[32,2,128,128]{3,2,1,0:T(8,128)(2,1)}, u32[]{:S(2)}, u32[]{:S(2)}) collective-permute-start(bf16[32,2,128,128]{3,2,1,0:T(8,128)(2,1)S(1)} %collective-permute-done.rest_2_), channel_id=1, source_target_pairs={{0,1},{1,0},{2,3},{3,2},{4,5},{5,4},{6,7},{7,6},{8,9},{9,8},{10,11... | collective-permute-start | bytes 6291464 | tf_op jit(solution)/shard_map/ppermute | solution.py:45
  77.3 27.1 %collective-permute-start.10 = (bf16[16,2,128,128]{3,2,1,0:T(8,128)(2,1)}, bf16[16,2,128,128]{3,2,1,0:T(8,128)(2,1)}, u32[]{:S(2)}, u32[]{:S(2)}) collective-permute-start(bf16[16,2,128,128]{3,2,1,0:T(8,128)(2,1)} %slice.56), channel_id=1, source_target_pairs={{0,6},{2,0},{4,2},{6,4},{1,7},{3,1},{5,3},{7,5},{8,14},{10,8},{12,... | collective-permute-start | bytes 3145736 | tf_op jit(solution)/shard_map/ppermute | solution.py:49
  80.1 26.0 %collective-permute-start.9 = (bf16[16,2,128,128]{3,2,1,0:T(8,128)(2,1)}, bf16[16,2,128,128]{3,2,1,0:T(8,128)(2,1)}, u32[]{:S(2)}, u32[]{:S(2)}) collective-permute-start(bf16[16,2,128,128]{3,2,1,0:T(8,128)(2,1)} %slice.55), channel_id=1, source_target_pairs={{0,2},{2,4},{4,6},{6,0},{1,3},{3,5},{5,7},{7,1},{8,10},{10,12},{12... | collective-permute-start | bytes 3145736 | tf_op jit(solution)/shard_map/ppermute | solution.py:49
  80.1 27.1 %collective-permute-start.15 = (bf16[32,2,128,128]{3,2,1,0:T(8,128)(2,1)}, bf16[32,2,128,128]{3,2,1,0:T(8,128)(2,1)}, u32[]{:S(2)}, u32[]{:S(2)}) collective-permute-start(bf16[32,2,128,128]{3,2,1,0:T(8,128)(2,1)} %collective-permute-done.1.rest_4_), channel_id=1, source_target_pairs={{0,1},{1,0},{2,3},{3,2},{4,5},{5,4},{6,7},{7,6},{8,9},{9,8},{10,11... | collective-permute-start | bytes 6291464 | tf_op jit(solution)/shard_map/ppermute | solution.py:45
  84.7 22.5 %copy-start.3 = (f32[6,8,128]{2,1,0:T(8,128)}, f32[6,8,128]{2,1,0:T(8,128)S(1)}, u32[]{:S(2)}) copy-start(f32[6,8,128]{2,1,0:T(8,128)S(1)} %get-tuple-element.71.v_ref) | copy-start | bytes 73732
  84.7 22.5 %copy-start.5 = (f32[6,8,128]{2,1,0:T(8,128)}, f32[6,8,128]{2,1,0:T(8,128)S(1)}, u32[]{:S(2)}) copy-start(f32[6,8,128]{2,1,0:T(8,128)S(1)} %get-tuple-element.70.k_ref) | copy-start | bytes 73732
  106.1 9.4 %collective-permute-start.11 = (bf16[16,2,128,128]{3,2,1,0:T(8,128)(2,1)}, bf16[16,2,128,128]{3,2,1,0:T(8,128)(2,1)S(1)}, u32[]{:S(2)}, u32[]{:S(2)}) collective-permute-start(bf16[16,2,128,128]{3,2,1,0:T(8,128)(2,1)} %collective-permute-done.9.rest_0_), channel_id=1, source_target_pairs={{0,1},{1,0},{2,3},{3,2},{4,5},{5,4},{6,7},{7,6},{8,9},{9,8},{10,11... | collective-permute-start | bytes 3145736 | tf_op jit(solution)/shard_map/ppermute | solution.py:45
  107.2 8.3 %collective-permute-start.12 = (bf16[16,2,128,128]{3,2,1,0:T(8,128)(2,1)}, bf16[16,2,128,128]{3,2,1,0:T(8,128)(2,1)S(1)}, u32[]{:S(2)}, u32[]{:S(2)}) collective-permute-start(bf16[16,2,128,128]{3,2,1,0:T(8,128)(2,1)} %collective-permute-done.10.rest_1_), channel_id=1, source_target_pairs={{0,1},{1,0},{2,3},{3,2},{4,5},{5,4},{6,7},{7,6},{8,9},{9,8},{10,11... | collective-permute-start | bytes 3145736 | tf_op jit(solution)/shard_map/ppermute | solution.py:45
  107.2 1.6 copy-start
  108.8 0.9 copy-start.1
  111.0 4.5 %copy-start.11 = (s32[256]{0:T(256)S(1)}, s32[256]{0:T(256)}, u32[]{:S(2)}) copy-start(s32[256]{0:T(256)} %copy-done.10) | copy-start | bytes 3076
  115.5 13.7 %copy-start.2 = (bf16[1024,64]{0,1:T(8,128)(2,1)S(1)}, bf16[1024,64]{0,1:T(8,128)(2,1)}, u32[]{:S(2)}) copy-start(bf16[1024,64]{0,1:T(8,128)(2,1)} %param.15) | copy-start | bytes 393220
  115.5 30.1 %copy-start.4 = (f32[6,8,128]{2,1,0:T(8,128)S(1)}, f32[6,8,128]{2,1,0:T(8,128)}, u32[]{:S(2)}) copy-start(f32[6,8,128]{2,1,0:T(8,128)} %copy-done.3) | copy-start | bytes 73732
  115.5 30.0 %copy-start.6 = (f32[6,8,128]{2,1,0:T(8,128)S(1)}, f32[6,8,128]{2,1,0:T(8,128)}, u32[]{:S(2)}) copy-start(f32[6,8,128]{2,1,0:T(8,128)} %copy-done.5) | copy-start | bytes 73732
  118.0 27.6 %all-to-all-start.4 = ((bf16[8,216,128]{2,1,0:T(8,128)(2,1)}), bf16[8,216,128]{2,1,0:T(8,128)(2,1)S(1)}, u32[]{:S(2)}, u32[]{:S(2)}) async-start(bf16[8,216,128]{2,1,0:T(8,128)(2,1)} %shard_map.117), calls=%async_computation.4 | async-start | bytes 884736 | tf_op jit(solution)/shard_map/all_to_all | solution.py:37
  129.2 9.5 %collective-permute-start.16 = (bf16[64,1024]{1,0:T(8,128)(2,1)S(1)}, bf16[64,1024]{1,0:T(8,128)(2,1)S(1)}, u32[]{:S(2)}, u32[]{:S(2)}) collective-permute-start(bf16[64,1024]{1,0:T(8,128)(2,1)S(1)} %bitcast.56), channel_id=1, source_target_pairs={{0,2},{2,4},{4,6},{6,0},{1,3},{3,5},{5,7},{7,1},{8,10},{10,12},{12... | collective-permute-start | bytes 393224 | tf_op jit(solution)/shard_map/ppermute | solution.py:49
  129.3 9.9 %collective-permute-start.17 = (bf16[64,1024]{1,0:T(8,128)(2,1)S(1)}, bf16[64,1024]{1,0:T(8,128)(2,1)S(1)}, u32[]{:S(2)}, u32[]{:S(2)}) collective-permute-start(bf16[64,1024]{1,0:T(8,128)(2,1)S(1)} %bitcast.57), channel_id=1, source_target_pairs={{0,4},{2,6},{4,0},{6,2},{1,5},{3,7},{5,1},{7,3},{8,12},{10,14},{12... | collective-permute-start | bytes 393224 | tf_op jit(solution)/shard_map/ppermute | solution.py:49
  129.4 9.8 %collective-permute-start.18 = (bf16[64,1024]{1,0:T(8,128)(2,1)S(1)}, bf16[64,1024]{1,0:T(8,128)(2,1)S(1)}, u32[]{:S(2)}, u32[]{:S(2)}) collective-permute-start(bf16[64,1024]{1,0:T(8,128)(2,1)S(1)} %bitcast.58), channel_id=1, source_target_pairs={{0,6},{2,0},{4,2},{6,4},{1,7},{3,1},{5,3},{7,5},{8,14},{10,8},{12,... | collective-permute-start | bytes 393224 | tf_op jit(solution)/shard_map/ppermute | solution.py:49
  132.0 7.9 %collective-permute-start.19 = (bf16[64,1024]{1,0:T(8,128)(2,1)S(1)}, bf16[64,1024]{1,0:T(8,128)(2,1)S(1)}, u32[]{:S(2)}, u32[]{:S(2)}) collective-permute-start(bf16[64,1024]{1,0:T(8,128)(2,1)S(1)} %bitcast.59), channel_id=1, source_target_pairs={{0,1},{1,0},{2,3},{3,2},{4,5},{5,4},{6,7},{7,6},{8,9},{9,8},{10,11... | collective-permute-start | bytes 393224 | tf_op jit(solution)/shard_map/ppermute | solution.py:45
  138.8 1.5 collective-permute-start.20
  139.3 1.3 collective-permute-start.21
  139.3 1.6 collective-permute-start.22
  164.9 5.3 %collective-permute-start.23 = (f32[4,48,128]{2,1,0:T(8,128)S(1)}, f32[4,48,128]{2,1,0:T(8,128)S(1)}, u32[]{:S(2)}, u32[]{:S(2)}) collective-permute-start(f32[4,48,128]{2,1,0:T(8,128)S(1)} %get-tuple-element.81), channel_id=1, source_target_pairs={{0,64},{64,128},{128,192},{192,0},{1,65},{65,129},{129,193},{193,1... | collective-permute-start | bytes 294920 | tf_op jit(solution)/shard_map/ppermute | solution.py:521
  166.3 7.1 %collective-permute-start.24 = (f32[4,48,128]{2,1,0:T(8,128)S(1)}, f32[4,48,128]{2,1,0:T(8,128)S(1)}, u32[]{:S(2)}, u32[]{:S(2)}) collective-permute-start(f32[4,48,128]{2,1,0:T(8,128)S(1)} %get-tuple-element.82), channel_id=1, source_target_pairs={{0,128},{64,192},{128,0},{192,64},{1,129},{65,193},{129,1},{193,65... | collective-permute-start | bytes 294920 | tf_op jit(solution)/shard_map/ppermute | solution.py:521
  168.9 4.5 %collective-permute-start.25 = (f32[4,48,128]{2,1,0:T(8,128)S(1)}, f32[4,48,128]{2,1,0:T(8,128)S(1)}, u32[]{:S(2)}, u32[]{:S(2)}) collective-permute-start(f32[4,48,128]{2,1,0:T(8,128)S(1)} %get-tuple-element.83), channel_id=1, source_target_pairs={{0,192},{64,0},{128,64},{192,128},{1,193},{65,1},{129,65},{193,129... | collective-permute-start | bytes 294920 | tf_op jit(solution)/shard_map/ppermute | solution.py:521
  174.7 14.5 %all-to-all-start.6 = ((bf16[32,24,128]{2,1,0:T(8,128)(2,1)}), bf16[32,24,128]{2,1,0:T(8,128)(2,1)S(1)}, u32[]{:S(2)}, u32[]{:S(2)}) async-start(bf16[32,24,128]{2,1,0:T(8,128)(2,1)} %bitcast.26), calls=%async_computation.6 | async-start | bytes 393216 | tf_op jit(solution)/shard_map/all_to_all | solution.py:37
  (3 other events, 1.9 us)

commit v10 on v6

--- a/solution.py
+++ b/solution.py
@@ -141,13 +141,21 @@
                     ref[index, pl.ds(beam, 1), :] = ref[before, pl.ds(parent, 1), :]
 
 
-def scan(place_ref, table_ref, length_ref, near_list, far_list, count_ref):
+def scan(
+    place_ref, parent_ref, table_ref, length_ref, near_list, far_list, count_ref
+):
     x, core, z = place_ref[0], place_ref[1], place_ref[3]
     blocks = table_ref.shape[0] // (ZN * GROUP)
     half = SLOTS // 2
 
     def scan_beam(beam, found):
+        group = lax.shift_right_logical(beam, 3) * JN + x * CN + core
+        heirs = jnp.int32(0)
+        for member in range(GROUP):
+            parent = jnp.bitwise_and(parent_ref[group * GROUP + member], GROUP - 1)
+            heirs = heirs + (parent == jnp.bitwise_and(beam, GROUP - 1)).astype(jnp.int32)
         used = lax.shift_right_logical(length_ref[beam] + (HD - 1), 7)
+        used = jnp.where(heirs > 0, used, 0)
 
         def scan_block(block, found):
             slot = table_ref[beam * blocks + block]
@@ -390,9 +398,9 @@
         scan,
         compiler_params=SMALL,
         out_shape=(listing, listing, jax.ShapeDtypeStruct((2,), jnp.int32)),
-        in_specs=[smem] * 3,
+        in_specs=[smem] * 4,
         out_specs=(smem,) * 3,
-    )(place, table, spans)
+    )(place, parents.reshape(-1), table, spans)
     root_tiles = lax.dynamic_index_in_dim(
         roots_near.reshape(STEPS, ZN, JN, GROUP), lead, 2, keepdims=False
     )
@@ -471,7 +479,7 @@
         pltpu.VMEM((DEPTH,) + cache.shape[1:], jnp.bfloat16),
         pltpu.SemaphoreType.DMA((DEPTH,)),
     ]
-    anywhere = pl.BlockSpec(memory_space=pl.ANY)
+    anywhere = pl.BlockSpec(memory_space=pltpu.HBM)
     before = pl.pallas_call(
         attend_near,
         compiler_params=SMALL,

time: 193 us -> 191 us (0.990); the launches traced: 193 us -> 188 us
  starting transfers between devices: 65.4 us -> 61.7 us
  Pallas kernels: 21.7 us -> 18.7 us
  other arithmetic: 3.83 us -> 6.32 us
  blocking collectives: 43.4 us -> 41.4 us
    ppermute x13, starting transfers between devices: 15.5 us -> 9.97 us  [swap(): return lax.ppermute(value, 'core', [(0, 1), (1, 0)])]
    pallas_call x1, Pallas kernels: 7.7 us -> 5.19 us  [body(): pl.pallas_call(attend_near, compiler_params=SMALL, out_shape=state, in_sp...]
    ppermute x10, starting transfers between devices: 12.7 us -> 14.8 us  [shift(): return lax.ppermute(value, 'x', [(i, (i + hop) % XN) for i in range(XN)])]
    all_to_all x2, blocking collectives: 43.4 us -> 41.4 us  [exchange(): return lax.all_to_all(value, axis, 0, 0, tiled=True)]
  transfers between devices with their start and end apart: 31 -> 31, of which waited for: 10 -> 11; matrix products, arithmetic and copies ran while one was open for 13% -> 16% of each run, Pallas kernels for 8% -> 7%
where the time goes in v10:
time: 191 us; the launch traced here: 188 us
  starting transfers between devices  61.7 us (32%)
  blocking collectives  41.4 us (22%)
  local copies, waits for them, and re-layouts  32.6 us (17%)
  waiting for transfers between devices  26.2 us (14%)
  Pallas kernels  18.7 us (10%)
  other arithmetic  6.32 us (3%)
    all_to_all x2, blocking collectives, exchange(): return lax.all_to_all(value, axis, 0, 0, tiled=True)  41.4 us
    all_to_all x5, starting transfers between devices, exchange(): return lax.all_to_all(value, axis, 0, 0, tiled=True)  31.8 us
    ppermute x10, starting transfers between devices, shift(): return lax.ppermute(value, 'x', [(i, (i + hop) % XN) for i in range(XN)])  14.8 us
    ppermute x10, waiting for transfers between devices, shift(): return lax.ppermute(value, 'x', [(i, (i + hop) % XN) for i in range(XN)])  12.5 us
    ppermute x13, starting transfers between devices, swap(): return lax.ppermute(value, 'core', [(0, 1), (1, 0)])  9.97 us
    unnamed x51, local copies, waits for them, and re-layouts  9.61 us
    all_to_all x5, waiting for transfers between devices, exchange(): return lax.all_to_all(value, axis, 0, 0, tiled=True)  7.64 us
    convert_element_type x3, local copies, waits for them, and re-layouts, body(): stream = stream.reshape(XN, rows, 2 * PART).astype(jnp.float32)  5.58 us
  transfers between devices with their start and end apart: 31, of which 11 were waited for; matrix products, arithmetic and copies ran while one was open for 16% of the time, Pallas kernels for 7%

profile of v10, /device:TPU:1, one launch (start us, length us, event | category | flops | bytes accessed | tf_op | source)
XLA Modules:
  0.0 188.2 jit_solution(7117068337457573668)
XLA Ops:
  1.4 1.1 copy.89
  4.1 6.5 %all-to-all-start = ((bf16[8,104,128]{2,1,0:T(8,128)(2,1)}), bf16[8,104,128]{2,1,0:T(8,128)(2,1)S(1)}, u32[]{:S(2)}, u32[]{:S(2)}) async-start(bf16[8,104,128]{2,1,0:T(8,128)(2,1)} %pad_maximum_fusion), calls=%async_computation | async-start | bytes 425984 | tf_op jit(solution)/shard_map/all_to_all | solution.py:37
  10.7 1.5 collective-permute-start
  12.1 2.4 %collective-permute-start.1 = (bf16[64,1280]{1,0:T(8,128)(2,1)S(1)}, bf16[64,1280]{1,0:T(8,128)(2,1)S(1)}, u32[]{:S(2)}, u32[]{:S(2)}) collective-permute-start(bf16[64,1280]{1,0:T(8,128)(2,1)S(1)} %pad_maximum_fusion.1.rest_0_), channel_id=1, source_target_pairs={{0,4},{2,6},{4,0},{6,2},{1,5},{3,7},{5,1},{7,3},{8,12},{10,14},{12... | collective-permute-start | bytes 491528 | tf_op jit(solution)/shard_map/ppermute | solution.py:49
  14.6 1.2 collective-permute-start.2
  15.8 1.4 collective-permute-start.7
  17.3 2.9 %collective-permute-done.rest_1_ = bf16[64,1280]{1,0:T(8,128)(2,1)S(1)} collective-permute-done((bf16[64,1280]{1,0:T(8,128)(2,1)S(1)}, bf16[64,1280]{1,0:T(8,128)(2,1)S(1)}, u32[]{:S(2)}, u32[]{:S(2)}) %collective-permute-start) | collective-permute-done | bytes 163872 | tf_op jit(solution)/shard_map/ppermute | solution.py:49
  20.2 3.7 %collective-permute-done.1.rest_2_ = bf16[64,1280]{1,0:T(8,128)(2,1)S(1)} collective-permute-done((bf16[64,1280]{1,0:T(8,128)(2,1)S(1)}, bf16[64,1280]{1,0:T(8,128)(2,1)S(1)}, u32[]{:S(2)}, u32[]{:S(2)}) %collective-permute-start.1) | collective-permute-done | bytes 163872 | tf_op jit(solution)/shard_map/ppermute | solution.py:49
  25.0 7.4 %all-to-all-start.1 = ((f32[8,2,128]{2,1,0:T(2,128)}), f32[8,2,128]{2,1,0:T(2,128)S(1)}, u32[]{:S(2)}, u32[]{:S(2)}) async-start(f32[8,2,128]{2,1,0:T(2,128)} %broadcast_in_dim.68), calls=%async_computation.1 | async-start | bytes 16384 | tf_op jit(solution)/shard_map/all_to_all | solution.py:37
  32.6 1.4 reshape.170
  33.9 2.6 %copy.91 = f32[4,4,2,24,2,64]{5,4,3,2,1,0:T(2,128)} copy(f32[4,4,2,24,2,64]{5,2,3,1,4,0:T(2,128)} %bitcast.59) | data formatting | bytes 786432 | tf_op jit(solution)/shard_map/convert_element_type | solution.py:431
  36.6 1.6 reshape.169.rest_4_
  38.2 1.6 collective-permute-start.3
  40.9 1.0 collective-permute-start.6
  43.0 1.7 shard_map.114
  44.7 1.0 copy-done
  45.6 6.3 %all-to-all-start.2 = ((f32[8,24,1280]{2,1,0:T(8,128)}), f32[8,24,1280]{2,1,0:T(8,128)S(1)}, u32[]{:S(2)}, u32[]{:S(2)}) async-start(f32[8,24,1280]{2,1,0:T(8,128)} %bitcast.47), calls=%async_computation.2 | async-start | bytes 1966080 | tf_op jit(solution)/shard_map/all_to_all | solution.py:37
  51.9 1.8 copy.88
  53.7 1.7 reshape.155
  56.1 1.0 broadcast_subtract_fusion
  59.2 1.4 copy.95
  63.8 0.9 constant_dynamic-slice_fusion.2
  65.0 2.4 %collective-permute-done.9.rest_4_ = bf16[32,2,128,128]{3,2,1,0:T(8,128)(2,1)S(1)} collective-permute-done((bf16[32,2,128,128]{3,2,1,0:T(8,128)(2,1)}, bf16[32,2,128,128]{3,2,1,0:T(8,128)(2,1)S(1)}, u32[]{:S(2)}, u32[]{:S(2)}) %collective-permute-start.9) | collective-permute-done | bytes 2097184 | tf_op jit(solution)/shard_map/ppermute | solution.py:49
  67.4 1.0 slice.61
  68.4 2.6 %collective-permute-start.10 = (bf16[16,2,128,128]{3,2,1,0:T(8,128)(2,1)}, bf16[16,2,128,128]{3,2,1,0:T(8,128)(2,1)}, u32[]{:S(2)}, u32[]{:S(2)}) collective-permute-start(bf16[16,2,128,128]{3,2,1,0:T(8,128)(2,1)} %slice.61), channel_id=1, source_target_pairs={{0,6},{2,0},{4,2},{6,4},{1,7},{3,1},{5,3},{7,5},{8,14},{10,8},{12,... | collective-permute-start | bytes 3145736 | tf_op jit(solution)/shard_map/ppermute | solution.py:49
  71.1 2.3 %slice.60 = bf16[16,2,128,128]{3,2,1,0:T(8,128)(2,1)} slice(bf16[32,2,128,128]{3,2,1,0:T(8,128)(2,1)} %collective-permute-done.7.rest_2_), slice={[0:16], [0:2], [0:128], [0:128]} | slice | bytes 2097152 | tf_op jit(solution)/shard_map/slice | solution.py:426
  76.3 5.1 %shard_map.113 = (s32[256]{0:T(256)S(1)}, s32[256]{0:T(256)S(1)}, s32[2]{0:T(128)S(1)}) custom-call(s32[4]{0:T(128)S(1)} %pad_add_fusion.place_ref, s32[1536]{0:T(1024)S(1)} %reshape.154.parent_ref, s32[4096]{0:T(1024)S(1)} %bitcast.58, s32[64]{0:T(128)S(1)} %reshape.158.length_ref), custom_call_target="tpu_custom_call" | custom-call | tf_op jit(solution)/shard_map/pallas_call | solution.py:397
  83.7 20.7 %all_to_all.35.q_ref = bf16[8,192,128]{2,1,0:T(8,128)(2,1)S(1)} all-to-all(bf16[8,192,128]{2,1,0:T(8,128)(2,1)S(1)} %get-tuple-element.48), channel_id=1, replica_groups=mesh['kv'=4,'z'=8,'x'=4,'core'=2] {'z'}, dimensions={0} | all-to-all | bytes 786432 | tf_op jit(solution)/shard_map/all_to_all | solution.py:37
  104.4 2.2 %collective-permute-start.11 = (bf16[16,2,128,128]{3,2,1,0:T(8,128)(2,1)}, bf16[16,2,128,128]{3,2,1,0:T(8,128)(2,1)}, u32[]{:S(2)}, u32[]{:S(2)}) collective-permute-start(bf16[16,2,128,128]{3,2,1,0:T(8,128)(2,1)} %collective-permute-done.8.rest_0_), channel_id=1, source_target_pairs={{0,1},{1,0},{2,3},{3,2},{4,5},{5,4},{6,7},{7,6},{8,9},{9,8},{10,11... | collective-permute-start | bytes 3145736 | tf_op jit(solution)/shard_map/ppermute | solution.py:45
  109.7 1.6 copy-done.1
  112.5 5.2 %shard_map.116 = (f32[8,192,128]{2,1,0:T(8,128)S(1)}, f32[8,192,128]{2,1,0:T(8,128)S(1)}, f32[8,192,128]{2,1,0:T(8,128)S(1)}) custom-call(s32[256]{0:T(256)S(1)} %copy-done.14, s32[2]{0:T(128)S(1)} %copy-done.9, s32[64]{0:T(128)S(1)} %reshape.158.length_ref, bf16[8,192,128]{2,1,0:T(8,128)(2,1)S(1)} %all_to_all.35.q_ref, ...), custom_call_target="tpu_custom_call" | custom-call | flops 1 | bytes 1 | tf_op jit(solution)/shard_map/pallas_call | solution.py:483
  117.8 3.0 %shard_map.117 = bf16[8,216,128]{2,1,0:T(8,128)(2,1)} custom-call(s32[256]{0:T(256)S(1)} %copy-done.12, s32[2]{0:T(128)S(1)} %copy-done.10, s32[64]{0:T(128)S(1)} %reshape.158.length_ref, bf16[8,192,128]{2,1,0:T(8,128)(2,1)S(1)} %all_to_all.35.q_ref, s32[8,24,128]{2,1,0:T(8,128)S(1)} %broadcast_in_dim.77.root_ref, ...), custom_call_target="tpu_custom_call" | custom-call | tf_op jit(solution)/shard_map/pallas_call | solution.py:492
  120.7 3.5 %all-to-all-start.4 = ((bf16[8,216,128]{2,1,0:T(8,128)(2,1)}), bf16[8,216,128]{2,1,0:T(8,128)(2,1)S(1)}, u32[]{:S(2)}, u32[]{:S(2)}) async-start(bf16[8,216,128]{2,1,0:T(8,128)(2,1)} %shard_map.117), calls=%async_computation.4 | async-start | bytes 884736 | tf_op jit(solution)/shard_map/all_to_all | solution.py:37
  124.2 1.7 collective-permute-start.16
  125.9 3.7 %collective-permute-start.17 = (bf16[64,1024]{1,0:T(8,128)(2,1)S(1)}, bf16[64,1024]{1,0:T(8,128)(2,1)S(1)}, u32[]{:S(2)}, u32[]{:S(2)}) collective-permute-start(bf16[64,1024]{1,0:T(8,128)(2,1)S(1)} %bitcast.54), channel_id=1, source_target_pairs={{0,4},{2,6},{4,0},{6,2},{1,5},{3,7},{5,1},{7,3},{8,12},{10,14},{12... | collective-permute-start | bytes 393224 | tf_op jit(solution)/shard_map/ppermute | solution.py:49
  129.9 0.9 collective-permute-start.19
  130.8 2.2 %collective-permute-start.20 = (bf16[64,1024]{1,0:T(8,128)(2,1)S(1)}, bf16[64,1024]{1,0:T(8,128)(2,1)S(1)}, u32[]{:S(2)}, u32[]{:S(2)}) collective-permute-start(bf16[64,1024]{1,0:T(8,128)(2,1)S(1)} %collective-permute-done.16.rest_1_), channel_id=1, source_target_pairs={{0,1},{1,0},{2,3},{3,2},{4,5},{5,4},{6,7},{7,6},{8,9},{9,8},{10,11... | collective-permute-start | bytes 393224 | tf_op jit(solution)/shard_map/ppermute | solution.py:45
  133.0 3.5 %collective-permute-done.17.rest_2_ = bf16[64,1024]{1,0:T(8,128)(2,1)S(1)} collective-permute-done((bf16[64,1024]{1,0:T(8,128)(2,1)S(1)}, bf16[64,1024]{1,0:T(8,128)(2,1)S(1)}, u32[]{:S(2)}, u32[]{:S(2)}) %collective-permute-start.17) | collective-permute-done | bytes 131104 | tf_op jit(solution)/shard_map/ppermute | solution.py:49
  138.8 20.7 %all_to_all.36 = bf16[8,24,1024]{2,1,0:T(8,128)(2,1)S(1)} all-to-all(bf16[8,24,1024]{2,1,0:T(8,128)(2,1)S(1)} %shard_map.118), channel_id=1, replica_groups=mesh['kv'=4,'z'=8,'x'=4,'core'=2] {'z'}, dimensions={0} | all-to-all | bytes 786432 | tf_op jit(solution)/shard_map/all_to_all | solution.py:37
  159.4 1.2 shard_map.119
  160.7 1.4 collective-permute-start.23
  162.0 2.6 %collective-permute-start.24 = (f32[4,48,128]{2,1,0:T(8,128)S(1)}, f32[4,48,128]{2,1,0:T(8,128)S(1)}, u32[]{:S(2)}, u32[]{:S(2)}) collective-permute-start(f32[4,48,128]{2,1,0:T(8,128)S(1)} %get-tuple-element.72), channel_id=1, source_target_pairs={{0,128},{64,192},{128,0},{192,64},{1,129},{65,193},{129,1},{193,65... | collective-permute-start | bytes 294920 | tf_op jit(solution)/shard_map/ppermute | solution.py:526
  164.7 1.1 collective-permute-start.25
  165.7 2.3 %collective-permute-done.24.rest_2_ = f32[4,48,128]{2,1,0:T(8,128)S(1)} collective-permute-done((f32[4,48,128]{2,1,0:T(8,128)S(1)}, f32[4,48,128]{2,1,0:T(8,128)S(1)}, u32[]{:S(2)}, u32[]{:S(2)}) %collective-permute-start.24) | collective-permute-done | bytes 98336 | tf_op jit(solution)/shard_map/ppermute | solution.py:526
  168.0 1.3 collective-permute-done.25.rest_3_
  169.4 1.3 shard_map.120
  170.7 8.1 %all-to-all-start.6 = ((bf16[32,24,128]{2,1,0:T(8,128)(2,1)}), bf16[32,24,128]{2,1,0:T(8,128)(2,1)S(1)}, u32[]{:S(2)}, u32[]{:S(2)}) async-start(bf16[32,24,128]{2,1,0:T(8,128)(2,1)} %bitcast.26), calls=%async_computation.6 | async-start | bytes 393216 | tf_op jit(solution)/shard_map/all_to_all | solution.py:37
  179.4 7.6 %all-to-all-done.6 = bf16[32,24,128]{2,1,0:T(8,128)(2,1)S(1)} async-done(((bf16[32,24,128]{2,1,0:T(8,128)(2,1)}), bf16[32,24,128]{2,1,0:T(8,128)(2,1)S(1)}, u32[]{:S(2)}, u32[]{:S(2)}) %all-to-all-start.6) | async-done | bytes 196640 | tf_op jit(solution)/shard_map/all_to_all | solution.py:37
  (142 shorter events, 25.5 us)
Async XLA Ops:
  0.6 10.0 %copy-start.16 = (bf16[64,1024]{1,0:T(8,128)(2,1)S(1)}, bf16[64,1024]{1,0:T(8,128)(2,1)}, u32[]{:S(2)}) copy-start(bf16[64,1024]{1,0:T(8,128)(2,1)} %param.12) | copy-start | bytes 393220
  0.6 10.0 %copy-start.21 = (bf16[64,128]{1,0:T(8,128)(2,1)S(1)}, bf16[64,128]{1,0:T(8,128)(2,1)}, u32[]{:S(2)}) copy-start(bf16[64,128]{1,0:T(8,128)(2,1)} %param.13) | copy-start | bytes 49156
  0.7 10.0 %copy-start.20 = (bf16[64,128]{1,0:T(8,128)(2,1)S(1)}, bf16[64,128]{1,0:T(8,128)(2,1)}, u32[]{:S(2)}) copy-start(bf16[64,128]{1,0:T(8,128)(2,1)} %param.14) | copy-start | bytes 49156
  4.1 19.8 %all-to-all-start = ((bf16[8,104,128]{2,1,0:T(8,128)(2,1)}), bf16[8,104,128]{2,1,0:T(8,128)(2,1)S(1)}, u32[]{:S(2)}, u32[]{:S(2)}) async-start(bf16[8,104,128]{2,1,0:T(8,128)(2,1)} %pad_maximum_fusion), calls=%async_computation | async-start | bytes 425984 | tf_op jit(solution)/shard_map/all_to_all | solution.py:37
  10.7 9.5 %collective-permute-start = (bf16[64,1280]{1,0:T(8,128)(2,1)S(1)}, bf16[64,1280]{1,0:T(8,128)(2,1)S(1)}, u32[]{:S(2)}, u32[]{:S(2)}) collective-permute-start(bf16[64,1280]{1,0:T(8,128)(2,1)S(1)} %pad_maximum_fusion.1.rest_0_), channel_id=1, source_target_pairs={{0,2},{2,4},{4,6},{6,0},{1,3},{3,5},{5,7},{7,1},{8,10},{10,12},{12... | collective-permute-start | bytes 491528 | tf_op jit(solution)/shard_map/ppermute | solution.py:49
  12.1 11.7 %collective-permute-start.1 = (bf16[64,1280]{1,0:T(8,128)(2,1)S(1)}, bf16[64,1280]{1,0:T(8,128)(2,1)S(1)}, u32[]{:S(2)}, u32[]{:S(2)}) collective-permute-start(bf16[64,1280]{1,0:T(8,128)(2,1)S(1)} %pad_maximum_fusion.1.rest_0_), channel_id=1, source_target_pairs={{0,4},{2,6},{4,0},{6,2},{1,5},{3,7},{5,1},{7,3},{8,12},{10,14},{12... | collective-permute-start | bytes 491528 | tf_op jit(solution)/shard_map/ppermute | solution.py:49
  14.6 9.3 %collective-permute-start.2 = (bf16[64,1280]{1,0:T(8,128)(2,1)S(1)}, bf16[64,1280]{1,0:T(8,128)(2,1)S(1)}, u32[]{:S(2)}, u32[]{:S(2)}) collective-permute-start(bf16[64,1280]{1,0:T(8,128)(2,1)S(1)} %pad_maximum_fusion.1.rest_0_), channel_id=1, source_target_pairs={{0,6},{2,0},{4,2},{6,4},{1,7},{3,1},{5,3},{7,5},{8,14},{10,8},{12,... | collective-permute-start | bytes 491528 | tf_op jit(solution)/shard_map/ppermute | solution.py:49
  15.7 51.7 %collective-permute-start.9 = (bf16[32,2,128,128]{3,2,1,0:T(8,128)(2,1)}, bf16[32,2,128,128]{3,2,1,0:T(8,128)(2,1)S(1)}, u32[]{:S(2)}, u32[]{:S(2)}) collective-permute-start(bf16[32,2,128,128]{3,2,1,0:T(8,128)(2,1)} %bitcast.48), channel_id=1, source_target_pairs={{0,6},{2,0},{4,2},{6,4},{1,7},{3,1},{5,3},{7,5},{8,14},{10,8},{12,... | collective-permute-start | bytes 6291464 | tf_op jit(solution)/shard_map/ppermute | solution.py:49
  15.8 55.3 %collective-permute-start.7 = (bf16[32,2,128,128]{3,2,1,0:T(8,128)(2,1)}, bf16[32,2,128,128]{3,2,1,0:T(8,128)(2,1)}, u32[]{:S(2)}, u32[]{:S(2)}) collective-permute-start(bf16[32,2,128,128]{3,2,1,0:T(8,128)(2,1)} %bitcast.49), channel_id=1, source_target_pairs={{0,2},{2,4},{4,6},{6,0},{1,3},{3,5},{5,7},{7,1},{8,10},{10,12},{12... | collective-permute-start | bytes 6291464 | tf_op jit(solution)/shard_map/ppermute | solution.py:49
  25.0 15.4 %all-to-all-start.1 = ((f32[8,2,128]{2,1,0:T(2,128)}), f32[8,2,128]{2,1,0:T(2,128)S(1)}, u32[]{:S(2)}, u32[]{:S(2)}) async-start(f32[8,2,128]{2,1,0:T(2,128)} %broadcast_in_dim.68), calls=%async_computation.1 | async-start | bytes 16384 | tf_op jit(solution)/shard_map/all_to_all | solution.py:37
  38.2 2.7 %collective-permute-start.3 = (bf16[64,1280]{1,0:T(8,128)(2,1)S(1)}, bf16[64,1280]{1,0:T(8,128)(2,1)S(1)}, u32[]{:S(2)}, u32[]{:S(2)}) collective-permute-start(bf16[64,1280]{1,0:T(8,128)(2,1)S(1)} %pad_maximum_fusion.1.rest_0_), channel_id=1, source_target_pairs={{0,1},{1,0},{2,3},{3,2},{4,5},{5,4},{6,7},{7,6},{8,9},{9,8},{10,11... | collective-permute-start | bytes 491528 | tf_op jit(solution)/shard_map/ppermute | solution.py:45
  39.9 2.2 %collective-permute-start.4 = (bf16[64,1280]{1,0:T(8,128)(2,1)S(1)}, bf16[64,1280]{1,0:T(8,128)(2,1)S(1)}, u32[]{:S(2)}, u32[]{:S(2)}) collective-permute-start(bf16[64,1280]{1,0:T(8,128)(2,1)S(1)} %collective-permute-done.rest_1_), channel_id=1, source_target_pairs={{0,1},{1,0},{2,3},{3,2},{4,5},{5,4},{6,7},{7,6},{8,9},{9,8},{10,11... | collective-permute-start | bytes 491528 | tf_op jit(solution)/shard_map/ppermute | solution.py:45
  40.0 2.2 %collective-permute-start.5 = (bf16[64,1280]{1,0:T(8,128)(2,1)S(1)}, bf16[64,1280]{1,0:T(8,128)(2,1)}, u32[]{:S(2)}, u32[]{:S(2)}) collective-permute-start(bf16[64,1280]{1,0:T(8,128)(2,1)S(1)} %collective-permute-done.1.rest_2_), channel_id=1, source_target_pairs={{0,1},{1,0},{2,3},{3,2},{4,5},{5,4},{6,7},{7,6},{8,9},{9,8},{10,11... | collective-permute-start | bytes 491528 | tf_op jit(solution)/shard_map/ppermute | solution.py:45
  40.9 2.1 %collective-permute-start.6 = (bf16[64,1280]{1,0:T(8,128)(2,1)S(1)}, bf16[64,1280]{1,0:T(8,128)(2,1)S(1)}, u32[]{:S(2)}, u32[]{:S(2)}) collective-permute-start(bf16[64,1280]{1,0:T(8,128)(2,1)S(1)} %collective-permute-done.2.rest_3_), channel_id=1, source_target_pairs={{0,1},{1,0},{2,3},{3,2},{4,5},{5,4},{6,7},{7,6},{8,9},{9,8},{10,11... | collective-permute-start | bytes 491528 | tf_op jit(solution)/shard_map/ppermute | solution.py:45
  42.1 13.3 %copy-start.19 = (s32[3,512]{1,0:T(4,128)S(1)}, s32[3,512]{1,0:T(4,128)}, u32[]{:S(2)}) copy-start(s32[3,512]{1,0:T(4,128)} %param.19) | copy-start | bytes 18436
  42.1 67.4 %collective-permute-start.13 = (bf16[32,2,128,128]{3,2,1,0:T(8,128)(2,1)}, bf16[32,2,128,128]{3,2,1,0:T(8,128)(2,1)}, u32[]{:S(2)}, u32[]{:S(2)}) collective-permute-start(bf16[32,2,128,128]{3,2,1,0:T(8,128)(2,1)} %bitcast.50), channel_id=1, source_target_pairs={{0,1},{1,0},{2,3},{3,2},{4,5},{5,4},{6,7},{7,6},{8,9},{9,8},{10,11... | collective-permute-start | bytes 6291464 | tf_op jit(solution)/shard_map/ppermute | solution.py:45
  44.7 1.0 copy-start
  45.6 36.7 %all-to-all-start.2 = ((f32[8,24,1280]{2,1,0:T(8,128)}), f32[8,24,1280]{2,1,0:T(8,128)S(1)}, u32[]{:S(2)}, u32[]{:S(2)}) async-start(f32[8,24,1280]{2,1,0:T(8,128)} %bitcast.47), calls=%async_computation.2 | async-start | bytes 1966080 | tf_op jit(solution)/shard_map/all_to_all | solution.py:37
  62.9 2.1 %copy-start.17 = (s32[64,8]{0,1:T(8,128)}, s32[64,8]{0,1:T(8,128)S(1)}, u32[]{:S(2)}) copy-start(s32[64,8]{0,1:T(8,128)S(1)} %select_reduce_fusion.1) | copy-start | bytes 6148
  63.6 1.4 copy-start.18
  65.0 9.7 %copy-start.22 = (s32[512]{0:T(512)S(1)}, s32[512]{0:T(512)}, u32[]{:S(2)}) copy-start(s32[512]{0:T(512)} %param.17) | copy-start | bytes 6148
  68.4 36.0 %collective-permute-start.10 = (bf16[16,2,128,128]{3,2,1,0:T(8,128)(2,1)}, bf16[16,2,128,128]{3,2,1,0:T(8,128)(2,1)}, u32[]{:S(2)}, u32[]{:S(2)}) collective-permute-start(bf16[16,2,128,128]{3,2,1,0:T(8,128)(2,1)} %slice.61), channel_id=1, source_target_pairs={{0,6},{2,0},{4,2},{6,4},{1,7},{3,1},{5,3},{7,5},{8,14},{10,8},{12,... | collective-permute-start | bytes 3145736 | tf_op jit(solution)/shard_map/ppermute | solution.py:49
  73.4 31.0 %collective-permute-start.8 = (bf16[16,2,128,128]{3,2,1,0:T(8,128)(2,1)}, bf16[16,2,128,128]{3,2,1,0:T(8,128)(2,1)}, u32[]{:S(2)}, u32[]{:S(2)}) collective-permute-start(bf16[16,2,128,128]{3,2,1,0:T(8,128)(2,1)} %slice.60), channel_id=1, source_target_pairs={{0,2},{2,4},{4,6},{6,0},{1,3},{3,5},{5,7},{7,1},{8,10},{10,12},{12... | collective-permute-start | bytes 3145736 | tf_op jit(solution)/shard_map/ppermute | solution.py:49
  73.4 36.1 %collective-permute-start.14 = (bf16[32,2,128,128]{3,2,1,0:T(8,128)(2,1)}, bf16[32,2,128,128]{3,2,1,0:T(8,128)(2,1)}, u32[]{:S(2)}, u32[]{:S(2)}) collective-permute-start(bf16[32,2,128,128]{3,2,1,0:T(8,128)(2,1)} %collective-permute-done.7.rest_2_), channel_id=1, source_target_pairs={{0,1},{1,0},{2,3},{3,2},{4,5},{5,4},{6,7},{7,6},{8,9},{9,8},{10,11... | collective-permute-start | bytes 6291464 | tf_op jit(solution)/shard_map/ppermute | solution.py:45
  74.2 35.4 %collective-permute-start.15 = (bf16[32,2,128,128]{3,2,1,0:T(8,128)(2,1)S(1)}, bf16[32,2,128,128]{3,2,1,0:T(8,128)(2,1)}, u32[]{:S(2)}, u32[]{:S(2)}) collective-permute-start(bf16[32,2,128,128]{3,2,1,0:T(8,128)(2,1)S(1)} %collective-permute-done.9.rest_4_), channel_id=1, source_target_pairs={{0,1},{1,0},{2,3},{3,2},{4,5},{5,4},{6,7},{7,6},{8,9},{9,8},{10,11... | collective-permute-start | bytes 6291464 | tf_op jit(solution)/shard_map/ppermute | solution.py:45
  81.5 0.9 copy-start.13
  83.7 20.8 %copy-start.3 = (f32[6,8,128]{2,1,0:T(8,128)}, f32[6,8,128]{2,1,0:T(8,128)S(1)}, u32[]{:S(2)}) copy-start(f32[6,8,128]{2,1,0:T(8,128)S(1)} %get-tuple-element.61.v_ref) | copy-start | bytes 73732
  83.7 20.7 %copy-start.5 = (f32[6,8,128]{2,1,0:T(8,128)}, f32[6,8,128]{2,1,0:T(8,128)S(1)}, u32[]{:S(2)}) copy-start(f32[6,8,128]{2,1,0:T(8,128)S(1)} %get-tuple-element.60.k_ref) | copy-start | bytes 73732
  104.4 13.2 %collective-permute-start.11 = (bf16[16,2,128,128]{3,2,1,0:T(8,128)(2,1)}, bf16[16,2,128,128]{3,2,1,0:T(8,128)(2,1)}, u32[]{:S(2)}, u32[]{:S(2)}) collective-permute-start(bf16[16,2,128,128]{3,2,1,0:T(8,128)(2,1)} %collective-permute-done.8.rest_0_), channel_id=1, source_target_pairs={{0,1},{1,0},{2,3},{3,2},{4,5},{5,4},{6,7},{7,6},{8,9},{9,8},{10,11... | collective-permute-start | bytes 3145736 | tf_op jit(solution)/shard_map/ppermute | solution.py:45
  106.7 11.0 %collective-permute-start.12 = (bf16[16,2,128,128]{3,2,1,0:T(8,128)(2,1)}, bf16[16,2,128,128]{3,2,1,0:T(8,128)(2,1)}, u32[]{:S(2)}, u32[]{:S(2)}) collective-permute-start(bf16[16,2,128,128]{3,2,1,0:T(8,128)(2,1)} %collective-permute-done.10.rest_1_), channel_id=1, source_target_pairs={{0,1},{1,0},{2,3},{3,2},{4,5},{5,4},{6,7},{7,6},{8,9},{9,8},{10,11... | collective-permute-start | bytes 3145736 | tf_op jit(solution)/shard_map/ppermute | solution.py:45
  109.7 1.6 copy-start.1
  112.5 5.2 %copy-start.10 = (s32[2]{0:T(128)S(1)}, s32[2]{0:T(128)}, u32[]{:S(2)}) copy-start(s32[2]{0:T(128)} %copy-done.8) | copy-start | bytes 28
  112.5 5.2 %copy-start.12 = (s32[256]{0:T(256)S(1)}, s32[256]{0:T(256)}, u32[]{:S(2)}) copy-start(s32[256]{0:T(256)} %copy-done.11) | copy-start | bytes 3076
  117.7 6.5 %copy-start.2 = (bf16[1024,64]{0,1:T(8,128)(2,1)S(1)}, bf16[1024,64]{0,1:T(8,128)(2,1)}, u32[]{:S(2)}) copy-start(bf16[1024,64]{0,1:T(8,128)(2,1)} %param.15) | copy-start | bytes 393220
  117.7 20.5 %copy-start.4 = (f32[6,8,128]{2,1,0:T(8,128)S(1)}, f32[6,8,128]{2,1,0:T(8,128)}, u32[]{:S(2)}) copy-start(f32[6,8,128]{2,1,0:T(8,128)} %copy-done.3) | copy-start | bytes 73732
  117.7 20.5 %copy-start.6 = (f32[6,8,128]{2,1,0:T(8,128)S(1)}, f32[6,8,128]{2,1,0:T(8,128)}, u32[]{:S(2)}) copy-start(f32[6,8,128]{2,1,0:T(8,128)} %copy-done.5) | copy-start | bytes 73732
  120.7 17.5 %all-to-all-start.4 = ((bf16[8,216,128]{2,1,0:T(8,128)(2,1)}), bf16[8,216,128]{2,1,0:T(8,128)(2,1)S(1)}, u32[]{:S(2)}, u32[]{:S(2)}) async-start(bf16[8,216,128]{2,1,0:T(8,128)(2,1)} %shard_map.117), calls=%async_computation.4 | async-start | bytes 884736 | tf_op jit(solution)/shard_map/all_to_all | solution.py:37
  124.2 6.6 %collective-permute-start.16 = (bf16[64,1024]{1,0:T(8,128)(2,1)S(1)}, bf16[64,1024]{1,0:T(8,128)(2,1)S(1)}, u32[]{:S(2)}, u32[]{:S(2)}) collective-permute-start(bf16[64,1024]{1,0:T(8,128)(2,1)S(1)} %bitcast.53), channel_id=1, source_target_pairs={{0,2},{2,4},{4,6},{6,0},{1,3},{3,5},{5,7},{7,1},{8,10},{10,12},{12... | collective-permute-start | bytes 393224 | tf_op jit(solution)/shard_map/ppermute | solution.py:49
  125.9 10.6 %collective-permute-start.17 = (bf16[64,1024]{1,0:T(8,128)(2,1)S(1)}, bf16[64,1024]{1,0:T(8,128)(2,1)S(1)}, u32[]{:S(2)}, u32[]{:S(2)}) collective-permute-start(bf16[64,1024]{1,0:T(8,128)(2,1)S(1)} %bitcast.54), channel_id=1, source_target_pairs={{0,4},{2,6},{4,0},{6,2},{1,5},{3,7},{5,1},{7,3},{8,12},{10,14},{12... | collective-permute-start | bytes 393224 | tf_op jit(solution)/shard_map/ppermute | solution.py:49
  129.6 7.2 %collective-permute-start.18 = (bf16[64,1024]{1,0:T(8,128)(2,1)S(1)}, bf16[64,1024]{1,0:T(8,128)(2,1)S(1)}, u32[]{:S(2)}, u32[]{:S(2)}) collective-permute-start(bf16[64,1024]{1,0:T(8,128)(2,1)S(1)} %bitcast.55), channel_id=1, source_target_pairs={{0,6},{2,0},{4,2},{6,4},{1,7},{3,1},{5,3},{7,5},{8,14},{10,8},{12,... | collective-permute-start | bytes 393224 | tf_op jit(solution)/shard_map/ppermute | solution.py:49
  129.9 7.1 %collective-permute-start.19 = (bf16[64,1024]{1,0:T(8,128)(2,1)S(1)}, bf16[64,1024]{1,0:T(8,128)(2,1)S(1)}, u32[]{:S(2)}, u32[]{:S(2)}) collective-permute-start(bf16[64,1024]{1,0:T(8,128)(2,1)S(1)} %bitcast.56), channel_id=1, source_target_pairs={{0,1},{1,0},{2,3},{3,2},{4,5},{5,4},{6,7},{7,6},{8,9},{9,8},{10,11... | collective-permute-start | bytes 393224 | tf_op jit(solution)/shard_map/ppermute | solution.py:45
  130.8 6.2 %collective-permute-start.20 = (bf16[64,1024]{1,0:T(8,128)(2,1)S(1)}, bf16[64,1024]{1,0:T(8,128)(2,1)S(1)}, u32[]{:S(2)}, u32[]{:S(2)}) collective-permute-start(bf16[64,1024]{1,0:T(8,128)(2,1)S(1)} %collective-permute-done.16.rest_1_), channel_id=1, source_target_pairs={{0,1},{1,0},{2,3},{3,2},{4,5},{5,4},{6,7},{7,6},{8,9},{9,8},{10,11... | collective-permute-start | bytes 393224 | tf_op jit(solution)/shard_map/ppermute | solution.py:45
  136.5 1.4 collective-permute-start.21
  136.8 1.3 collective-permute-start.22
  160.7 5.1 %collective-permute-start.23 = (f32[4,48,128]{2,1,0:T(8,128)S(1)}, f32[4,48,128]{2,1,0:T(8,128)S(1)}, u32[]{:S(2)}, u32[]{:S(2)}) collective-permute-start(f32[4,48,128]{2,1,0:T(8,128)S(1)} %get-tuple-element.71), channel_id=1, source_target_pairs={{0,64},{64,128},{128,192},{192,0},{1,65},{65,129},{129,193},{193,1... | collective-permute-start | bytes 294920 | tf_op jit(solution)/shard_map/ppermute | solution.py:526
  162.0 6.0 %collective-permute-start.24 = (f32[4,48,128]{2,1,0:T(8,128)S(1)}, f32[4,48,128]{2,1,0:T(8,128)S(1)}, u32[]{:S(2)}, u32[]{:S(2)}) collective-permute-start(f32[4,48,128]{2,1,0:T(8,128)S(1)} %get-tuple-element.72), channel_id=1, source_target_pairs={{0,128},{64,192},{128,0},{192,64},{1,129},{65,193},{129,1},{193,65... | collective-permute-start | bytes 294920 | tf_op jit(solution)/shard_map/ppermute | solution.py:526
  164.7 4.7 %collective-permute-start.25 = (f32[4,48,128]{2,1,0:T(8,128)S(1)}, f32[4,48,128]{2,1,0:T(8,128)S(1)}, u32[]{:S(2)}, u32[]{:S(2)}) collective-permute-start(f32[4,48,128]{2,1,0:T(8,128)S(1)} %get-tuple-element.73), channel_id=1, source_target_pairs={{0,192},{64,0},{128,64},{192,128},{1,193},{65,1},{129,65},{193,129... | collective-permute-start | bytes 294920 | tf_op jit(solution)/shard_map/ppermute | solution.py:526
  170.7 16.4 %all-to-all-start.6 = ((bf16[32,24,128]{2,1,0:T(8,128)(2,1)}), bf16[32,24,128]{2,1,0:T(8,128)(2,1)S(1)}, u32[]{:S(2)}, u32[]{:S(2)}) async-start(bf16[32,24,128]{2,1,0:T(8,128)(2,1)} %bitcast.26), calls=%async_computation.6 | async-start | bytes 393216 | tf_op jit(solution)/shard_map/all_to_all | solution.py:37
  (6 other events, 4.1 us)
